TPU v7x, 128 devices: a whole 4x4x4 slice. The times are simulated.
128 devices in a mesh: dp: 16 (over z, y_hi, core), seq: 8 (over x, y_lo).
Axes of the slice: x: 4, y: 4 (y_hi: 2, y_lo: 2; y = y_hi * 2 + y_lo), z: 4, core: 2. Of those that a mesh axis runs over, the one named last changes fastest.
Arguments:
- streams: bfloat16 [3, 16, 2048, 512], P(None, 'dp', 'seq'), may hold values from -6 to 6
- short_filter: float32 [3, 3, 512], replicated, may hold values from -3 to 3
- long_filter: float32 [2048, 512], P('seq'), may hold values from -4 to 4
- skip_gain: float32 [512], replicated, may hold values from -4 to 4
- out_weight: bfloat16 [512, 4096], replicated, may hold values from -0.25 to 0.25
- out_grad: bfloat16 [16, 2048, 4096], P('dp', 'seq'), may hold values from -6 to 6
Outputs:
- layer_out: bfloat16 [16, 2048, 4096], P('dp', 'seq')
- grad_streams: bfloat16 [3, 16, 2048, 512], P(None, 'dp', 'seq')
- grad_filter: float32 [2048, 512], P('seq')
- grad_out_weight: float32 [512, 4096], replicated
All inputs are finite; a program needn't handle non-finite values.
Results may differ from a plain program's by a relative error of at most 0.0049.
Values may be sent and summed in bfloat16 or wider, within the bound.
No kernel may reach another device: no remote copies, remote signals or barrier semaphores. Data moves between devices by JAX's collectives and lax.ppermute only.
A program may use at most 128 MiB of HBM per device.

v0:
```python
import math

import jax
import jax.numpy as jnp
from jax import lax
from jax.sharding import PartitionSpec as P


def swapped(array, axis, apart):
    return lax.ppermute(array, axis, [(i, i ^ 1 << apart) for i in range(lax.axis_size(axis))])


def passed_along(block, axis, distance):
    devices = range(lax.axis_size(axis))
    route = [(i - distance, i) for i in devices if i - distance in devices]
    return lax.ppermute(block, axis, route)


def spectral_table(length_here):
    row_index = lax.broadcasted_iota(jnp.int32, (length_here, length_here), 0)
    col_index = lax.broadcasted_iota(jnp.int32, (length_here, length_here), 1)
    phase_angle = (row_index * col_index % length_here).astype(jnp.float32) * (
        2.0 * math.pi / length_here
    )
    return (jnp.cos(phase_angle), jnp.sin(phase_angle))


def table_apply(matrix, values, pattern):
    return jnp.einsum(pattern, matrix, values, precision=lax.Precision.HIGHEST)


def transform_along(real_part, imaginary, direction, pattern):
    cosine, sine_table = spectral_table(real_part.shape[1])
    cosine_real = table_apply(cosine, real_part, pattern)
    cosine_imaginary = table_apply(cosine, imaginary, pattern)
    sine_real = table_apply(sine_table, real_part, pattern)
    sine_imaginary = table_apply(sine_table, imaginary, pattern)
    return (cosine_real - direction * sine_imaginary, cosine_imaginary + direction * sine_real)


def rotate_complex(real_part, imaginary, cosine, sine_value):
    return (
        real_part * cosine - imaginary * sine_value,
        real_part * sine_value + imaginary * cosine,
    )


def branch_angle(start_row, block_rows, total_length):
    positions = start_row + lax.broadcasted_iota(jnp.int32, (1, block_rows, 1), 1)
    return positions.astype(jnp.float32) * (math.pi / total_length)


def padded_branches(signal, start_row, total_length):
    phase_angle = branch_angle(start_row, signal.shape[1], total_length)
    real_part = jnp.concatenate([signal, signal * jnp.cos(phase_angle)], axis=0)
    imaginary = jnp.concatenate([jnp.zeros_like(signal), -signal * jnp.sin(phase_angle)], axis=0)
    return (real_part, imaginary)


def combine_branches(real_part, imaginary, start_row, total_length):
    members = real_part.shape[0] // 2
    phase_angle = branch_angle(start_row, real_part.shape[1], total_length)
    return 0.5 * (
        real_part[:members]
        + jnp.cos(phase_angle) * real_part[members:]
        - jnp.sin(phase_angle) * imaginary[members:]
    )


def level_twiddle(position, split_bit, block_rows):
    half_span = block_rows * (1 << split_bit)
    within = position % (1 << split_bit) * block_rows + lax.broadcasted_iota(
        jnp.int32, (1, block_rows, 1), 1
    )
    phase_angle = within.astype(jnp.float32) * (math.pi / half_span)
    return (jnp.cos(phase_angle), -jnp.sin(phase_angle))


def forward_levels(real_part, imaginary):
    seq_count = lax.axis_size("seq")
    position = lax.axis_index("seq")
    block_rows = real_part.shape[1]
    for split_bit in reversed(range(seq_count.bit_length() - 1)):
        upper_half = position >> split_bit & 1 == 1
        cosine, sine_value = level_twiddle(position, split_bit, block_rows)
        other_real, other_imaginary = swapped((real_part, imaginary), "seq", split_bit)
        turned_real, turned_imaginary = rotate_complex(
            other_real - real_part, other_imaginary - imaginary, cosine, sine_value
        )
        real_part = jnp.where(upper_half, turned_real, real_part + other_real)
        imaginary = jnp.where(upper_half, turned_imaginary, imaginary + other_imaginary)
    return (real_part, imaginary)


def inverse_levels(real_part, imaginary):
    seq_count = lax.axis_size("seq")
    position = lax.axis_index("seq")
    block_rows = real_part.shape[1]
    for split_bit in range(seq_count.bit_length() - 1):
        upper_half = position >> split_bit & 1 == 1
        cosine, sine_value = level_twiddle(position, split_bit, block_rows)
        turned_real, turned_imaginary = rotate_complex(real_part, imaginary, cosine, -sine_value)
        own_real = jnp.where(upper_half, turned_real, real_part)
        own_imaginary = jnp.where(upper_half, turned_imaginary, imaginary)
        other_real, other_imaginary = swapped((own_real, own_imaginary), "seq", split_bit)
        real_part = 0.5 * jnp.where(upper_half, other_real - own_real, other_real + own_real)
        imaginary = 0.5 * jnp.where(
            upper_half, other_imaginary - own_imaginary, other_imaginary + own_imaginary
        )
    return (real_part, imaginary)


def forward_spectrum(signal, start_row, total_length):
    real_part, imaginary = padded_branches(signal, start_row, total_length)
    real_part, imaginary = forward_levels(real_part, imaginary)
    return transform_along(real_part, imaginary, -1.0, "js,msc->mjc")


def inverse_signal(real_part, imaginary, start_row, total_length):
    block_rows = real_part.shape[1]
    real_part, imaginary = transform_along(real_part, imaginary, 1.0, "js,msc->mjc")
    real_part = real_part / block_rows
    imaginary = imaginary / block_rows
    real_part, imaginary = inverse_levels(real_part, imaginary)
    return combine_branches(real_part, imaginary, start_row, total_length)


def on_device(streams, short_filter, long_filter, skip_gain, out_weight, out_grad):
    seq_count = lax.axis_size("seq")
    batch_here = streams.shape[1]
    block_rows = streams.shape[2]
    channels = streams.shape[3]
    total_length = block_rows * seq_count
    start_row = lax.axis_index("seq") * block_rows
    grad_scale = 1.0 / math.sqrt(batch_here * lax.axis_size("dp") * total_length)
    earlier = passed_along(streams[:, :, block_rows - 2 :, :], "seq", 1)
    extended = jnp.concatenate([earlier, streams], axis=2).astype(jnp.float32)
    shortened = sum(
        (
            short_filter[:, offset, None, None, :]
            * extended[:, :, 2 - offset : 2 - offset + block_rows, :]
            for offset in range(3)
        )
    )
    gate_out, gate_in, value_stream = (shortened[0], shortened[1], shortened[2])
    product = gate_in * value_stream
    members = batch_here + 1
    spectrum_real, spectrum_imaginary = forward_spectrum(
        jnp.concatenate([product, long_filter[None]], axis=0), start_row, total_length
    )
    spectrum_real = spectrum_real.reshape(2, members, block_rows, channels)
    spectrum_imaginary = spectrum_imaginary.reshape(2, members, block_rows, channels)
    product_real, product_imaginary = (
        spectrum_real[:, :batch_here],
        spectrum_imaginary[:, :batch_here],
    )
    filter_real, filter_imaginary = (
        spectrum_real[:, batch_here:],
        spectrum_imaginary[:, batch_here:],
    )
    conv_real = product_real * filter_real - product_imaginary * filter_imaginary
    conv_imaginary = product_real * filter_imaginary + product_imaginary * filter_real
    convolved = inverse_signal(
        conv_real.reshape(2 * batch_here, block_rows, channels),
        conv_imaginary.reshape(2 * batch_here, block_rows, channels),
        start_row,
        total_length,
    )
    convolved = convolved + skip_gain * product
    mixed_out = (gate_out * convolved).astype(jnp.bfloat16)
    mixed_flat = mixed_out.reshape(batch_here * block_rows, channels)
    grad_flat = out_grad.reshape(batch_here * block_rows, out_grad.shape[2])
    layer_out = (
        jnp.dot(mixed_flat, out_weight, preferred_element_type=jnp.float32)
        .astype(jnp.bfloat16)
        .reshape(out_grad.shape)
    )
    grad_mixed = lax.dot_general(
        grad_flat, out_weight, (((1,), (1,)), ((), ())), preferred_element_type=jnp.float32
    ).reshape(batch_here, block_rows, channels)
    grad_conv = grad_mixed * gate_out
    grad_gate_out = grad_mixed * convolved
    grad_real, grad_imaginary = forward_spectrum(grad_conv, start_row, total_length)
    grad_real = grad_real.reshape(2, batch_here, block_rows, channels)
    grad_imaginary = grad_imaginary.reshape(2, batch_here, block_rows, channels)
    back_real = filter_real * grad_real + filter_imaginary * grad_imaginary
    back_imaginary = filter_real * grad_imaginary - filter_imaginary * grad_real
    lag_real = jnp.sum(
        product_real * grad_real + product_imaginary * grad_imaginary, axis=1, keepdims=True
    )
    lag_imaginary = jnp.sum(
        product_real * grad_imaginary - product_imaginary * grad_real, axis=1, keepdims=True
    )
    joined_real = jnp.concatenate([back_real, lag_real], axis=1).reshape(
        2 * members, block_rows, channels
    )
    joined_imaginary = jnp.concatenate([back_imaginary, lag_imaginary], axis=1).reshape(
        2 * members, block_rows, channels
    )
    inverse_rows = inverse_signal(joined_real, joined_imaginary, start_row, total_length)
    grad_product = inverse_rows[:batch_here] + skip_gain * grad_conv
    filter_part = inverse_rows[batch_here]
    grad_shortened = jnp.stack([grad_gate_out, grad_product * value_stream, grad_product * gate_in])
    later_rows = passed_along(grad_shortened[:, :, :2, :], "seq", -1)
    extended_grad = jnp.concatenate([grad_shortened, later_rows], axis=2)
    grad_streams = sum(
        (
            short_filter[:, offset, None, None, :]
            * extended_grad[:, :, offset : offset + block_rows, :]
            for offset in range(3)
        )
    )
    partial_value = lax.dot_general(
        mixed_flat, grad_flat, (((0,), (0,)), ((), ())), preferred_element_type=jnp.float32
    )
    grad_out_weight = lax.psum(partial_value, ("dp", "seq")) * grad_scale
    grad_filter = lax.psum(filter_part, "dp") * grad_scale
    return (layer_out, grad_streams.astype(jnp.bfloat16), grad_filter, grad_out_weight)


def solution(mesh):
    placed = (P(None, "dp", "seq", None), P(), P("seq", None), P(), P(), P("dp", "seq", None))
    return jax.shard_map(
        on_device,
        mesh=mesh,
        in_specs=placed,
        out_specs=(P("dp", "seq", None), P(None, "dp", "seq", None), P("seq", None), P()),
        check_vma=False,
    )
```

profile of v0, /device:TPU:1, one launch (start us, length us, event | category | flops | bytes accessed | tf_op | source)
XLA Modules:
  0.0 1175.4 jit_solution(6477687003662021271)
XLA Ops:
  31.0 34.8 %collective-permute-done.1 = f32[4,256,512]{2,1,0:T(8,128)} collective-permute-done((f32[4,256,512]{2,1,0:T(8,128)}, f32[4,256,512]{2,1,0:T(8,128)}, u32[]{:S(2)}, u32[]{:S(2)}) %collective-permute-start.1) | collective-permute-done | bytes 2097184 | tf_op jit(solution)/shard_map/ppermute | solution.py:10
  65.7 44.9 %collective-permute-done.2 = f32[4,256,512]{2,1,0:T(8,128)} collective-permute-done((f32[4,256,512]{2,1,0:T(8,128)}, f32[4,256,512]{2,1,0:T(8,128)}, u32[]{:S(2)}, u32[]{:S(2)}) %collective-permute-start.2) | collective-permute-done | bytes 2097184 | tf_op jit(solution)/shard_map/ppermute | solution.py:10
  110.7 6.2 add_select_fusion.9
  118.4 14.8 %collective-permute-done.13 = f32[2,256,512]{2,1,0:T(8,128)} collective-permute-done((f32[2,256,512]{2,1,0:T(8,128)}, f32[2,256,512]{2,1,0:T(8,128)}, u32[]{:S(2)}, u32[]{:S(2)}) %collective-permute-start.13) | collective-permute-done | bytes 1048608 | tf_op jit(solution)/shard_map/ppermute | solution.py:10
  133.1 22.5 %collective-permute-done.14 = f32[2,256,512]{2,1,0:T(8,128)} collective-permute-done((f32[2,256,512]{2,1,0:T(8,128)}, f32[2,256,512]{2,1,0:T(8,128)}, u32[]{:S(2)}, u32[]{:S(2)}) %collective-permute-start.14) | collective-permute-done | bytes 1048608 | tf_op jit(solution)/shard_map/ppermute | solution.py:10
  160.6 107.4 %collective-permute-done.15 = f32[2,256,512]{2,1,0:T(8,128)} collective-permute-done((f32[2,256,512]{2,1,0:T(8,128)}, f32[2,256,512]{2,1,0:T(8,128)}, u32[]{:S(2)}, u32[]{:S(2)}) %collective-permute-start.15) | collective-permute-done | bytes 1048608 | tf_op jit(solution)/shard_map/ppermute | solution.py:10
  268.0 22.5 %collective-permute-done.16 = f32[2,256,512]{2,1,0:T(8,128)} collective-permute-done((f32[2,256,512]{2,1,0:T(8,128)}, f32[2,256,512]{2,1,0:T(8,128)}, u32[]{:S(2)}, u32[]{:S(2)}) %collective-permute-start.16) | collective-permute-done | bytes 1048608 | tf_op jit(solution)/shard_map/ppermute | solution.py:10
  296.1 6.7 add_select_fusion.7
  304.8 12.0 %collective-permute-done.17 = f32[2,256,512]{2,1,0:T(8,128)} collective-permute-done((f32[2,256,512]{2,1,0:T(8,128)}, f32[2,256,512]{2,1,0:T(8,128)}, u32[]{:S(2)}, u32[]{:S(2)}) %collective-permute-start.17) | collective-permute-done | bytes 1048608 | tf_op jit(solution)/shard_map/ppermute | solution.py:10
  316.8 22.5 %collective-permute-done.18 = f32[2,256,512]{2,1,0:T(8,128)} collective-permute-done((f32[2,256,512]{2,1,0:T(8,128)}, f32[2,256,512]{2,1,0:T(8,128)}, u32[]{:S(2)}, u32[]{:S(2)}) %collective-permute-start.18) | collective-permute-done | bytes 1048608 | tf_op jit(solution)/shard_map/ppermute | solution.py:10
  350.0 34.2 %collective-permute-done.5 = f32[4,256,512]{2,1,0:T(8,128)} collective-permute-done((f32[4,256,512]{2,1,0:T(8,128)}, f32[4,256,512]{2,1,0:T(8,128)}, u32[]{:S(2)}, u32[]{:S(2)}) %collective-permute-start.5) | collective-permute-done | bytes 2097184 | tf_op jit(solution)/shard_map/ppermute | solution.py:10
  384.2 44.9 %collective-permute-done.6 = f32[4,256,512]{2,1,0:T(8,128)} collective-permute-done((f32[4,256,512]{2,1,0:T(8,128)}, f32[4,256,512]{2,1,0:T(8,128)}, u32[]{:S(2)}, u32[]{:S(2)}) %collective-permute-start.6) | collective-permute-done | bytes 2097184 | tf_op jit(solution)/shard_map/ppermute | solution.py:10
  429.2 4.6 add_select_fusion.5
  433.8 4.7 fusion.39
  438.5 4.5 fusion.41
  447.5 4.9 multiply_subtract_fusion
  452.4 6.3 multiply_subtract_fusion.2
  469.0 4.8 fusion.43
  492.1 35.7 %collective-permute-done.19 = f32[4,256,512]{2,1,0:T(8,128)S(1)} collective-permute-done((f32[4,256,512]{2,1,0:T(8,128)S(1)}, f32[4,256,512]{2,1,0:T(8,128)S(1)}, u32[]{:S(2)}, u32[]{:S(2)}) %collective-permute-start.19) | collective-permute-done | bytes 2097184 | tf_op jit(solution)/shard_map/ppermute | solution.py:10
  527.8 44.9 %collective-permute-done.20 = f32[4,256,512]{2,1,0:T(8,128)S(1)} collective-permute-done((f32[4,256,512]{2,1,0:T(8,128)S(1)}, f32[4,256,512]{2,1,0:T(8,128)S(1)}, u32[]{:S(2)}, u32[]{:S(2)}) %collective-permute-start.20) | collective-permute-done | bytes 2097184 | tf_op jit(solution)/shard_map/ppermute | solution.py:10
  580.0 18.0 %collective-permute-done.7 = f32[2,256,512]{2,1,0:T(8,128)S(1)} collective-permute-done((f32[2,256,512]{2,1,0:T(8,128)S(1)}, f32[2,256,512]{2,1,0:T(8,128)S(1)}, u32[]{:S(2)}, u32[]{:S(2)}) %collective-permute-start.7) | collective-permute-done | bytes 1048608 | tf_op jit(solution)/shard_map/ppermute | solution.py:10
  598.0 22.5 %collective-permute-done.8 = f32[2,256,512]{2,1,0:T(8,128)S(1)} collective-permute-done((f32[2,256,512]{2,1,0:T(8,128)S(1)}, f32[2,256,512]{2,1,0:T(8,128)S(1)}, u32[]{:S(2)}, u32[]{:S(2)}) %collective-permute-start.8) | collective-permute-done | bytes 1048608 | tf_op jit(solution)/shard_map/ppermute | solution.py:10
  622.7 39.0 %collective-permute-done.22 = f32[4,256,512]{2,1,0:T(8,128)S(1)} collective-permute-done((f32[4,256,512]{2,1,0:T(8,128)S(1)}, f32[4,256,512]{2,1,0:T(8,128)S(1)}, u32[]{:S(2)}, u32[]{:S(2)}) %collective-permute-start.22) | collective-permute-done | bytes 2097184 | tf_op jit(solution)/shard_map/ppermute | solution.py:10
  666.3 17.9 %collective-permute-done.10 = f32[2,256,512]{2,1,0:T(8,128)S(1)} collective-permute-done((f32[2,256,512]{2,1,0:T(8,128)S(1)}, f32[2,256,512]{2,1,0:T(8,128)S(1)}, u32[]{:S(2)}, u32[]{:S(2)}) %collective-permute-start.10) | collective-permute-done | bytes 1048608 | tf_op jit(solution)/shard_map/ppermute | solution.py:10
  684.2 22.5 %collective-permute-done.9 = f32[2,256,512]{2,1,0:T(8,128)S(1)} collective-permute-done((f32[2,256,512]{2,1,0:T(8,128)S(1)}, f32[2,256,512]{2,1,0:T(8,128)S(1)}, u32[]{:S(2)}, u32[]{:S(2)}) %collective-permute-start.9) | collective-permute-done | bytes 1048608 | tf_op jit(solution)/shard_map/ppermute | solution.py:10
  710.5 109.4 %collective-permute-done.11 = f32[2,256,512]{2,1,0:T(8,128)S(1)} collective-permute-done((f32[2,256,512]{2,1,0:T(8,128)S(1)}, f32[2,256,512]{2,1,0:T(8,128)S(1)}, u32[]{:S(2)}, u32[]{:S(2)}) %collective-permute-start.11) | collective-permute-done | bytes 1048608 | tf_op jit(solution)/shard_map/ppermute | solution.py:10
  820.2 22.2 %collective-permute-done.12 = f32[2,256,512]{2,1,0:T(8,128)S(1)} collective-permute-done((f32[2,256,512]{2,1,0:T(8,128)S(1)}, f32[2,256,512]{2,1,0:T(8,128)S(1)}, u32[]{:S(2)}, u32[]{:S(2)}) %collective-permute-start.12) | collective-permute-done | bytes 1048608 | tf_op jit(solution)/shard_map/ppermute | solution.py:10
  845.8 4.7 fusion.1
  854.5 4.8 fusion
  860.8 130.1 %all-reduce.5.cloned.1.call-done = f32[256,512]{1,0:T(8,128)} async-done(((f32[256,512]{1,0:T(8,128)}), f32[256,512]{1,0:T(8,128)}) %all-reduce.5.cloned.1.call-update) | async-done | bytes 524304 | tf_op jit(solution)/shard_map/psum | solution.py:217
  992.7 167.3 %all-reduce.7.cloned.1.call-done = f32[512,4096]{1,0:T(8,128)} async-done(((f32[512,4096]{1,0:T(8,128)}), f32[512,4096]{1,0:T(8,128)}) %all-reduce.7.cloned.1.call-update) | async-done | bytes 8388624 | tf_op jit(solution)/shard_map/psum | solution.py:216
  1160.1 8.3 broadcast_multiply_fusion
  (132 shorter events, 110.1 us)
Async XLA Ops:
  7.2 983.7 %all-reduce.5.cloned.1.call-start = ((), (), s32[]{:S(2)}) async-start(), calls=%async_computation | async-start | bytes 1048576 | tf_op jit(solution)/shard_map/psum | solution.py:217
  8.1 5.0 collective-permute-start
  17.5 48.2 %collective-permute-start.1 = (f32[4,256,512]{2,1,0:T(8,128)}, f32[4,256,512]{2,1,0:T(8,128)}, u32[]{:S(2)}, u32[]{:S(2)}) collective-permute-start(f32[4,256,512]{2,1,0:T(8,128)} %pad_maximum_fusion), channel_id=1, source_target_pairs={{0,4},{1,5},{2,6},{3,7},{4,0},{5,1},{6,2},{7,3},{8,12},{9,13},{10,... | collective-permute-start | bytes 6291464 | tf_op jit(solution)/shard_map/ppermute | solution.py:10
  22.9 87.8 %collective-permute-start.2 = (f32[4,256,512]{2,1,0:T(8,128)}, f32[4,256,512]{2,1,0:T(8,128)}, u32[]{:S(2)}, u32[]{:S(2)}) collective-permute-start(f32[4,256,512]{2,1,0:T(8,128)} %concatenate.47), channel_id=1, source_target_pairs={{0,4},{1,5},{2,6},{3,7},{4,0},{5,1},{6,2},{7,3},{8,12},{9,13},{10,... | collective-permute-start | bytes 6291464 | tf_op jit(solution)/shard_map/ppermute | solution.py:10
  26.8 106.3 %collective-permute-start.13 = (f32[2,256,512]{2,1,0:T(8,128)}, f32[2,256,512]{2,1,0:T(8,128)}, u32[]{:S(2)}, u32[]{:S(2)}) collective-permute-start(f32[2,256,512]{2,1,0:T(8,128)} %pad_maximum_fusion.6), channel_id=1, source_target_pairs={{0,4},{1,5},{2,6},{3,7},{4,0},{5,1},{6,2},{7,3},{8,12},{9,13},{10,... | collective-permute-start | bytes 3145736 | tf_op jit(solution)/shard_map/ppermute | solution.py:10
  30.5 125.1 %collective-permute-start.14 = (f32[2,256,512]{2,1,0:T(8,128)}, f32[2,256,512]{2,1,0:T(8,128)}, u32[]{:S(2)}, u32[]{:S(2)}) collective-permute-start(f32[2,256,512]{2,1,0:T(8,128)} %concatenate.49), channel_id=1, source_target_pairs={{0,4},{1,5},{2,6},{3,7},{4,0},{5,1},{6,2},{7,3},{8,12},{9,13},{10,... | collective-permute-start | bytes 3145736 | tf_op jit(solution)/shard_map/ppermute | solution.py:10
  110.7 44.9 %copy-start.15 = (f32[1,256,512]{2,1,0:T(8,128)S(1)}, f32[1,256,512]{2,1,0:T(8,128)}, u32[]{:S(2)}) copy-start(f32[1,256,512]{2,1,0:T(8,128)} %copy-done.14) | copy-start | bytes 1572868
  116.9 179.2 %collective-permute-start.3 = (f32[4,256,512]{2,1,0:T(8,128)}, f32[4,256,512]{2,1,0:T(8,128)}, u32[]{:S(2)}, u32[]{:S(2)}) collective-permute-start(f32[4,256,512]{2,1,0:T(8,128)} %get-tuple-element.16), channel_id=1, source_target_pairs={{0,2},{1,3},{2,0},{3,1},{4,6},{5,7},{6,4},{7,5},{8,10},{9,11},{10,... | collective-permute-start | bytes 6291464 | tf_op jit(solution)/shard_map/ppermute | solution.py:10
  118.0 178.0 %collective-permute-start.4 = (f32[4,256,512]{2,1,0:T(8,128)}, f32[4,256,512]{2,1,0:T(8,128)}, u32[]{:S(2)}, u32[]{:S(2)}) collective-permute-start(f32[4,256,512]{2,1,0:T(8,128)} %get-tuple-element.17), channel_id=1, source_target_pairs={{0,2},{1,3},{2,0},{3,1},{4,6},{5,7},{6,4},{7,5},{8,10},{9,11},{10,... | collective-permute-start | bytes 6291464 | tf_op jit(solution)/shard_map/ppermute | solution.py:10
  159.1 108.9 %collective-permute-start.15 = (f32[2,256,512]{2,1,0:T(8,128)}, f32[2,256,512]{2,1,0:T(8,128)}, u32[]{:S(2)}, u32[]{:S(2)}) collective-permute-start(f32[2,256,512]{2,1,0:T(8,128)} %get-tuple-element.35), channel_id=1, source_target_pairs={{0,2},{1,3},{2,0},{3,1},{4,6},{5,7},{6,4},{7,5},{8,10},{9,11},{10,... | collective-permute-start | bytes 3145736 | tf_op jit(solution)/shard_map/ppermute | solution.py:10
  160.2 130.2 %collective-permute-start.16 = (f32[2,256,512]{2,1,0:T(8,128)}, f32[2,256,512]{2,1,0:T(8,128)}, u32[]{:S(2)}, u32[]{:S(2)}) collective-permute-start(f32[2,256,512]{2,1,0:T(8,128)} %get-tuple-element.34), channel_id=1, source_target_pairs={{0,2},{1,3},{2,0},{3,1},{4,6},{5,7},{6,4},{7,5},{8,10},{9,11},{10,... | collective-permute-start | bytes 3145736 | tf_op jit(solution)/shard_map/ppermute | solution.py:10
  294.6 22.2 %collective-permute-start.17 = (f32[2,256,512]{2,1,0:T(8,128)}, f32[2,256,512]{2,1,0:T(8,128)}, u32[]{:S(2)}, u32[]{:S(2)}) collective-permute-start(f32[2,256,512]{2,1,0:T(8,128)} %get-tuple-element.27), channel_id=1, source_target_pairs={{0,1},{1,0},{2,3},{3,2},{4,5},{5,4},{6,7},{7,6},{8,9},{9,8},{10,11... | collective-permute-start | bytes 3145736 | tf_op jit(solution)/shard_map/ppermute | solution.py:10
  295.0 44.3 %collective-permute-start.18 = (f32[2,256,512]{2,1,0:T(8,128)}, f32[2,256,512]{2,1,0:T(8,128)}, u32[]{:S(2)}, u32[]{:S(2)}) collective-permute-start(f32[2,256,512]{2,1,0:T(8,128)} %get-tuple-element.26), channel_id=1, source_target_pairs={{0,1},{1,0},{2,3},{3,2},{4,5},{5,4},{6,7},{7,6},{8,9},{9,8},{10,11... | collective-permute-start | bytes 3145736 | tf_op jit(solution)/shard_map/ppermute | solution.py:10
  302.7 81.5 %collective-permute-start.5 = (f32[4,256,512]{2,1,0:T(8,128)}, f32[4,256,512]{2,1,0:T(8,128)}, u32[]{:S(2)}, u32[]{:S(2)}) collective-permute-start(f32[4,256,512]{2,1,0:T(8,128)} %get-tuple-element.14), channel_id=1, source_target_pairs={{0,1},{1,0},{2,3},{3,2},{4,5},{5,4},{6,7},{7,6},{8,9},{9,8},{10,11... | collective-permute-start | bytes 6291464 | tf_op jit(solution)/shard_map/ppermute | solution.py:10
  303.1 126.0 %collective-permute-start.6 = (f32[4,256,512]{2,1,0:T(8,128)}, f32[4,256,512]{2,1,0:T(8,128)}, u32[]{:S(2)}, u32[]{:S(2)}) collective-permute-start(f32[4,256,512]{2,1,0:T(8,128)} %get-tuple-element.15), channel_id=1, source_target_pairs={{0,1},{1,0},{2,3},{3,2},{4,5},{5,4},{6,7},{7,6},{8,9},{9,8},{10,11... | collective-permute-start | bytes 6291464 | tf_op jit(solution)/shard_map/ppermute | solution.py:10
  484.3 43.5 %collective-permute-start.19 = (f32[4,256,512]{2,1,0:T(8,128)S(1)}, f32[4,256,512]{2,1,0:T(8,128)S(1)}, u32[]{:S(2)}, u32[]{:S(2)}) collective-permute-start(f32[4,256,512]{2,1,0:T(8,128)S(1)} %get-tuple-element.23), channel_id=1, source_target_pairs={{0,1},{1,0},{2,3},{3,2},{4,5},{5,4},{6,7},{7,6},{8,9},{9,8},{10,11... | collective-permute-start | bytes 6291464 | tf_op jit(solution)/shard_map/ppermute | solution.py:10
  484.7 88.0 %collective-permute-start.20 = (f32[4,256,512]{2,1,0:T(8,128)S(1)}, f32[4,256,512]{2,1,0:T(8,128)S(1)}, u32[]{:S(2)}, u32[]{:S(2)}) collective-permute-start(f32[4,256,512]{2,1,0:T(8,128)S(1)} %get-tuple-element.22), channel_id=1, source_target_pairs={{0,1},{1,0},{2,3},{3,2},{4,5},{5,4},{6,7},{7,6},{8,9},{9,8},{10,11... | collective-permute-start | bytes 6291464 | tf_op jit(solution)/shard_map/ppermute | solution.py:10
  574.2 48.5 %collective-permute-start.21 = (f32[4,256,512]{2,1,0:T(8,128)S(1)}, f32[4,256,512]{2,1,0:T(8,128)S(1)}, u32[]{:S(2)}, u32[]{:S(2)}) collective-permute-start(f32[4,256,512]{2,1,0:T(8,128)S(1)} %get-tuple-element.11), channel_id=1, source_target_pairs={{0,2},{1,3},{2,0},{3,1},{4,6},{5,7},{6,4},{7,5},{8,10},{9,11},{10,... | collective-permute-start | bytes 6291464 | tf_op jit(solution)/shard_map/ppermute | solution.py:10
  575.5 86.3 %collective-permute-start.22 = (f32[4,256,512]{2,1,0:T(8,128)S(1)}, f32[4,256,512]{2,1,0:T(8,128)S(1)}, u32[]{:S(2)}, u32[]{:S(2)}) collective-permute-start(f32[4,256,512]{2,1,0:T(8,128)S(1)} %get-tuple-element.10), channel_id=1, source_target_pairs={{0,2},{1,3},{2,0},{3,1},{4,6},{5,7},{6,4},{7,5},{8,10},{9,11},{10,... | collective-permute-start | bytes 6291464 | tf_op jit(solution)/shard_map/ppermute | solution.py:10
  578.4 19.6 %collective-permute-start.7 = (f32[2,256,512]{2,1,0:T(8,128)S(1)}, f32[2,256,512]{2,1,0:T(8,128)S(1)}, u32[]{:S(2)}, u32[]{:S(2)}) collective-permute-start(f32[2,256,512]{2,1,0:T(8,128)S(1)} %get-tuple-element.39), channel_id=1, source_target_pairs={{0,1},{1,0},{2,3},{3,2},{4,5},{5,4},{6,7},{7,6},{8,9},{9,8},{10,11... | collective-permute-start | bytes 3145736 | tf_op jit(solution)/shard_map/ppermute | solution.py:10
  578.9 41.6 %collective-permute-start.8 = (f32[2,256,512]{2,1,0:T(8,128)S(1)}, f32[2,256,512]{2,1,0:T(8,128)S(1)}, u32[]{:S(2)}, u32[]{:S(2)}) collective-permute-start(f32[2,256,512]{2,1,0:T(8,128)S(1)} %get-tuple-element.38), channel_id=1, source_target_pairs={{0,1},{1,0},{2,3},{3,2},{4,5},{5,4},{6,7},{7,6},{8,9},{9,8},{10,11... | collective-permute-start | bytes 3145736 | tf_op jit(solution)/shard_map/ppermute | solution.py:10
  621.1 63.1 %collective-permute-start.10 = (f32[2,256,512]{2,1,0:T(8,128)S(1)}, f32[2,256,512]{2,1,0:T(8,128)S(1)}, u32[]{:S(2)}, u32[]{:S(2)}) collective-permute-start(f32[2,256,512]{2,1,0:T(8,128)S(1)} %get-tuple-element.30), channel_id=1, source_target_pairs={{0,2},{1,3},{2,0},{3,1},{4,6},{5,7},{6,4},{7,5},{8,10},{9,11},{10,... | collective-permute-start | bytes 3145736 | tf_op jit(solution)/shard_map/ppermute | solution.py:10
  622.4 84.3 %collective-permute-start.9 = (f32[2,256,512]{2,1,0:T(8,128)S(1)}, f32[2,256,512]{2,1,0:T(8,128)S(1)}, u32[]{:S(2)}, u32[]{:S(2)}) collective-permute-start(f32[2,256,512]{2,1,0:T(8,128)S(1)} %get-tuple-element.31), channel_id=1, source_target_pairs={{0,2},{1,3},{2,0},{3,1},{4,6},{5,7},{6,4},{7,5},{8,10},{9,11},{10,... | collective-permute-start | bytes 3145736 | tf_op jit(solution)/shard_map/ppermute | solution.py:10
  663.3 180.2 %collective-permute-start.23 = (f32[4,256,512]{2,1,0:T(8,128)S(1)}, f32[4,256,512]{2,1,0:T(8,128)S(1)}, u32[]{:S(2)}, u32[]{:S(2)}) collective-permute-start(f32[4,256,512]{2,1,0:T(8,128)S(1)} %get-tuple-element.9), channel_id=1, source_target_pairs={{0,4},{1,5},{2,6},{3,7},{4,0},{5,1},{6,2},{7,3},{8,12},{9,13},{10,... | collective-permute-start | bytes 6291464 | tf_op jit(solution)/shard_map/ppermute | solution.py:10
  665.1 178.9 %collective-permute-start.24 = (f32[4,256,512]{2,1,0:T(8,128)S(1)}, f32[4,256,512]{2,1,0:T(8,128)S(1)}, u32[]{:S(2)}, u32[]{:S(2)}) collective-permute-start(f32[4,256,512]{2,1,0:T(8,128)S(1)} %get-tuple-element.8), channel_id=1, source_target_pairs={{0,4},{1,5},{2,6},{3,7},{4,0},{5,1},{6,2},{7,3},{8,12},{9,13},{10,... | collective-permute-start | bytes 6291464 | tf_op jit(solution)/shard_map/ppermute | solution.py:10
  707.4 135.0 %copy-start.2 = (f32[3,1,256,512]{3,2,1,0:T(8,128)S(1)}, f32[3,1,256,512]{3,2,1,0:T(8,128)}, u32[]{:S(2)}) copy-start(f32[3,1,256,512]{3,2,1,0:T(8,128)} %copy-done.1) | copy-start | bytes 4718596
  707.4 135.0 %copy-start.17 = (f32[256,512]{1,0:T(8,128)S(1)}, f32[256,512]{1,0:T(8,128)}, u32[]{:S(2)}) copy-start(f32[256,512]{1,0:T(8,128)} %copy-done.16) | copy-start | bytes 1572868
  707.4 135.0 %copy-start.18 = (f32[512]{0:T(512)S(1)}, f32[512]{0:T(512)}, u32[]{:S(2)}) copy-start(f32[512]{0:T(512)} %param.9) | copy-start | bytes 6148
  707.4 112.5 %collective-permute-start.11 = (f32[2,256,512]{2,1,0:T(8,128)S(1)}, f32[2,256,512]{2,1,0:T(8,128)S(1)}, u32[]{:S(2)}, u32[]{:S(2)}) collective-permute-start(f32[2,256,512]{2,1,0:T(8,128)S(1)} %get-tuple-element.28), channel_id=1, source_target_pairs={{0,4},{1,5},{2,6},{3,7},{4,0},{5,1},{6,2},{7,3},{8,12},{9,13},{10,... | collective-permute-start | bytes 3145736 | tf_op jit(solution)/shard_map/ppermute | solution.py:10
  709.2 133.1 %collective-permute-start.12 = (f32[2,256,512]{2,1,0:T(8,128)S(1)}, f32[2,256,512]{2,1,0:T(8,128)S(1)}, u32[]{:S(2)}, u32[]{:S(2)}) collective-permute-start(f32[2,256,512]{2,1,0:T(8,128)S(1)} %get-tuple-element.29), channel_id=1, source_target_pairs={{0,4},{1,5},{2,6},{3,7},{4,0},{5,1},{6,2},{7,3},{8,12},{9,13},{10,... | collective-permute-start | bytes 3145736 | tf_op jit(solution)/shard_map/ppermute | solution.py:10
  845.8 314.3 %all-reduce.7.cloned.1.call-start = ((), (), s32[]{:S(2)}) async-start(), calls=%async_computation.1 | async-start | bytes 16777216 | tf_op jit(solution)/shard_map/psum | solution.py:216
  852.8 6.5 collective-permute-start.25
  (16 other events, 120.2 us)
Sparse Core Ops, SparseCore 0:
  845.9 144.8 all-reduce.4
  997.3 162.7 all-reduce.6
where the time goes:
time: 1180 us
  waiting for transfers between devices  990 us (84%)
  matrix products  67.5 us (6%)
  other arithmetic  58.3 us (5%)
  starting transfers between devices  31.8 us (3%)
  between operations  14.8 us (1%)
  local copies, waits for them, and re-layouts  12.9 us (1%)
    ppermute x24, waiting for transfers between devices, swapped(): lax.ppermute(array, axis, [(i, i ^ 1 << apart) for i in range(lax.axis_si...  693 us
    psum x1, waiting for transfers between devices, on_device(): grad_out_weight = lax.psum(partial_value, ('dp', 'seq')) * grad_scale  167 us
    psum x1, waiting for transfers between devices, on_device(): grad_filter = lax.psum(filter_part, 'dp') * grad_scale  130 us
    dot_general x16, matrix products, table_apply(): return jnp.einsum(pattern, matrix, values, precision=lax.Precision.HIGHEST)  56.8 us
    ppermute x24, starting transfers between devices, swapped(): lax.ppermute(array, axis, [(i, i ^ 1 << apart) for i in range(lax.axis_si...  26 us
  transfers between devices with their start and end apart: 28, of which 21 were waited for; matrix products, arithmetic and copies ran while one was open for 6% of the time, Pallas kernels for 0%

commit v1 on v0

v1 whole, which is shorter than its diff:
```python
import functools
import math

import jax
import jax.numpy as jnp
import numpy as np
from jax import lax
from jax.experimental import pallas as pl
from jax.experimental.pallas import tpu as pltpu
from jax.sharding import Mesh, PartitionSpec as P

BF = jnp.bfloat16
F32 = jnp.float32
BLOCK = 256
HALF = 64
SEQ = ("x", "yl")
DEPTH = ("z", "yh")
CHIPS = DEPTH + SEQ


@functools.lru_cache(maxsize=None)
def tables():
    order = np.concatenate([np.arange(0, BLOCK, 2), np.arange(1, BLOCK, 2)])
    angle = np.pi * ((2 * order[:, None] + 1) * np.arange(BLOCK)[None, :] % 1024) / 512.0
    ahead = np.concatenate([np.cos(angle), -np.sin(angle)], axis=0)
    back = ahead.T / BLOCK

    def two(table):
        table = table.astype(np.float32)
        high = table.astype(jnp.bfloat16)
        return high, (table - high.astype(np.float32)).astype(jnp.bfloat16)

    return two(ahead) + two(back)


def mm(a, b):
    return jnp.dot(a, b, preferred_element_type=F32)


def low_lanes(rows):
    return lax.broadcasted_iota(jnp.int32, (rows, 128), 1) < HALF


def turned(x):
    return pltpu.roll(x, HALF, 1)


def pack_kernel(streams, out_grad, weight, filt, packed, total):
    step = pl.program_id(0)

    @pl.when(step == 0)
    def _():
        total[...] = jnp.zeros_like(total)

    total[...] += lax.dot_general(
        out_grad[...], weight[...], (((1,), (1,)), ((), ())), preferred_element_type=F32
    )

    @pl.when(step == pl.num_programs(0) - 1)
    def _():
        low = low_lanes(BLOCK)
        for q in range(4):
            lanes = slice(128 * q, 128 * q + 128)
            whole = filt[:, lanes]
            high = whole.astype(BF).astype(F32)
            pairs = (
                (streams[0, :, lanes].astype(F32), streams[1, :, lanes].astype(F32)),
                (streams[2, :, lanes].astype(F32), total[:, lanes]),
                (high, whole - high),
            )
            for n, (a, b) in enumerate(pairs):
                there = slice(128 * n, 128 * n + 128)
                packed[2 * q, :, there] = jnp.where(low, a, turned(b)).astype(BF)
                packed[2 * q + 1, :, there] = jnp.where(low, turned(a), b).astype(BF)


def pack(streams, out_grad, weight, filt):
    steps = 4
    wide = out_grad.shape[1] // steps
    return pl.pallas_call(
        pack_kernel,
        grid=(steps,),
        in_specs=[
            pl.BlockSpec((3, BLOCK, 512), lambda k: (0, 0, 0)),
            pl.BlockSpec((BLOCK, wide), lambda k: (0, k)),
            pl.BlockSpec((512, wide), lambda k: (0, k)),
            pl.BlockSpec((BLOCK, 512), lambda k: (0, 0)),
        ],
        out_specs=pl.BlockSpec((8, BLOCK, 384), lambda k: (0, 0, 0)),
        out_shape=jax.ShapeDtypeStruct((8, BLOCK, 384), BF),
        scratch_shapes=[pltpu.VMEM((BLOCK, 512), F32)],
        name="pack",
    )(streams, out_grad, weight, filt)


def conv_kernel(
    place, got, short, skip, ahead_h, ahead_l, back_h, back_l,
    sent, lags,
    sa_pad, sv_pad, sa, sv, prod, spec, fspec, res, lres, time, u_pad, x_pad,
):
    low = low_lanes(BLOCK)
    low1 = low_lanes(1)
    sigma = jnp.where(low, 1.0, -1.0)
    odd = place[0] % 2 == 1

    taps = short[...]
    taps = jnp.where(odd, turned(taps), taps)
    taps_up = turned(taps)
    gain = skip[...]
    gain = jnp.where(odd, turned(gain), gain)
    gain = jnp.where(low1, gain, turned(gain))

    def tap(i, j):
        return taps[3 * i + j : 3 * i + j + 1]

    def tap_up(i, j):
        return taps_up[3 * i + j : 3 * i + j + 1]

    def unit(j):
        return jnp.full((1, 128), 1.0 if j == 0 else 0.0, F32)

    w_a = [jnp.where(low1, tap(0, j), tap_up(1, j)) for j in range(3)]
    w_v = [jnp.where(low1, tap(2, j), unit(j)) for j in range(3)]
    w_u = [jnp.where(low1, tap(1, j), tap_up(0, j)) for j in range(3)]
    w_x = [jnp.where(low1, unit(j), tap_up(2, j)) for j in range(3)]

    def split(x):
        high = x.astype(BF)
        return high, (x - high.astype(F32)).astype(BF)

    def apply(table_h, table_l, high, rest):
        both = mm(table_h[...], jnp.concatenate([high, rest], axis=1))
        return both[:, :128] + both[:, 128:] + mm(table_l[...], high)

    sa_pad[0:8] = jnp.zeros((8, 128), F32)
    sv_pad[0:8] = jnp.zeros((8, 128), F32)

    def unpack(b, carry):
        rows = pl.ds(pl.multiple_of(8 + BLOCK * b, 8), BLOCK)
        sa_pad[rows] = got[b, :, 0:128].astype(F32)
        sv_pad[rows] = got[b, :, 128:256].astype(F32)
        f = got[b, :, 256:384].astype(F32)
        g = turned(f)
        high = jnp.where(low, f, g).astype(BF)
        rest = jnp.where(low, g, f).astype(BF)
        fspec[b] = apply(ahead_h, ahead_l, high, rest)
        return carry

    lax.fori_loop(0, 8, unpack, 0)

    for b in range(8):
        start = 8 + BLOCK * b
        a = sum(w_a[j] * sa_pad[start - j : start - j + BLOCK] for j in range(3))
        v = sum(w_v[j] * sv_pad[start - j : start - j + BLOCK] for j in range(3))
        sa[b] = a
        sv[b] = v
        prod[b] = turned(a) * v

    def transform(b, carry):
        high, rest = split(jnp.where(low, prod[b], prod[7 - b]))
        out = apply(ahead_h, ahead_l, high, rest)
        spec[b, 0:BLOCK] = out[:BLOCK]
        spec[b, BLOCK:] = out[BLOCK:] * sigma
        return carry

    lax.fori_loop(0, 8, transform, 0)

    for sign, base in ((1.0, 0), (-1.0, 128)):

        def multiply(n, carry, sign=sign, base=base):
            re = pl.ds(pl.multiple_of(base + 8 * n, 8), 8)
            im = pl.ds(pl.multiple_of(BLOCK + base + 8 * n, 8), 8)
            own = [(spec[j, re], spec[j, im]) for j in range(8)]
            both = [own[0]]
            for j in range(1, 8):
                both.append(
                    (own[j][0] - sign * own[j - 1][1], own[j][1] + sign * own[j - 1][0])
                )
            filt = [(fspec[m, re], fspec[m, im]) for m in range(8)]

            def summed(pairs):
                first = True
                for (ar, ai), (br, bi) in pairs:
                    pr = ar * br - ai * bi
                    pi = ar * bi + ai * br
                    tr, ti = (pr, pi) if first else (tr + pr, ti + pi)
                    first = False
                return tr, ti

            for i in range(8):
                tr, ti = summed([(filt[m], both[i - m]) for m in range(i + 1)])
                res[i, re] = tr
                res[i, im] = ti
            moved = [(turned(r), turned(i)) for r, i in both]
            for m in range(8):
                tr, ti = summed([(own[7 - i], moved[i - m]) for i in range(m, 8)])
                lres[m, re] = tr
                lres[m, im] = ti
            return carry

        lax.fori_loop(0, 16, multiply, 0)

    def invert(b, carry):
        def one(src):
            x = jnp.concatenate([src[b, 0:BLOCK], src[b, BLOCK:] * sigma], axis=0)
            return apply(back_h, back_l, *split(x))

        time[b] = one(res)
        lag = one(lres)
        low16 = low_lanes(16)
        for k in range(8):
            a = lag[32 * k : 32 * k + 16]
            c = lag[32 * k + 16 : 32 * k + 32]
            lags[b, k] = jnp.where(low16, turned(a), c).astype(BF)
        return carry

    lax.fori_loop(0, 8, invert, 0)

    def gate(b, carry):
        t = jnp.where(low, time[b], time[7 - b]) + gain * prod[b]
        rows = pl.ds(pl.multiple_of(BLOCK * b, 8), BLOCK)
        u_pad[rows] = turned(t) * sv[b]
        x_pad[rows] = t * sa[b]
        return carry

    lax.fori_loop(0, 8, gate, 0)
    u_pad[8 * BLOCK :] = jnp.zeros((8, 128), F32)
    x_pad[8 * BLOCK :] = jnp.zeros((8, 128), F32)
    for b in range(8):
        start = BLOCK * b
        y = sum(w_u[j] * u_pad[start + j : start + j + BLOCK] for j in range(3))
        sent[b, :, 0:128] = y.astype(BF)
        y = sum(w_x[j] * x_pad[start + j : start + j + BLOCK] for j in range(3))
        sent[b, :, 128:256] = y.astype(BF)


def conv(place, got, short, skip):
    ahead_h, ahead_l, back_h, back_l = (jnp.asarray(t) for t in tables())
    full = lambda *shape: pl.BlockSpec(shape, lambda n, p: (0,) * len(shape))
    return pl.pallas_call(
        conv_kernel,
        grid_spec=pltpu.PrefetchScalarGridSpec(
            num_scalar_prefetch=1,
            grid=(1,),
            in_specs=[
                full(8, BLOCK, 384),
                pl.BlockSpec((9, 128), lambda n, p: (0, p[0] // 2)),
                pl.BlockSpec((1, 128), lambda n, p: (0, p[0] // 2)),
                full(512, BLOCK),
                full(512, BLOCK),
                full(BLOCK, 512),
                full(BLOCK, 512),
            ],
            out_specs=[full(8, BLOCK, 256), full(8, 8, 16, 128)],
            scratch_shapes=[
                pltpu.VMEM((8 + 8 * BLOCK, 128), F32),
                pltpu.VMEM((8 + 8 * BLOCK, 128), F32),
                pltpu.VMEM((8, BLOCK, 128), F32),
                pltpu.VMEM((8, BLOCK, 128), F32),
                pltpu.VMEM((8, BLOCK, 128), F32),
                pltpu.VMEM((8, 512, 128), F32),
                pltpu.VMEM((8, 512, 128), F32),
                pltpu.VMEM((8, 512, 128), F32),
                pltpu.VMEM((8, 512, 128), F32),
                pltpu.VMEM((8, BLOCK, 128), F32),
                pltpu.VMEM((8 + 8 * BLOCK, 128), F32),
                pltpu.VMEM((8 + 8 * BLOCK, 128), F32),
            ],
        ),
        out_shape=[
            jax.ShapeDtypeStruct((8, BLOCK, 256), BF),
            jax.ShapeDtypeStruct((8, 8, 16, 128), BF),
        ],
        name="conv",
    )(place, got, short, skip, ahead_h, ahead_l, back_h, back_l)


def unpack_kernel(got, mixed, grads):
    low = low_lanes(BLOCK)
    for q in range(4):
        lanes = slice(128 * q, 128 * q + 128)
        for n, (first, second) in enumerate(((grads.at[1], grads.at[0]), (mixed, grads.at[2]))):
            there = slice(128 * n, 128 * n + 128)
            a = got[2 * q, :, there].astype(F32)
            b = got[2 * q + 1, :, there].astype(F32)
            first[:, lanes] = jnp.where(low, a, turned(b)).astype(BF)
            second[:, lanes] = jnp.where(low, turned(a), b).astype(BF)


def unpack(got):
    return pl.pallas_call(
        unpack_kernel,
        out_shape=[
            jax.ShapeDtypeStruct((BLOCK, 512), BF),
            jax.ShapeDtypeStruct((3, BLOCK, 512), BF),
        ],
        name="unpack",
    )(got)


def partial_kernel(place, mine, theirs, grad_mine, grad_theirs, lags, packed):
    def term(mixed, grad):
        return lax.dot_general(
            mixed[...], grad[...], (((0,), (0,)), ((), ())), preferred_element_type=F32
        )

    part = (term(mine, grad_mine) + term(theirs, grad_theirs)).astype(BF)
    for s in range(8):
        for a in range(4):
            start = 64 * s + 16 * a
            packed[a, 0, s, :, 0:1024] = part[start : start + 16]
            packed[a, 0, s, :, 1024:1152] = lags[s, 2 * a + pl.program_id(0)]


def partial(place, mine, theirs, out_grad, grad_theirs, lags):
    return pl.pallas_call(
        partial_kernel,
        grid_spec=pltpu.PrefetchScalarGridSpec(
            num_scalar_prefetch=1,
            grid=(2,),
            in_specs=[
                pl.BlockSpec((BLOCK, 512), lambda h, p: (0, 0)),
                pl.BlockSpec((BLOCK, 512), lambda h, p: (0, 0)),
                pl.BlockSpec((BLOCK, 1024), lambda h, p: (0, 2 * p[0] + h)),
                pl.BlockSpec((BLOCK, 1024), lambda h, p: (0, h)),
                pl.BlockSpec((8, 8, 16, 128), lambda h, p: (0, 0, 0, 0)),
            ],
            out_specs=pl.BlockSpec((4, 1, 8, 16, 1152), lambda h, p: (0, h, 0, 0, 0)),
        ),
        out_shape=jax.ShapeDtypeStruct((4, 2, 8, 16, 1152), BF),
        name="partial",
    )(place, mine, theirs, out_grad, grad_theirs, lags)


def reduce_kernel(scale, got, shared):
    total = jnp.zeros((16, 1024), F32)
    for n in range(64):
        total = total + got[n, :, 0:1024].astype(F32)
    total = (total * scale).astype(BF)
    for k in range(8):
        shared[k, :, 0:1024] = total
    for s in range(8):
        lag = jnp.zeros((16, 128), F32)
        for k in range(8):
            lag = lag + got[8 * k + s, :, 1024:1152].astype(F32)
        lag = (lag * scale).astype(BF)
        for k in range(8):
            shared[k, :, 1024 + 128 * s : 1152 + 128 * s] = lag


def reduce(got, scale):
    return pl.pallas_call(
        functools.partial(reduce_kernel, scale),
        out_shape=jax.ShapeDtypeStruct((8, 16, 2048), BF),
        name="reduce",
    )(got)


def finish_kernel(place, mine, theirs, lag_mine, lag_theirs, grad_weight, grad_filter):
    core = place[0]
    for k in range(8):
        rows = slice(16 * (k // 2), 16 * (k // 2) + 16)
        for half, src in ((core, mine), (1 - core, theirs)):
            lanes = pl.ds(pl.multiple_of(2048 * half + 1024 * (k % 2), 1024), 1024)
            grad_weight[rows, lanes] = src[0, k].astype(F32)

    @pl.when(pl.program_id(0) == 0)
    def _():
        low = low_lanes(16)
        for k in range(8):
            for q in range(4):
                def both(s):
                    there = slice(128 * s, 128 * s + 128)
                    return lag_mine[k, :, there].astype(F32) + lag_theirs[k, :, there].astype(F32)

                a, b = both(2 * q), both(2 * q + 1)
                lanes = slice(128 * q, 128 * q + 128)
                grad_filter[32 * k : 32 * k + 16, lanes] = jnp.where(low, a, turned(b))
                grad_filter[32 * k + 16 : 32 * k + 32, lanes] = jnp.where(low, turned(a), b)


def finish(place, mine, theirs, lag_mine, lag_theirs):
    lag_spec = pl.BlockSpec((8, 16, 1024), lambda s, p: (0, 0, 0))
    half_spec = pl.BlockSpec((1, 8, 16, 1024), lambda s, p: (s, 0, 0, 0))
    return pl.pallas_call(
        finish_kernel,
        grid_spec=pltpu.PrefetchScalarGridSpec(
            num_scalar_prefetch=1,
            grid=(8,),
            in_specs=[half_spec, half_spec, lag_spec, lag_spec],
            out_specs=[
                pl.BlockSpec((64, 4096), lambda s, p: (s, 0)),
                pl.BlockSpec((BLOCK, 512), lambda s, p: (0, 0)),
            ],
        ),
        out_shape=[
            jax.ShapeDtypeStruct((512, 4096), F32),
            jax.ShapeDtypeStruct((BLOCK, 512), F32),
        ],
        name="finish",
    )(place, mine, theirs, lag_mine, lag_theirs)


def exchange(x, axes):
    return lax.all_to_all(x, axes, 0, 0, tiled=True)


def across(x):
    return lax.ppermute(x, "c", [(0, 1), (1, 0)])


def on_device(streams, short_filter, long_filter, skip_gain, out_weight, out_grad):
    scale = 1.0 / math.sqrt(16 * 2048)
    core = lax.axis_index("c").astype(jnp.int32)
    seq = lax.axis_index(SEQ).astype(jnp.int32)
    grad = out_grad[0]
    grad_theirs = across(lax.dynamic_slice(grad, (0, (1 - core) * 2048), (BLOCK, 2048)))
    got = exchange(pack(streams[:, 0], grad, out_weight, long_filter), SEQ)
    sent, lags = conv(
        seq[None], got, short_filter.reshape(9, 512), skip_gain.reshape(1, 512)
    )
    mixed, grad_streams = unpack(exchange(sent, SEQ))
    mixed_theirs = across(mixed)
    layer_out = jnp.dot(mixed, out_weight, preferred_element_type=F32).astype(BF)
    part = partial(core[None], mixed, mixed_theirs, grad, grad_theirs, lags)
    part = exchange(part.reshape(64, 16, 1152), CHIPS)
    shared = exchange(reduce(part, scale), DEPTH)
    lag_mine = shared[:, :, 1024:]
    rows = jnp.broadcast_to(shared[None, :, :, :1024], (8, 8, 16, 1024))
    mine = exchange(rows, SEQ)
    grad_weight, grad_filter = finish(core[None], mine, across(mine), lag_mine, across(lag_mine))
    return layer_out[None], grad_streams[:, None], grad_filter, grad_weight


def solution(mesh):
    fine = Mesh(mesh.devices.reshape(4, 2, 2, 4, 2), ("z", "yh", "c", "x", "yl"))
    dp = ("z", "yh", "c")
    placed = (P(None, dp, SEQ, None), P(), P(SEQ, None), P(), P(), P(dp, SEQ, None))
    return jax.shard_map(
        on_device,
        mesh=fine,
        in_specs=placed,
        out_specs=(P(dp, SEQ, None), P(None, dp, SEQ, None), P(SEQ, None), P()),
        check_vma=False,
    )
```

time: 1180 us -> 188 us (0.16)
  waiting for transfers between devices: 990 us -> 37 us
  blocking collectives: 0 us -> 81.5 us
  matrix products: 67.5 us -> 2.58 us
  other arithmetic: 58.3 us -> 0 us
  Pallas kernels: 0 us -> 41.4 us
  starting transfers between devices: 31.8 us -> 17.2 us
  between operations: 14.8 us -> 0.71 us
    ppermute x26 -> x4, waiting for transfers between devices: 693 us -> 2.86 us  [across(): return lax.ppermute(x, 'c', [(0, 1), (1, 0)])]
    psum x2 -> x0, waiting for transfers between devices: 297 us -> none  [the longest x1 167 us: on_device(): grad_out_weight = lax.psum(partial_value, ('dp', 'seq')) * grad_scale]
    all_to_all x0 -> x3, blocking collectives: none -> 81.5 us  [exchange(): return lax.all_to_all(x, axes, 0, 0, tiled=True)]
    dot_general x19 -> x1, matrix products: 67.5 us -> 2.58 us  [on_device(): jnp.dot(mixed, out_weight, preferred_element_type=F32).astype(BF)]
    pallas_call x0 -> x6, Pallas kernels: none -> 41.4 us  [the longest x1 17.7 us: conv(): pl.pallas_call(conv_kernel, grid_spec=pltpu.PrefetchScalarGridSpec(num_sc...]
    all_to_all x0 -> x2, waiting for transfers between devices: none -> 34.1 us  [exchange(): return lax.all_to_all(x, axes, 0, 0, tiled=True)]
    select_n x10 -> x0, other arithmetic: 32.1 us -> none  [the longest x3 17.5 us: forward_levels(): real_part = jnp.where(upper_half, turned_real, real_part + other_real)]
    ppermute x26 -> x4, starting transfers between devices: 31.7 us -> 7.67 us  [across(): return lax.ppermute(x, 'c', [(0, 1), (1, 0)])]
  transfers between devices with their start and end apart: 28 -> 6, of which waited for: 21 -> 4; matrix products, arithmetic and copies ran while one was open for 6% -> 2% of each run, Pallas kernels for 0% -> 1%
where the time goes in v1:
time: 188 us; the launch traced here: 187 us
  blocking collectives  81.5 us (43%)
  Pallas kernels  41.4 us (22%)
  waiting for transfers between devices  37 us (20%)
  starting transfers between devices  17.2 us (9%)
  local copies, waits for them, and re-layouts  6.83 us (4%)
  matrix products  2.58 us (1%)
    all_to_all x3, blocking collectives, exchange(): return lax.all_to_all(x, axes, 0, 0, tiled=True)  81.5 us
    all_to_all x2, waiting for transfers between devices, exchange(): return lax.all_to_all(x, axes, 0, 0, tiled=True)  34.1 us
    pallas_call x1, Pallas kernels, conv(): pl.pallas_call(conv_kernel, grid_spec=pltpu.PrefetchScalarGridSpec(num_sc...  17.7 us
    all_to_all x2, starting transfers between devices, exchange(): return lax.all_to_all(x, axes, 0, 0, tiled=True)  9.55 us
    pallas_call x1, Pallas kernels, finish(): pl.pallas_call(finish_kernel, grid_spec=pltpu.PrefetchScalarGridSpec(num_...  7.77 us
    ppermute x4, starting transfers between devices, across(): return lax.ppermute(x, 'c', [(0, 1), (1, 0)])  7.67 us
    pallas_call x1, Pallas kernels, pack(): pl.pallas_call(pack_kernel, grid=(steps,), in_specs=[pl.BlockSpec((3, BLO...  6.51 us
    unnamed x24, local copies, waits for them, and re-layouts  4.85 us
  transfers between devices with their start and end apart: 6, of which 4 were waited for; matrix products, arithmetic and copies ran while one was open for 2% of the time, Pallas kernels for 1%

profile of v1, /device:TPU:1, one launch (start us, length us, event | category | flops | bytes accessed | tf_op | source)
XLA Modules:
  0.0 187.2 jit_solution(7767134293554685214)
XLA Ops:
  0.6 6.5 %pack.1 = bf16[8,256,384]{2,1,0:T(8,128)(2,1)} custom-call(bf16[3,256,512]{2,1,0:T(8,128)(2,1)} %bitcast.18, bf16[256,4096]{1,0:T(8,128)(2,1)} %bitcast.15, bf16[512,4096]{1,0:T(8,128)(2,1)} %weight.1, f32[256,512]{1,0:T(8,128)} %filt.1), custom_call_target="tpu_custom_call" | custom-call | tf_op jit(solution)/shard_map/pack/pallas_call | solution.py:80
  7.1 6.0 %all-to-all-start = ((bf16[8,256,384]{2,1,0:T(8,128)(2,1)}), bf16[8,256,384]{2,1,0:T(8,128)(2,1)S(1)}, u32[]{:S(2)}, u32[]{:S(2)}) async-start(bf16[8,256,384]{2,1,0:T(8,128)(2,1)} %pack.1), calls=%async_computation | async-start | bytes 3145728 | tf_op jit(solution)/shard_map/all_to_all | solution.py:405
  13.1 0.6 reshape.19.short
  13.8 22.4 %all-to-all-done.got = bf16[8,256,384]{2,1,0:T(8,128)(2,1)S(1)} async-done(((bf16[8,256,384]{2,1,0:T(8,128)(2,1)}), bf16[8,256,384]{2,1,0:T(8,128)(2,1)S(1)}, u32[]{:S(2)}, u32[]{:S(2)}) %all-to-all-start) | async-done | bytes 1572896 | tf_op jit(solution)/shard_map/all_to_all | solution.py:405
  36.2 1.1 copy-done.2
  37.3 17.7 %conv.1 = (bf16[8,256,256]{2,1,0:T(8,128)(2,1)}, bf16[8,8,16,128]{3,2,1,0:T(8,128)(2,1)}) custom-call(s32[1]{0:T(128)} %bitcast.place, bf16[8,256,384]{2,1,0:T(8,128)(2,1)} %copy-done.2, f32[9,512]{1,0:T(8,128)} %reshape.19.short, f32[1,512]{1,0:T(1,128)} %bitcast.19, bf16[512,256]{1,0:T(8,128)(2,1)} %constant.30.clone.ahead_h, ...), custom_call_target="tpu_custom_call" | custom-call | tf_op jit(solution)/shard_map/conv/pallas_call | solution.py:240
  55.0 3.6 %all-to-all-start.1 = ((bf16[8,256,256]{2,1,0:T(8,128)(2,1)}), bf16[8,256,256]{2,1,0:T(8,128)(2,1)S(1)}, u32[]{:S(2)}, u32[]{:S(2)}) async-start(bf16[8,256,256]{2,1,0:T(8,128)(2,1)} %get-tuple-element.10), calls=%async_computation.1 | async-start | bytes 2097152 | tf_op jit(solution)/shard_map/all_to_all | solution.py:405
  58.6 1.1 dynamic-slice_bitcast_fusion
  59.7 1.6 collective-permute-start.1
  61.3 11.7 %all-to-all-done.1.got = bf16[8,256,256]{2,1,0:T(8,128)(2,1)S(1)} async-done(((bf16[8,256,256]{2,1,0:T(8,128)(2,1)}), bf16[8,256,256]{2,1,0:T(8,128)(2,1)S(1)}, u32[]{:S(2)}, u32[]{:S(2)}) %all-to-all-start.1) | async-done | bytes 1048608 | tf_op jit(solution)/shard_map/all_to_all | solution.py:405
  73.0 1.0 copy-done.4
  73.9 2.6 %unpack.1 = (bf16[256,512]{1,0:T(8,128)(2,1)}, bf16[3,256,512]{2,1,0:T(8,128)(2,1)}) custom-call(bf16[8,256,256]{2,1,0:T(8,128)(2,1)} %copy-done.4), custom_call_target="tpu_custom_call" | custom-call | tf_op jit(solution)/shard_map/unpack/pallas_call | solution.py:291
  76.5 2.1 %collective-permute-start = (bf16[256,512]{1,0:T(8,128)(2,1)}, bf16[256,512]{1,0:T(8,128)(2,1)S(1)}, u32[]{:S(2)}, u32[]{:S(2)}) collective-permute-start(bf16[256,512]{1,0:T(8,128)(2,1)} %get-tuple-element.11.mine), channel_id=1, source_target_pairs={{0,8},{8,0},{1,9},{9,1},{2,10},{10,2},{3,11},{11,3},{4,12},{12,4},... | collective-permute-start | bytes 786440 | tf_op jit(solution)/shard_map/ppermute | solution.py:409
  78.6 0.0 collective-permute-done.1.grad_theirs
  78.6 1.4 collective-permute-done.theirs
  80.0 0.7 copy-done.10
  80.7 4.0 %partial.1 = bf16[4,2,8,16,1152]{4,3,2,1,0:T(8,128)(2,1)} custom-call(s32[1]{0:T(128)} %bitcast.7.place, bf16[256,512]{1,0:T(8,128)(2,1)} %get-tuple-element.11.mine, bf16[256,512]{1,0:T(8,128)(2,1)} %copy-done.10, bf16[256,4096]{1,0:T(8,128)(2,1)} %bitcast.16, bf16[256,2048]{1,0:T(8,128)(2,1)} %copy-done.6, bf16[8,8,16,128]{3,2,1,0:T(8,128)(2,1)} %get-tuple-element.13.lags), custom_call_target="tpu_custom_call" | custom-call | tf_op jit(solution)/shard_map/partial/pallas_call | solution.py:316
  84.7 41.2 %all_to_all.25.got = bf16[64,16,1152]{2,1,0:T(8,128)(2,1)} all-to-all(bf16[64,16,1152]{2,1,0:T(8,128)(2,1)} %bitcast.17), channel_id=1, replica_groups=mesh['z'=4,'yh'=2,'c'=2,'x'=4,'yl'=2] {'z','yh','x','yl'}, dimensions={0} | all-to-all | bytes 4718592 | tf_op jit(solution)/shard_map/all_to_all | solution.py:405
  125.9 2.8 %reduce.1 = bf16[8,16,2048]{2,1,0:T(8,128)(2,1)} custom-call(bf16[64,16,1152]{2,1,0:T(8,128)(2,1)} %all_to_all.25.got), custom_call_target="tpu_custom_call" | custom-call | tf_op jit(solution)/shard_map/reduce/pallas_call | solution.py:352
  128.7 13.4 %all_to_all.26 = bf16[8,16,2048]{2,1,0:T(8,128)(2,1)S(1)} all-to-all(bf16[8,16,2048]{2,1,0:T(8,128)(2,1)} %reduce.1), channel_id=1, replica_groups=mesh['z'=4,'yh'=2,'c'=2,'x'=4,'yl'=2] {'z','yh'}, dimensions={0} | all-to-all | bytes 1048576 | tf_op jit(solution)/shard_map/all_to_all | solution.py:405
  142.2 0.3 broadcast_in_dim.23
  142.5 0.0 copy-start.3
  142.5 26.9 %all_to_all.27.mine = bf16[8,8,16,1024]{3,2,1,0:T(8,128)(2,1)S(1)} all-to-all(bf16[8,8,16,1024]{3,2,1,0:T(8,128)(2,1)S(1)} %broadcast_in_dim.23), channel_id=1, replica_groups=mesh['z'=4,'yh'=2,'c'=2,'x'=4,'yl'=2] {'x','yl'}, dimensions={0} | all-to-all | bytes 4194304 | tf_op jit(solution)/shard_map/all_to_all | solution.py:405
  169.4 3.9 %collective-permute-start.2 = (bf16[8,8,16,1024]{3,2,1,0:T(8,128)(2,1)S(1)}, bf16[8,8,16,1024]{3,2,1,0:T(8,128)(2,1)S(1)}, u32[]{:S(2)}, u32[]{:S(2)}) collective-permute-start(bf16[8,8,16,1024]{3,2,1,0:T(8,128)(2,1)S(1)} %all_to_all.27.mine), channel_id=1, source_target_pairs={{0,8},{8,0},{1,9},{9,1},{2,10},{10,2},{3,11},{11,3},{4,12},{12,4},... | collective-permute-start | bytes 6291464 | tf_op jit(solution)/shard_map/ppermute | solution.py:409
  173.3 0.1 collective-permute-start.3
  173.4 2.6 %fusion = bf16[1,256,4096]{2,1,0:T(8,128)(2,1)} fusion(bf16[256,512]{1,0:T(8,128)(2,1)S(1)} %copy-done.8, bf16[512,4096]{1,0:T(8,128)(2,1)S(1)} %copy-done.3), kind=kOutput, calls=%fused_computation.1 | convolution fusion | flops 1074790400 | bytes 6553600 | tf_op jit(solution)/shard_map/dot_general | solution.py:424
  175.9 0.0 copy-done.1
  175.9 1.5 collective-permute-done.3.lag_theirs
  177.4 0.0 collective-permute-done.2.theirs
  177.4 0.7 copy-done.9
  178.2 1.3 copy-done.5
  179.4 7.8 %finish.1 = (f32[512,4096]{1,0:T(8,128)}, f32[256,512]{1,0:T(8,128)}) custom-call(s32[1]{0:T(128)} %bitcast.7.place, bf16[8,8,16,1024]{3,2,1,0:T(8,128)(2,1)} %copy-done.1, bf16[8,8,16,1024]{3,2,1,0:T(8,128)(2,1)} %copy-done.5, bf16[8,16,1024]{2,1,0:T(8,128)(2,1)} %copy-done.7, bf16[8,16,1024]{2,1,0:T(8,128)(2,1)} %copy-done.9), custom_call_target="tpu_custom_call" | custom-call | tf_op jit(solution)/shard_map/finish/pallas_call | solution.py:385
  (18 shorter events, 0.1 us)
Async XLA Ops:
  7.1 6.0 %copy-start.11 = (f32[3,3,512]{2,1,0:T(4,128)S(1)}, f32[3,3,512]{2,1,0:T(4,128)}, u32[]{:S(2)}) copy-start(f32[3,3,512]{2,1,0:T(4,128)} %param.11) | copy-start | bytes 55300
  7.1 29.0 %all-to-all-start = ((bf16[8,256,384]{2,1,0:T(8,128)(2,1)}), bf16[8,256,384]{2,1,0:T(8,128)(2,1)S(1)}, u32[]{:S(2)}, u32[]{:S(2)}) async-start(bf16[8,256,384]{2,1,0:T(8,128)(2,1)} %pack.1), calls=%async_computation | async-start | bytes 3145728 | tf_op jit(solution)/shard_map/all_to_all | solution.py:405
  36.2 1.1 copy-start.2
  37.3 21.3 %copy-start = (bf16[1,256,4096]{2,1,0:T(8,128)(2,1)S(1)}, bf16[1,256,4096]{2,1,0:T(8,128)(2,1)}, u32[]{:S(2)}) copy-start(bf16[1,256,4096]{2,1,0:T(8,128)(2,1)} %param.15) | copy-start | bytes 6291460
  55.0 18.0 %all-to-all-start.1 = ((bf16[8,256,256]{2,1,0:T(8,128)(2,1)}), bf16[8,256,256]{2,1,0:T(8,128)(2,1)S(1)}, u32[]{:S(2)}, u32[]{:S(2)}) async-start(bf16[8,256,256]{2,1,0:T(8,128)(2,1)} %get-tuple-element.10), calls=%async_computation.1 | async-start | bytes 2097152 | tf_op jit(solution)/shard_map/all_to_all | solution.py:405
  59.7 19.0 %collective-permute-start.1 = (bf16[256,2048]{1,0:T(8,128)(2,1)}, bf16[256,2048]{1,0:T(8,128)(2,1)S(1)}, u32[]{:S(2)}, u32[]{:S(2)}) collective-permute-start(bf16[256,2048]{1,0:T(8,128)(2,1)} %dynamic-slice_bitcast_fusion), channel_id=1, source_target_pairs={{0,8},{8,0},{1,9},{9,1},{2,10},{10,2},{3,11},{11,3},{4,12},{12,4},... | collective-permute-start | bytes 3145736 | tf_op jit(solution)/shard_map/ppermute | solution.py:409
  73.0 1.0 copy-start.4
  76.5 3.4 %collective-permute-start = (bf16[256,512]{1,0:T(8,128)(2,1)}, bf16[256,512]{1,0:T(8,128)(2,1)S(1)}, u32[]{:S(2)}, u32[]{:S(2)}) collective-permute-start(bf16[256,512]{1,0:T(8,128)(2,1)} %get-tuple-element.11.mine), channel_id=1, source_target_pairs={{0,8},{8,0},{1,9},{9,1},{2,10},{10,2},{3,11},{11,3},{4,12},{12,4},... | collective-permute-start | bytes 786440 | tf_op jit(solution)/shard_map/ppermute | solution.py:409
  78.6 1.4 copy-start.6
  80.0 0.7 copy-start.10
  142.2 31.1 %copy-start.7 = (bf16[8,16,1024]{2,1,0:T(8,128)(2,1)}, bf16[8,16,1024]{2,1,0:T(8,128)(2,1)S(1)}, u32[]{:S(2)}) copy-start(bf16[8,16,1024]{2,1,0:T(8,128)(2,1)S(1)} %get-tuple-element.20.lag_mine) | copy-start | bytes 786436
  142.2 31.2 %copy-start.8 = (bf16[256,512]{1,0:T(8,128)(2,1)S(1)}, bf16[256,512]{1,0:T(8,128)(2,1)}, u32[]{:S(2)}) copy-start(bf16[256,512]{1,0:T(8,128)(2,1)} %get-tuple-element.11.mine) | copy-start | bytes 786436
  142.5 30.9 %copy-start.3 = (bf16[512,4096]{1,0:T(8,128)(2,1)S(1)}, bf16[512,4096]{1,0:T(8,128)(2,1)}, u32[]{:S(2)}) copy-start(bf16[512,4096]{1,0:T(8,128)(2,1)} %weight.1) | copy-start | bytes 12582916
  169.4 6.6 %copy-start.1 = (bf16[8,8,16,1024]{3,2,1,0:T(8,128)(2,1)}, bf16[8,8,16,1024]{3,2,1,0:T(8,128)(2,1)S(1)}, u32[]{:S(2)}) copy-start(bf16[8,8,16,1024]{3,2,1,0:T(8,128)(2,1)S(1)} %all_to_all.27.mine) | copy-start | bytes 6291460
  169.4 8.1 %collective-permute-start.2 = (bf16[8,8,16,1024]{3,2,1,0:T(8,128)(2,1)S(1)}, bf16[8,8,16,1024]{3,2,1,0:T(8,128)(2,1)S(1)}, u32[]{:S(2)}, u32[]{:S(2)}) collective-permute-start(bf16[8,8,16,1024]{3,2,1,0:T(8,128)(2,1)S(1)} %all_to_all.27.mine), channel_id=1, source_target_pairs={{0,8},{8,0},{1,9},{9,1},{2,10},{10,2},{3,11},{11,3},{4,12},{12,4},... | collective-permute-start | bytes 6291464 | tf_op jit(solution)/shard_map/ppermute | solution.py:409
  173.3 4.2 %collective-permute-start.3 = (bf16[8,16,1024]{2,1,0:T(8,128)(2,1)S(1)}, bf16[8,16,1024]{2,1,0:T(8,128)(2,1)S(1)}, u32[]{:S(2)}, u32[]{:S(2)}) collective-permute-start(bf16[8,16,1024]{2,1,0:T(8,128)(2,1)S(1)} %get-tuple-element.20.lag_mine), channel_id=1, source_target_pairs={{0,8},{8,0},{1,9},{9,1},{2,10},{10,2},{3,11},{11,3},{4,12},{12,4},... | collective-permute-start | bytes 786440 | tf_op jit(solution)/shard_map/ppermute | solution.py:409
  177.4 0.7 copy-start.9
  178.2 1.3 copy-start.5

commit v2 on v1

--- a/solution.py
+++ b/solution.py
@@ -13,6 +13,7 @@
 F32 = jnp.float32
 BLOCK = 256
 HALF = 64
+SENT_ROWS = BLOCK + 64
 SEQ = ("x", "yl")
 DEPTH = ("z", "yh")
 CHIPS = DEPTH + SEQ
@@ -47,6 +48,7 @@
 
 def pack_kernel(streams, out_grad, weight, filt, packed, total):
     step = pl.program_id(0)
+    low = low_lanes(BLOCK)
 
     @pl.when(step == 0)
     def _():
@@ -56,22 +58,30 @@
         out_grad[...], weight[...], (((1,), (1,)), ((), ())), preferred_element_type=F32
     )
 
+    def put(q, tile, a, b):
+        lanes = slice(128 * tile, 128 * tile + 128)
+        packed[2 * q, 0:BLOCK, lanes] = jnp.where(low, a, turned(b)).astype(BF)
+        packed[2 * q + 1, 0:BLOCK, lanes] = jnp.where(low, turned(a), b).astype(BF)
+
+    for q in range(4):
+        lanes = slice(128 * q, 128 * q + 128)
+
+        @pl.when(step == q)
+        def _(q=q, lanes=lanes):
+            put(q, 0, streams[0, :, lanes].astype(F32), streams[1, :, lanes].astype(F32))
+            low64 = low_lanes(64)
+            for n in range(2):
+                a = filt[128 * n : 128 * n + 64, lanes]
+                b = filt[128 * n + 64 : 128 * n + 128, lanes]
+                there = slice(128 * n, 128 * n + 128)
+                packed[2 * q, BLOCK:, there] = jnp.where(low64, a, turned(b)).astype(BF)
+                packed[2 * q + 1, BLOCK:, there] = jnp.where(low64, turned(a), b).astype(BF)
+
     @pl.when(step == pl.num_programs(0) - 1)
     def _():
-        low = low_lanes(BLOCK)
         for q in range(4):
             lanes = slice(128 * q, 128 * q + 128)
-            whole = filt[:, lanes]
-            high = whole.astype(BF).astype(F32)
-            pairs = (
-                (streams[0, :, lanes].astype(F32), streams[1, :, lanes].astype(F32)),
-                (streams[2, :, lanes].astype(F32), total[:, lanes]),
-                (high, whole - high),
-            )
-            for n, (a, b) in enumerate(pairs):
-                there = slice(128 * n, 128 * n + 128)
-                packed[2 * q, :, there] = jnp.where(low, a, turned(b)).astype(BF)
-                packed[2 * q + 1, :, there] = jnp.where(low, turned(a), b).astype(BF)
+            put(q, 1, streams[2, :, lanes].astype(F32), total[:, lanes])
 
 
 def pack(streams, out_grad, weight, filt):
@@ -86,8 +96,8 @@
             pl.BlockSpec((512, wide), lambda k: (0, k)),
             pl.BlockSpec((BLOCK, 512), lambda k: (0, 0)),
         ],
-        out_specs=pl.BlockSpec((8, BLOCK, 384), lambda k: (0, 0, 0)),
-        out_shape=jax.ShapeDtypeStruct((8, BLOCK, 384), BF),
+        out_specs=pl.BlockSpec((8, SENT_ROWS, 256), lambda k: (0, 0, 0)),
+        out_shape=jax.ShapeDtypeStruct((8, SENT_ROWS, 256), BF),
         scratch_shapes=[pltpu.VMEM((BLOCK, 512), F32)],
         name="pack",
     )(streams, out_grad, weight, filt)
@@ -129,24 +139,42 @@
         return high, (x - high.astype(F32)).astype(BF)
 
     def apply(table_h, table_l, high, rest):
-        both = mm(table_h[...], jnp.concatenate([high, rest], axis=1))
-        return both[:, :128] + both[:, 128:] + mm(table_l[...], high)
+        return mm(table_h[...], high) + mm(table_h[...], rest) + mm(table_l[...], high)
 
     sa_pad[0:8] = jnp.zeros((8, 128), F32)
     sv_pad[0:8] = jnp.zeros((8, 128), F32)
 
-    def unpack(b, carry):
+    def load(b, carry):
         rows = pl.ds(pl.multiple_of(8 + BLOCK * b, 8), BLOCK)
-        sa_pad[rows] = got[b, :, 0:128].astype(F32)
-        sv_pad[rows] = got[b, :, 128:256].astype(F32)
-        f = got[b, :, 256:384].astype(F32)
-        g = turned(f)
-        high = jnp.where(low, f, g).astype(BF)
-        rest = jnp.where(low, g, f).astype(BF)
-        fspec[b] = apply(ahead_h, ahead_l, high, rest)
+        sa_pad[rows] = got[b, 0:BLOCK, 0:128].astype(F32)
+        sv_pad[rows] = got[b, 0:BLOCK, 128:256].astype(F32)
         return carry
 
-    lax.fori_loop(0, 8, unpack, 0)
+    lax.fori_loop(0, 8, load, 0)
+
+    low64 = low_lanes(64)
+
+    def filters(n, carry):
+        def pair(b):
+            parts = []
+            for t in range(2):
+                x = got[b, BLOCK:, 128 * t : 128 * t + 128].astype(F32)
+                y = got[b + 1, BLOCK:, 128 * t : 128 * t + 128].astype(F32)
+                parts.append(jnp.where(low64, x, turned(y)))
+                parts.append(jnp.where(low64, turned(x), y))
+            return jnp.concatenate(parts, axis=0).astype(BF)
+
+        f = jnp.concatenate([pair(4 * n), pair(4 * n + 2)], axis=1)
+        out = mm(ahead_h[...], f) + mm(ahead_l[...], f)
+        low512 = low_lanes(512)
+        for t in range(2):
+            x = out[:, 128 * t : 128 * t + 128]
+            y = turned(x)
+            fspec[4 * n + 2 * t] = jnp.where(low512, x, y)
+            fspec[4 * n + 2 * t + 1] = jnp.where(low512, y, x)
+        return carry
+
+    lax.fori_loop(0, 2, filters, 0)
 
     for b in range(8):
         start = 8 + BLOCK * b
@@ -156,14 +184,17 @@
         sv[b] = v
         prod[b] = turned(a) * v
 
-    def transform(b, carry):
-        high, rest = split(jnp.where(low, prod[b], prod[7 - b]))
-        out = apply(ahead_h, ahead_l, high, rest)
-        spec[b, 0:BLOCK] = out[:BLOCK]
-        spec[b, BLOCK:] = out[BLOCK:] * sigma
+    def transform(n, carry):
+        x = jnp.concatenate(
+            [jnp.where(low, prod[b], prod[7 - b]) for b in (2 * n, 2 * n + 1)], axis=1
+        )
+        out = apply(ahead_h, ahead_l, *split(x))
+        for t in range(2):
+            spec[2 * n + t, 0:BLOCK] = out[:BLOCK, 128 * t : 128 * t + 128]
+            spec[2 * n + t, BLOCK:] = out[BLOCK:, 128 * t : 128 * t + 128] * sigma
         return carry
 
-    lax.fori_loop(0, 8, transform, 0)
+    lax.fori_loop(0, 4, transform, 0)
 
     for sign, base in ((1.0, 0), (-1.0, 128)):
 
@@ -191,30 +222,51 @@
                 tr, ti = summed([(filt[m], both[i - m]) for m in range(i + 1)])
                 res[i, re] = tr
                 res[i, im] = ti
-            moved = [(turned(r), turned(i)) for r, i in both]
-            for m in range(8):
-                tr, ti = summed([(own[7 - i], moved[i - m]) for i in range(m, 8)])
-                lres[m, re] = tr
-                lres[m, im] = ti
+            zero = jnp.zeros((8, 128), F32)
+            low8 = low_lanes(8)
+            grads, shifted = [], []
+            for i in range(8):
+                grads.append(
+                    tuple(jnp.where(low8, turned(own[7 - i][k]), own[7 - i][k]) for k in range(2))
+                )
+                before = both[i - 1] if i else (zero, zero)
+                shifted.append(
+                    tuple(jnp.where(low8, before[k], turned(both[i][k])) for k in range(2))
+                )
+            for a in range(4):
+                tr, ti = summed([(grads[i], shifted[i - 2 * a]) for i in range(2 * a, 8)])
+                lres[a, re] = tr
+                lres[a, im] = ti
             return carry
 
         lax.fori_loop(0, 16, multiply, 0)
 
-    def invert(b, carry):
-        def one(src):
-            x = jnp.concatenate([src[b, 0:BLOCK], src[b, BLOCK:] * sigma], axis=0)
-            return apply(back_h, back_l, *split(x))
-
-        time[b] = one(res)
-        lag = one(lres)
+    def flipped(x, sign):
+        return jnp.concatenate([x[0:BLOCK], x[BLOCK:] * sign], axis=0)
+
+    def invert(n, carry):
+        x = jnp.concatenate([flipped(res[b], sigma) for b in (2 * n, 2 * n + 1)], axis=1)
+        out = apply(back_h, back_l, *split(x))
+        time[2 * n] = out[:, :128]
+        time[2 * n + 1] = out[:, 128:]
+        return carry
+
+    lax.fori_loop(0, 4, invert, 0)
+
+    def invert_lags(n, carry):
+        x = jnp.concatenate([flipped(lres[a], -1.0) for a in (2 * n, 2 * n + 1)], axis=1)
+        out = apply(back_h, back_l, *split(x))
         low16 = low_lanes(16)
-        for k in range(8):
-            a = lag[32 * k : 32 * k + 16]
-            c = lag[32 * k + 16 : 32 * k + 32]
-            lags[b, k] = jnp.where(low16, turned(a), c).astype(BF)
+        for t in range(2):
+            for k in range(8):
+                x = out[32 * k : 32 * k + 16, 128 * t : 128 * t + 128]
+                y = out[32 * k + 16 : 32 * k + 32, 128 * t : 128 * t + 128]
+                m = 4 * n + 2 * t
+                lags[m, k] = jnp.where(low16, turned(x), y).astype(BF)
+                lags[m + 1, k] = jnp.where(low16, x, turned(y)).astype(BF)
         return carry
 
-    lax.fori_loop(0, 8, invert, 0)
+    lax.fori_loop(0, 2, invert_lags, 0)
 
     def gate(b, carry):
         t = jnp.where(low, time[b], time[7 - b]) + gain * prod[b]
@@ -243,7 +295,7 @@
             num_scalar_prefetch=1,
             grid=(1,),
             in_specs=[
-                full(8, BLOCK, 384),
+                full(8, SENT_ROWS, 256),
                 pl.BlockSpec((9, 128), lambda n, p: (0, p[0] // 2)),
                 pl.BlockSpec((1, 128), lambda n, p: (0, p[0] // 2)),
                 full(512, BLOCK),
@@ -261,7 +313,7 @@
                 pltpu.VMEM((8, 512, 128), F32),
                 pltpu.VMEM((8, 512, 128), F32),
                 pltpu.VMEM((8, 512, 128), F32),
-                pltpu.VMEM((8, 512, 128), F32),
+                pltpu.VMEM((4, 512, 128), F32),
                 pltpu.VMEM((8, BLOCK, 128), F32),
                 pltpu.VMEM((8 + 8 * BLOCK, 128), F32),
                 pltpu.VMEM((8 + 8 * BLOCK, 128), F32),
@@ -275,26 +327,44 @@
     )(place, got, short, skip, ahead_h, ahead_l, back_h, back_l)
 
 
-def unpack_kernel(got, mixed, grads):
-    low = low_lanes(BLOCK)
+def spread(got, there, first, second, low):
     for q in range(4):
         lanes = slice(128 * q, 128 * q + 128)
-        for n, (first, second) in enumerate(((grads.at[1], grads.at[0]), (mixed, grads.at[2]))):
-            there = slice(128 * n, 128 * n + 128)
-            a = got[2 * q, :, there].astype(F32)
-            b = got[2 * q + 1, :, there].astype(F32)
+        a = got[2 * q, :, there].astype(F32)
+        b = got[2 * q + 1, :, there].astype(F32)
+        if first is not None:
             first[:, lanes] = jnp.where(low, a, turned(b)).astype(BF)
+        if second is not None:
             second[:, lanes] = jnp.where(low, turned(a), b).astype(BF)
 
 
-def unpack(got):
-    return pl.pallas_call(
-        unpack_kernel,
-        out_shape=[
-            jax.ShapeDtypeStruct((BLOCK, 512), BF),
-            jax.ShapeDtypeStruct((3, BLOCK, 512), BF),
-        ],
-        name="unpack",
+def mixed_kernel(got, mixed):
+    spread(got, slice(0, 128), mixed, None, low_lanes(BLOCK))
+
+
+def unpack_mixed(got):
+    return pl.pallas_call(
+        mixed_kernel,
+        grid=(1,),
+        in_specs=[pl.BlockSpec((8, BLOCK, 128), lambda n: (0, 0, 1))],
+        out_specs=pl.BlockSpec((BLOCK, 512), lambda n: (0, 0)),
+        out_shape=jax.ShapeDtypeStruct((BLOCK, 512), BF),
+        name="unpack_mixed",
+    )(got)
+
+
+def grads_kernel(got, grads):
+    low = low_lanes(BLOCK)
+    spread(got, slice(0, 128), grads.at[1], grads.at[0], low)
+    spread(got, slice(128, 256), None, grads.at[2], low)
+
+
+def unpack_grads(got):
+    return pl.pallas_call(
+        grads_kernel,
+        out_shape=jax.ShapeDtypeStruct((3, BLOCK, 512), BF),
+        cost_estimate=pl.CostEstimate(flops=10**6, bytes_accessed=2 * 10**6, transcendentals=0),
+        name="unpack_grads",
     )(got)
 
 
@@ -356,49 +426,53 @@
     )(got)
 
 
-def finish_kernel(place, mine, theirs, lag_mine, lag_theirs, grad_weight, grad_filter):
-    core = place[0]
+def half_kernel(place, mine, *refs):
+    grad_weight = refs[-1]
     for k in range(8):
         rows = slice(16 * (k // 2), 16 * (k // 2) + 16)
-        for half, src in ((core, mine), (1 - core, theirs)):
-            lanes = pl.ds(pl.multiple_of(2048 * half + 1024 * (k % 2), 1024), 1024)
-            grad_weight[rows, lanes] = src[0, k].astype(F32)
-
-    @pl.when(pl.program_id(0) == 0)
-    def _():
-        low = low_lanes(16)
-        for k in range(8):
-            for q in range(4):
-                def both(s):
-                    there = slice(128 * s, 128 * s + 128)
-                    return lag_mine[k, :, there].astype(F32) + lag_theirs[k, :, there].astype(F32)
-
-                a, b = both(2 * q), both(2 * q + 1)
-                lanes = slice(128 * q, 128 * q + 128)
-                grad_filter[32 * k : 32 * k + 16, lanes] = jnp.where(low, a, turned(b))
-                grad_filter[32 * k + 16 : 32 * k + 32, lanes] = jnp.where(low, turned(a), b)
-
-
-def finish(place, mine, theirs, lag_mine, lag_theirs):
-    lag_spec = pl.BlockSpec((8, 16, 1024), lambda s, p: (0, 0, 0))
-    half_spec = pl.BlockSpec((1, 8, 16, 1024), lambda s, p: (s, 0, 0, 0))
-    return pl.pallas_call(
-        finish_kernel,
+        lanes = slice(1024 * (k % 2), 1024 * (k % 2) + 1024)
+        grad_weight[rows, lanes] = mine[0, k].astype(F32)
+
+
+def write_half(half, rows, whole=None):
+    more = [] if whole is None else [whole]
+    return pl.pallas_call(
+        half_kernel,
         grid_spec=pltpu.PrefetchScalarGridSpec(
             num_scalar_prefetch=1,
             grid=(8,),
-            in_specs=[half_spec, half_spec, lag_spec, lag_spec],
-            out_specs=[
-                pl.BlockSpec((64, 4096), lambda s, p: (s, 0)),
-                pl.BlockSpec((BLOCK, 512), lambda s, p: (0, 0)),
-            ],
+            in_specs=[pl.BlockSpec((1, 8, 16, 1024), lambda s, p: (s, 0, 0, 0))]
+            + [pl.BlockSpec(memory_space=pl.ANY)] * len(more),
+            out_specs=pl.BlockSpec((64, 2048), lambda s, p: (s, p[0])),
         ),
-        out_shape=[
-            jax.ShapeDtypeStruct((512, 4096), F32),
-            jax.ShapeDtypeStruct((BLOCK, 512), F32),
-        ],
-        name="finish",
-    )(place, mine, theirs, lag_mine, lag_theirs)
+        out_shape=jax.ShapeDtypeStruct((512, 4096), F32),
+        input_output_aliases={2: 0} if more else {},
+        cost_estimate=pl.CostEstimate(flops=10**6, bytes_accessed=6 * 10**6, transcendentals=0),
+        name="write_half",
+    )(half, rows, *more)
+
+
+def filter_kernel(lag_mine, lag_theirs, grad_filter):
+    low = low_lanes(16)
+    for k in range(8):
+        for q in range(4):
+            def both(s):
+                there = slice(128 * s, 128 * s + 128)
+                return lag_mine[k, :, there].astype(F32) + lag_theirs[k, :, there].astype(F32)
+
+            a, b = both(2 * q), both(2 * q + 1)
+            lanes = slice(128 * q, 128 * q + 128)
+            grad_filter[32 * k : 32 * k + 16, lanes] = jnp.where(low, a, turned(b))
+            grad_filter[32 * k + 16 : 32 * k + 32, lanes] = jnp.where(low, turned(a), b)
+
+
+def write_filter(lag_mine, lag_theirs):
+    return pl.pallas_call(
+        filter_kernel,
+        out_shape=jax.ShapeDtypeStruct((BLOCK, 512), F32),
+        cost_estimate=pl.CostEstimate(flops=10**6, bytes_accessed=2 * 10**6, transcendentals=0),
+        name="write_filter",
+    )(lag_mine, lag_theirs)
 
 
 def exchange(x, axes):
@@ -419,16 +493,24 @@
     sent, lags = conv(
         seq[None], got, short_filter.reshape(9, 512), skip_gain.reshape(1, 512)
     )
-    mixed, grad_streams = unpack(exchange(sent, SEQ))
+    back = exchange(sent, SEQ)
+    mixed = unpack_mixed(back)
     mixed_theirs = across(mixed)
+    part = partial(core[None], mixed, mixed_theirs, grad, grad_theirs, lags)
+    part, mixed, back = lax.optimization_barrier((part, mixed, back))
+    part = exchange(part.reshape(64, 16, 1152), CHIPS)
     layer_out = jnp.dot(mixed, out_weight, preferred_element_type=F32).astype(BF)
-    part = partial(core[None], mixed, mixed_theirs, grad, grad_theirs, lags)
-    part = exchange(part.reshape(64, 16, 1152), CHIPS)
+    grad_streams = unpack_grads(back)
+    part, layer_out, grad_streams = lax.optimization_barrier((part, layer_out, grad_streams))
     shared = exchange(reduce(part, scale), DEPTH)
     lag_mine = shared[:, :, 1024:]
+    lag_theirs = across(lag_mine)
     rows = jnp.broadcast_to(shared[None, :, :, :1024], (8, 8, 16, 1024))
     mine = exchange(rows, SEQ)
-    grad_weight, grad_filter = finish(core[None], mine, across(mine), lag_mine, across(lag_mine))
+    grad_filter = write_filter(lag_mine, lag_theirs)
+    theirs = across(mine)
+    grad_weight = write_half(core[None], mine)
+    grad_weight = write_half(1 - core[None], theirs, grad_weight)
     return layer_out[None], grad_streams[:, None], grad_filter, grad_weight
 
 

time: 188 us -> 185 us (0.984)
  blocking collectives: 81.5 us -> 40.2 us
  waiting for transfers between devices: 37 us -> 60.4 us
  starting transfers between devices: 17.2 us -> 26.4 us
  Pallas kernels: 41.4 us -> 44.4 us
  matrix products: 2.58 us -> 4.77 us
    all_to_all x3 -> x2, blocking collectives: 81.5 us -> 40.2 us  [exchange(): return lax.all_to_all(x, axes, 0, 0, tiled=True)]
    all_to_all x2 -> x3, waiting for transfers between devices: 34.1 us -> 55.1 us  [exchange(): return lax.all_to_all(x, axes, 0, 0, tiled=True)]
    all_to_all x2 -> x3, starting transfers between devices: 9.55 us -> 18.5 us  [exchange(): return lax.all_to_all(x, axes, 0, 0, tiled=True)]
    pallas_call x2 -> x5, Pallas kernels: 10.4 us -> 18.3 us  [the longest x2 11.9 us: write_half(): pl.pallas_call(half_kernel, grid_spec=pltpu.PrefetchScalarGridSpec(num_sc...]
    pallas_call x1, Pallas kernels: 17.7 us -> 13 us  [conv(): pl.pallas_call(conv_kernel, grid_spec=pltpu.PrefetchScalarGridSpec(num_sc...]
    ppermute x4, waiting for transfers between devices: 2.86 us -> 5.31 us  [across(): return lax.ppermute(x, 'c', [(0, 1), (1, 0)])]
    dot_general x1, matrix products: 2.58 us -> 4.77 us  [on_device(): jnp.dot(mixed, out_weight, preferred_element_type=F32).astype(BF)]
    unnamed x24 -> x22, local copies, waits for them, and re-layouts: 4.85 us -> 4.87 us
  transfers between devices with their start and end apart: 6 -> 7, of which waited for: 4 -> 5; matrix products, arithmetic and copies ran while one was open for 2% -> 4% of each run, Pallas kernels for 1% -> 7%
where the time goes in v2:
time: 185 us; the launch traced here: 184 us
  waiting for transfers between devices  60.4 us (33%)
  Pallas kernels  44.4 us (24%)
  blocking collectives  40.2 us (22%)
  starting transfers between devices  26.4 us (14%)
  local copies, waits for them, and re-layouts  6.86 us (4%)
  matrix products  4.77 us (3%)
    all_to_all x3, waiting for transfers between devices, exchange(): return lax.all_to_all(x, axes, 0, 0, tiled=True)  55.1 us
    all_to_all x2, blocking collectives, exchange(): return lax.all_to_all(x, axes, 0, 0, tiled=True)  40.2 us
    all_to_all x3, starting transfers between devices, exchange(): return lax.all_to_all(x, axes, 0, 0, tiled=True)  18.5 us
    pallas_call x1, Pallas kernels, conv(): pl.pallas_call(conv_kernel, grid_spec=pltpu.PrefetchScalarGridSpec(num_sc...  13 us
    pallas_call x2, Pallas kernels, write_half(): pl.pallas_call(half_kernel, grid_spec=pltpu.PrefetchScalarGridSpec(num_sc...  11.9 us
    ppermute x4, starting transfers between devices, across(): return lax.ppermute(x, 'c', [(0, 1), (1, 0)])  7.96 us
    pallas_call x1, Pallas kernels, pack(): pl.pallas_call(pack_kernel, grid=(steps,), in_specs=[pl.BlockSpec((3, BLO...  6.38 us
    ppermute x4, waiting for transfers between devices, across(): return lax.ppermute(x, 'c', [(0, 1), (1, 0)])  5.31 us
  transfers between devices with their start and end apart: 7, of which 5 were waited for; matrix products, arithmetic and copies ran while one was open for 4% of the time, Pallas kernels for 7%

profile of v2, /device:TPU:1, one launch (start us, length us, event | category | flops | bytes accessed | tf_op | source)
XLA Modules:
  0.0 183.8 jit_solution(8129862970996185783)
XLA Ops:
  0.6 6.4 %pack.1 = bf16[8,320,256]{2,1,0:T(8,128)(2,1)} custom-call(bf16[3,256,512]{2,1,0:T(8,128)(2,1)} %bitcast.17, bf16[256,4096]{1,0:T(8,128)(2,1)} %bitcast.14, bf16[512,4096]{1,0:T(8,128)(2,1)} %weight.1, f32[256,512]{1,0:T(8,128)} %filt.1), custom_call_target="tpu_custom_call" | custom-call | tf_op jit(solution)/shard_map/pack/pallas_call | solution.py:90
  7.0 6.0 %all-to-all-start = ((bf16[8,320,256]{2,1,0:T(8,128)(2,1)}), bf16[8,320,256]{2,1,0:T(8,128)(2,1)S(1)}, u32[]{:S(2)}, u32[]{:S(2)}) async-start(bf16[8,320,256]{2,1,0:T(8,128)(2,1)} %pack.1), calls=%async_computation | async-start | bytes 2621440 | tf_op jit(solution)/shard_map/all_to_all | solution.py:479
  13.0 0.6 reshape.19.short
  13.7 18.6 %all-to-all-done.got = bf16[8,320,256]{2,1,0:T(8,128)(2,1)S(1)} async-done(((bf16[8,320,256]{2,1,0:T(8,128)(2,1)}), bf16[8,320,256]{2,1,0:T(8,128)(2,1)S(1)}, u32[]{:S(2)}, u32[]{:S(2)}) %all-to-all-start) | async-done | bytes 1310752 | tf_op jit(solution)/shard_map/all_to_all | solution.py:479
  32.3 1.1 copy-done.4
  33.3 13.0 %conv.1 = (bf16[8,256,256]{2,1,0:T(8,128)(2,1)}, bf16[8,8,16,128]{3,2,1,0:T(8,128)(2,1)}) custom-call(s32[1]{0:T(128)} %bitcast.1.place, bf16[8,320,256]{2,1,0:T(8,128)(2,1)} %copy-done.4, f32[9,512]{1,0:T(8,128)} %reshape.19.short, f32[1,512]{1,0:T(1,128)} %bitcast.19, bf16[512,256]{1,0:T(8,128)(2,1)} %constant.32.clone.ahead_h, ...), custom_call_target="tpu_custom_call" | custom-call | tf_op jit(solution)/shard_map/conv/pallas_call | solution.py:292
  46.3 3.6 %all-to-all-start.1 = ((bf16[8,256,256]{2,1,0:T(8,128)(2,1)}), bf16[8,256,256]{2,1,0:T(8,128)(2,1)S(1)}, u32[]{:S(2)}, u32[]{:S(2)}) async-start(bf16[8,256,256]{2,1,0:T(8,128)(2,1)} %get-tuple-element.12), calls=%async_computation.1 | async-start | bytes 2097152 | tf_op jit(solution)/shard_map/all_to_all | solution.py:479
  49.9 1.1 dynamic-slice_bitcast_fusion
  50.9 1.6 collective-permute-start.1
  52.6 11.7 %all-to-all-done.1.got = bf16[8,256,256]{2,1,0:T(8,128)(2,1)S(1)} async-done(((bf16[8,256,256]{2,1,0:T(8,128)(2,1)}), bf16[8,256,256]{2,1,0:T(8,128)(2,1)S(1)}, u32[]{:S(2)}, u32[]{:S(2)}) %all-to-all-start.1) | async-done | bytes 1048608 | tf_op jit(solution)/shard_map/all_to_all | solution.py:479
  64.3 1.0 copy-done.1
  65.2 1.9 %unpack_mixed.1.mine = bf16[256,512]{1,0:T(8,128)(2,1)} custom-call(bf16[8,256,256]{2,1,0:T(8,128)(2,1)} %copy-done.1), custom_call_target="tpu_custom_call" | custom-call | tf_op jit(solution)/shard_map/unpack_mixed/pallas_call | solution.py:346
  67.1 2.1 %collective-permute-start = (bf16[256,512]{1,0:T(8,128)(2,1)}, bf16[256,512]{1,0:T(8,128)(2,1)S(1)}, u32[]{:S(2)}, u32[]{:S(2)}) collective-permute-start(bf16[256,512]{1,0:T(8,128)(2,1)} %unpack_mixed.1.mine), channel_id=1, source_target_pairs={{0,8},{8,0},{1,9},{9,1},{2,10},{10,2},{3,11},{11,3},{4,12},{12,4},... | collective-permute-start | bytes 786440 | tf_op jit(solution)/shard_map/ppermute | solution.py:483
  69.2 1.4 collective-permute-done.theirs
  70.5 0.7 copy-done.8
  71.2 4.0 %partial.1 = bf16[4,2,8,16,1152]{4,3,2,1,0:T(8,128)(2,1)} custom-call(s32[1]{0:T(128)} %bitcast.place, bf16[256,512]{1,0:T(8,128)(2,1)} %unpack_mixed.1.mine, bf16[256,512]{1,0:T(8,128)(2,1)} %copy-done.8, bf16[256,4096]{1,0:T(8,128)(2,1)} %bitcast.15, bf16[256,2048]{1,0:T(8,128)(2,1)} %copy-done.5, bf16[8,8,16,128]{3,2,1,0:T(8,128)(2,1)} %get-tuple-element.13.lags), custom_call_target="tpu_custom_call" | custom-call | tf_op jit(solution)/shard_map/partial/pallas_call | solution.py:386
  75.2 8.9 %all-to-all-start.2 = ((bf16[64,16,1152]{2,1,0:T(8,128)(2,1)}), bf16[64,16,1152]{2,1,0:T(8,128)(2,1)S(1)}, u32[]{:S(2)}, u32[]{:S(2)}) async-start(bf16[64,16,1152]{2,1,0:T(8,128)(2,1)} %bitcast.16), calls=%async_computation.2 | async-start | bytes 4718592 | tf_op jit(solution)/shard_map/all_to_all | solution.py:479
  84.2 2.4 %unpack_grads.1 = bf16[3,256,512]{2,1,0:T(8,128)(2,1)} custom-call(bf16[8,256,256]{2,1,0:T(8,128)(2,1)} %copy-done.1), custom_call_target="tpu_custom_call" | custom-call | flops 1000000 | bytes 2000000 | tf_op jit(solution)/shard_map/unpack_grads/pallas_call | solution.py:363
  86.6 4.8 %convolution_convert_fusion = bf16[256,4096]{1,0:T(8,128)(2,1)} fusion(bf16[256,512]{1,0:T(8,128)(2,1)S(1)} %copy-done.6, bf16[512,4096]{1,0:T(8,128)(2,1)} %weight.1), kind=kOutput, calls=%fused_computation | convolution fusion | flops 1074790400 | bytes 6553600 | tf_op jit(solution)/shard_map/dot_general | solution.py:502
  91.3 24.8 %all-to-all-done.2.got = bf16[64,16,1152]{2,1,0:T(8,128)(2,1)S(1)} async-done(((bf16[64,16,1152]{2,1,0:T(8,128)(2,1)}), bf16[64,16,1152]{2,1,0:T(8,128)(2,1)S(1)}, u32[]{:S(2)}, u32[]{:S(2)}) %all-to-all-start.2) | async-done | bytes 2359328 | tf_op jit(solution)/shard_map/all_to_all | solution.py:479
  116.2 1.4 copy-done.2
  117.6 2.8 %reduce.1 = bf16[8,16,2048]{2,1,0:T(8,128)(2,1)} custom-call(bf16[64,16,1152]{2,1,0:T(8,128)(2,1)} %copy-done.2), custom_call_target="tpu_custom_call" | custom-call | tf_op jit(solution)/shard_map/reduce/pallas_call | solution.py:422
  120.4 13.3 %all_to_all.25 = bf16[8,16,2048]{2,1,0:T(8,128)(2,1)S(1)} all-to-all(bf16[8,16,2048]{2,1,0:T(8,128)(2,1)} %reduce.1), channel_id=1, replica_groups=mesh['z'=4,'yh'=2,'c'=2,'x'=4,'yl'=2] {'z','yh'}, dimensions={0} | all-to-all | bytes 1048576 | tf_op jit(solution)/shard_map/all_to_all | solution.py:479
  133.7 0.3 broadcast_in_dim.24
  134.0 26.9 %all_to_all.26.mine = bf16[8,8,16,1024]{3,2,1,0:T(8,128)(2,1)S(1)} all-to-all(bf16[8,8,16,1024]{3,2,1,0:T(8,128)(2,1)S(1)} %broadcast_in_dim.24), channel_id=1, replica_groups=mesh['z'=4,'yh'=2,'c'=2,'x'=4,'yl'=2] {'x','yl'}, dimensions={0} | all-to-all | bytes 4194304 | tf_op jit(solution)/shard_map/all_to_all | solution.py:479
  160.9 4.2 %collective-permute-start.3 = (bf16[8,8,16,1024]{3,2,1,0:T(8,128)(2,1)S(1)}, bf16[8,8,16,1024]{3,2,1,0:T(8,128)(2,1)}, u32[]{:S(2)}, u32[]{:S(2)}) collective-permute-start(bf16[8,8,16,1024]{3,2,1,0:T(8,128)(2,1)S(1)} %all_to_all.26.mine), channel_id=1, source_target_pairs={{0,8},{8,0},{1,9},{9,1},{2,10},{10,2},{3,11},{11,3},{4,12},{12,4},... | collective-permute-start | bytes 6291464 | tf_op jit(solution)/shard_map/ppermute | solution.py:483
  165.1 0.1 collective-permute-start.2
  165.2 3.9 %collective-permute-done.2.lag_theirs = bf16[8,16,1024]{2,1,0:T(8,128)(2,1)S(1)} collective-permute-done((bf16[8,16,1024]{2,1,0:T(8,128)(2,1)S(1)}, bf16[8,16,1024]{2,1,0:T(8,128)(2,1)S(1)}, u32[]{:S(2)}, u32[]{:S(2)}) %collective-permute-start.2) | collective-permute-done | bytes 262176 | tf_op jit(solution)/shard_map/ppermute | solution.py:483
  169.1 0.7 copy-done.9
  169.8 2.0 %write_filter.1 = f32[256,512]{1,0:T(8,128)} custom-call(bf16[8,16,1024]{2,1,0:T(8,128)(2,1)} %copy-done.7, bf16[8,16,1024]{2,1,0:T(8,128)(2,1)} %copy-done.9), custom_call_target="tpu_custom_call" | custom-call | flops 1000000 | bytes 2000000 | tf_op jit(solution)/shard_map/write_filter/pallas_call | solution.py:470
  171.9 6.0 %write_half.2.refs_0_ = f32[512,4096]{1,0:T(8,128)} custom-call(s32[1]{0:T(128)} %bitcast.place, bf16[8,8,16,1024]{3,2,1,0:T(8,128)(2,1)} %copy-done.3), custom_call_target="tpu_custom_call" | custom-call | flops 1000000 | bytes 6000000 | tf_op jit(solution)/shard_map/write_half/pallas_call | solution.py:439
  177.8 6.0 %write_half.3 = f32[512,4096]{1,0:T(8,128)} custom-call(s32[1]{0:T(128)S(6)} %sub.7.place, bf16[8,8,16,1024]{3,2,1,0:T(8,128)(2,1)} %collective-permute-done.3.mine, f32[512,4096]{1,0:T(8,128)} %write_half.2.refs_0_), custom_call_target="tpu_custom_call", output_to_operand_aliasing={{}: (2, {})} | custom-call | flops 1000000 | bytes 6000000 | tf_op jit(solution)/shard_map/write_half/pallas_call | solution.py:439
  (20 shorter events, 0.1 us)
Async XLA Ops:
  7.0 6.0 %copy-start.10 = (f32[3,3,512]{2,1,0:T(4,128)S(1)}, f32[3,3,512]{2,1,0:T(4,128)}, u32[]{:S(2)}) copy-start(f32[3,3,512]{2,1,0:T(4,128)} %param.11) | copy-start | bytes 55300
  7.0 25.2 %all-to-all-start = ((bf16[8,320,256]{2,1,0:T(8,128)(2,1)}), bf16[8,320,256]{2,1,0:T(8,128)(2,1)S(1)}, u32[]{:S(2)}, u32[]{:S(2)}) async-start(bf16[8,320,256]{2,1,0:T(8,128)(2,1)} %pack.1), calls=%async_computation | async-start | bytes 2621440 | tf_op jit(solution)/shard_map/all_to_all | solution.py:479
  13.0 36.8 %copy-start = (bf16[1,256,4096]{2,1,0:T(8,128)(2,1)S(1)}, bf16[1,256,4096]{2,1,0:T(8,128)(2,1)}, u32[]{:S(2)}) copy-start(bf16[1,256,4096]{2,1,0:T(8,128)(2,1)} %param.15) | copy-start | bytes 6291460
  32.3 1.1 copy-start.4
  46.3 18.0 %all-to-all-start.1 = ((bf16[8,256,256]{2,1,0:T(8,128)(2,1)}), bf16[8,256,256]{2,1,0:T(8,128)(2,1)S(1)}, u32[]{:S(2)}, u32[]{:S(2)}) async-start(bf16[8,256,256]{2,1,0:T(8,128)(2,1)} %get-tuple-element.12), calls=%async_computation.1 | async-start | bytes 2097152 | tf_op jit(solution)/shard_map/all_to_all | solution.py:479
  50.9 18.2 %collective-permute-start.1 = (bf16[256,2048]{1,0:T(8,128)(2,1)}, bf16[256,2048]{1,0:T(8,128)(2,1)S(1)}, u32[]{:S(2)}, u32[]{:S(2)}) collective-permute-start(bf16[256,2048]{1,0:T(8,128)(2,1)} %dynamic-slice_bitcast_fusion), channel_id=1, source_target_pairs={{0,8},{8,0},{1,9},{9,1},{2,10},{10,2},{3,11},{11,3},{4,12},{12,4},... | collective-permute-start | bytes 3145736 | tf_op jit(solution)/shard_map/ppermute | solution.py:483
  64.3 1.0 copy-start.1
  67.1 3.4 %collective-permute-start = (bf16[256,512]{1,0:T(8,128)(2,1)}, bf16[256,512]{1,0:T(8,128)(2,1)S(1)}, u32[]{:S(2)}, u32[]{:S(2)}) collective-permute-start(bf16[256,512]{1,0:T(8,128)(2,1)} %unpack_mixed.1.mine), channel_id=1, source_target_pairs={{0,8},{8,0},{1,9},{9,1},{2,10},{10,2},{3,11},{11,3},{4,12},{12,4},... | collective-permute-start | bytes 786440 | tf_op jit(solution)/shard_map/ppermute | solution.py:483
  69.2 1.4 copy-start.5
  70.5 0.7 copy-start.8
  75.2 11.3 %copy-start.6 = (bf16[256,512]{1,0:T(8,128)(2,1)S(1)}, bf16[256,512]{1,0:T(8,128)(2,1)}, u32[]{:S(2)}) copy-start(bf16[256,512]{1,0:T(8,128)(2,1)} %unpack_mixed.1.mine) | copy-start | bytes 786436
  75.2 40.9 %all-to-all-start.2 = ((bf16[64,16,1152]{2,1,0:T(8,128)(2,1)}), bf16[64,16,1152]{2,1,0:T(8,128)(2,1)S(1)}, u32[]{:S(2)}, u32[]{:S(2)}) async-start(bf16[64,16,1152]{2,1,0:T(8,128)(2,1)} %bitcast.16), calls=%async_computation.2 | async-start | bytes 4718592 | tf_op jit(solution)/shard_map/all_to_all | solution.py:479
  116.2 1.4 copy-start.2
  133.7 31.4 %copy-start.7 = (bf16[8,16,1024]{2,1,0:T(8,128)(2,1)}, bf16[8,16,1024]{2,1,0:T(8,128)(2,1)S(1)}, u32[]{:S(2)}) copy-start(bf16[8,16,1024]{2,1,0:T(8,128)(2,1)S(1)} %get-tuple-element.25.lag_mine) | copy-start | bytes 786436
  160.9 11.0 %copy-start.3 = (bf16[8,8,16,1024]{3,2,1,0:T(8,128)(2,1)}, bf16[8,8,16,1024]{3,2,1,0:T(8,128)(2,1)S(1)}, u32[]{:S(2)}) copy-start(bf16[8,8,16,1024]{3,2,1,0:T(8,128)(2,1)S(1)} %all_to_all.26.mine) | copy-start | bytes 6291460
  160.9 16.9 %collective-permute-start.3 = (bf16[8,8,16,1024]{3,2,1,0:T(8,128)(2,1)S(1)}, bf16[8,8,16,1024]{3,2,1,0:T(8,128)(2,1)}, u32[]{:S(2)}, u32[]{:S(2)}) collective-permute-start(bf16[8,8,16,1024]{3,2,1,0:T(8,128)(2,1)S(1)} %all_to_all.26.mine), channel_id=1, source_target_pairs={{0,8},{8,0},{1,9},{9,1},{2,10},{10,2},{3,11},{11,3},{4,12},{12,4},... | collective-permute-start | bytes 6291464 | tf_op jit(solution)/shard_map/ppermute | solution.py:483
  165.1 4.0 %collective-permute-start.2 = (bf16[8,16,1024]{2,1,0:T(8,128)(2,1)S(1)}, bf16[8,16,1024]{2,1,0:T(8,128)(2,1)S(1)}, u32[]{:S(2)}, u32[]{:S(2)}) collective-permute-start(bf16[8,16,1024]{2,1,0:T(8,128)(2,1)S(1)} %get-tuple-element.25.lag_mine), channel_id=1, source_target_pairs={{0,8},{8,0},{1,9},{9,1},{2,10},{10,2},{3,11},{11,3},{4,12},{12,4},... | collective-permute-start | bytes 786440 | tf_op jit(solution)/shard_map/ppermute | solution.py:483
  169.1 0.7 copy-start.9

commit v3 on v2

--- a/solution.py
+++ b/solution.py
@@ -16,7 +16,6 @@
 SENT_ROWS = BLOCK + 64
 SEQ = ("x", "yl")
 DEPTH = ("z", "yh")
-CHIPS = DEPTH + SEQ
 
 
 @functools.lru_cache(maxsize=None)
@@ -281,9 +280,13 @@
     for b in range(8):
         start = BLOCK * b
         y = sum(w_u[j] * u_pad[start + j : start + j + BLOCK] for j in range(3))
-        sent[b, :, 0:128] = y.astype(BF)
+        sent[b, 0:BLOCK, 0:128] = y.astype(BF)
         y = sum(w_x[j] * x_pad[start + j : start + j + BLOCK] for j in range(3))
-        sent[b, :, 128:256] = y.astype(BF)
+        sent[b, 0:BLOCK, 128:256] = y.astype(BF)
+        for t in range(2):
+            first, second = y[128 * t : 128 * t + 64], y[128 * t + 64 : 128 * t + 128]
+            there = slice(128 * t, 128 * t + 128)
+            sent[b ^ 1, BLOCK:, there] = jnp.where(low64, first, turned(second)).astype(BF)
 
 
 def conv(place, got, short, skip):
@@ -303,7 +306,7 @@
                 full(BLOCK, 512),
                 full(BLOCK, 512),
             ],
-            out_specs=[full(8, BLOCK, 256), full(8, 8, 16, 128)],
+            out_specs=[full(8, SENT_ROWS, 256), full(8, 8, 16, 128)],
             scratch_shapes=[
                 pltpu.VMEM((8 + 8 * BLOCK, 128), F32),
                 pltpu.VMEM((8 + 8 * BLOCK, 128), F32),
@@ -320,7 +323,7 @@
             ],
         ),
         out_shape=[
-            jax.ShapeDtypeStruct((8, BLOCK, 256), BF),
+            jax.ShapeDtypeStruct((8, SENT_ROWS, 256), BF),
             jax.ShapeDtypeStruct((8, 8, 16, 128), BF),
         ],
         name="conv",
@@ -330,8 +333,8 @@
 def spread(got, there, first, second, low):
     for q in range(4):
         lanes = slice(128 * q, 128 * q + 128)
-        a = got[2 * q, :, there].astype(F32)
-        b = got[2 * q + 1, :, there].astype(F32)
+        a = got[2 * q, 0:BLOCK, there].astype(F32)
+        b = got[2 * q + 1, 0:BLOCK, there].astype(F32)
         if first is not None:
             first[:, lanes] = jnp.where(low, a, turned(b)).astype(BF)
         if second is not None:
@@ -339,16 +342,22 @@
 
 
 def mixed_kernel(got, mixed):
-    spread(got, slice(0, 128), mixed, None, low_lanes(BLOCK))
+    spread(got, slice(128, 256), mixed.at[0], None, low_lanes(BLOCK))
+    low = low_lanes(64)
+    for q in range(4):
+        lanes = slice(128 * q, 128 * q + 128)
+        for t in range(2):
+            there = slice(128 * t, 128 * t + 128)
+            a = got[2 * q, BLOCK:, there].astype(F32)
+            b = got[2 * q + 1, BLOCK:, there].astype(F32)
+            mixed[1, 128 * t : 128 * t + 64, lanes] = jnp.where(low, a, turned(b)).astype(BF)
+            mixed[1, 128 * t + 64 : 128 * t + 128, lanes] = jnp.where(low, turned(a), b).astype(BF)
 
 
 def unpack_mixed(got):
     return pl.pallas_call(
         mixed_kernel,
-        grid=(1,),
-        in_specs=[pl.BlockSpec((8, BLOCK, 128), lambda n: (0, 0, 1))],
-        out_specs=pl.BlockSpec((BLOCK, 512), lambda n: (0, 0)),
-        out_shape=jax.ShapeDtypeStruct((BLOCK, 512), BF),
+        out_shape=jax.ShapeDtypeStruct((2, BLOCK, 512), BF),
         name="unpack_mixed",
     )(got)
 
@@ -368,54 +377,61 @@
     )(got)
 
 
-def partial_kernel(place, mine, theirs, grad_mine, grad_theirs, lags, packed):
+def partial_kernel(place, mine, theirs, g00, g01, g10, g11, lags, packed):
     def term(mixed, grad):
         return lax.dot_general(
-            mixed[...], grad[...], (((0,), (0,)), ((), ())), preferred_element_type=F32
+            mixed, grad[...], (((0,), (0,)), ((), ())), preferred_element_type=F32
         )
 
-    part = (term(mine, grad_mine) + term(theirs, grad_theirs)).astype(BF)
-    for s in range(8):
-        for a in range(4):
-            start = 64 * s + 16 * a
-            packed[a, 0, s, :, 0:1024] = part[start : start + 16]
-            packed[a, 0, s, :, 1024:1152] = lags[s, 2 * a + pl.program_id(0)]
-
-
-def partial(place, mine, theirs, out_grad, grad_theirs, lags):
+    part = term(mine[0], g00) + term(mine[1], g01) + term(theirs[0], g10) + term(theirs[1], g11)
+    part = part.astype(BF)
+    for x in range(4):
+        for k in range(8):
+            start = 128 * x + 16 * k
+            packed[4 * k + x, :, 0:1024] = part[start : start + 16]
+            packed[4 * k + x, :, 1024:1152] = lags[2 * x, k]
+            packed[4 * k + x, :, 1152:1280] = lags[2 * x + 1, k]
+
+
+def partial(place, mine, theirs, grad, grads, lags):
+    full = lambda *shape: pl.BlockSpec(shape, lambda n, p: (0,) * len(shape))
     return pl.pallas_call(
         partial_kernel,
         grid_spec=pltpu.PrefetchScalarGridSpec(
             num_scalar_prefetch=1,
-            grid=(2,),
+            grid=(1,),
             in_specs=[
-                pl.BlockSpec((BLOCK, 512), lambda h, p: (0, 0)),
-                pl.BlockSpec((BLOCK, 512), lambda h, p: (0, 0)),
-                pl.BlockSpec((BLOCK, 1024), lambda h, p: (0, 2 * p[0] + h)),
-                pl.BlockSpec((BLOCK, 1024), lambda h, p: (0, h)),
-                pl.BlockSpec((8, 8, 16, 128), lambda h, p: (0, 0, 0, 0)),
+                full(2, BLOCK, 512),
+                full(2, BLOCK, 512),
+                pl.BlockSpec((BLOCK, 1024), lambda n, p: (0, p[0])),
+                full(BLOCK, 1024),
+                full(BLOCK, 1024),
+                full(BLOCK, 1024),
+                full(8, 8, 16, 128),
             ],
-            out_specs=pl.BlockSpec((4, 1, 8, 16, 1152), lambda h, p: (0, h, 0, 0, 0)),
+            out_specs=full(32, 16, 1280),
         ),
-        out_shape=jax.ShapeDtypeStruct((4, 2, 8, 16, 1152), BF),
+        out_shape=jax.ShapeDtypeStruct((32, 16, 1280), BF),
         name="partial",
-    )(place, mine, theirs, out_grad, grad_theirs, lags)
+    )(place, mine, theirs, grad, *grads, lags)
 
 
 def reduce_kernel(scale, got, shared):
     total = jnp.zeros((16, 1024), F32)
-    for n in range(64):
+    for n in range(32):
         total = total + got[n, :, 0:1024].astype(F32)
     total = (total * scale).astype(BF)
     for k in range(8):
         shared[k, :, 0:1024] = total
-    for s in range(8):
-        lag = jnp.zeros((16, 128), F32)
+    for x in range(4):
+        lag = jnp.zeros((16, 256), F32)
         for k in range(8):
-            lag = lag + got[8 * k + s, :, 1024:1152].astype(F32)
+            lag = lag + got[4 * k + x, :, 1024:1280].astype(F32)
         lag = (lag * scale).astype(BF)
         for k in range(8):
-            shared[k, :, 1024 + 128 * s : 1152 + 128 * s] = lag
+            for m in range(2):
+                there = slice(1024 + 512 * m + 128 * x, 1152 + 512 * m + 128 * x)
+                shared[k, :, there] = lag[:, 128 * m : 128 * m + 128]
 
 
 def reduce(got, scale):
@@ -427,11 +443,22 @@
 
 
 def half_kernel(place, mine, *refs):
-    grad_weight = refs[-1]
+    grad_weight, wide, sems = refs[-3:]
+    s = pl.program_id(0)
+
+    def copy(n):
+        rows = pl.ds(pl.multiple_of(128 * (n // 2), 128), 128)
+        lanes = pl.ds(pl.multiple_of(2048 * place[0] + 1024 * (n % 2), 1024), 1024)
+        return pltpu.make_async_copy(wide.at[n], grad_weight.at[rows, lanes], sems.at[n])
+
     for k in range(8):
-        rows = slice(16 * (k // 2), 16 * (k // 2) + 16)
-        lanes = slice(1024 * (k % 2), 1024 * (k % 2) + 1024)
-        grad_weight[rows, lanes] = mine[0, k].astype(F32)
+        wide[s, 16 * k : 16 * k + 16] = mine[0, k].astype(F32)
+    copy(s).start()
+
+    @pl.when(s == 7)
+    def _():
+        for n in range(8):
+            copy(n).wait()
 
 
 def write_half(half, rows, whole=None):
@@ -442,8 +469,12 @@
             num_scalar_prefetch=1,
             grid=(8,),
             in_specs=[pl.BlockSpec((1, 8, 16, 1024), lambda s, p: (s, 0, 0, 0))]
-            + [pl.BlockSpec(memory_space=pl.ANY)] * len(more),
-            out_specs=pl.BlockSpec((64, 2048), lambda s, p: (s, p[0])),
+            + [pl.BlockSpec(memory_space=pltpu.HBM)] * len(more),
+            out_specs=pl.BlockSpec(memory_space=pltpu.HBM),
+            scratch_shapes=[
+                pltpu.VMEM((8, 128, 1024), F32),
+                pltpu.SemaphoreType.DMA((8,)),
+            ],
         ),
         out_shape=jax.ShapeDtypeStruct((512, 4096), F32),
         input_output_aliases={2: 0} if more else {},
@@ -452,27 +483,33 @@
     )(half, rows, *more)
 
 
-def filter_kernel(lag_mine, lag_theirs, grad_filter):
+def filter_kernel(place, own, own_c, other, other_c, grad_filter):
     low = low_lanes(16)
+    first = place[0] == 0
     for k in range(8):
         for q in range(4):
-            def both(s):
-                there = slice(128 * s, 128 * s + 128)
-                return lag_mine[k, :, there].astype(F32) + lag_theirs[k, :, there].astype(F32)
-
-            a, b = both(2 * q), both(2 * q + 1)
-            lanes = slice(128 * q, 128 * q + 128)
-            grad_filter[32 * k : 32 * k + 16, lanes] = jnp.where(low, a, turned(b))
-            grad_filter[32 * k + 16 : 32 * k + 32, lanes] = jnp.where(low, turned(a), b)
-
-
-def write_filter(lag_mine, lag_theirs):
+            there = slice(128 * q, 128 * q + 128)
+            a = own[k, :, there].astype(F32) + own_c[k, :, there].astype(F32)
+            b = other[k, :, there].astype(F32) + other_c[k, :, there].astype(F32)
+            a, b = jnp.where(first, a, b), jnp.where(first, b, a)
+            grad_filter[32 * k : 32 * k + 16, there] = jnp.where(low, a, turned(b))
+            grad_filter[32 * k + 16 : 32 * k + 32, there] = jnp.where(low, turned(a), b)
+
+
+def write_filter(side, own, own_c, other, other_c):
+    full = lambda *shape: pl.BlockSpec(shape, lambda n, p: (0,) * len(shape))
     return pl.pallas_call(
         filter_kernel,
+        grid_spec=pltpu.PrefetchScalarGridSpec(
+            num_scalar_prefetch=1,
+            grid=(1,),
+            in_specs=[full(8, 16, 512)] * 4,
+            out_specs=full(BLOCK, 512),
+        ),
         out_shape=jax.ShapeDtypeStruct((BLOCK, 512), F32),
         cost_estimate=pl.CostEstimate(flops=10**6, bytes_accessed=2 * 10**6, transcendentals=0),
         name="write_filter",
-    )(lag_mine, lag_theirs)
+    )(side, own, own_c, other, other_c)
 
 
 def exchange(x, axes):
@@ -481,14 +518,31 @@
 
 def across(x):
     return lax.ppermute(x, "c", [(0, 1), (1, 0)])
+
+
+def beside(x):
+    return lax.ppermute(x, "yl", [(0, 1), (1, 0)])
+
+
+def opposite(x):
+    return lax.ppermute(x, ("c", "yl"), [(n, 3 - n) for n in range(4)])
 
 
 def on_device(streams, short_filter, long_filter, skip_gain, out_weight, out_grad):
     scale = 1.0 / math.sqrt(16 * 2048)
     core = lax.axis_index("c").astype(jnp.int32)
+    side = lax.axis_index("yl").astype(jnp.int32)
     seq = lax.axis_index(SEQ).astype(jnp.int32)
     grad = out_grad[0]
-    grad_theirs = across(lax.dynamic_slice(grad, (0, (1 - core) * 2048), (BLOCK, 2048)))
+
+    def quarter(c, y):
+        return lax.dynamic_slice(grad, (0, 1024 * (2 * c + y)), (BLOCK, 1024))
+
+    grads = (
+        beside(quarter(core, 1 - side)),
+        across(quarter(1 - core, side)),
+        opposite(quarter(1 - core, 1 - side)),
+    )
     got = exchange(pack(streams[:, 0], grad, out_weight, long_filter), SEQ)
     sent, lags = conv(
         seq[None], got, short_filter.reshape(9, 512), skip_gain.reshape(1, 512)
@@ -496,18 +550,20 @@
     back = exchange(sent, SEQ)
     mixed = unpack_mixed(back)
     mixed_theirs = across(mixed)
-    part = partial(core[None], mixed, mixed_theirs, grad, grad_theirs, lags)
+    part = partial((2 * core + side)[None], mixed, mixed_theirs, grad, grads, lags)
     part, mixed, back = lax.optimization_barrier((part, mixed, back))
-    part = exchange(part.reshape(64, 16, 1152), CHIPS)
-    layer_out = jnp.dot(mixed, out_weight, preferred_element_type=F32).astype(BF)
+    part = exchange(part, DEPTH + ("x",))
+    layer_out = jnp.dot(mixed[0], out_weight, preferred_element_type=F32).astype(BF)
     grad_streams = unpack_grads(back)
     part, layer_out, grad_streams = lax.optimization_barrier((part, layer_out, grad_streams))
     shared = exchange(reduce(part, scale), DEPTH)
-    lag_mine = shared[:, :, 1024:]
-    lag_theirs = across(lag_mine)
     rows = jnp.broadcast_to(shared[None, :, :, :1024], (8, 8, 16, 1024))
+    rows, shared = lax.optimization_barrier((rows, shared))
     mine = exchange(rows, SEQ)
-    grad_filter = write_filter(lag_mine, lag_theirs)
+    own = lax.dynamic_slice(shared, (0, 0, 1024 + 512 * side), (8, 16, 512))
+    other = beside(lax.dynamic_slice(shared, (0, 0, 1536 - 512 * side), (8, 16, 512)))
+    grad_filter = write_filter(side[None], own, across(own), other, across(other))
+    mine, grad_filter = lax.optimization_barrier((mine, grad_filter))
     theirs = across(mine)
     grad_weight = write_half(core[None], mine)
     grad_weight = write_half(1 - core[None], theirs, grad_weight)

time: 185 us -> 193 us (1.043)
  blocking collectives: 40.2 us -> 12.6 us
  waiting for transfers between devices: 60.4 us -> 80.8 us
  starting transfers between devices: 26.4 us -> 38.8 us
  local copies, waits for them, and re-layouts: 6.86 us -> 9.35 us
    ppermute x0 -> x3, waiting for transfers between devices: none -> 35.6 us  [the longest x2 29.5 us: beside(): return lax.ppermute(x, 'yl', [(0, 1), (1, 0)])]
    all_to_all x2 -> x1, blocking collectives: 40.2 us -> 12.6 us  [exchange(): return lax.all_to_all(x, axes, 0, 0, tiled=True)]
    all_to_all x3 -> x4, waiting for transfers between devices: 55.1 us -> 44.2 us  [exchange(): return lax.all_to_all(x, axes, 0, 0, tiled=True)]
    all_to_all x3 -> x4, starting transfers between devices: 18.5 us -> 25.1 us  [exchange(): return lax.all_to_all(x, axes, 0, 0, tiled=True)]
    ppermute x0 -> x3, starting transfers between devices: none -> 4.64 us  [the longest x1 3.09 us: opposite(): return lax.ppermute(x, ('c', 'yl'), [(n, 3 - n) for n in range(4)])]
    ppermute x4 -> x5, waiting for transfers between devices: 5.31 us -> 0.99 us  [across(): return lax.ppermute(x, 'c', [(0, 1), (1, 0)])]
    ppermute x4 -> x5, starting transfers between devices: 7.96 us -> 9.14 us  [across(): return lax.ppermute(x, 'c', [(0, 1), (1, 0)])]
    unnamed x22 -> x30, local copies, waits for them, and re-layouts: 4.87 us -> 5.9 us
  transfers between devices with their start and end apart: 7 -> 12, of which waited for: 5 -> 7; matrix products, arithmetic and copies ran while one was open for 4% -> 3% of each run, Pallas kernels for 7% -> 7%
where the time goes in v3:
time: 193 us; the launch traced here: 192 us
  waiting for transfers between devices  80.8 us (42%)
  Pallas kernels  44.6 us (23%)
  starting transfers between devices  38.8 us (20%)
  blocking collectives  12.6 us (7%)
  local copies, waits for them, and re-layouts  9.35 us (5%)
  matrix products  4.77 us (2%)
    all_to_all x4, waiting for transfers between devices, exchange(): return lax.all_to_all(x, axes, 0, 0, tiled=True)  44.2 us
    ppermute x2, waiting for transfers between devices, beside(): return lax.ppermute(x, 'yl', [(0, 1), (1, 0)])  29.5 us
    all_to_all x4, starting transfers between devices, exchange(): return lax.all_to_all(x, axes, 0, 0, tiled=True)  25.1 us
    pallas_call x1, Pallas kernels, conv(): pl.pallas_call(conv_kernel, grid_spec=pltpu.PrefetchScalarGridSpec(num_sc...  13.2 us
    all_to_all x1, blocking collectives, exchange(): return lax.all_to_all(x, axes, 0, 0, tiled=True)  12.6 us
    pallas_call x2, Pallas kernels, write_half(): pl.pallas_call(half_kernel, grid_spec=pltpu.PrefetchScalarGridSpec(num_sc...  11.5 us
    ppermute x5, starting transfers between devices, across(): return lax.ppermute(x, 'c', [(0, 1), (1, 0)])  9.14 us
    pallas_call x1, Pallas kernels, pack(): pl.pallas_call(pack_kernel, grid=(steps,), in_specs=[pl.BlockSpec((3, BLO...  6.38 us
  transfers between devices with their start and end apart: 12, of which 7 were waited for; matrix products, arithmetic and copies ran while one was open for 3% of the time, Pallas kernels for 7%

profile of v3, /device:TPU:1, one launch (start us, length us, event | category | flops | bytes accessed | tf_op | source)
XLA Modules:
  0.0 191.6 jit_solution(5752457060396077636)
XLA Ops:
  0.6 6.4 %pack.1 = bf16[8,320,256]{2,1,0:T(8,128)(2,1)} custom-call(bf16[3,256,512]{2,1,0:T(8,128)(2,1)} %bitcast.23, bf16[256,4096]{1,0:T(8,128)(2,1)} %bitcast.21, bf16[512,4096]{1,0:T(8,128)(2,1)} %weight.1, f32[256,512]{1,0:T(8,128)} %filt.1), custom_call_target="tpu_custom_call" | custom-call | tf_op jit(solution)/shard_map/pack/pallas_call | solution.py:89
  7.0 6.0 %all-to-all-start = ((bf16[8,320,256]{2,1,0:T(8,128)(2,1)}), bf16[8,320,256]{2,1,0:T(8,128)(2,1)S(1)}, u32[]{:S(2)}, u32[]{:S(2)}) async-start(bf16[8,320,256]{2,1,0:T(8,128)(2,1)} %pack.1), calls=%async_computation | async-start | bytes 2621440 | tf_op jit(solution)/shard_map/all_to_all | solution.py:516
  13.6 18.6 %all-to-all-done.got = bf16[8,320,256]{2,1,0:T(8,128)(2,1)S(1)} async-done(((bf16[8,320,256]{2,1,0:T(8,128)(2,1)}), bf16[8,320,256]{2,1,0:T(8,128)(2,1)S(1)}, u32[]{:S(2)}, u32[]{:S(2)}) %all-to-all-start) | async-done | bytes 1310752 | tf_op jit(solution)/shard_map/all_to_all | solution.py:516
  32.3 1.1 copy-done.3
  33.3 13.2 %conv.1 = (bf16[8,320,256]{2,1,0:T(8,128)(2,1)}, bf16[8,8,16,128]{3,2,1,0:T(8,128)(2,1)}) custom-call(s32[1]{0:T(128)} %bitcast.1.place, bf16[8,320,256]{2,1,0:T(8,128)(2,1)} %copy-done.3, f32[9,512]{1,0:T(8,128)} %reshape.18.short, f32[1,512]{1,0:T(1,128)} %bitcast.25, bf16[512,256]{1,0:T(8,128)(2,1)} %constant.43.clone.ahead_h, ...), custom_call_target="tpu_custom_call" | custom-call | tf_op jit(solution)/shard_map/conv/pallas_call | solution.py:295
  46.6 3.6 %all-to-all-start.1 = ((bf16[8,320,256]{2,1,0:T(8,128)(2,1)}), bf16[8,320,256]{2,1,0:T(8,128)(2,1)S(1)}, u32[]{:S(2)}, u32[]{:S(2)}) async-start(bf16[8,320,256]{2,1,0:T(8,128)(2,1)} %get-tuple-element.16), calls=%async_computation.1 | async-start | bytes 2621440 | tf_op jit(solution)/shard_map/all_to_all | solution.py:516
  50.2 1.2 dynamic-slice_bitcast_fusion
  51.4 3.1 %collective-permute-start.3 = (bf16[256,1024]{1,0:T(8,128)(2,1)}, bf16[256,1024]{1,0:T(8,128)(2,1)S(1)}, u32[]{:S(2)}, u32[]{:S(2)}) collective-permute-start(bf16[256,1024]{1,0:T(8,128)(2,1)} %get-tuple-element.32), channel_id=1, source_target_pairs={{0,9},{1,8},{8,1},{9,0},{2,11},{3,10},{10,3},{11,2},{4,13},{5,12},... | collective-permute-start | bytes 1572872 | tf_op jit(solution)/shard_map/ppermute | solution.py:528
  54.9 13.3 %all-to-all-done.1.got = bf16[8,320,256]{2,1,0:T(8,128)(2,1)S(1)} async-done(((bf16[8,320,256]{2,1,0:T(8,128)(2,1)}), bf16[8,320,256]{2,1,0:T(8,128)(2,1)S(1)}, u32[]{:S(2)}, u32[]{:S(2)}) %all-to-all-start.1) | async-done | bytes 1310752 | tf_op jit(solution)/shard_map/all_to_all | solution.py:516
  68.2 1.1 copy-done.1
  69.2 2.3 %unpack_mixed.1.mine = bf16[2,256,512]{2,1,0:T(8,128)(2,1)} custom-call(bf16[8,320,256]{2,1,0:T(8,128)(2,1)} %copy-done.1), custom_call_target="tpu_custom_call" | custom-call | tf_op jit(solution)/shard_map/unpack_mixed/pallas_call | solution.py:358
  71.6 1.9 %collective-permute-start = (bf16[2,256,512]{2,1,0:T(8,128)(2,1)}, bf16[2,256,512]{2,1,0:T(8,128)(2,1)S(1)}, u32[]{:S(2)}, u32[]{:S(2)}) collective-permute-start(bf16[2,256,512]{2,1,0:T(8,128)(2,1)} %unpack_mixed.1.mine), channel_id=1, source_target_pairs={{0,8},{8,0},{1,9},{9,1},{2,10},{10,2},{3,11},{11,3},{4,12},{12,4},... | collective-permute-start | bytes 1572872 | tf_op jit(solution)/shard_map/ppermute | solution.py:520
  73.5 6.0 %collective-permute-done.3.g11 = bf16[256,1024]{1,0:T(8,128)(2,1)S(1)} collective-permute-done((bf16[256,1024]{1,0:T(8,128)(2,1)}, bf16[256,1024]{1,0:T(8,128)(2,1)S(1)}, u32[]{:S(2)}, u32[]{:S(2)}) %collective-permute-start.3) | collective-permute-done | bytes 524320 | tf_op jit(solution)/shard_map/ppermute | solution.py:528
  79.5 8.9 %collective-permute-done.1.g01 = bf16[256,1024]{1,0:T(8,128)(2,1)S(1)} collective-permute-done((bf16[256,1024]{1,0:T(8,128)(2,1)}, bf16[256,1024]{1,0:T(8,128)(2,1)S(1)}, u32[]{:S(2)}, u32[]{:S(2)}) %collective-permute-start.1) | collective-permute-done | bytes 524320 | tf_op jit(solution)/shard_map/ppermute | solution.py:524
  89.6 4.2 %partial.1 = bf16[32,16,1280]{2,1,0:T(8,128)(2,1)} custom-call(s32[1]{0:T(128)} %bitcast.place, bf16[2,256,512]{2,1,0:T(8,128)(2,1)} %unpack_mixed.1.mine, bf16[2,256,512]{2,1,0:T(8,128)(2,1)} %copy-done.9, bf16[256,4096]{1,0:T(8,128)(2,1)} %bitcast.22, bf16[256,1024]{1,0:T(8,128)(2,1)} %copy-done.7, bf16[256,1024]{1,0:T(8,128)(2,1)} %copy-done.8, ...), custom_call_target="tpu_custom_call" | custom-call | tf_op jit(solution)/shard_map/partial/pallas_call | solution.py:398
  93.8 10.9 %all-to-all-start.2 = ((bf16[32,16,1280]{2,1,0:T(8,128)(2,1)}), bf16[32,16,1280]{2,1,0:T(8,128)(2,1)S(1)}, u32[]{:S(2)}, u32[]{:S(2)}) async-start(bf16[32,16,1280]{2,1,0:T(8,128)(2,1)} %partial.1), calls=%async_computation.2 | async-start | bytes 2621440 | tf_op jit(solution)/shard_map/all_to_all | solution.py:516
  104.7 2.5 %unpack_grads.1 = bf16[3,256,512]{2,1,0:T(8,128)(2,1)} custom-call(bf16[8,320,256]{2,1,0:T(8,128)(2,1)} %copy-done.1), custom_call_target="tpu_custom_call" | custom-call | flops 1000000 | bytes 2000000 | tf_op jit(solution)/shard_map/unpack_grads/pallas_call | solution.py:372
  107.2 4.8 %convolution_convert_fusion = bf16[256,4096]{1,0:T(8,128)(2,1)} fusion(bf16[512,4096]{1,0:T(8,128)(2,1)} %weight.1, bf16[2,256,512]{2,1,0:T(8,128)(2,1)S(1)} %copy-done.5), kind=kOutput, calls=%fused_computation | convolution fusion | flops 1074790400 | bytes 6553600 | tf_op jit(solution)/shard_map/dot_general | solution.py:556
  112.0 12.3 %all-to-all-done.2.got = bf16[32,16,1280]{2,1,0:T(8,128)(2,1)S(1)} async-done(((bf16[32,16,1280]{2,1,0:T(8,128)(2,1)}), bf16[32,16,1280]{2,1,0:T(8,128)(2,1)S(1)}, u32[]{:S(2)}, u32[]{:S(2)}) %all-to-all-start.2) | async-done | bytes 1310752 | tf_op jit(solution)/shard_map/all_to_all | solution.py:516
  124.3 1.1 copy-done.4
  125.3 2.3 %reduce.1 = bf16[8,16,2048]{2,1,0:T(8,128)(2,1)} custom-call(bf16[32,16,1280]{2,1,0:T(8,128)(2,1)} %copy-done.4), custom_call_target="tpu_custom_call" | custom-call | tf_op jit(solution)/shard_map/reduce/pallas_call | solution.py:438
  127.7 12.6 %all_to_all.25 = bf16[8,16,2048]{2,1,0:T(8,128)(2,1)S(1)} all-to-all(bf16[8,16,2048]{2,1,0:T(8,128)(2,1)} %reduce.1), channel_id=1, replica_groups=mesh['z'=4,'yh'=2,'c'=2,'x'=4,'yl'=2] {'z','yh'}, dimensions={0} | all-to-all | bytes 1048576 | tf_op jit(solution)/shard_map/all_to_all | solution.py:516
  140.3 1.6 broadcast_in_dim.29
  141.8 4.6 %all-to-all-start.4 = ((bf16[8,8,16,1024]{3,2,1,0:T(8,128)(2,1)}), bf16[8,8,16,1024]{3,2,1,0:T(8,128)(2,1)S(1)}, u32[]{:S(2)}, u32[]{:S(2)}) async-start(bf16[8,8,16,1024]{3,2,1,0:T(8,128)(2,1)} %broadcast_in_dim.29), calls=%async_computation.4 | async-start | bytes 4194304 | tf_op jit(solution)/shard_map/all_to_all | solution.py:516
  146.5 1.5 collective-permute-start.5
  148.0 3.4 %collective-permute-start.4 = (bf16[8,16,512]{2,1,0:T(8,128)(2,1)S(1)}, bf16[8,16,512]{2,1,0:T(8,128)(2,1)S(1)}, u32[]{:S(2)}, u32[]{:S(2)}) collective-permute-start(bf16[8,16,512]{2,1,0:T(8,128)(2,1)S(1)} %get-tuple-element.36.own), channel_id=1, source_target_pairs={{0,8},{8,0},{1,9},{9,1},{2,10},{10,2},{3,11},{11,3},{4,12},{12,4},... | collective-permute-start | bytes 393224 | tf_op jit(solution)/shard_map/ppermute | solution.py:520
  151.4 20.6 %collective-permute-done.5.other = bf16[8,16,512]{2,1,0:T(8,128)(2,1)S(1)} collective-permute-done((bf16[8,16,512]{2,1,0:T(8,128)(2,1)S(1)}, bf16[8,16,512]{2,1,0:T(8,128)(2,1)S(1)}, u32[]{:S(2)}, u32[]{:S(2)}) %collective-permute-start.5) | collective-permute-done | bytes 131104 | tf_op jit(solution)/shard_map/ppermute | solution.py:524
  172.0 3.0 %collective-permute-start.6 = (bf16[8,16,512]{2,1,0:T(8,128)(2,1)S(1)}, bf16[8,16,512]{2,1,0:T(8,128)(2,1)S(1)}, u32[]{:S(2)}, u32[]{:S(2)}) collective-permute-start(bf16[8,16,512]{2,1,0:T(8,128)(2,1)S(1)} %collective-permute-done.5.other), channel_id=1, source_target_pairs={{0,8},{8,0},{1,9},{9,1},{2,10},{10,2},{3,11},{11,3},{4,12},{12,4},... | collective-permute-start | bytes 393224 | tf_op jit(solution)/shard_map/ppermute | solution.py:520
  175.1 1.0 collective-permute-done.6.other_c
  176.7 2.1 %write_filter.1 = f32[256,512]{1,0:T(8,128)} custom-call(s32[1]{0:T(128)} %bitcast.12.place, bf16[8,16,512]{2,1,0:T(8,128)(2,1)} %copy-done.10, bf16[8,16,512]{2,1,0:T(8,128)(2,1)} %copy-done.12, bf16[8,16,512]{2,1,0:T(8,128)(2,1)} %copy-done.11, bf16[8,16,512]{2,1,0:T(8,128)(2,1)} %copy-done.13), custom_call_target="tpu_custom_call" | custom-call | flops 1000000 | bytes 2000000 | tf_op jit(solution)/shard_map/write_filter/pallas_call | solution.py:501
  180.1 5.7 %write_half.2.refs_0_ = f32[512,4096]{1,0:T(8,128)} custom-call(s32[1]{0:T(128)} %bitcast.13.place, bf16[8,8,16,1024]{3,2,1,0:T(8,128)(2,1)} %copy-done.2), custom_call_target="tpu_custom_call" | custom-call | flops 1000000 | bytes 6000000 | tf_op jit(solution)/shard_map/write_half/pallas_call | solution.py:466
  185.9 5.8 %write_half.3 = f32[512,4096]{1,0:T(8,128)} custom-call(s32[1]{0:T(128)S(6)} %sub.17.place, bf16[8,8,16,1024]{3,2,1,0:T(8,128)(2,1)} %collective-permute-done.7.mine, f32[512,4096]{1,0:T(8,128)} %write_half.2.refs_0_), custom_call_target="tpu_custom_call", output_to_operand_aliasing={{}: (2, {})} | custom-call | flops 1000000 | bytes 6000000 | tf_op jit(solution)/shard_map/write_half/pallas_call | solution.py:466
  (38 shorter events, 4.2 us)
Async XLA Ops:
  7.0 6.0 %copy-start.14 = (f32[3,3,512]{2,1,0:T(4,128)S(1)}, f32[3,3,512]{2,1,0:T(4,128)}, u32[]{:S(2)}) copy-start(f32[3,3,512]{2,1,0:T(4,128)} %param.11) | copy-start | bytes 55300
  7.0 25.2 %all-to-all-start = ((bf16[8,320,256]{2,1,0:T(8,128)(2,1)}), bf16[8,320,256]{2,1,0:T(8,128)(2,1)S(1)}, u32[]{:S(2)}, u32[]{:S(2)}) async-start(bf16[8,320,256]{2,1,0:T(8,128)(2,1)} %pack.1), calls=%async_computation | async-start | bytes 2621440 | tf_op jit(solution)/shard_map/all_to_all | solution.py:516
  32.3 1.1 copy-start.3
  33.3 16.8 %copy-start = (bf16[1,256,4096]{2,1,0:T(8,128)(2,1)S(1)}, bf16[1,256,4096]{2,1,0:T(8,128)(2,1)}, u32[]{:S(2)}) copy-start(bf16[1,256,4096]{2,1,0:T(8,128)(2,1)} %param.15) | copy-start | bytes 6291460
  46.6 21.6 %all-to-all-start.1 = ((bf16[8,320,256]{2,1,0:T(8,128)(2,1)}), bf16[8,320,256]{2,1,0:T(8,128)(2,1)S(1)}, u32[]{:S(2)}, u32[]{:S(2)}) async-start(bf16[8,320,256]{2,1,0:T(8,128)(2,1)} %get-tuple-element.16), calls=%async_computation.1 | async-start | bytes 2621440 | tf_op jit(solution)/shard_map/all_to_all | solution.py:516
  51.4 28.2 %collective-permute-start.3 = (bf16[256,1024]{1,0:T(8,128)(2,1)}, bf16[256,1024]{1,0:T(8,128)(2,1)S(1)}, u32[]{:S(2)}, u32[]{:S(2)}) collective-permute-start(bf16[256,1024]{1,0:T(8,128)(2,1)} %get-tuple-element.32), channel_id=1, source_target_pairs={{0,9},{1,8},{8,1},{9,0},{2,11},{3,10},{10,3},{11,2},{4,13},{5,12},... | collective-permute-start | bytes 1572872 | tf_op jit(solution)/shard_map/ppermute | solution.py:528
  54.5 34.0 %collective-permute-start.1 = (bf16[256,1024]{1,0:T(8,128)(2,1)}, bf16[256,1024]{1,0:T(8,128)(2,1)S(1)}, u32[]{:S(2)}, u32[]{:S(2)}) collective-permute-start(bf16[256,1024]{1,0:T(8,128)(2,1)} %get-tuple-element.33), channel_id=1, source_target_pairs={{0,1},{1,0},{2,3},{3,2},{4,5},{5,4},{6,7},{7,6},{8,9},{9,8},{10,11... | collective-permute-start | bytes 1572872 | tf_op jit(solution)/shard_map/ppermute | solution.py:524
  54.5 34.0 %collective-permute-start.2 = (bf16[256,1024]{1,0:T(8,128)(2,1)}, bf16[256,1024]{1,0:T(8,128)(2,1)S(1)}, u32[]{:S(2)}, u32[]{:S(2)}) collective-permute-start(bf16[256,1024]{1,0:T(8,128)(2,1)} %get-tuple-element.34), channel_id=1, source_target_pairs={{0,8},{8,0},{1,9},{9,1},{2,10},{10,2},{3,11},{11,3},{4,12},{12,4},... | collective-permute-start | bytes 1572872 | tf_op jit(solution)/shard_map/ppermute | solution.py:520
  68.2 1.1 copy-start.1
  71.6 16.9 %collective-permute-start = (bf16[2,256,512]{2,1,0:T(8,128)(2,1)}, bf16[2,256,512]{2,1,0:T(8,128)(2,1)S(1)}, u32[]{:S(2)}, u32[]{:S(2)}) collective-permute-start(bf16[2,256,512]{2,1,0:T(8,128)(2,1)} %unpack_mixed.1.mine), channel_id=1, source_target_pairs={{0,8},{8,0},{1,9},{9,1},{2,10},{10,2},{3,11},{11,3},{4,12},{12,4},... | collective-permute-start | bytes 1572872 | tf_op jit(solution)/shard_map/ppermute | solution.py:520
  79.5 9.0 %copy-start.6 = (bf16[256,1024]{1,0:T(8,128)(2,1)}, bf16[256,1024]{1,0:T(8,128)(2,1)S(1)}, u32[]{:S(2)}) copy-start(bf16[256,1024]{1,0:T(8,128)(2,1)S(1)} %collective-permute-done.3.g11) | copy-start | bytes 1572868
  88.5 0.8 copy-start.7
  88.5 1.0 copy-start.8
  88.5 1.1 copy-start.9
  93.8 13.4 %copy-start.5 = (bf16[2,256,512]{2,1,0:T(8,128)(2,1)S(1)}, bf16[2,256,512]{2,1,0:T(8,128)(2,1)}, u32[]{:S(2)}) copy-start(bf16[2,256,512]{2,1,0:T(8,128)(2,1)} %unpack_mixed.1.mine) | copy-start | bytes 1572868
  93.8 30.5 %all-to-all-start.2 = ((bf16[32,16,1280]{2,1,0:T(8,128)(2,1)}), bf16[32,16,1280]{2,1,0:T(8,128)(2,1)S(1)}, u32[]{:S(2)}, u32[]{:S(2)}) async-start(bf16[32,16,1280]{2,1,0:T(8,128)(2,1)} %partial.1), calls=%async_computation.2 | async-start | bytes 2621440 | tf_op jit(solution)/shard_map/all_to_all | solution.py:516
  124.3 1.1 copy-start.4
  141.8 37.0 %all-to-all-start.4 = ((bf16[8,8,16,1024]{3,2,1,0:T(8,128)(2,1)}), bf16[8,8,16,1024]{3,2,1,0:T(8,128)(2,1)S(1)}, u32[]{:S(2)}, u32[]{:S(2)}) async-start(bf16[8,8,16,1024]{3,2,1,0:T(8,128)(2,1)} %broadcast_in_dim.29), calls=%async_computation.4 | async-start | bytes 4194304 | tf_op jit(solution)/shard_map/all_to_all | solution.py:516
  146.5 29.6 %copy-start.10 = (bf16[8,16,512]{2,1,0:T(8,128)(2,1)}, bf16[8,16,512]{2,1,0:T(8,128)(2,1)S(1)}, u32[]{:S(2)}) copy-start(bf16[8,16,512]{2,1,0:T(8,128)(2,1)S(1)} %get-tuple-element.36.own) | copy-start | bytes 393220
  146.5 25.5 %collective-permute-start.5 = (bf16[8,16,512]{2,1,0:T(8,128)(2,1)S(1)}, bf16[8,16,512]{2,1,0:T(8,128)(2,1)S(1)}, u32[]{:S(2)}, u32[]{:S(2)}) collective-permute-start(bf16[8,16,512]{2,1,0:T(8,128)(2,1)S(1)} %get-tuple-element.35), channel_id=1, source_target_pairs={{0,1},{1,0},{2,3},{3,2},{4,5},{5,4},{6,7},{7,6},{8,9},{9,8},{10,11... | collective-permute-start | bytes 393224 | tf_op jit(solution)/shard_map/ppermute | solution.py:524
  148.0 27.0 %collective-permute-start.4 = (bf16[8,16,512]{2,1,0:T(8,128)(2,1)S(1)}, bf16[8,16,512]{2,1,0:T(8,128)(2,1)S(1)}, u32[]{:S(2)}, u32[]{:S(2)}) collective-permute-start(bf16[8,16,512]{2,1,0:T(8,128)(2,1)S(1)} %get-tuple-element.36.own), channel_id=1, source_target_pairs={{0,8},{8,0},{1,9},{9,1},{2,10},{10,2},{3,11},{11,3},{4,12},{12,4},... | collective-permute-start | bytes 393224 | tf_op jit(solution)/shard_map/ppermute | solution.py:520
  172.0 4.0 %copy-start.11 = (bf16[8,16,512]{2,1,0:T(8,128)(2,1)}, bf16[8,16,512]{2,1,0:T(8,128)(2,1)S(1)}, u32[]{:S(2)}) copy-start(bf16[8,16,512]{2,1,0:T(8,128)(2,1)S(1)} %collective-permute-done.5.other) | copy-start | bytes 393220
  172.0 4.0 %collective-permute-start.6 = (bf16[8,16,512]{2,1,0:T(8,128)(2,1)S(1)}, bf16[8,16,512]{2,1,0:T(8,128)(2,1)S(1)}, u32[]{:S(2)}, u32[]{:S(2)}) collective-permute-start(bf16[8,16,512]{2,1,0:T(8,128)(2,1)S(1)} %collective-permute-done.5.other), channel_id=1, source_target_pairs={{0,8},{8,0},{1,9},{9,1},{2,10},{10,2},{3,11},{11,3},{4,12},{12,4},... | collective-permute-start | bytes 393224 | tf_op jit(solution)/shard_map/ppermute | solution.py:520
  175.1 1.0 copy-start.12
  176.0 0.7 copy-start.13
  178.8 1.3 copy-start.2
  178.8 7.1 %collective-permute-start.7 = (bf16[8,8,16,1024]{3,2,1,0:T(8,128)(2,1)S(1)}, bf16[8,8,16,1024]{3,2,1,0:T(8,128)(2,1)}, u32[]{:S(2)}, u32[]{:S(2)}) collective-permute-start(bf16[8,8,16,1024]{3,2,1,0:T(8,128)(2,1)S(1)} %all-to-all-done.4.mine), channel_id=1, source_target_pairs={{0,8},{8,0},{1,9},{9,1},{2,10},{10,2},{3,11},{11,3},{4,12},{12,4},... | collective-permute-start | bytes 6291464 | tf_op jit(solution)/shard_map/ppermute | solution.py:520

commit v4 on v3

--- a/solution.py
+++ b/solution.py
@@ -377,7 +377,7 @@
     )(got)
 
 
-def partial_kernel(place, mine, theirs, g00, g01, g10, g11, lags, packed):
+def partial_kernel(place, mine, theirs, g00, g01, g10, g11, lags, lags_beside, packed):
     def term(mixed, grad):
         return lax.dot_general(
             mixed, grad[...], (((0,), (0,)), ((), ())), preferred_element_type=F32
@@ -389,11 +389,11 @@
         for k in range(8):
             start = 128 * x + 16 * k
             packed[4 * k + x, :, 0:1024] = part[start : start + 16]
-            packed[4 * k + x, :, 1024:1152] = lags[2 * x, k]
-            packed[4 * k + x, :, 1152:1280] = lags[2 * x + 1, k]
-
-
-def partial(place, mine, theirs, grad, grads, lags):
+            packed[4 * k + x, :, 1024:1152] = lags[x, k]
+            packed[4 * k + x, :, 1152:1280] = lags_beside[x, k]
+
+
+def partial(place, mine, theirs, grad, grads, lags, lags_beside):
     full = lambda *shape: pl.BlockSpec(shape, lambda n, p: (0,) * len(shape))
     return pl.pallas_call(
         partial_kernel,
@@ -407,13 +407,14 @@
                 full(BLOCK, 1024),
                 full(BLOCK, 1024),
                 full(BLOCK, 1024),
-                full(8, 8, 16, 128),
+                full(4, 8, 16, 128),
+                full(4, 8, 16, 128),
             ],
             out_specs=full(32, 16, 1280),
         ),
         out_shape=jax.ShapeDtypeStruct((32, 16, 1280), BF),
         name="partial",
-    )(place, mine, theirs, grad, *grads, lags)
+    )(place, mine, theirs, grad, *grads, lags, lags_beside)
 
 
 def reduce_kernel(scale, got, shared):
@@ -444,21 +445,18 @@
 
 def half_kernel(place, mine, *refs):
     grad_weight, wide, sems = refs[-3:]
-    s = pl.program_id(0)
 
     def copy(n):
-        rows = pl.ds(pl.multiple_of(128 * (n // 2), 128), 128)
+        rows = slice(128 * (n // 2), 128 * (n // 2) + 128)
         lanes = pl.ds(pl.multiple_of(2048 * place[0] + 1024 * (n % 2), 1024), 1024)
         return pltpu.make_async_copy(wide.at[n], grad_weight.at[rows, lanes], sems.at[n])
 
-    for k in range(8):
-        wide[s, 16 * k : 16 * k + 16] = mine[0, k].astype(F32)
-    copy(s).start()
-
-    @pl.when(s == 7)
-    def _():
-        for n in range(8):
-            copy(n).wait()
+    for n in range(8):
+        for k in range(8):
+            wide[n, 16 * k : 16 * k + 16] = mine[n, k].astype(F32)
+        copy(n).start()
+    for n in range(8):
+        copy(n).wait()
 
 
 def write_half(half, rows, whole=None):
@@ -467,8 +465,8 @@
         half_kernel,
         grid_spec=pltpu.PrefetchScalarGridSpec(
             num_scalar_prefetch=1,
-            grid=(8,),
-            in_specs=[pl.BlockSpec((1, 8, 16, 1024), lambda s, p: (s, 0, 0, 0))]
+            grid=(1,),
+            in_specs=[pl.BlockSpec((8, 8, 16, 1024), lambda n, p: (0, 0, 0, 0))]
             + [pl.BlockSpec(memory_space=pltpu.HBM)] * len(more),
             out_specs=pl.BlockSpec(memory_space=pltpu.HBM),
             scratch_shapes=[
@@ -483,33 +481,36 @@
     )(half, rows, *more)
 
 
-def filter_kernel(place, own, own_c, other, other_c, grad_filter):
+def filter_kernel(place, lags, lags_c, grad_filter):
     low = low_lanes(16)
     first = place[0] == 0
     for k in range(8):
         for q in range(4):
-            there = slice(128 * q, 128 * q + 128)
-            a = own[k, :, there].astype(F32) + own_c[k, :, there].astype(F32)
-            b = other[k, :, there].astype(F32) + other_c[k, :, there].astype(F32)
-            a, b = jnp.where(first, a, b), jnp.where(first, b, a)
-            grad_filter[32 * k : 32 * k + 16, there] = jnp.where(low, a, turned(b))
-            grad_filter[32 * k + 16 : 32 * k + 32, there] = jnp.where(low, turned(a), b)
-
-
-def write_filter(side, own, own_c, other, other_c):
+            def both(start):
+                there = slice(start + 128 * q, start + 128 * q + 128)
+                return lags[k, :, there].astype(F32) + lags_c[k, :, there].astype(F32)
+
+            own, other = both(0), both(512)
+            a, b = jnp.where(first, own, other), jnp.where(first, other, own)
+            lanes = slice(128 * q, 128 * q + 128)
+            grad_filter[32 * k : 32 * k + 16, lanes] = jnp.where(low, a, turned(b))
+            grad_filter[32 * k + 16 : 32 * k + 32, lanes] = jnp.where(low, turned(a), b)
+
+
+def write_filter(side, lags, lags_c):
     full = lambda *shape: pl.BlockSpec(shape, lambda n, p: (0,) * len(shape))
     return pl.pallas_call(
         filter_kernel,
         grid_spec=pltpu.PrefetchScalarGridSpec(
             num_scalar_prefetch=1,
             grid=(1,),
-            in_specs=[full(8, 16, 512)] * 4,
+            in_specs=[full(8, 16, 1024)] * 2,
             out_specs=full(BLOCK, 512),
         ),
         out_shape=jax.ShapeDtypeStruct((BLOCK, 512), F32),
         cost_estimate=pl.CostEstimate(flops=10**6, bytes_accessed=2 * 10**6, transcendentals=0),
         name="write_filter",
-    )(side, own, own_c, other, other_c)
+    )(side, lags, lags_c)
 
 
 def exchange(x, axes):
@@ -547,10 +548,17 @@
     sent, lags = conv(
         seq[None], got, short_filter.reshape(9, 512), skip_gain.reshape(1, 512)
     )
+    sent, grads = lax.optimization_barrier((sent, grads))
+    lags = lags.reshape(4, 2, 8, 16, 128)
+    lags_own = lax.dynamic_index_in_dim(lags, side, 1, False)
+    lags_beside = beside(lax.dynamic_index_in_dim(lags, 1 - side, 1, False))
     back = exchange(sent, SEQ)
+    back, lags_own, lags_beside = lax.optimization_barrier((back, lags_own, lags_beside))
     mixed = unpack_mixed(back)
     mixed_theirs = across(mixed)
-    part = partial((2 * core + side)[None], mixed, mixed_theirs, grad, grads, lags)
+    part = partial(
+        (2 * core + side)[None], mixed, mixed_theirs, grad, grads, lags_own, lags_beside
+    )
     part, mixed, back = lax.optimization_barrier((part, mixed, back))
     part = exchange(part, DEPTH + ("x",))
     layer_out = jnp.dot(mixed[0], out_weight, preferred_element_type=F32).astype(BF)
@@ -560,9 +568,8 @@
     rows = jnp.broadcast_to(shared[None, :, :, :1024], (8, 8, 16, 1024))
     rows, shared = lax.optimization_barrier((rows, shared))
     mine = exchange(rows, SEQ)
-    own = lax.dynamic_slice(shared, (0, 0, 1024 + 512 * side), (8, 16, 512))
-    other = beside(lax.dynamic_slice(shared, (0, 0, 1536 - 512 * side), (8, 16, 512)))
-    grad_filter = write_filter(side[None], own, across(own), other, across(other))
+    shared_lags = shared[:, :, 1024:]
+    grad_filter = write_filter(side[None], shared_lags, across(shared_lags))
     mine, grad_filter = lax.optimization_barrier((mine, grad_filter))
     theirs = across(mine)
     grad_weight = write_half(core[None], mine)

time: 193 us -> 179 us (0.927)
  waiting for transfers between devices: 80.8 us -> 74 us
  Pallas kernels: 44.6 us -> 40.2 us
  starting transfers between devices: 38.8 us -> 36.4 us
    ppermute x2, waiting for transfers between devices: 29.5 us -> 21 us  [beside(): return lax.ppermute(x, 'yl', [(0, 1), (1, 0)])]
    ppermute x1, waiting for transfers between devices: 6.01 us -> 0.01 us  [opposite(): return lax.ppermute(x, ('c', 'yl'), [(n, 3 - n) for n in range(4)])]
    all_to_all x4, waiting for transfers between devices: 44.2 us -> 49.9 us  [exchange(): return lax.all_to_all(x, axes, 0, 0, tiled=True)]
    pallas_call x2, Pallas kernels: 11.5 us -> 7.39 us  [write_half(): pl.pallas_call(half_kernel, grid_spec=pltpu.PrefetchScalarGridSpec(num_sc...]
    ppermute x5 -> x4, waiting for transfers between devices: 0.99 us -> 3.13 us  [across(): return lax.ppermute(x, 'c', [(0, 1), (1, 0)])]
    ppermute x5 -> x4, starting transfers between devices: 9.14 us -> 7.38 us  [across(): return lax.ppermute(x, 'c', [(0, 1), (1, 0)])]
  transfers between devices with their start and end apart: 12 -> 11, of which waited for: 7 -> 9; matrix products, arithmetic and copies ran while one was open for 3% -> 4% of each run, Pallas kernels for 7% -> 12%
where the time goes in v4:
time: 179 us; the launch traced here: 178 us
  waiting for transfers between devices  74 us (41%)
  Pallas kernels  40.2 us (22%)
  starting transfers between devices  36.4 us (20%)
  blocking collectives  12.8 us (7%)
  local copies, waits for them, and re-layouts  8.85 us (5%)
  matrix products  4.77 us (3%)
    all_to_all x4, waiting for transfers between devices, exchange(): return lax.all_to_all(x, axes, 0, 0, tiled=True)  49.9 us
    all_to_all x4, starting transfers between devices, exchange(): return lax.all_to_all(x, axes, 0, 0, tiled=True)  25 us
    ppermute x2, waiting for transfers between devices, beside(): return lax.ppermute(x, 'yl', [(0, 1), (1, 0)])  21 us
    pallas_call x1, Pallas kernels, conv(): pl.pallas_call(conv_kernel, grid_spec=pltpu.PrefetchScalarGridSpec(num_sc...  13.1 us
    all_to_all x1, blocking collectives, exchange(): return lax.all_to_all(x, axes, 0, 0, tiled=True)  12.8 us
    pallas_call x2, Pallas kernels, write_half(): pl.pallas_call(half_kernel, grid_spec=pltpu.PrefetchScalarGridSpec(num_sc...  7.39 us
    ppermute x4, starting transfers between devices, across(): return lax.ppermute(x, 'c', [(0, 1), (1, 0)])  7.38 us
    pallas_call x1, Pallas kernels, pack(): pl.pallas_call(pack_kernel, grid=(steps,), in_specs=[pl.BlockSpec((3, BLO...  6.38 us
  transfers between devices with their start and end apart: 11, of which 9 were waited for; matrix products, arithmetic and copies ran while one was open for 4% of the time, Pallas kernels for 12%

profile of v4, /device:TPU:1, one launch (start us, length us, event | category | flops | bytes accessed | tf_op | source)
XLA Modules:
  0.0 177.8 jit_solution(14900755053743360839)
XLA Ops:
  0.6 6.4 %pack.1 = bf16[8,320,256]{2,1,0:T(8,128)(2,1)} custom-call(bf16[3,256,512]{2,1,0:T(8,128)(2,1)} %bitcast.32, bf16[256,4096]{1,0:T(8,128)(2,1)} %bitcast.30, bf16[512,4096]{1,0:T(8,128)(2,1)} %weight.1, f32[256,512]{1,0:T(8,128)} %filt.1), custom_call_target="tpu_custom_call" | custom-call | tf_op jit(solution)/shard_map/pack/pallas_call | solution.py:89
  7.0 6.0 %all-to-all-start = ((bf16[8,320,256]{2,1,0:T(8,128)(2,1)}), bf16[8,320,256]{2,1,0:T(8,128)(2,1)S(1)}, u32[]{:S(2)}, u32[]{:S(2)}) async-start(bf16[8,320,256]{2,1,0:T(8,128)(2,1)} %pack.1), calls=%async_computation | async-start | bytes 2621440 | tf_op jit(solution)/shard_map/all_to_all | solution.py:517
  13.0 1.2 dynamic-slice_bitcast_fusion
  14.3 2.6 %collective-permute-start.2 = (bf16[256,1024]{1,0:T(8,128)(2,1)}, bf16[256,1024]{1,0:T(8,128)(2,1)S(1)}, u32[]{:S(2)}, u32[]{:S(2)}) collective-permute-start(bf16[256,1024]{1,0:T(8,128)(2,1)} %get-tuple-element.46), channel_id=1, source_target_pairs={{0,9},{1,8},{8,1},{9,0},{2,11},{3,10},{10,3},{11,2},{4,13},{5,12},... | collective-permute-start | bytes 1572872 | tf_op jit(solution)/shard_map/ppermute | solution.py:529
  17.9 14.4 %all-to-all-done.got = bf16[8,320,256]{2,1,0:T(8,128)(2,1)S(1)} async-done(((bf16[8,320,256]{2,1,0:T(8,128)(2,1)}), bf16[8,320,256]{2,1,0:T(8,128)(2,1)S(1)}, u32[]{:S(2)}, u32[]{:S(2)}) %all-to-all-start) | async-done | bytes 1310752 | tf_op jit(solution)/shard_map/all_to_all | solution.py:517
  32.3 1.1 copy-done.3
  33.3 13.1 %conv.1 = (bf16[8,320,256]{2,1,0:T(8,128)(2,1)}, bf16[8,8,16,128]{3,2,1,0:T(8,128)(2,1)}) custom-call(s32[1]{0:T(128)} %bitcast.1.place, bf16[8,320,256]{2,1,0:T(8,128)(2,1)} %copy-done.3, f32[9,512]{1,0:T(8,128)} %reshape.21.short, f32[1,512]{1,0:T(1,128)} %bitcast.35, bf16[512,256]{1,0:T(8,128)(2,1)} %constant.42.clone.ahead_h, ...), custom_call_target="tpu_custom_call" | custom-call | tf_op jit(solution)/shard_map/conv/pallas_call | solution.py:295
  46.4 4.6 %collective-permute-done.g01 = bf16[256,1024]{1,0:T(8,128)(2,1)S(1)} collective-permute-done((bf16[256,1024]{1,0:T(8,128)(2,1)}, bf16[256,1024]{1,0:T(8,128)(2,1)S(1)}, u32[]{:S(2)}, u32[]{:S(2)}) %collective-permute-start) | collective-permute-done | bytes 524320 | tf_op jit(solution)/shard_map/ppermute | solution.py:525
  51.0 5.3 %all-to-all-start.1 = ((bf16[8,320,256]{2,1,0:T(8,128)(2,1)}), bf16[8,320,256]{2,1,0:T(8,128)(2,1)S(1)}, u32[]{:S(2)}, u32[]{:S(2)}) async-start(bf16[8,320,256]{2,1,0:T(8,128)(2,1)} %get-tuple-element.24), calls=%async_computation.1 | async-start | bytes 2621440 | tf_op jit(solution)/shard_map/all_to_all | solution.py:517
  57.0 1.4 collective-permute-start.3
  58.5 16.3 %collective-permute-done.3.lags_beside = bf16[4,8,16,128]{3,2,1,0:T(8,128)(2,1)S(1)} collective-permute-done((bf16[4,8,16,128]{3,2,1,0:T(8,128)(2,1)S(1)}, bf16[4,8,16,128]{3,2,1,0:T(8,128)(2,1)S(1)}, u32[]{:S(2)}, u32[]{:S(2)}) %collective-permute-start.3) | collective-permute-done | bytes 131104 | tf_op jit(solution)/shard_map/ppermute | solution.py:525
  75.9 1.1 copy-done.1
  76.9 2.3 %unpack_mixed.1.mine = bf16[2,256,512]{2,1,0:T(8,128)(2,1)} custom-call(bf16[8,320,256]{2,1,0:T(8,128)(2,1)} %copy-done.1), custom_call_target="tpu_custom_call" | custom-call | tf_op jit(solution)/shard_map/unpack_mixed/pallas_call | solution.py:358
  79.3 1.6 collective-permute-start.4
  80.9 1.7 collective-permute-done.4.theirs
  83.4 4.2 %partial.1 = bf16[32,16,1280]{2,1,0:T(8,128)(2,1)} custom-call(s32[1]{0:T(128)} %bitcast.place, bf16[2,256,512]{2,1,0:T(8,128)(2,1)} %unpack_mixed.1.mine, bf16[2,256,512]{2,1,0:T(8,128)(2,1)} %copy-done.10, bf16[256,4096]{1,0:T(8,128)(2,1)} %bitcast.31, bf16[256,1024]{1,0:T(8,128)(2,1)} %copy-done.8, bf16[256,1024]{1,0:T(8,128)(2,1)} %copy-done.9, ...), custom_call_target="tpu_custom_call" | custom-call | tf_op jit(solution)/shard_map/partial/pallas_call | solution.py:398
  87.6 9.5 %all-to-all-start.2 = ((bf16[32,16,1280]{2,1,0:T(8,128)(2,1)}), bf16[32,16,1280]{2,1,0:T(8,128)(2,1)S(1)}, u32[]{:S(2)}, u32[]{:S(2)}) async-start(bf16[32,16,1280]{2,1,0:T(8,128)(2,1)} %partial.1), calls=%async_computation.2 | async-start | bytes 2621440 | tf_op jit(solution)/shard_map/all_to_all | solution.py:517
  97.1 2.5 %unpack_grads.1 = bf16[3,256,512]{2,1,0:T(8,128)(2,1)} custom-call(bf16[8,320,256]{2,1,0:T(8,128)(2,1)} %copy-done.1), custom_call_target="tpu_custom_call" | custom-call | flops 1000000 | bytes 2000000 | tf_op jit(solution)/shard_map/unpack_grads/pallas_call | solution.py:372
  99.6 4.8 %convolution_convert_fusion = bf16[256,4096]{1,0:T(8,128)(2,1)} fusion(bf16[512,4096]{1,0:T(8,128)(2,1)} %weight.1, bf16[2,256,512]{2,1,0:T(8,128)(2,1)S(1)} %copy-done.5), kind=kOutput, calls=%fused_computation | convolution fusion | flops 1074790400 | bytes 6553600 | tf_op jit(solution)/shard_map/dot_general | solution.py:564
  104.4 12.8 %all-to-all-done.2.got = bf16[32,16,1280]{2,1,0:T(8,128)(2,1)S(1)} async-done(((bf16[32,16,1280]{2,1,0:T(8,128)(2,1)}), bf16[32,16,1280]{2,1,0:T(8,128)(2,1)S(1)}, u32[]{:S(2)}, u32[]{:S(2)}) %all-to-all-start.2) | async-done | bytes 1310752 | tf_op jit(solution)/shard_map/all_to_all | solution.py:517
  117.2 1.1 copy-done.4
  118.2 2.3 %reduce.1 = bf16[8,16,2048]{2,1,0:T(8,128)(2,1)} custom-call(bf16[32,16,1280]{2,1,0:T(8,128)(2,1)} %copy-done.4), custom_call_target="tpu_custom_call" | custom-call | tf_op jit(solution)/shard_map/reduce/pallas_call | solution.py:439
  120.5 12.8 %all_to_all.25 = bf16[8,16,2048]{2,1,0:T(8,128)(2,1)S(1)} all-to-all(bf16[8,16,2048]{2,1,0:T(8,128)(2,1)} %reduce.1), channel_id=1, replica_groups=mesh['z'=4,'yh'=2,'c'=2,'x'=4,'yl'=2] {'z','yh'}, dimensions={0} | all-to-all | bytes 1048576 | tf_op jit(solution)/shard_map/all_to_all | solution.py:517
  133.3 1.6 broadcast_in_dim.29
  134.9 4.3 %all-to-all-start.4 = ((bf16[8,8,16,1024]{3,2,1,0:T(8,128)(2,1)}), bf16[8,8,16,1024]{3,2,1,0:T(8,128)(2,1)S(1)}, u32[]{:S(2)}, u32[]{:S(2)}) async-start(bf16[8,8,16,1024]{3,2,1,0:T(8,128)(2,1)} %broadcast_in_dim.29), calls=%async_computation.4 | async-start | bytes 4194304 | tf_op jit(solution)/shard_map/all_to_all | solution.py:517
  139.2 2.9 %collective-permute-start.5 = (bf16[8,16,1024]{2,1,0:T(8,128)(2,1)S(1)}, bf16[8,16,1024]{2,1,0:T(8,128)(2,1)S(1)}, u32[]{:S(2)}, u32[]{:S(2)}) collective-permute-start(bf16[8,16,1024]{2,1,0:T(8,128)(2,1)S(1)} %slice.11.lags), channel_id=1, source_target_pairs={{0,8},{8,0},{1,9},{9,1},{2,10},{10,2},{3,11},{11,3},{4,12},{12,4},... | collective-permute-start | bytes 786440 | tf_op jit(solution)/shard_map/ppermute | solution.py:521
  142.1 1.2 collective-permute-done.5.lags_c
  144.0 2.0 %write_filter.1 = f32[256,512]{1,0:T(8,128)} custom-call(s32[1]{0:T(128)} %bitcast.15.place, bf16[8,16,1024]{2,1,0:T(8,128)(2,1)} %copy-done.6, bf16[8,16,1024]{2,1,0:T(8,128)(2,1)} %copy-done.12), custom_call_target="tpu_custom_call" | custom-call | flops 1000000 | bytes 2000000 | tf_op jit(solution)/shard_map/write_filter/pallas_call | solution.py:502
  146.0 21.7 %all-to-all-done.4.mine = bf16[8,8,16,1024]{3,2,1,0:T(8,128)(2,1)S(1)} async-done(((bf16[8,8,16,1024]{3,2,1,0:T(8,128)(2,1)}), bf16[8,8,16,1024]{3,2,1,0:T(8,128)(2,1)S(1)}, u32[]{:S(2)}, u32[]{:S(2)}) %all-to-all-start.4) | async-done | bytes 2097184 | tf_op jit(solution)/shard_map/all_to_all | solution.py:517
  167.7 2.5 %collective-permute-start.6 = (bf16[8,8,16,1024]{3,2,1,0:T(8,128)(2,1)S(1)}, bf16[8,8,16,1024]{3,2,1,0:T(8,128)(2,1)}, u32[]{:S(2)}, u32[]{:S(2)}) collective-permute-start(bf16[8,8,16,1024]{3,2,1,0:T(8,128)(2,1)S(1)} %all-to-all-done.4.mine), channel_id=1, source_target_pairs={{0,8},{8,0},{1,9},{9,1},{2,10},{10,2},{3,11},{11,3},{4,12},{12,4},... | collective-permute-start | bytes 6291464 | tf_op jit(solution)/shard_map/ppermute | solution.py:521
  170.2 3.7 %write_half.2.refs_0_ = f32[512,4096]{1,0:T(8,128)} custom-call(s32[1]{0:T(128)} %bitcast.16.place, bf16[8,8,16,1024]{3,2,1,0:T(8,128)(2,1)} %copy-done.2), custom_call_target="tpu_custom_call" | custom-call | flops 1000000 | bytes 6000000 | tf_op jit(solution)/shard_map/write_half/pallas_call | solution.py:464
  174.1 3.7 %write_half.3 = f32[512,4096]{1,0:T(8,128)} custom-call(s32[1]{0:T(128)S(6)} %sub.14.place, bf16[8,8,16,1024]{3,2,1,0:T(8,128)(2,1)} %collective-permute-done.6.mine, f32[512,4096]{1,0:T(8,128)} %write_half.2.refs_0_), custom_call_target="tpu_custom_call", output_to_operand_aliasing={{}: (2, {})} | custom-call | flops 1000000 | bytes 6000000 | tf_op jit(solution)/shard_map/write_half/pallas_call | solution.py:464
  (37 shorter events, 4.6 us)
Async XLA Ops:
  7.0 6.0 %copy-start = (bf16[1,256,4096]{2,1,0:T(8,128)(2,1)S(1)}, bf16[1,256,4096]{2,1,0:T(8,128)(2,1)}, u32[]{:S(2)}) copy-start(bf16[1,256,4096]{2,1,0:T(8,128)(2,1)} %param.15) | copy-start | bytes 6291460
  7.0 25.2 %all-to-all-start = ((bf16[8,320,256]{2,1,0:T(8,128)(2,1)}), bf16[8,320,256]{2,1,0:T(8,128)(2,1)S(1)}, u32[]{:S(2)}, u32[]{:S(2)}) async-start(bf16[8,320,256]{2,1,0:T(8,128)(2,1)} %pack.1), calls=%async_computation | async-start | bytes 2621440 | tf_op jit(solution)/shard_map/all_to_all | solution.py:517
  13.0 4.2 %copy-start.14 = (f32[3,3,512]{2,1,0:T(4,128)S(1)}, f32[3,3,512]{2,1,0:T(4,128)}, u32[]{:S(2)}) copy-start(f32[3,3,512]{2,1,0:T(4,128)} %param.11) | copy-start | bytes 55300
  14.3 32.1 %collective-permute-start.2 = (bf16[256,1024]{1,0:T(8,128)(2,1)}, bf16[256,1024]{1,0:T(8,128)(2,1)S(1)}, u32[]{:S(2)}, u32[]{:S(2)}) collective-permute-start(bf16[256,1024]{1,0:T(8,128)(2,1)} %get-tuple-element.46), channel_id=1, source_target_pairs={{0,9},{1,8},{8,1},{9,0},{2,11},{3,10},{10,3},{11,2},{4,13},{5,12},... | collective-permute-start | bytes 1572872 | tf_op jit(solution)/shard_map/ppermute | solution.py:529
  16.8 34.2 %collective-permute-start = (bf16[256,1024]{1,0:T(8,128)(2,1)}, bf16[256,1024]{1,0:T(8,128)(2,1)S(1)}, u32[]{:S(2)}, u32[]{:S(2)}) collective-permute-start(bf16[256,1024]{1,0:T(8,128)(2,1)} %get-tuple-element.47), channel_id=1, source_target_pairs={{0,1},{1,0},{2,3},{3,2},{4,5},{5,4},{6,7},{7,6},{8,9},{9,8},{10,11... | collective-permute-start | bytes 1572872 | tf_op jit(solution)/shard_map/ppermute | solution.py:525
  16.8 34.2 %collective-permute-start.1 = (bf16[256,1024]{1,0:T(8,128)(2,1)}, bf16[256,1024]{1,0:T(8,128)(2,1)S(1)}, u32[]{:S(2)}, u32[]{:S(2)}) collective-permute-start(bf16[256,1024]{1,0:T(8,128)(2,1)} %get-tuple-element.48), channel_id=1, source_target_pairs={{0,8},{8,0},{1,9},{9,1},{2,10},{10,2},{3,11},{11,3},{4,12},{12,4},... | collective-permute-start | bytes 1572872 | tf_op jit(solution)/shard_map/ppermute | solution.py:521
  32.3 1.1 copy-start.3
  46.4 9.9 %copy-start.11 = (bf16[8,8,16,128]{3,2,1,0:T(8,128)(2,1)S(1)}, bf16[8,8,16,128]{3,2,1,0:T(8,128)(2,1)}, u32[]{:S(2)}) copy-start(bf16[8,8,16,128]{3,2,1,0:T(8,128)(2,1)} %get-tuple-element.25) | copy-start | bytes 786436
  46.4 32.8 %copy-start.7 = (bf16[256,1024]{1,0:T(8,128)(2,1)}, bf16[256,1024]{1,0:T(8,128)(2,1)S(1)}, u32[]{:S(2)}) copy-start(bf16[256,1024]{1,0:T(8,128)(2,1)S(1)} %collective-permute-done.2.g11) | copy-start | bytes 1572868
  51.0 28.2 %copy-start.8 = (bf16[256,1024]{1,0:T(8,128)(2,1)}, bf16[256,1024]{1,0:T(8,128)(2,1)S(1)}, u32[]{:S(2)}) copy-start(bf16[256,1024]{1,0:T(8,128)(2,1)S(1)} %collective-permute-done.g01) | copy-start | bytes 1572868
  51.0 28.2 %copy-start.9 = (bf16[256,1024]{1,0:T(8,128)(2,1)}, bf16[256,1024]{1,0:T(8,128)(2,1)S(1)}, u32[]{:S(2)}) copy-start(bf16[256,1024]{1,0:T(8,128)(2,1)S(1)} %collective-permute-done.1.g10) | copy-start | bytes 1572868
  51.0 24.8 %all-to-all-start.1 = ((bf16[8,320,256]{2,1,0:T(8,128)(2,1)}), bf16[8,320,256]{2,1,0:T(8,128)(2,1)S(1)}, u32[]{:S(2)}, u32[]{:S(2)}) async-start(bf16[8,320,256]{2,1,0:T(8,128)(2,1)} %get-tuple-element.24), calls=%async_computation.1 | async-start | bytes 2621440 | tf_op jit(solution)/shard_map/all_to_all | solution.py:517
  57.0 17.8 %collective-permute-start.3 = (bf16[4,8,16,128]{3,2,1,0:T(8,128)(2,1)S(1)}, bf16[4,8,16,128]{3,2,1,0:T(8,128)(2,1)S(1)}, u32[]{:S(2)}, u32[]{:S(2)}) collective-permute-start(bf16[4,8,16,128]{3,2,1,0:T(8,128)(2,1)S(1)} %get-tuple-element.49), channel_id=1, source_target_pairs={{0,1},{1,0},{2,3},{3,2},{4,5},{5,4},{6,7},{7,6},{8,9},{9,8},{10,11... | collective-permute-start | bytes 393224 | tf_op jit(solution)/shard_map/ppermute | solution.py:525
  74.8 7.8 %copy-start.13 = (bf16[4,8,16,128]{3,2,1,0:T(8,128)(2,1)}, bf16[4,8,16,128]{3,2,1,0:T(8,128)(2,1)S(1)}, u32[]{:S(2)}) copy-start(bf16[4,8,16,128]{3,2,1,0:T(8,128)(2,1)S(1)} %collective-permute-done.3.lags_beside) | copy-start | bytes 393220
  75.9 1.1 copy-start.1
  79.3 3.3 %collective-permute-start.4 = (bf16[2,256,512]{2,1,0:T(8,128)(2,1)}, bf16[2,256,512]{2,1,0:T(8,128)(2,1)S(1)}, u32[]{:S(2)}, u32[]{:S(2)}) collective-permute-start(bf16[2,256,512]{2,1,0:T(8,128)(2,1)} %unpack_mixed.1.mine), channel_id=1, source_target_pairs={{0,8},{8,0},{1,9},{9,1},{2,10},{10,2},{3,11},{11,3},{4,12},{12,4},... | collective-permute-start | bytes 1572872 | tf_op jit(solution)/shard_map/ppermute | solution.py:521
  82.6 0.8 copy-start.10
  87.6 12.0 %copy-start.5 = (bf16[2,256,512]{2,1,0:T(8,128)(2,1)S(1)}, bf16[2,256,512]{2,1,0:T(8,128)(2,1)}, u32[]{:S(2)}) copy-start(bf16[2,256,512]{2,1,0:T(8,128)(2,1)} %unpack_mixed.1.mine) | copy-start | bytes 1572868
  87.6 29.5 %all-to-all-start.2 = ((bf16[32,16,1280]{2,1,0:T(8,128)(2,1)}), bf16[32,16,1280]{2,1,0:T(8,128)(2,1)S(1)}, u32[]{:S(2)}, u32[]{:S(2)}) async-start(bf16[32,16,1280]{2,1,0:T(8,128)(2,1)} %partial.1), calls=%async_computation.2 | async-start | bytes 2621440 | tf_op jit(solution)/shard_map/all_to_all | solution.py:517
  117.2 1.1 copy-start.4
  134.9 32.8 %all-to-all-start.4 = ((bf16[8,8,16,1024]{3,2,1,0:T(8,128)(2,1)}), bf16[8,8,16,1024]{3,2,1,0:T(8,128)(2,1)S(1)}, u32[]{:S(2)}, u32[]{:S(2)}) async-start(bf16[8,8,16,1024]{3,2,1,0:T(8,128)(2,1)} %broadcast_in_dim.29), calls=%async_computation.4 | async-start | bytes 4194304 | tf_op jit(solution)/shard_map/all_to_all | solution.py:517
  139.2 4.0 %copy-start.6 = (bf16[8,16,1024]{2,1,0:T(8,128)(2,1)}, bf16[8,16,1024]{2,1,0:T(8,128)(2,1)S(1)}, u32[]{:S(2)}) copy-start(bf16[8,16,1024]{2,1,0:T(8,128)(2,1)S(1)} %slice.11.lags) | copy-start | bytes 786436
  139.2 4.0 %collective-permute-start.5 = (bf16[8,16,1024]{2,1,0:T(8,128)(2,1)S(1)}, bf16[8,16,1024]{2,1,0:T(8,128)(2,1)S(1)}, u32[]{:S(2)}, u32[]{:S(2)}) collective-permute-start(bf16[8,16,1024]{2,1,0:T(8,128)(2,1)S(1)} %slice.11.lags), channel_id=1, source_target_pairs={{0,8},{8,0},{1,9},{9,1},{2,10},{10,2},{3,11},{11,3},{4,12},{12,4},... | collective-permute-start | bytes 786440 | tf_op jit(solution)/shard_map/ppermute | solution.py:521
  143.2 0.7 copy-start.12
  167.7 2.5 %copy-start.2 = (bf16[8,8,16,1024]{3,2,1,0:T(8,128)(2,1)}, bf16[8,8,16,1024]{3,2,1,0:T(8,128)(2,1)S(1)}, u32[]{:S(2)}) copy-start(bf16[8,8,16,1024]{3,2,1,0:T(8,128)(2,1)S(1)} %all-to-all-done.4.mine) | copy-start | bytes 6291460
  167.7 6.4 %collective-permute-start.6 = (bf16[8,8,16,1024]{3,2,1,0:T(8,128)(2,1)S(1)}, bf16[8,8,16,1024]{3,2,1,0:T(8,128)(2,1)}, u32[]{:S(2)}, u32[]{:S(2)}) collective-permute-start(bf16[8,8,16,1024]{3,2,1,0:T(8,128)(2,1)S(1)} %all-to-all-done.4.mine), channel_id=1, source_target_pairs={{0,8},{8,0},{1,9},{9,1},{2,10},{10,2},{3,11},{11,3},{4,12},{12,4},... | collective-permute-start | bytes 6291464 | tf_op jit(solution)/shard_map/ppermute | solution.py:521

commit v5 on v2

--- a/solution.py
+++ b/solution.py
@@ -15,8 +15,8 @@
 HALF = 64
 SENT_ROWS = BLOCK + 64
 SEQ = ("x", "yl")
-DEPTH = ("z", "yh")
-CHIPS = DEPTH + SEQ
+MOST = ("zh", "yh") + SEQ
+CHIPS = ("zh", "zl", "yh") + SEQ
 
 
 @functools.lru_cache(maxsize=None)
@@ -281,9 +281,9 @@
     for b in range(8):
         start = BLOCK * b
         y = sum(w_u[j] * u_pad[start + j : start + j + BLOCK] for j in range(3))
-        sent[b, :, 0:128] = y.astype(BF)
+        sent[b, 0:BLOCK, 0:128] = y.astype(BF)
         y = sum(w_x[j] * x_pad[start + j : start + j + BLOCK] for j in range(3))
-        sent[b, :, 128:256] = y.astype(BF)
+        sent[b, 0:BLOCK, 128:256] = y.astype(BF)
 
 
 def conv(place, got, short, skip):
@@ -330,8 +330,8 @@
 def spread(got, there, first, second, low):
     for q in range(4):
         lanes = slice(128 * q, 128 * q + 128)
-        a = got[2 * q, :, there].astype(F32)
-        b = got[2 * q + 1, :, there].astype(F32)
+        a = got[2 * q, 0:BLOCK, there].astype(F32)
+        b = got[2 * q + 1, 0:BLOCK, there].astype(F32)
         if first is not None:
             first[:, lanes] = jnp.where(low, a, turned(b)).astype(BF)
         if second is not None:
@@ -368,70 +368,79 @@
     )(got)
 
 
-def partial_kernel(place, mine, theirs, grad_mine, grad_theirs, lags, packed):
+def partial_kernel(place, m00, m01, m10, m11, g00, g01, g10, g11, lags, lags_z, packed):
     def term(mixed, grad):
         return lax.dot_general(
             mixed[...], grad[...], (((0,), (0,)), ((), ())), preferred_element_type=F32
         )
 
-    part = (term(mine, grad_mine) + term(theirs, grad_theirs)).astype(BF)
-    for s in range(8):
-        for a in range(4):
-            start = 64 * s + 16 * a
-            packed[a, 0, s, :, 0:1024] = part[start : start + 16]
-            packed[a, 0, s, :, 1024:1152] = lags[s, 2 * a + pl.program_id(0)]
-
-
-def partial(place, mine, theirs, out_grad, grad_theirs, lags):
+    part = term(m00, g00) + term(m01, g01) + term(m10, g10) + term(m11, g11)
+    part = part.astype(BF)
+    for n in range(32):
+        packed[n, :, 0:1024] = part[16 * n : 16 * n + 16]
+        s, k = n % 8, n // 8
+        lag = lags[s, k].astype(F32) + lags_z[s, k].astype(F32)
+        packed[n, :, 1024:1152] = lag.astype(BF)
+
+
+def partial(place, mixed, grad, grads, lags, lags_z):
+    full = lambda *shape: pl.BlockSpec(shape, lambda n, p: (0,) * len(shape))
     return pl.pallas_call(
         partial_kernel,
         grid_spec=pltpu.PrefetchScalarGridSpec(
             num_scalar_prefetch=1,
-            grid=(2,),
-            in_specs=[
-                pl.BlockSpec((BLOCK, 512), lambda h, p: (0, 0)),
-                pl.BlockSpec((BLOCK, 512), lambda h, p: (0, 0)),
-                pl.BlockSpec((BLOCK, 1024), lambda h, p: (0, 2 * p[0] + h)),
-                pl.BlockSpec((BLOCK, 1024), lambda h, p: (0, h)),
-                pl.BlockSpec((8, 8, 16, 128), lambda h, p: (0, 0, 0, 0)),
-            ],
-            out_specs=pl.BlockSpec((4, 1, 8, 16, 1152), lambda h, p: (0, h, 0, 0, 0)),
+            grid=(1,),
+            in_specs=[full(BLOCK, 512)] * 4
+            + [pl.BlockSpec((BLOCK, 1024), lambda n, p: (0, p[0]))]
+            + [full(BLOCK, 1024)] * 3
+            + [full(8, 4, 16, 128)] * 2,
+            out_specs=full(32, 16, 1152),
         ),
-        out_shape=jax.ShapeDtypeStruct((4, 2, 8, 16, 1152), BF),
+        out_shape=jax.ShapeDtypeStruct((32, 16, 1152), BF),
         name="partial",
-    )(place, mine, theirs, out_grad, grad_theirs, lags)
-
-
-def reduce_kernel(scale, got, shared):
+    )(place, *mixed, grad, *grads, lags, lags_z)
+
+
+def reduce_kernel(scale, got, shared, lags):
     total = jnp.zeros((16, 1024), F32)
-    for n in range(64):
+    for n in range(32):
         total = total + got[n, :, 0:1024].astype(F32)
     total = (total * scale).astype(BF)
-    for k in range(8):
-        shared[k, :, 0:1024] = total
+    for n in range(64):
+        shared[n] = total
     for s in range(8):
         lag = jnp.zeros((16, 128), F32)
-        for k in range(8):
+        for k in range(4):
             lag = lag + got[8 * k + s, :, 1024:1152].astype(F32)
-        lag = (lag * scale).astype(BF)
-        for k in range(8):
-            shared[k, :, 1024 + 128 * s : 1152 + 128 * s] = lag
+        lags[:, 128 * s : 128 * s + 128] = lag * scale
 
 
 def reduce(got, scale):
     return pl.pallas_call(
         functools.partial(reduce_kernel, scale),
-        out_shape=jax.ShapeDtypeStruct((8, 16, 2048), BF),
+        out_shape=[
+            jax.ShapeDtypeStruct((64, 16, 1024), BF),
+            jax.ShapeDtypeStruct((16, 1024), F32),
+        ],
         name="reduce",
     )(got)
 
 
 def half_kernel(place, mine, *refs):
-    grad_weight = refs[-1]
-    for k in range(8):
-        rows = slice(16 * (k // 2), 16 * (k // 2) + 16)
-        lanes = slice(1024 * (k % 2), 1024 * (k % 2) + 1024)
-        grad_weight[rows, lanes] = mine[0, k].astype(F32)
+    grad_weight, wide, sems = refs[-3:]
+
+    def copy(n):
+        zh, zl, yh = n // 4, n // 2 % 2, n % 2
+        rows = slice(128 * (2 * zh + yh), 128 * (2 * zh + yh) + 128)
+        lanes = pl.ds(pl.multiple_of(2048 * place[0] + 1024 * zl, 1024), 1024)
+        return pltpu.make_async_copy(wide.at[n], grad_weight.at[rows, lanes], sems.at[n])
+
+    for n in range(8):
+        for k in range(8):
+            wide[n, 16 * k : 16 * k + 16] = mine[8 * n + k].astype(F32)
+        copy(n).start()
+    for n in range(8):
+        copy(n).wait()
 
 
 def write_half(half, rows, whole=None):
@@ -440,10 +449,14 @@
         half_kernel,
         grid_spec=pltpu.PrefetchScalarGridSpec(
             num_scalar_prefetch=1,
-            grid=(8,),
-            in_specs=[pl.BlockSpec((1, 8, 16, 1024), lambda s, p: (s, 0, 0, 0))]
-            + [pl.BlockSpec(memory_space=pl.ANY)] * len(more),
-            out_specs=pl.BlockSpec((64, 2048), lambda s, p: (s, p[0])),
+            grid=(1,),
+            in_specs=[pl.BlockSpec((64, 16, 1024), lambda n, p: (0, 0, 0))]
+            + [pl.BlockSpec(memory_space=pltpu.HBM)] * len(more),
+            out_specs=pl.BlockSpec(memory_space=pltpu.HBM),
+            scratch_shapes=[
+                pltpu.VMEM((8, 128, 1024), F32),
+                pltpu.SemaphoreType.DMA((8,)),
+            ],
         ),
         out_shape=jax.ShapeDtypeStruct((512, 4096), F32),
         input_output_aliases={2: 0} if more else {},
@@ -452,27 +465,37 @@
     )(half, rows, *more)
 
 
-def filter_kernel(lag_mine, lag_theirs, grad_filter):
+def filter_kernel(place, *refs):
+    grad_filter = refs[-1]
     low = low_lanes(16)
-    for k in range(8):
-        for q in range(4):
-            def both(s):
-                there = slice(128 * s, 128 * s + 128)
-                return lag_mine[k, :, there].astype(F32) + lag_theirs[k, :, there].astype(F32)
-
-            a, b = both(2 * q), both(2 * q + 1)
-            lanes = slice(128 * q, 128 * q + 128)
-            grad_filter[32 * k : 32 * k + 16, lanes] = jnp.where(low, a, turned(b))
-            grad_filter[32 * k + 16 : 32 * k + 32, lanes] = jnp.where(low, turned(a), b)
-
-
-def write_filter(lag_mine, lag_theirs):
+    for d in range(4):
+        z = (place[0] + 4 - d) % 4
+        for n in range(2):
+            yh = place[1] if n == 0 else 1 - place[1]
+            row = pl.multiple_of(32 * (2 * z + yh), 32)
+            lags = refs[2 * d + n]
+            for q in range(4):
+                a = lags[:, 256 * q : 256 * q + 128].astype(F32)
+                b = lags[:, 256 * q + 128 : 256 * q + 256].astype(F32)
+                lanes = slice(128 * q, 128 * q + 128)
+                grad_filter[pl.ds(row, 16), lanes] = jnp.where(low, a, turned(b))
+                grad_filter[pl.ds(row + 16, 16), lanes] = jnp.where(low, turned(a), b)
+
+
+def write_filter(place, lags):
+    full = lambda *shape: pl.BlockSpec(shape, lambda n, p: (0,) * len(shape))
     return pl.pallas_call(
         filter_kernel,
+        grid_spec=pltpu.PrefetchScalarGridSpec(
+            num_scalar_prefetch=1,
+            grid=(1,),
+            in_specs=[full(16, 1024)] * 8,
+            out_specs=full(BLOCK, 512),
+        ),
         out_shape=jax.ShapeDtypeStruct((BLOCK, 512), F32),
         cost_estimate=pl.CostEstimate(flops=10**6, bytes_accessed=2 * 10**6, transcendentals=0),
         name="write_filter",
-    )(lag_mine, lag_theirs)
+    )(place, *lags)
 
 
 def exchange(x, axes):
@@ -481,33 +504,69 @@
 
 def across(x):
     return lax.ppermute(x, "c", [(0, 1), (1, 0)])
+
+
+def above(x):
+    return lax.ppermute(x, "zl", [(0, 1), (1, 0)])
+
+
+def opposite(x):
+    return lax.ppermute(x, ("zl", "c"), [(n, 3 - n) for n in range(4)])
+
+
+def gathered(lags):
+    pair = (lags, lax.ppermute(lags, "yh", [(0, 1), (1, 0)]))
+    out = list(pair)
+    for d in range(1, 4):
+        route = [(n, (n + d) % 4) for n in range(4)]
+        out += [lax.ppermute(part, ("zh", "zl"), route) for part in pair]
+    return out
 
 
 def on_device(streams, short_filter, long_filter, skip_gain, out_weight, out_grad):
     scale = 1.0 / math.sqrt(16 * 2048)
     core = lax.axis_index("c").astype(jnp.int32)
+    side = lax.axis_index("zl").astype(jnp.int32)
     seq = lax.axis_index(SEQ).astype(jnp.int32)
     grad = out_grad[0]
-    grad_theirs = across(lax.dynamic_slice(grad, (0, (1 - core) * 2048), (BLOCK, 2048)))
+
+    def quarter(c, z):
+        return lax.dynamic_slice(grad, (0, 1024 * (2 * c + z)), (BLOCK, 1024))
+
+    grads = (
+        above(quarter(core, 1 - side)),
+        across(quarter(1 - core, side)),
+        opposite(quarter(1 - core, 1 - side)),
+    )
     got = exchange(pack(streams[:, 0], grad, out_weight, long_filter), SEQ)
     sent, lags = conv(
         seq[None], got, short_filter.reshape(9, 512), skip_gain.reshape(1, 512)
     )
+    sent, grads = lax.optimization_barrier((sent, grads))
+    lags = lags.reshape(8, 2, 2, 2, 16, 128)
+
+    def of_side(z):
+        return lax.dynamic_index_in_dim(lags, z, 2, False).reshape(8, 4, 16, 128)
+
+    lags_own, lags_z = of_side(side), above(of_side(1 - side))
     back = exchange(sent, SEQ)
-    mixed = unpack_mixed(back)
-    mixed_theirs = across(mixed)
-    part = partial(core[None], mixed, mixed_theirs, grad, grad_theirs, lags)
-    part, mixed, back = lax.optimization_barrier((part, mixed, back))
-    part = exchange(part.reshape(64, 16, 1152), CHIPS)
-    layer_out = jnp.dot(mixed, out_weight, preferred_element_type=F32).astype(BF)
+    back, lags_own, lags_z = lax.optimization_barrier((back, lags_own, lags_z))
+    m00 = unpack_mixed(back)
+    m01, m10 = above(m00), across(m00)
+    mixed = (m00, m01, m10, across(m01))
+    part = partial((2 * core + side)[None], mixed, grad, grads, lags_own, lags_z)
+    part, m00, back = lax.optimization_barrier((part, m00, back))
+    part = exchange(part, MOST)
+    layer_out = jnp.dot(m00, out_weight, preferred_element_type=F32).astype(BF)
     grad_streams = unpack_grads(back)
     part, layer_out, grad_streams = lax.optimization_barrier((part, layer_out, grad_streams))
-    shared = exchange(reduce(part, scale), DEPTH)
-    lag_mine = shared[:, :, 1024:]
-    lag_theirs = across(lag_mine)
-    rows = jnp.broadcast_to(shared[None, :, :, :1024], (8, 8, 16, 1024))
-    mine = exchange(rows, SEQ)
-    grad_filter = write_filter(lag_mine, lag_theirs)
+    rows, lags = reduce(part, scale)
+    rows, lags = lax.optimization_barrier((rows, lags))
+    mine = exchange(rows, CHIPS)
+    lags = (lags + across(lags)).astype(BF)
+    place = jnp.stack([lax.axis_index(("zh", "zl")), lax.axis_index("yh")]).astype(jnp.int32)
+    grad_filter = write_filter(place, gathered(lags))
+    mine, grad_filter = lax.optimization_barrier((mine, grad_filter))
     theirs = across(mine)
     grad_weight = write_half(core[None], mine)
     grad_weight = write_half(1 - core[None], theirs, grad_weight)
@@ -515,8 +574,10 @@
 
 
 def solution(mesh):
-    fine = Mesh(mesh.devices.reshape(4, 2, 2, 4, 2), ("z", "yh", "c", "x", "yl"))
-    dp = ("z", "yh", "c")
+    fine = Mesh(
+        mesh.devices.reshape(2, 2, 2, 2, 4, 2), ("zh", "zl", "yh", "c", "x", "yl")
+    )
+    dp = ("zh", "zl", "yh", "c")
     placed = (P(None, dp, SEQ, None), P(), P(SEQ, None), P(), P(), P(dp, SEQ, None))
     return jax.shard_map(
         on_device,

time: 185 us -> 167 us (0.903)
  the two profiles are of different devices: /device:TPU:1 before, /device:TPU:2 now
where the time goes in v5:
time: 167 us; the launch traced here: 166 us
  waiting for transfers between devices  65.4 us (39%)
  starting transfers between devices  45.8 us (27%)
  Pallas kernels  40.7 us (24%)
  local copies, waits for them, and re-layouts  8.39 us (5%)
  matrix products  4.77 us (3%)
    all_to_all x4, waiting for transfers between devices, exchange(): return lax.all_to_all(x, axes, 0, 0, tiled=True)  34.5 us
    all_to_all x4, starting transfers between devices, exchange(): return lax.all_to_all(x, axes, 0, 0, tiled=True)  27.5 us
    ppermute x1, waiting for transfers between devices, gathered(): pair = (lags, lax.ppermute(lags, 'yh', [(0, 1), (1, 0)]))  16.3 us
    pallas_call x1, Pallas kernels, conv(): pl.pallas_call(conv_kernel, grid_spec=pltpu.PrefetchScalarGridSpec(num_sc...  13 us
    ppermute x6, starting transfers between devices, gathered(): out += [lax.ppermute(part, ('zh', 'zl'), route) for part in pair]  9.16 us
    ppermute x3, waiting for transfers between devices, above(): return lax.ppermute(x, 'zl', [(0, 1), (1, 0)])  8.16 us
    pallas_call x2, Pallas kernels, write_half(): pl.pallas_call(half_kernel, grid_spec=pltpu.PrefetchScalarGridSpec(num_sc...  7.39 us
    pallas_call x1, Pallas kernels, pack(): pl.pallas_call(pack_kernel, grid=(steps,), in_specs=[pl.BlockSpec((3, BLO...  6.38 us
  transfers between devices with their start and end apart: 20, of which 10 were waited for; matrix products, arithmetic and copies ran while one was open for 5% of the time, Pallas kernels for 13%

profile of v5, /device:TPU:2, one launch (start us, length us, event | category | flops | bytes accessed | tf_op | source)
XLA Modules:
  0.0 166.4 jit_solution(7018311155036505540)
XLA Ops:
  0.6 6.4 %pack.1 = bf16[8,320,256]{2,1,0:T(8,128)(2,1)} custom-call(bf16[3,256,512]{2,1,0:T(8,128)(2,1)} %bitcast.29, bf16[256,4096]{1,0:T(8,128)(2,1)} %bitcast.27, bf16[512,4096]{1,0:T(8,128)(2,1)} %weight.1, f32[256,512]{1,0:T(8,128)} %filt.1), custom_call_target="tpu_custom_call" | custom-call | tf_op jit(solution)/shard_map/pack/pallas_call | solution.py:90
  7.0 6.0 %all-to-all-start = ((bf16[8,320,256]{2,1,0:T(8,128)(2,1)}), bf16[8,320,256]{2,1,0:T(8,128)(2,1)S(1)}, u32[]{:S(2)}, u32[]{:S(2)}) async-start(bf16[8,320,256]{2,1,0:T(8,128)(2,1)} %pack.1), calls=%async_computation | async-start | bytes 2621440 | tf_op jit(solution)/shard_map/all_to_all | solution.py:502
  13.0 1.2 dynamic-slice_bitcast_fusion
  15.0 1.2 collective-permute-start
  16.9 14.0 %all-to-all-done.got = bf16[8,320,256]{2,1,0:T(8,128)(2,1)S(1)} async-done(((bf16[8,320,256]{2,1,0:T(8,128)(2,1)}), bf16[8,320,256]{2,1,0:T(8,128)(2,1)S(1)}, u32[]{:S(2)}, u32[]{:S(2)}) %all-to-all-start) | async-done | bytes 1310752 | tf_op jit(solution)/shard_map/all_to_all | solution.py:502
  31.9 13.0 %conv.1 = (bf16[8,256,256]{2,1,0:T(8,128)(2,1)}, bf16[8,8,16,128]{3,2,1,0:T(8,128)(2,1)}) custom-call(s32[1]{0:T(128)} %bitcast.1.place, bf16[8,320,256]{2,1,0:T(8,128)(2,1)} %copy-done.3, f32[9,512]{1,0:T(8,128)} %reshape.28.short, f32[1,512]{1,0:T(1,128)} %bitcast.34, bf16[512,256]{1,0:T(8,128)(2,1)} %constant.54.clone.ahead_h, ...), custom_call_target="tpu_custom_call" | custom-call | tf_op jit(solution)/shard_map/conv/pallas_call | solution.py:292
  45.0 5.7 %all-to-all-start.1 = ((bf16[8,256,256]{2,1,0:T(8,128)(2,1)}), bf16[8,256,256]{2,1,0:T(8,128)(2,1)S(1)}, u32[]{:S(2)}, u32[]{:S(2)}) async-start(bf16[8,256,256]{2,1,0:T(8,128)(2,1)} %get-tuple-element.24), calls=%async_computation.1 | async-start | bytes 2097152 | tf_op jit(solution)/shard_map/all_to_all | solution.py:502
  51.3 1.9 %collective-permute-start.3 = (bf16[8,4,16,128]{3,2,1,0:T(8,128)(2,1)S(1)}, bf16[8,4,16,128]{3,2,1,0:T(8,128)(2,1)S(1)}, u32[]{:S(2)}, u32[]{:S(2)}) collective-permute-start(bf16[8,4,16,128]{3,2,1,0:T(8,128)(2,1)S(1)} %bitcast.33), channel_id=1, source_target_pairs={{0,32},{32,0},{1,33},{33,1},{2,34},{34,2},{3,35},{35,3},{4,36},{36... | collective-permute-start | bytes 393224 | tf_op jit(solution)/shard_map/ppermute | solution.py:510
  53.2 3.0 %collective-permute-done.3.lags_z = bf16[8,4,16,128]{3,2,1,0:T(8,128)(2,1)S(1)} collective-permute-done((bf16[8,4,16,128]{3,2,1,0:T(8,128)(2,1)S(1)}, bf16[8,4,16,128]{3,2,1,0:T(8,128)(2,1)S(1)}, u32[]{:S(2)}, u32[]{:S(2)}) %collective-permute-start.3) | collective-permute-done | bytes 131104 | tf_op jit(solution)/shard_map/ppermute | solution.py:510
  56.3 7.8 %all-to-all-done.1.got = bf16[8,256,256]{2,1,0:T(8,128)(2,1)S(1)} async-done(((bf16[8,256,256]{2,1,0:T(8,128)(2,1)}), bf16[8,256,256]{2,1,0:T(8,128)(2,1)S(1)}, u32[]{:S(2)}, u32[]{:S(2)}) %all-to-all-start.1) | async-done | bytes 1048608 | tf_op jit(solution)/shard_map/all_to_all | solution.py:502
  65.1 1.9 %unpack_mixed.1.m00 = bf16[256,512]{1,0:T(8,128)(2,1)} custom-call(bf16[8,256,256]{2,1,0:T(8,128)(2,1)} %copy-done.1), custom_call_target="tpu_custom_call" | custom-call | tf_op jit(solution)/shard_map/unpack_mixed/pallas_call | solution.py:346
  67.0 1.9 %collective-permute-start.4 = (bf16[256,512]{1,0:T(8,128)(2,1)}, bf16[256,512]{1,0:T(8,128)(2,1)S(1)}, u32[]{:S(2)}, u32[]{:S(2)}) collective-permute-start(bf16[256,512]{1,0:T(8,128)(2,1)} %unpack_mixed.1.m00), channel_id=1, source_target_pairs={{0,32},{32,0},{1,33},{33,1},{2,34},{34,2},{3,35},{35,3},{4,36},{36... | collective-permute-start | bytes 786440 | tf_op jit(solution)/shard_map/ppermute | solution.py:510
  68.9 5.1 %collective-permute-done.4.m01 = bf16[256,512]{1,0:T(8,128)(2,1)S(1)} collective-permute-done((bf16[256,512]{1,0:T(8,128)(2,1)}, bf16[256,512]{1,0:T(8,128)(2,1)S(1)}, u32[]{:S(2)}, u32[]{:S(2)}) %collective-permute-start.4) | collective-permute-done | bytes 262176 | tf_op jit(solution)/shard_map/ppermute | solution.py:510
  74.0 1.5 collective-permute-done.6.m11
  76.3 4.2 %partial.1 = bf16[32,16,1152]{2,1,0:T(8,128)(2,1)} custom-call(s32[1]{0:T(128)} %bitcast.place, bf16[256,512]{1,0:T(8,128)(2,1)} %unpack_mixed.1.m00, bf16[256,512]{1,0:T(8,128)(2,1)} %copy-done.9, bf16[256,512]{1,0:T(8,128)(2,1)} %copy-done.10, bf16[256,512]{1,0:T(8,128)(2,1)} %copy-done.11, bf16[256,4096]{1,0:T(8,128)(2,1)} %bitcast.28, ...), custom_call_target="tpu_custom_call" | custom-call | tf_op jit(solution)/shard_map/partial/pallas_call | solution.py:388
  80.4 10.1 %all-to-all-start.2 = ((bf16[32,16,1152]{2,1,0:T(8,128)(2,1)}), bf16[32,16,1152]{2,1,0:T(8,128)(2,1)S(1)}, u32[]{:S(2)}, u32[]{:S(2)}) async-start(bf16[32,16,1152]{2,1,0:T(8,128)(2,1)} %partial.1), calls=%async_computation.2 | async-start | bytes 2359296 | tf_op jit(solution)/shard_map/all_to_all | solution.py:502
  90.6 2.4 %unpack_grads.1 = bf16[3,256,512]{2,1,0:T(8,128)(2,1)} custom-call(bf16[8,256,256]{2,1,0:T(8,128)(2,1)} %copy-done.1), custom_call_target="tpu_custom_call" | custom-call | flops 1000000 | bytes 2000000 | tf_op jit(solution)/shard_map/unpack_grads/pallas_call | solution.py:363
  93.0 4.8 %convolution_convert_fusion = bf16[256,4096]{1,0:T(8,128)(2,1)} fusion(bf16[256,512]{1,0:T(8,128)(2,1)S(1)} %copy-done.5, bf16[512,4096]{1,0:T(8,128)(2,1)} %weight.1), kind=kOutput, calls=%fused_computation | convolution fusion | flops 1074790400 | bytes 6553600 | tf_op jit(solution)/shard_map/dot_general | solution.py:560
  97.7 12.6 %all-to-all-done.2.got = bf16[32,16,1152]{2,1,0:T(8,128)(2,1)S(1)} async-done(((bf16[32,16,1152]{2,1,0:T(8,128)(2,1)}), bf16[32,16,1152]{2,1,0:T(8,128)(2,1)S(1)}, u32[]{:S(2)}, u32[]{:S(2)}) %all-to-all-start.2) | async-done | bytes 1179680 | tf_op jit(solution)/shard_map/all_to_all | solution.py:502
  110.4 1.1 copy-done.4
  111.5 3.0 %reduce.1 = (bf16[64,16,1024]{2,1,0:T(8,128)(2,1)}, f32[16,1024]{1,0:T(8,128)}) custom-call(bf16[32,16,1152]{2,1,0:T(8,128)(2,1)} %copy-done.4), custom_call_target="tpu_custom_call" | custom-call | tf_op jit(solution)/shard_map/reduce/pallas_call | solution.py:419
  114.4 5.7 %all-to-all-start.3 = ((bf16[64,16,1024]{2,1,0:T(8,128)(2,1)}), bf16[64,16,1024]{2,1,0:T(8,128)(2,1)S(1)}, u32[]{:S(2)}, u32[]{:S(2)}) async-start(bf16[64,16,1024]{2,1,0:T(8,128)(2,1)} %get-tuple-element.38), calls=%async_computation.3 | async-start | bytes 4194304 | tf_op jit(solution)/shard_map/all_to_all | solution.py:502
  120.2 1.2 collective-permute-done.7
  121.5 3.1 %collective-permute-start.8 = (bf16[16,1024]{1,0:T(8,128)(2,1)S(1)}, bf16[16,1024]{1,0:T(8,128)(2,1)S(1)}, u32[]{:S(2)}, u32[]{:S(2)}) collective-permute-start(bf16[16,1024]{1,0:T(8,128)(2,1)S(1)} %add_convert_fusion.refs_0_), channel_id=1, source_target_pairs={{0,16},{16,0},{1,17},{17,1},{2,18},{18,2},{3,19},{19,3},{4,20},{20... | collective-permute-start | bytes 98312 | tf_op jit(solution)/shard_map/ppermute | solution.py:518
  124.6 3.0 %collective-permute-start.13 = (bf16[16,1024]{1,0:T(8,128)(2,1)S(1)}, bf16[16,1024]{1,0:T(8,128)(2,1)S(1)}, u32[]{:S(2)}, u32[]{:S(2)}) collective-permute-start(bf16[16,1024]{1,0:T(8,128)(2,1)S(1)} %add_convert_fusion.refs_0_), channel_id=1, source_target_pairs={{0,96},{32,0},{64,32},{96,64},{1,97},{33,1},{65,33},{97,65},{2,98}... | collective-permute-start | bytes 98312 | tf_op jit(solution)/shard_map/ppermute | solution.py:522
  129.2 16.3 %collective-permute-done.8.refs_1_ = bf16[16,1024]{1,0:T(8,128)(2,1)S(1)} collective-permute-done((bf16[16,1024]{1,0:T(8,128)(2,1)S(1)}, bf16[16,1024]{1,0:T(8,128)(2,1)S(1)}, u32[]{:S(2)}, u32[]{:S(2)}) %collective-permute-start.8) | collective-permute-done | bytes 32800 | tf_op jit(solution)/shard_map/ppermute | solution.py:518
  145.5 3.1 %collective-permute-start.14 = (bf16[16,1024]{1,0:T(8,128)(2,1)S(1)}, bf16[16,1024]{1,0:T(8,128)(2,1)S(1)}, u32[]{:S(2)}, u32[]{:S(2)}) collective-permute-start(bf16[16,1024]{1,0:T(8,128)(2,1)S(1)} %collective-permute-done.8.refs_1_), channel_id=1, source_target_pairs={{0,96},{32,0},{64,32},{96,64},{1,97},{33,1},{65,33},{97,65},{2,98}... | collective-permute-start | bytes 98312 | tf_op jit(solution)/shard_map/ppermute | solution.py:522
  150.7 3.3 %collective-permute-done.12.refs_5_ = bf16[16,1024]{1,0:T(8,128)(2,1)S(1)} collective-permute-done((bf16[16,1024]{1,0:T(8,128)(2,1)S(1)}, bf16[16,1024]{1,0:T(8,128)(2,1)S(1)}, u32[]{:S(2)}, u32[]{:S(2)}) %collective-permute-start.12) | collective-permute-done | bytes 32800 | tf_op jit(solution)/shard_map/ppermute | solution.py:522
  155.2 2.5 %write_filter.1 = f32[256,512]{1,0:T(8,128)} custom-call(s32[2]{0:T(128)} %pad_add_fusion.place, bf16[16,1024]{1,0:T(8,128)(2,1)} %copy-done.14, bf16[16,1024]{1,0:T(8,128)(2,1)} %copy-done.16, bf16[16,1024]{1,0:T(8,128)(2,1)} %copy-done.19, bf16[16,1024]{1,0:T(8,128)(2,1)} %copy-done.22, bf16[16,1024]{1,0:T(8,128)(2,1)} %copy-done.18, ...), custom_call_target="tpu_custom_call" | custom-call | flops 1000000 | bytes 2000000 | tf_op jit(solution)/shard_map/write_filter/pallas_call | solution.py:487
  157.8 1.2 copy-done.2
  159.0 3.7 %write_half.2.refs_0_ = f32[512,4096]{1,0:T(8,128)} custom-call(s32[1]{0:T(128)} %bitcast.16.place, bf16[64,16,1024]{2,1,0:T(8,128)(2,1)} %copy-done.2), custom_call_target="tpu_custom_call" | custom-call | flops 1000000 | bytes 6000000 | tf_op jit(solution)/shard_map/write_half/pallas_call | solution.py:448
  162.7 3.7 %write_half.3 = f32[512,4096]{1,0:T(8,128)} custom-call(s32[1]{0:T(128)S(6)} %sub.14.place, bf16[64,16,1024]{2,1,0:T(8,128)(2,1)} %collective-permute-done.15.mine, f32[512,4096]{1,0:T(8,128)} %write_half.2.refs_0_), custom_call_target="tpu_custom_call", output_to_operand_aliasing={{}: (2, {})} | custom-call | flops 1000000 | bytes 6000000 | tf_op jit(solution)/shard_map/write_half/pallas_call | solution.py:448
  (71 shorter events, 10.0 us)
Async XLA Ops:
  7.0 6.0 %copy-start = (bf16[1,256,4096]{2,1,0:T(8,128)(2,1)S(1)}, bf16[1,256,4096]{2,1,0:T(8,128)(2,1)}, u32[]{:S(2)}) copy-start(bf16[1,256,4096]{2,1,0:T(8,128)(2,1)} %param.15) | copy-start | bytes 6291460
  7.0 23.8 %all-to-all-start = ((bf16[8,320,256]{2,1,0:T(8,128)(2,1)}), bf16[8,320,256]{2,1,0:T(8,128)(2,1)S(1)}, u32[]{:S(2)}, u32[]{:S(2)}) async-start(bf16[8,320,256]{2,1,0:T(8,128)(2,1)} %pack.1), calls=%async_computation | async-start | bytes 2621440 | tf_op jit(solution)/shard_map/all_to_all | solution.py:502
  14.2 30.7 %collective-permute-start.2 = (bf16[256,1024]{1,0:T(8,128)(2,1)}, bf16[256,1024]{1,0:T(8,128)(2,1)S(1)}, u32[]{:S(2)}, u32[]{:S(2)}) collective-permute-start(bf16[256,1024]{1,0:T(8,128)(2,1)} %get-tuple-element.46), channel_id=1, source_target_pairs={{0,40},{8,32},{32,8},{40,0},{1,41},{9,33},{33,9},{41,1},{2,42},{10... | collective-permute-start | bytes 1572872 | tf_op jit(solution)/shard_map/ppermute | solution.py:514
  15.0 29.9 %collective-permute-start = (bf16[256,1024]{1,0:T(8,128)(2,1)}, bf16[256,1024]{1,0:T(8,128)(2,1)S(1)}, u32[]{:S(2)}, u32[]{:S(2)}) collective-permute-start(bf16[256,1024]{1,0:T(8,128)(2,1)} %get-tuple-element.47), channel_id=1, source_target_pairs={{0,32},{32,0},{1,33},{33,1},{2,34},{34,2},{3,35},{35,3},{4,36},{36... | collective-permute-start | bytes 1572872 | tf_op jit(solution)/shard_map/ppermute | solution.py:510
  16.2 28.8 %collective-permute-start.1 = (bf16[256,1024]{1,0:T(8,128)(2,1)}, bf16[256,1024]{1,0:T(8,128)(2,1)S(1)}, u32[]{:S(2)}, u32[]{:S(2)}) collective-permute-start(bf16[256,1024]{1,0:T(8,128)(2,1)} %get-tuple-element.48), channel_id=1, source_target_pairs={{0,8},{8,0},{1,9},{9,1},{2,10},{10,2},{3,11},{11,3},{4,12},{12,4},... | collective-permute-start | bytes 1572872 | tf_op jit(solution)/shard_map/ppermute | solution.py:506
  44.9 5.7 %copy-start.12 = (bf16[8,8,16,128]{3,2,1,0:T(8,128)(2,1)S(1)}, bf16[8,8,16,128]{3,2,1,0:T(8,128)(2,1)}, u32[]{:S(2)}) copy-start(bf16[8,8,16,128]{3,2,1,0:T(8,128)(2,1)} %get-tuple-element.25) | copy-start | bytes 786436
  44.9 30.6 %copy-start.6 = (bf16[256,1024]{1,0:T(8,128)(2,1)}, bf16[256,1024]{1,0:T(8,128)(2,1)S(1)}, u32[]{:S(2)}) copy-start(bf16[256,1024]{1,0:T(8,128)(2,1)S(1)} %collective-permute-done.2.g11) | copy-start | bytes 1572868
  44.9 30.6 %copy-start.7 = (bf16[256,1024]{1,0:T(8,128)(2,1)}, bf16[256,1024]{1,0:T(8,128)(2,1)S(1)}, u32[]{:S(2)}) copy-start(bf16[256,1024]{1,0:T(8,128)(2,1)S(1)} %collective-permute-done.g01) | copy-start | bytes 1572868
  44.9 30.6 %copy-start.8 = (bf16[256,1024]{1,0:T(8,128)(2,1)}, bf16[256,1024]{1,0:T(8,128)(2,1)S(1)}, u32[]{:S(2)}) copy-start(bf16[256,1024]{1,0:T(8,128)(2,1)S(1)} %collective-permute-done.1.g10) | copy-start | bytes 1572868
  45.0 19.1 %all-to-all-start.1 = ((bf16[8,256,256]{2,1,0:T(8,128)(2,1)}), bf16[8,256,256]{2,1,0:T(8,128)(2,1)S(1)}, u32[]{:S(2)}, u32[]{:S(2)}) async-start(bf16[8,256,256]{2,1,0:T(8,128)(2,1)} %get-tuple-element.24), calls=%async_computation.1 | async-start | bytes 2097152 | tf_op jit(solution)/shard_map/all_to_all | solution.py:502
  51.3 5.0 %collective-permute-start.3 = (bf16[8,4,16,128]{3,2,1,0:T(8,128)(2,1)S(1)}, bf16[8,4,16,128]{3,2,1,0:T(8,128)(2,1)S(1)}, u32[]{:S(2)}, u32[]{:S(2)}) collective-permute-start(bf16[8,4,16,128]{3,2,1,0:T(8,128)(2,1)S(1)} %bitcast.33), channel_id=1, source_target_pairs={{0,32},{32,0},{1,33},{33,1},{2,34},{34,2},{3,35},{35,3},{4,36},{36... | collective-permute-start | bytes 393224 | tf_op jit(solution)/shard_map/ppermute | solution.py:510
  56.3 19.3 %copy-start.13 = (bf16[8,4,16,128]{3,2,1,0:T(8,128)(2,1)}, bf16[8,4,16,128]{3,2,1,0:T(8,128)(2,1)S(1)}, u32[]{:S(2)}) copy-start(bf16[8,4,16,128]{3,2,1,0:T(8,128)(2,1)S(1)} %collective-permute-done.3.lags_z) | copy-start | bytes 393220
  67.0 7.0 %collective-permute-start.4 = (bf16[256,512]{1,0:T(8,128)(2,1)}, bf16[256,512]{1,0:T(8,128)(2,1)S(1)}, u32[]{:S(2)}, u32[]{:S(2)}) collective-permute-start(bf16[256,512]{1,0:T(8,128)(2,1)} %unpack_mixed.1.m00), channel_id=1, source_target_pairs={{0,32},{32,0},{1,33},{33,1},{2,34},{34,2},{3,35},{35,3},{4,36},{36... | collective-permute-start | bytes 786440 | tf_op jit(solution)/shard_map/ppermute | solution.py:510
  68.9 5.1 %collective-permute-start.5 = (bf16[256,512]{1,0:T(8,128)(2,1)}, bf16[256,512]{1,0:T(8,128)(2,1)S(1)}, u32[]{:S(2)}, u32[]{:S(2)}) collective-permute-start(bf16[256,512]{1,0:T(8,128)(2,1)} %unpack_mixed.1.m00), channel_id=1, source_target_pairs={{0,8},{8,0},{1,9},{9,1},{2,10},{10,2},{3,11},{11,3},{4,12},{12,4},... | collective-permute-start | bytes 786440 | tf_op jit(solution)/shard_map/ppermute | solution.py:506
  74.0 1.5 collective-permute-start.6
  80.4 12.5 %copy-start.5 = (bf16[256,512]{1,0:T(8,128)(2,1)S(1)}, bf16[256,512]{1,0:T(8,128)(2,1)}, u32[]{:S(2)}) copy-start(bf16[256,512]{1,0:T(8,128)(2,1)} %unpack_mixed.1.m00) | copy-start | bytes 786436
  80.4 29.9 %all-to-all-start.2 = ((bf16[32,16,1152]{2,1,0:T(8,128)(2,1)}), bf16[32,16,1152]{2,1,0:T(8,128)(2,1)S(1)}, u32[]{:S(2)}, u32[]{:S(2)}) async-start(bf16[32,16,1152]{2,1,0:T(8,128)(2,1)} %partial.1), calls=%async_computation.2 | async-start | bytes 2359296 | tf_op jit(solution)/shard_map/all_to_all | solution.py:502
  114.4 5.7 %copy-start.15 = (f32[16,1024]{1,0:T(8,128)S(1)}, f32[16,1024]{1,0:T(8,128)}, u32[]{:S(2)}) copy-start(f32[16,1024]{1,0:T(8,128)} %get-tuple-element.39) | copy-start | bytes 196612
  114.4 43.3 %all-to-all-start.3 = ((bf16[64,16,1024]{2,1,0:T(8,128)(2,1)}), bf16[64,16,1024]{2,1,0:T(8,128)(2,1)S(1)}, u32[]{:S(2)}, u32[]{:S(2)}) async-start(bf16[64,16,1024]{2,1,0:T(8,128)(2,1)} %get-tuple-element.38), calls=%async_computation.3 | async-start | bytes 4194304 | tf_op jit(solution)/shard_map/all_to_all | solution.py:502
  120.1 1.3 collective-permute-start.7
  121.5 32.8 %copy-start.14 = (bf16[16,1024]{1,0:T(8,128)(2,1)}, bf16[16,1024]{1,0:T(8,128)(2,1)S(1)}, u32[]{:S(2)}) copy-start(bf16[16,1024]{1,0:T(8,128)(2,1)S(1)} %add_convert_fusion.refs_0_) | copy-start | bytes 98308
  121.5 24.0 %collective-permute-start.8 = (bf16[16,1024]{1,0:T(8,128)(2,1)S(1)}, bf16[16,1024]{1,0:T(8,128)(2,1)S(1)}, u32[]{:S(2)}, u32[]{:S(2)}) collective-permute-start(bf16[16,1024]{1,0:T(8,128)(2,1)S(1)} %add_convert_fusion.refs_0_), channel_id=1, source_target_pairs={{0,16},{16,0},{1,17},{17,1},{2,18},{18,2},{3,19},{19,3},{4,20},{20... | collective-permute-start | bytes 98312 | tf_op jit(solution)/shard_map/ppermute | solution.py:518
  124.6 24.6 %collective-permute-start.13 = (bf16[16,1024]{1,0:T(8,128)(2,1)S(1)}, bf16[16,1024]{1,0:T(8,128)(2,1)S(1)}, u32[]{:S(2)}, u32[]{:S(2)}) collective-permute-start(bf16[16,1024]{1,0:T(8,128)(2,1)S(1)} %add_convert_fusion.refs_0_), channel_id=1, source_target_pairs={{0,96},{32,0},{64,32},{96,64},{1,97},{33,1},{65,33},{97,65},{2,98}... | collective-permute-start | bytes 98312 | tf_op jit(solution)/shard_map/ppermute | solution.py:522
  127.6 23.0 %collective-permute-start.11 = (bf16[16,1024]{1,0:T(8,128)(2,1)S(1)}, bf16[16,1024]{1,0:T(8,128)(2,1)S(1)}, u32[]{:S(2)}, u32[]{:S(2)}) collective-permute-start(bf16[16,1024]{1,0:T(8,128)(2,1)S(1)} %add_convert_fusion.refs_0_), channel_id=1, source_target_pairs={{0,64},{32,96},{64,0},{96,32},{1,65},{33,97},{65,1},{97,33},{2,66}... | collective-permute-start | bytes 98312 | tf_op jit(solution)/shard_map/ppermute | solution.py:522
  128.2 22.4 %collective-permute-start.9 = (bf16[16,1024]{1,0:T(8,128)(2,1)S(1)}, bf16[16,1024]{1,0:T(8,128)(2,1)S(1)}, u32[]{:S(2)}, u32[]{:S(2)}) collective-permute-start(bf16[16,1024]{1,0:T(8,128)(2,1)S(1)} %add_convert_fusion.refs_0_), channel_id=1, source_target_pairs={{0,32},{32,64},{64,96},{96,0},{1,33},{33,65},{65,97},{97,1},{2,34}... | collective-permute-start | bytes 98312 | tf_op jit(solution)/shard_map/ppermute | solution.py:522
  145.5 8.8 %copy-start.16 = (bf16[16,1024]{1,0:T(8,128)(2,1)}, bf16[16,1024]{1,0:T(8,128)(2,1)S(1)}, u32[]{:S(2)}) copy-start(bf16[16,1024]{1,0:T(8,128)(2,1)S(1)} %collective-permute-done.8.refs_1_) | copy-start | bytes 98308
  145.5 5.1 %collective-permute-start.14 = (bf16[16,1024]{1,0:T(8,128)(2,1)S(1)}, bf16[16,1024]{1,0:T(8,128)(2,1)S(1)}, u32[]{:S(2)}, u32[]{:S(2)}) collective-permute-start(bf16[16,1024]{1,0:T(8,128)(2,1)S(1)} %collective-permute-done.8.refs_1_), channel_id=1, source_target_pairs={{0,96},{32,0},{64,32},{96,64},{1,97},{33,1},{65,33},{97,65},{2,98}... | collective-permute-start | bytes 98312 | tf_op jit(solution)/shard_map/ppermute | solution.py:522
  148.6 5.4 %collective-permute-start.12 = (bf16[16,1024]{1,0:T(8,128)(2,1)S(1)}, bf16[16,1024]{1,0:T(8,128)(2,1)S(1)}, u32[]{:S(2)}, u32[]{:S(2)}) collective-permute-start(bf16[16,1024]{1,0:T(8,128)(2,1)S(1)} %collective-permute-done.8.refs_1_), channel_id=1, source_target_pairs={{0,64},{32,96},{64,0},{96,32},{1,65},{33,97},{65,1},{97,33},{2,66}... | collective-permute-start | bytes 98312 | tf_op jit(solution)/shard_map/ppermute | solution.py:522
  149.2 5.1 %copy-start.17 = (bf16[16,1024]{1,0:T(8,128)(2,1)}, bf16[16,1024]{1,0:T(8,128)(2,1)S(1)}, u32[]{:S(2)}) copy-start(bf16[16,1024]{1,0:T(8,128)(2,1)S(1)} %collective-permute-done.13.refs_6_) | copy-start | bytes 98308
  149.2 5.1 %collective-permute-start.10 = (bf16[16,1024]{1,0:T(8,128)(2,1)S(1)}, bf16[16,1024]{1,0:T(8,128)(2,1)S(1)}, u32[]{:S(2)}, u32[]{:S(2)}) collective-permute-start(bf16[16,1024]{1,0:T(8,128)(2,1)S(1)} %collective-permute-done.8.refs_1_), channel_id=1, source_target_pairs={{0,32},{32,64},{64,96},{96,0},{1,33},{33,65},{65,97},{97,1},{2,34}... | collective-permute-start | bytes 98312 | tf_op jit(solution)/shard_map/ppermute | solution.py:522
  150.6 3.7 %copy-start.19 = (bf16[16,1024]{1,0:T(8,128)(2,1)}, bf16[16,1024]{1,0:T(8,128)(2,1)S(1)}, u32[]{:S(2)}) copy-start(bf16[16,1024]{1,0:T(8,128)(2,1)S(1)} %collective-permute-done.9.refs_2_) | copy-start | bytes 98308
  157.7 5.0 %collective-permute-start.15 = (bf16[64,16,1024]{2,1,0:T(8,128)(2,1)S(1)}, bf16[64,16,1024]{2,1,0:T(8,128)(2,1)}, u32[]{:S(2)}, u32[]{:S(2)}) collective-permute-start(bf16[64,16,1024]{2,1,0:T(8,128)(2,1)S(1)} %all-to-all-done.3.mine), channel_id=1, source_target_pairs={{0,8},{8,0},{1,9},{9,1},{2,10},{10,2},{3,11},{11,3},{4,12},{12,4},... | collective-permute-start | bytes 6291464 | tf_op jit(solution)/shard_map/ppermute | solution.py:506
  (12 other events, 20.2 us)

commit v6 on v5

--- a/solution.py
+++ b/solution.py
@@ -103,16 +103,18 @@
     )(streams, out_grad, weight, filt)
 
 
-def conv_kernel(
-    place, got, short, skip, ahead_h, ahead_l, back_h, back_l,
-    sent, lags,
-    sa_pad, sv_pad, sa, sv, prod, spec, fspec, res, lres, time, u_pad, x_pad,
-):
-    low = low_lanes(BLOCK)
+def split(x):
+    high = x.astype(BF)
+    return high, (x - high.astype(F32)).astype(BF)
+
+
+def apply(table_h, table_l, high, rest):
+    return mm(table_h[...], high) + mm(table_h[...], rest) + mm(table_l[...], high)
+
+
+def weights(place, short, skip):
     low1 = low_lanes(1)
-    sigma = jnp.where(low, 1.0, -1.0)
     odd = place[0] % 2 == 1
-
     taps = short[...]
     taps = jnp.where(odd, turned(taps), taps)
     taps_up = turned(taps)
@@ -120,27 +122,21 @@
     gain = jnp.where(odd, turned(gain), gain)
     gain = jnp.where(low1, gain, turned(gain))
 
-    def tap(i, j):
-        return taps[3 * i + j : 3 * i + j + 1]
-
-    def tap_up(i, j):
-        return taps_up[3 * i + j : 3 * i + j + 1]
-
-    def unit(j):
-        return jnp.full((1, 128), 1.0 if j == 0 else 0.0, F32)
-
-    w_a = [jnp.where(low1, tap(0, j), tap_up(1, j)) for j in range(3)]
-    w_v = [jnp.where(low1, tap(2, j), unit(j)) for j in range(3)]
-    w_u = [jnp.where(low1, tap(1, j), tap_up(0, j)) for j in range(3)]
-    w_x = [jnp.where(low1, unit(j), tap_up(2, j)) for j in range(3)]
-
-    def split(x):
-        high = x.astype(BF)
-        return high, (x - high.astype(F32)).astype(BF)
-
-    def apply(table_h, table_l, high, rest):
-        return mm(table_h[...], high) + mm(table_h[...], rest) + mm(table_l[...], high)
-
+    def pair(first, second):
+        def row(table, i, j):
+            if i is None:
+                return jnp.full((1, 128), 1.0 if j == 0 else 0.0, F32)
+            return table[3 * i + j : 3 * i + j + 1]
+
+        return [
+            jnp.where(low1, row(taps, first, j), row(taps_up, second, j)) for j in range(3)
+        ]
+
+    return pair, gain
+
+
+def shorten(got, pair, sa_pad, sv_pad, use):
+    w_a, w_v = pair(0, 1), pair(2, None)
     sa_pad[0:8] = jnp.zeros((8, 128), F32)
     sv_pad[0:8] = jnp.zeros((8, 128), F32)
 
@@ -151,38 +147,16 @@
         return carry
 
     lax.fori_loop(0, 8, load, 0)
-
-    low64 = low_lanes(64)
-
-    def filters(n, carry):
-        def pair(b):
-            parts = []
-            for t in range(2):
-                x = got[b, BLOCK:, 128 * t : 128 * t + 128].astype(F32)
-                y = got[b + 1, BLOCK:, 128 * t : 128 * t + 128].astype(F32)
-                parts.append(jnp.where(low64, x, turned(y)))
-                parts.append(jnp.where(low64, turned(x), y))
-            return jnp.concatenate(parts, axis=0).astype(BF)
-
-        f = jnp.concatenate([pair(4 * n), pair(4 * n + 2)], axis=1)
-        out = mm(ahead_h[...], f) + mm(ahead_l[...], f)
-        low512 = low_lanes(512)
-        for t in range(2):
-            x = out[:, 128 * t : 128 * t + 128]
-            y = turned(x)
-            fspec[4 * n + 2 * t] = jnp.where(low512, x, y)
-            fspec[4 * n + 2 * t + 1] = jnp.where(low512, y, x)
-        return carry
-
-    lax.fori_loop(0, 2, filters, 0)
-
     for b in range(8):
         start = 8 + BLOCK * b
         a = sum(w_a[j] * sa_pad[start - j : start - j + BLOCK] for j in range(3))
         v = sum(w_v[j] * sv_pad[start - j : start - j + BLOCK] for j in range(3))
-        sa[b] = a
-        sv[b] = v
-        prod[b] = turned(a) * v
+        use(b, a, v)
+
+
+def spectra(prod, ahead_h, ahead_l, spec):
+    low = low_lanes(BLOCK)
+    sigma = jnp.where(low, 1.0, -1.0)
 
     def transform(n, carry):
         x = jnp.concatenate(
@@ -196,9 +170,11 @@
 
     lax.fori_loop(0, 4, transform, 0)
 
+
+def over_bins(spec, use):
     for sign, base in ((1.0, 0), (-1.0, 128)):
 
-        def multiply(n, carry, sign=sign, base=base):
+        def step(n, carry, sign=sign, base=base):
             re = pl.ds(pl.multiple_of(base + 8 * n, 8), 8)
             im = pl.ds(pl.multiple_of(BLOCK + base + 8 * n, 8), 8)
             own = [(spec[j, re], spec[j, im]) for j in range(8)]
@@ -207,42 +183,73 @@
                 both.append(
                     (own[j][0] - sign * own[j - 1][1], own[j][1] + sign * own[j - 1][0])
                 )
-            filt = [(fspec[m, re], fspec[m, im]) for m in range(8)]
-
-            def summed(pairs):
-                first = True
-                for (ar, ai), (br, bi) in pairs:
-                    pr = ar * br - ai * bi
-                    pi = ar * bi + ai * br
-                    tr, ti = (pr, pi) if first else (tr + pr, ti + pi)
-                    first = False
-                return tr, ti
-
-            for i in range(8):
-                tr, ti = summed([(filt[m], both[i - m]) for m in range(i + 1)])
-                res[i, re] = tr
-                res[i, im] = ti
-            zero = jnp.zeros((8, 128), F32)
-            low8 = low_lanes(8)
-            grads, shifted = [], []
-            for i in range(8):
-                grads.append(
-                    tuple(jnp.where(low8, turned(own[7 - i][k]), own[7 - i][k]) for k in range(2))
-                )
-                before = both[i - 1] if i else (zero, zero)
-                shifted.append(
-                    tuple(jnp.where(low8, before[k], turned(both[i][k])) for k in range(2))
-                )
-            for a in range(4):
-                tr, ti = summed([(grads[i], shifted[i - 2 * a]) for i in range(2 * a, 8)])
-                lres[a, re] = tr
-                lres[a, im] = ti
+            use(re, im, own, both)
             return carry
 
-        lax.fori_loop(0, 16, multiply, 0)
-
-    def flipped(x, sign):
-        return jnp.concatenate([x[0:BLOCK], x[BLOCK:] * sign], axis=0)
+        lax.fori_loop(0, 16, step, 0)
+
+
+def summed(pairs):
+    first = True
+    for (ar, ai), (br, bi) in pairs:
+        pr = ar * br - ai * bi
+        pi = ar * bi + ai * br
+        tr, ti = (pr, pi) if first else (tr + pr, ti + pi)
+        first = False
+    return tr, ti
+
+
+def flipped(x, sign):
+    return jnp.concatenate([x[0:BLOCK], x[BLOCK:] * sign], axis=0)
+
+
+def conv_kernel(
+    place, got, short, skip, ahead_h, ahead_l, back_h, back_l,
+    sent, whole,
+    sa_pad, sv_pad, sa, prod, spec, fspec, res, time,
+):
+    low = low_lanes(BLOCK)
+    low64 = low_lanes(64)
+    sigma = jnp.where(low, 1.0, -1.0)
+    pair, gain = weights(place, short, skip)
+
+    def filters(n, carry):
+        def blocks(b):
+            parts = []
+            for t in range(2):
+                x = got[b, BLOCK:, 128 * t : 128 * t + 128].astype(F32)
+                y = got[b + 1, BLOCK:, 128 * t : 128 * t + 128].astype(F32)
+                parts.append(jnp.where(low64, x, turned(y)))
+                parts.append(jnp.where(low64, turned(x), y))
+            return jnp.concatenate(parts, axis=0).astype(BF)
+
+        f = jnp.concatenate([blocks(4 * n), blocks(4 * n + 2)], axis=1)
+        out = mm(ahead_h[...], f) + mm(ahead_l[...], f)
+        low512 = low_lanes(512)
+        for t in range(2):
+            x = out[:, 128 * t : 128 * t + 128]
+            y = turned(x)
+            fspec[4 * n + 2 * t] = jnp.where(low512, x, y)
+            fspec[4 * n + 2 * t + 1] = jnp.where(low512, y, x)
+        return carry
+
+    lax.fori_loop(0, 2, filters, 0)
+
+    def keep(b, a, v):
+        sa[b] = a
+        prod[b] = turned(a) * v
+
+    shorten(got, pair, sa_pad, sv_pad, keep)
+    spectra(prod, ahead_h, ahead_l, spec)
+
+    def multiply(re, im, own, both):
+        filt = [(fspec[m, re], fspec[m, im]) for m in range(8)]
+        for i in range(8):
+            tr, ti = summed([(filt[m], both[i - m]) for m in range(i + 1)])
+            res[i, re] = tr
+            res[i, im] = ti
+
+    over_bins(spec, multiply)
 
     def invert(n, carry):
         x = jnp.concatenate([flipped(res[b], sigma) for b in (2 * n, 2 * n + 1)], axis=1)
@@ -253,7 +260,52 @@
 
     lax.fori_loop(0, 4, invert, 0)
 
-    def invert_lags(n, carry):
+    def gate(b, carry):
+        t = jnp.where(low, time[b], time[7 - b]) + gain * prod[b]
+        whole[b] = t
+        y = t * sa[b]
+        for n in range(2):
+            first, second = y[128 * n : 128 * n + 64], y[128 * n + 64 : 128 * n + 128]
+            there = slice(128 * n, 128 * n + 128)
+            sent[b, :, there] = jnp.where(low64, first, turned(second)).astype(BF)
+        return carry
+
+    lax.fori_loop(0, 8, gate, 0)
+
+
+def lag_kernel(
+    place, got, short, skip, ahead_h, ahead_l, back_h, back_l,
+    lags,
+    sa_pad, sv_pad, prod, spec, lres,
+):
+    pair, _ = weights(place, short, skip)
+
+    def keep(b, a, v):
+        prod[b] = turned(a) * v
+
+    shorten(got, pair, sa_pad, sv_pad, keep)
+    spectra(prod, ahead_h, ahead_l, spec)
+    zero = jnp.zeros((8, 128), F32)
+    low8 = low_lanes(8)
+
+    def multiply(re, im, own, both):
+        grads, shifted = [], []
+        for i in range(8):
+            grads.append(
+                tuple(jnp.where(low8, turned(own[7 - i][k]), own[7 - i][k]) for k in range(2))
+            )
+            before = both[i - 1] if i else (zero, zero)
+            shifted.append(
+                tuple(jnp.where(low8, before[k], turned(both[i][k])) for k in range(2))
+            )
+        for a in range(4):
+            tr, ti = summed([(grads[i], shifted[i - 2 * a]) for i in range(2 * a, 8)])
+            lres[a, re] = tr
+            lres[a, im] = ti
+
+    over_bins(spec, multiply)
+
+    def invert(n, carry):
         x = jnp.concatenate([flipped(lres[a], -1.0) for a in (2 * n, 2 * n + 1)], axis=1)
         out = apply(back_h, back_l, *split(x))
         low16 = low_lanes(16)
@@ -266,31 +318,37 @@
                 lags[m + 1, k] = jnp.where(low16, x, turned(y)).astype(BF)
         return carry
 
-    lax.fori_loop(0, 2, invert_lags, 0)
-
-    def gate(b, carry):
-        t = jnp.where(low, time[b], time[7 - b]) + gain * prod[b]
-        rows = pl.ds(pl.multiple_of(BLOCK * b, 8), BLOCK)
-        u_pad[rows] = turned(t) * sv[b]
-        x_pad[rows] = t * sa[b]
-        return carry
-
-    lax.fori_loop(0, 8, gate, 0)
+    lax.fori_loop(0, 2, invert, 0)
+
+
+def stream_kernel(place, got, short, skip, whole, *refs):
+    outs, (sa_pad, sv_pad, u_pad, x_pad, wide) = refs[:8], refs[8:]
+    pair, _ = weights(place, short, skip)
+
+    def keep(b, a, v):
+        t = whole[b]
+        u_pad[BLOCK * b : BLOCK * b + BLOCK] = turned(t) * v
+        x_pad[BLOCK * b : BLOCK * b + BLOCK] = t * a
+
+    shorten(got, pair, sa_pad, sv_pad, keep)
     u_pad[8 * BLOCK :] = jnp.zeros((8, 128), F32)
     x_pad[8 * BLOCK :] = jnp.zeros((8, 128), F32)
+    w_u, w_x = pair(1, 0), pair(None, 2)
+    low128 = low_lanes(128)
     for b in range(8):
         start = BLOCK * b
         y = sum(w_u[j] * u_pad[start + j : start + j + BLOCK] for j in range(3))
-        sent[b, 0:BLOCK, 0:128] = y.astype(BF)
+        wide[b, 0:BLOCK] = y.astype(BF)
         y = sum(w_x[j] * x_pad[start + j : start + j + BLOCK] for j in range(3))
-        sent[b, 0:BLOCK, 128:256] = y.astype(BF)
-
-
-def conv(place, got, short, skip):
-    ahead_h, ahead_l, back_h, back_l = (jnp.asarray(t) for t in tables())
+        wide[b, BLOCK:] = jnp.where(low128, turned(y[:128]), y[128:]).astype(BF)
+    for n in range(8):
+        outs[n][...] = wide[place[0] ^ n]
+
+
+def on_channels(kernel, name, inputs, in_shapes, outputs, scratch, cost):
     full = lambda *shape: pl.BlockSpec(shape, lambda n, p: (0,) * len(shape))
     return pl.pallas_call(
-        conv_kernel,
+        kernel,
         grid_spec=pltpu.PrefetchScalarGridSpec(
             num_scalar_prefetch=1,
             grid=(1,),
@@ -298,74 +356,104 @@
                 full(8, SENT_ROWS, 256),
                 pl.BlockSpec((9, 128), lambda n, p: (0, p[0] // 2)),
                 pl.BlockSpec((1, 128), lambda n, p: (0, p[0] // 2)),
-                full(512, BLOCK),
-                full(512, BLOCK),
-                full(BLOCK, 512),
-                full(BLOCK, 512),
-            ],
-            out_specs=[full(8, BLOCK, 256), full(8, 8, 16, 128)],
+            ]
+            + [full(*shape) for shape in in_shapes],
+            out_specs=[full(*shape) for shape, _ in outputs],
             scratch_shapes=[
-                pltpu.VMEM((8 + 8 * BLOCK, 128), F32),
-                pltpu.VMEM((8 + 8 * BLOCK, 128), F32),
-                pltpu.VMEM((8, BLOCK, 128), F32),
-                pltpu.VMEM((8, BLOCK, 128), F32),
-                pltpu.VMEM((8, BLOCK, 128), F32),
-                pltpu.VMEM((8, 512, 128), F32),
-                pltpu.VMEM((8, 512, 128), F32),
-                pltpu.VMEM((8, 512, 128), F32),
-                pltpu.VMEM((4, 512, 128), F32),
-                pltpu.VMEM((8, BLOCK, 128), F32),
-                pltpu.VMEM((8 + 8 * BLOCK, 128), F32),
-                pltpu.VMEM((8 + 8 * BLOCK, 128), F32),
+                pltpu.VMEM(shape, dtype)
+                for shape, dtype in [((8 + 8 * BLOCK, 128), F32)] * 2 + scratch
             ],
         ),
-        out_shape=[
-            jax.ShapeDtypeStruct((8, BLOCK, 256), BF),
-            jax.ShapeDtypeStruct((8, 8, 16, 128), BF),
-        ],
-        name="conv",
-    )(place, got, short, skip, ahead_h, ahead_l, back_h, back_l)
-
-
-def spread(got, there, first, second, low):
+        out_shape=[jax.ShapeDtypeStruct(shape, dtype) for shape, dtype in outputs],
+        cost_estimate=cost,
+        name=name,
+    )(*inputs)
+
+
+TABLES = [(512, BLOCK), (512, BLOCK), (BLOCK, 512), (BLOCK, 512)]
+BLOCKS = ((8, BLOCK, 128), F32)
+BINS = ((8, 512, 128), F32)
+
+
+def spent(flops):
+    return pl.CostEstimate(flops=flops, bytes_accessed=3 * 10**6, transcendentals=0)
+
+
+def conv(place, got, short, skip):
+    inputs = (place, got, short, skip, *(jnp.asarray(t) for t in tables()))
+    outputs = [((8, 64, 256), BF), BLOCKS]
+    scratch = [BLOCKS, BLOCKS, BINS, BINS, BINS, BLOCKS]
+    return on_channels(conv_kernel, "conv", inputs, TABLES, outputs, scratch, None)
+
+
+def lag_sums(place, got, short, skip):
+    inputs = (place, got, short, skip, *(jnp.asarray(t) for t in tables()))
+    outputs = [((8, 8, 16, 128), BF)]
+    scratch = [BLOCKS, BINS, ((4, 512, 128), F32)]
+    cost = spent(2 * 10**9)
+    return on_channels(lag_kernel, "lag_sums", inputs, TABLES, outputs, scratch, cost)[0]
+
+
+def stream_grads(place, got, short, skip, whole):
+    outputs = [((384, 128), BF)] * 8
+    pad = ((8 * BLOCK + 8, 128), F32)
+    scratch = [pad, pad, ((8, 384, 128), BF)]
+    inputs = (place, got, short, skip, whole)
+    cost = spent(10**9)
+    return on_channels(
+        stream_kernel, "stream_grads", inputs, [BLOCKS[0]], outputs, scratch, cost
+    )
+
+
+def mixed_kernel(got, mixed):
+    low = low_lanes(64)
     for q in range(4):
         lanes = slice(128 * q, 128 * q + 128)
-        a = got[2 * q, 0:BLOCK, there].astype(F32)
-        b = got[2 * q + 1, 0:BLOCK, there].astype(F32)
-        if first is not None:
-            first[:, lanes] = jnp.where(low, a, turned(b)).astype(BF)
-        if second is not None:
-            second[:, lanes] = jnp.where(low, turned(a), b).astype(BF)
-
-
-def mixed_kernel(got, mixed):
-    spread(got, slice(0, 128), mixed, None, low_lanes(BLOCK))
+        for t in range(2):
+            there = slice(128 * t, 128 * t + 128)
+            a = got[2 * q, :, there].astype(F32)
+            b = got[2 * q + 1, :, there].astype(F32)
+            mixed[128 * t : 128 * t + 64, lanes] = jnp.where(low, a, turned(b)).astype(BF)
+            mixed[128 * t + 64 : 128 * t + 128, lanes] = jnp.where(low, turned(a), b).astype(BF)
 
 
 def unpack_mixed(got):
     return pl.pallas_call(
         mixed_kernel,
-        grid=(1,),
-        in_specs=[pl.BlockSpec((8, BLOCK, 128), lambda n: (0, 0, 1))],
-        out_specs=pl.BlockSpec((BLOCK, 512), lambda n: (0, 0)),
         out_shape=jax.ShapeDtypeStruct((BLOCK, 512), BF),
         name="unpack_mixed",
     )(got)
 
 
-def grads_kernel(got, grads):
-    low = low_lanes(BLOCK)
-    spread(got, slice(0, 128), grads.at[1], grads.at[0], low)
-    spread(got, slice(128, 256), None, grads.at[2], low)
-
-
-def unpack_grads(got):
+def grads_kernel(place, *refs):
+    parts, grads = refs[:8], refs[8]
+    low, low128 = low_lanes(BLOCK), low_lanes(128)
+    even = place[0] % 2 == 0
+    for n in range(4):
+        lanes = pl.ds(pl.multiple_of(128 * ((place[0] // 2) ^ n), 128), 128)
+        first, second = parts[2 * n][...].astype(F32), parts[2 * n + 1][...].astype(F32)
+        a, b = jnp.where(even, first, second), jnp.where(even, second, first)
+        grads[1, :, lanes] = jnp.where(low, a[:BLOCK], turned(b[:BLOCK])).astype(BF)
+        grads[0, :, lanes] = jnp.where(low, turned(a[:BLOCK]), b[:BLOCK]).astype(BF)
+        a, b = a[BLOCK:], b[BLOCK:]
+        grads[2, 0:128, lanes] = jnp.where(low128, a, turned(b)).astype(BF)
+        grads[2, 128:256, lanes] = jnp.where(low128, turned(a), b).astype(BF)
+
+
+def unpack_grads(place, parts):
+    full = lambda *shape: pl.BlockSpec(shape, lambda n, p: (0,) * len(shape))
     return pl.pallas_call(
         grads_kernel,
+        grid_spec=pltpu.PrefetchScalarGridSpec(
+            num_scalar_prefetch=1,
+            grid=(1,),
+            in_specs=[full(384, 128)] * 8,
+            out_specs=full(3, BLOCK, 512),
+        ),
         out_shape=jax.ShapeDtypeStruct((3, BLOCK, 512), BF),
         cost_estimate=pl.CostEstimate(flops=10**6, bytes_accessed=2 * 10**6, transcendentals=0),
         name="unpack_grads",
-    )(got)
+    )(place, *parts)
 
 
 def partial_kernel(place, m00, m01, m10, m11, g00, g01, g10, g11, lags, lags_z, packed):
@@ -539,34 +627,41 @@
         opposite(quarter(1 - core, 1 - side)),
     )
     got = exchange(pack(streams[:, 0], grad, out_weight, long_filter), SEQ)
-    sent, lags = conv(
-        seq[None], got, short_filter.reshape(9, 512), skip_gain.reshape(1, 512)
-    )
-    sent, grads = lax.optimization_barrier((sent, grads))
-    lags = lags.reshape(8, 2, 2, 2, 16, 128)
+    channels = (seq[None], got, short_filter.reshape(9, 512), skip_gain.reshape(1, 512))
+    sent, whole = conv(*channels)
+    sent, whole, got, grads = lax.optimization_barrier((sent, whole, got, grads))
+    channels = (channels[0], got) + channels[2:]
+    lags = lag_sums(*channels).reshape(8, 2, 2, 2, 16, 128)
 
     def of_side(z):
         return lax.dynamic_index_in_dim(lags, z, 2, False).reshape(8, 4, 16, 128)
 
     lags_own, lags_z = of_side(side), above(of_side(1 - side))
     back = exchange(sent, SEQ)
-    back, lags_own, lags_z = lax.optimization_barrier((back, lags_own, lags_z))
+    back, lags_own = lax.optimization_barrier((back, lags_own))
     m00 = unpack_mixed(back)
     m01, m10 = above(m00), across(m00)
     mixed = (m00, m01, m10, across(m01))
     part = partial((2 * core + side)[None], mixed, grad, grads, lags_own, lags_z)
-    part, m00, back = lax.optimization_barrier((part, m00, back))
+    part, m00, whole, got = lax.optimization_barrier((part, m00, whole, got))
     part = exchange(part, MOST)
+    channels = (channels[0], got) + channels[2:]
+    parts = stream_grads(*channels, whole)
+    parts = [parts[0]] + [
+        lax.ppermute(parts[n], SEQ, [(i, i ^ n) for i in range(8)]) for n in range(1, 8)
+    ]
+    part, parts, m00 = lax.optimization_barrier((part, parts, m00))
+    rows, lags = reduce(part, scale)
+    rows, lags, parts, m00 = lax.optimization_barrier((rows, lags, parts, m00))
+    mine = exchange(rows, CHIPS)
     layer_out = jnp.dot(m00, out_weight, preferred_element_type=F32).astype(BF)
-    grad_streams = unpack_grads(back)
-    part, layer_out, grad_streams = lax.optimization_barrier((part, layer_out, grad_streams))
-    rows, lags = reduce(part, scale)
-    rows, lags = lax.optimization_barrier((rows, lags))
-    mine = exchange(rows, CHIPS)
+    grad_streams = unpack_grads(seq[None], parts)
     lags = (lags + across(lags)).astype(BF)
     place = jnp.stack([lax.axis_index(("zh", "zl")), lax.axis_index("yh")]).astype(jnp.int32)
     grad_filter = write_filter(place, gathered(lags))
-    mine, grad_filter = lax.optimization_barrier((mine, grad_filter))
+    mine, grad_filter, layer_out, grad_streams = lax.optimization_barrier(
+        (mine, grad_filter, layer_out, grad_streams)
+    )
     theirs = across(mine)
     grad_weight = write_half(core[None], mine)
     grad_weight = write_half(1 - core[None], theirs, grad_weight)

time: 167 us -> 182 us (1.090)
  the two profiles are of different devices: /device:TPU:2 before, /device:TPU:1 now
where the time goes in v6:
time: 182 us; the launch traced here: 181 us
  starting transfers between devices  69.8 us (38%)
  Pallas kernels  49.8 us (27%)
  waiting for transfers between devices  46.7 us (26%)
  local copies, waits for them, and re-layouts  8.32 us (5%)
  matrix products  4.77 us (3%)
    all_to_all x4, starting transfers between devices, exchange(): return lax.all_to_all(x, axes, 0, 0, tiled=True)  29 us
    pallas_call x3, Pallas kernels, on_channels(): pl.pallas_call(kernel, grid_spec=pltpu.PrefetchScalarGridSpec(num_scalar_...  22.2 us
    ppermute x5, starting transfers between devices, across(): return lax.ppermute(x, 'c', [(0, 1), (1, 0)])  15.2 us
    all_to_all x4, waiting for transfers between devices, exchange(): return lax.all_to_all(x, axes, 0, 0, tiled=True)  14.5 us
    ppermute x7, waiting for transfers between devices, on_device(): lax.ppermute(parts[n], SEQ, [(i, i ^ n) for i in range(8)])  14.5 us
    ppermute x1, waiting for transfers between devices, gathered(): pair = (lags, lax.ppermute(lags, 'yh', [(0, 1), (1, 0)]))  9.74 us
    ppermute x7, starting transfers between devices, on_device(): lax.ppermute(parts[n], SEQ, [(i, i ^ n) for i in range(8)])  9.64 us
    ppermute x6, starting transfers between devices, gathered(): out += [lax.ppermute(part, ('zh', 'zl'), route) for part in pair]  7.51 us
  transfers between devices with their start and end apart: 27, of which 11 were waited for; matrix products, arithmetic and copies ran while one was open for 5% of the time, Pallas kernels for 17%

profile of v6, /device:TPU:1, one launch (start us, length us, event | category | flops | bytes accessed | tf_op | source)
XLA Modules:
  0.0 181.1 jit_solution(11320852634292219126)
XLA Ops:
  0.6 6.4 %pack.1 = bf16[8,320,256]{2,1,0:T(8,128)(2,1)} custom-call(bf16[3,256,512]{2,1,0:T(8,128)(2,1)} %bitcast.29, bf16[256,4096]{1,0:T(8,128)(2,1)} %bitcast.27, bf16[512,4096]{1,0:T(8,128)(2,1)} %weight.1, f32[256,512]{1,0:T(8,128)} %filt.1), custom_call_target="tpu_custom_call" | custom-call | tf_op jit(solution)/shard_map/pack/pallas_call | solution.py:90
  7.0 6.0 %all-to-all-start = ((bf16[8,320,256]{2,1,0:T(8,128)(2,1)}), bf16[8,320,256]{2,1,0:T(8,128)(2,1)S(1)}, u32[]{:S(2)}, u32[]{:S(2)}) async-start(bf16[8,320,256]{2,1,0:T(8,128)(2,1)} %pack.1), calls=%async_computation | async-start | bytes 2621440 | tf_op jit(solution)/shard_map/all_to_all | solution.py:590
  14.2 2.5 %collective-permute-start.2 = (bf16[256,1024]{1,0:T(8,128)(2,1)}, bf16[256,1024]{1,0:T(8,128)(2,1)S(1)}, u32[]{:S(2)}, u32[]{:S(2)}) collective-permute-start(bf16[256,1024]{1,0:T(8,128)(2,1)} %get-tuple-element.106), channel_id=1, source_target_pairs={{0,40},{8,32},{32,8},{40,0},{1,41},{9,33},{33,9},{41,1},{2,42},{10... | collective-permute-start | bytes 1572872 | tf_op jit(solution)/shard_map/ppermute | solution.py:602
  17.8 14.5 %all-to-all-done.got = bf16[8,320,256]{2,1,0:T(8,128)(2,1)S(1)} async-done(((bf16[8,320,256]{2,1,0:T(8,128)(2,1)}), bf16[8,320,256]{2,1,0:T(8,128)(2,1)S(1)}, u32[]{:S(2)}, u32[]{:S(2)}) %all-to-all-start) | async-done | bytes 1310752 | tf_op jit(solution)/shard_map/all_to_all | solution.py:590
  33.3 9.5 %conv.1 = (bf16[8,64,256]{2,1,0:T(8,128)(2,1)}, f32[8,256,128]{2,1,0:T(8,128)}) custom-call(s32[1]{0:T(128)} %bitcast.1.place, bf16[8,320,256]{2,1,0:T(8,128)(2,1)} %copy-done.2, f32[9,512]{1,0:T(8,128)} %reshape.28.short, f32[1,512]{1,0:T(1,128)} %bitcast.34, bf16[512,256]{1,0:T(8,128)(2,1)} %constant.54.clone.ahead_h, ...), custom_call_target="tpu_custom_call" | custom-call | tf_op jit(solution)/shard_map/conv/pallas_call | solution.py:350
  42.9 3.4 %all-to-all-start.1 = ((bf16[8,64,256]{2,1,0:T(8,128)(2,1)}), bf16[8,64,256]{2,1,0:T(8,128)(2,1)S(1)}, u32[]{:S(2)}, u32[]{:S(2)}) async-start(bf16[8,64,256]{2,1,0:T(8,128)(2,1)} %get-tuple-element.55), calls=%async_computation.1 | async-start | bytes 524288 | tf_op jit(solution)/shard_map/all_to_all | solution.py:590
  46.3 8.8 %lag_sums.1 = bf16[8,8,16,128]{3,2,1,0:T(8,128)(2,1)} custom-call(s32[1]{0:T(128)} %bitcast.1.place, bf16[8,320,256]{2,1,0:T(8,128)(2,1)} %copy-done.2, f32[9,512]{1,0:T(8,128)} %reshape.28.short, f32[1,512]{1,0:T(1,128)} %bitcast.35, bf16[512,256]{1,0:T(8,128)(2,1)} %constant.54.clone.ahead_h, bf16[512,256]{1,0:T(8,128)(2,1)} %constant.55.clone.ahead_l, ...), custom_call_target="tpu_custom_call" | custom-call | flops 2000000000 | bytes 3000000 | tf_op jit(solution)/shard_map/lag_sums/pallas_call | solution.py:350
  60.9 1.9 %collective-permute-start.4 = (bf16[256,512]{1,0:T(8,128)(2,1)}, bf16[256,512]{1,0:T(8,128)(2,1)S(1)}, u32[]{:S(2)}, u32[]{:S(2)}) collective-permute-start(bf16[256,512]{1,0:T(8,128)(2,1)} %unpack_mixed.1.m00), channel_id=1, source_target_pairs={{0,8},{8,0},{1,9},{9,1},{2,10},{10,2},{3,11},{11,3},{4,12},{12,4},... | collective-permute-start | bytes 786440 | tf_op jit(solution)/shard_map/ppermute | solution.py:594
  62.8 3.2 %collective-permute-done.3.m01 = bf16[256,512]{1,0:T(8,128)(2,1)S(1)} collective-permute-done((bf16[256,512]{1,0:T(8,128)(2,1)}, bf16[256,512]{1,0:T(8,128)(2,1)S(1)}, u32[]{:S(2)}, u32[]{:S(2)}) %collective-permute-start.3) | collective-permute-done | bytes 262176 | tf_op jit(solution)/shard_map/ppermute | solution.py:598
  66.0 2.4 %collective-permute-start.5 = (bf16[256,512]{1,0:T(8,128)(2,1)S(1)}, bf16[256,512]{1,0:T(8,128)(2,1)S(1)}, u32[]{:S(2)}, u32[]{:S(2)}) collective-permute-start(bf16[256,512]{1,0:T(8,128)(2,1)S(1)} %collective-permute-done.3.m01), channel_id=1, source_target_pairs={{0,8},{8,0},{1,9},{9,1},{2,10},{10,2},{3,11},{11,3},{4,12},{12,4},... | collective-permute-start | bytes 786440 | tf_op jit(solution)/shard_map/ppermute | solution.py:594
  69.9 3.7 %collective-permute-done.6.lags_z = bf16[8,4,16,128]{3,2,1,0:T(8,128)(2,1)S(1)} collective-permute-done((bf16[8,4,16,128]{3,2,1,0:T(8,128)(2,1)S(1)}, bf16[8,4,16,128]{3,2,1,0:T(8,128)(2,1)S(1)}, u32[]{:S(2)}, u32[]{:S(2)}) %collective-permute-start.6) | collective-permute-done | bytes 131104 | tf_op jit(solution)/shard_map/ppermute | solution.py:598
  74.4 4.2 %partial.1 = bf16[32,16,1152]{2,1,0:T(8,128)(2,1)} custom-call(s32[1]{0:T(128)} %bitcast.place, bf16[256,512]{1,0:T(8,128)(2,1)} %unpack_mixed.1.m00, bf16[256,512]{1,0:T(8,128)(2,1)} %copy-done.9, bf16[256,512]{1,0:T(8,128)(2,1)} %copy-done.10, bf16[256,512]{1,0:T(8,128)(2,1)} %copy-done.11, bf16[256,4096]{1,0:T(8,128)(2,1)} %bitcast.28, ...), custom_call_target="tpu_custom_call" | custom-call | tf_op jit(solution)/shard_map/partial/pallas_call | solution.py:476
  78.5 10.0 %all-to-all-start.2 = ((bf16[32,16,1152]{2,1,0:T(8,128)(2,1)}), bf16[32,16,1152]{2,1,0:T(8,128)(2,1)S(1)}, u32[]{:S(2)}, u32[]{:S(2)}) async-start(bf16[32,16,1152]{2,1,0:T(8,128)(2,1)} %partial.1), calls=%async_computation.2 | async-start | bytes 2359296 | tf_op jit(solution)/shard_map/all_to_all | solution.py:590
  88.6 3.8 %stream_grads.1 = (bf16[384,128]{1,0:T(8,128)(2,1)}, bf16[384,128]{1,0:T(8,128)(2,1)}, bf16[384,128]{1,0:T(8,128)(2,1)}, bf16[384,128]{1,0:T(8,128)(2,1)}, bf16[...) custom-call(s32[1]{0:T(128)} %bitcast.1.place, ...), custom_call_target="tpu_custom_call" | custom-call | flops 1000000000 | bytes 3000000 | tf_op jit(solution)/shard_map/stream_grads/pallas_call | solution.py:350
  95.0 2.7 %collective-permute-start.10 = (bf16[384,128]{1,0:T(8,128)(2,1)}, bf16[384,128]{1,0:T(8,128)(2,1)S(1)}, u32[]{:S(2)}, u32[]{:S(2)}) collective-permute-start(bf16[384,128]{1,0:T(8,128)(2,1)} %get-tuple-element.70), channel_id=1, source_target_pairs={{0,4},{1,5},{2,6},{3,7},{4,0},{5,1},{6,2},{7,3},{8,12},{9,13},{10,... | collective-permute-start | bytes 294920 | tf_op jit(solution)/shard_map/ppermute | solution.py:651
  99.0 4.9 %collective-permute-done.7.refs_1_ = bf16[384,128]{1,0:T(8,128)(2,1)S(1)} collective-permute-done((bf16[384,128]{1,0:T(8,128)(2,1)}, bf16[384,128]{1,0:T(8,128)(2,1)S(1)}, u32[]{:S(2)}, u32[]{:S(2)}) %collective-permute-start.7) | collective-permute-done | bytes 98336 | tf_op jit(solution)/shard_map/ppermute | solution.py:651
  103.9 2.7 %collective-permute-start.12 = (bf16[384,128]{1,0:T(8,128)(2,1)}, bf16[384,128]{1,0:T(8,128)(2,1)S(1)}, u32[]{:S(2)}, u32[]{:S(2)}) collective-permute-start(bf16[384,128]{1,0:T(8,128)(2,1)} %get-tuple-element.72), channel_id=1, source_target_pairs={{0,6},{1,7},{2,4},{3,5},{4,2},{5,3},{6,0},{7,1},{8,14},{9,15},{10,... | collective-permute-start | bytes 294920 | tf_op jit(solution)/shard_map/ppermute | solution.py:651
  107.3 2.7 %collective-permute-done.10.refs_4_ = bf16[384,128]{1,0:T(8,128)(2,1)S(1)} collective-permute-done((bf16[384,128]{1,0:T(8,128)(2,1)}, bf16[384,128]{1,0:T(8,128)(2,1)S(1)}, u32[]{:S(2)}, u32[]{:S(2)}) %collective-permute-start.10) | collective-permute-done | bytes 98336 | tf_op jit(solution)/shard_map/ppermute | solution.py:651
  110.0 2.8 %collective-permute-done.11.refs_5_ = bf16[384,128]{1,0:T(8,128)(2,1)S(1)} collective-permute-done((bf16[384,128]{1,0:T(8,128)(2,1)}, bf16[384,128]{1,0:T(8,128)(2,1)S(1)}, u32[]{:S(2)}, u32[]{:S(2)}) %collective-permute-start.11) | collective-permute-done | bytes 98336 | tf_op jit(solution)/shard_map/ppermute | solution.py:651
  112.8 3.7 %collective-permute-done.13.refs_7_ = bf16[384,128]{1,0:T(8,128)(2,1)S(1)} collective-permute-done((bf16[384,128]{1,0:T(8,128)(2,1)}, bf16[384,128]{1,0:T(8,128)(2,1)S(1)}, u32[]{:S(2)}, u32[]{:S(2)}) %collective-permute-start.13) | collective-permute-done | bytes 98336 | tf_op jit(solution)/shard_map/ppermute | solution.py:651
  117.6 3.0 %reduce.1 = (bf16[64,16,1024]{2,1,0:T(8,128)(2,1)}, f32[16,1024]{1,0:T(8,128)}) custom-call(bf16[32,16,1152]{2,1,0:T(8,128)(2,1)} %copy-done.3), custom_call_target="tpu_custom_call" | custom-call | tf_op jit(solution)/shard_map/reduce/pallas_call | solution.py:507
  120.5 9.6 %all-to-all-start.3 = ((bf16[64,16,1024]{2,1,0:T(8,128)(2,1)}), bf16[64,16,1024]{2,1,0:T(8,128)(2,1)S(1)}, u32[]{:S(2)}, u32[]{:S(2)}) async-start(bf16[64,16,1024]{2,1,0:T(8,128)(2,1)} %get-tuple-element.87), calls=%async_computation.3 | async-start | bytes 4194304 | tf_op jit(solution)/shard_map/all_to_all | solution.py:590
  131.9 2.8 %collective-permute-start.20 = (bf16[16,1024]{1,0:T(8,128)(2,1)S(1)}, bf16[16,1024]{1,0:T(8,128)(2,1)S(1)}, u32[]{:S(2)}, u32[]{:S(2)}) collective-permute-start(bf16[16,1024]{1,0:T(8,128)(2,1)S(1)} %add_convert_fusion.refs_0_), channel_id=1, source_target_pairs={{0,96},{32,0},{64,32},{96,64},{1,97},{33,1},{65,33},{97,65},{2,98}... | collective-permute-start | bytes 98312 | tf_op jit(solution)/shard_map/ppermute | solution.py:610
  134.7 2.7 %collective-permute-start.15 = (bf16[16,1024]{1,0:T(8,128)(2,1)S(1)}, bf16[16,1024]{1,0:T(8,128)(2,1)S(1)}, u32[]{:S(2)}, u32[]{:S(2)}) collective-permute-start(bf16[16,1024]{1,0:T(8,128)(2,1)S(1)} %add_convert_fusion.refs_0_), channel_id=1, source_target_pairs={{0,16},{16,0},{1,17},{17,1},{2,18},{18,2},{3,19},{19,3},{4,20},{20... | collective-permute-start | bytes 98312 | tf_op jit(solution)/shard_map/ppermute | solution.py:606
  139.1 9.7 %collective-permute-done.15.refs_1_ = bf16[16,1024]{1,0:T(8,128)(2,1)S(1)} collective-permute-done((bf16[16,1024]{1,0:T(8,128)(2,1)S(1)}, bf16[16,1024]{1,0:T(8,128)(2,1)S(1)}, u32[]{:S(2)}, u32[]{:S(2)}) %collective-permute-start.15) | collective-permute-done | bytes 32800 | tf_op jit(solution)/shard_map/ppermute | solution.py:606
  148.9 2.7 %collective-permute-start.21 = (bf16[16,1024]{1,0:T(8,128)(2,1)S(1)}, bf16[16,1024]{1,0:T(8,128)(2,1)S(1)}, u32[]{:S(2)}, u32[]{:S(2)}) collective-permute-start(bf16[16,1024]{1,0:T(8,128)(2,1)S(1)} %collective-permute-done.15.refs_1_), channel_id=1, source_target_pairs={{0,96},{32,0},{64,32},{96,64},{1,97},{33,1},{65,33},{97,65},{2,98}... | collective-permute-start | bytes 98312 | tf_op jit(solution)/shard_map/ppermute | solution.py:610
  152.6 4.8 %convolution_convert_fusion = bf16[256,4096]{1,0:T(8,128)(2,1)} fusion(bf16[256,512]{1,0:T(8,128)(2,1)S(1)} %copy-done.4, bf16[512,4096]{1,0:T(8,128)(2,1)} %weight.1), kind=kOutput, calls=%fused_computation | convolution fusion | flops 1074790400 | bytes 6553600 | tf_op jit(solution)/shard_map/dot_general | solution.py:657
  157.4 2.5 %unpack_grads.1 = bf16[3,256,512]{2,1,0:T(8,128)(2,1)} custom-call(s32[1]{0:T(128)} %bitcast.1.place, bf16[384,128]{1,0:T(8,128)(2,1)} %get-tuple-element.90.refs_0_, bf16[384,128]{1,0:T(8,128)(2,1)} %copy-done.14, bf16[384,128]{1,0:T(8,128)(2,1)} %copy-done.15, bf16[384,128]{1,0:T(8,128)(2,1)} %copy-done.16, bf16[384,128]{1,0:T(8,128)(2,1)} %copy-done.17, ...), custom_call_target="tpu_custom_call" | custom-call | flops 1000000 | bytes 2000000 | tf_op jit(solution)/shard_map/unpack_grads/pallas_call | solution.py:445
  161.1 2.5 %write_filter.1 = f32[256,512]{1,0:T(8,128)} custom-call(s32[2]{0:T(128)} %pad_add_fusion.place, bf16[16,1024]{1,0:T(8,128)(2,1)} %copy-done.13, bf16[16,1024]{1,0:T(8,128)(2,1)} %copy-done.23, bf16[16,1024]{1,0:T(8,128)(2,1)} %copy-done.25, bf16[16,1024]{1,0:T(8,128)(2,1)} %copy-done.28, bf16[16,1024]{1,0:T(8,128)(2,1)} %copy-done.24, ...), custom_call_target="tpu_custom_call" | custom-call | flops 1000000 | bytes 2000000 | tf_op jit(solution)/shard_map/write_filter/pallas_call | solution.py:575
  163.6 9.7 %collective-permute-start.22 = (bf16[64,16,1024]{2,1,0:T(8,128)(2,1)S(1)}, bf16[64,16,1024]{2,1,0:T(8,128)(2,1)}, u32[]{:S(2)}, u32[]{:S(2)}) collective-permute-start(bf16[64,16,1024]{2,1,0:T(8,128)(2,1)S(1)} %all-to-all-done.3.mine), channel_id=1, source_target_pairs={{0,8},{8,0},{1,9},{9,1},{2,10},{10,2},{3,11},{11,3},{4,12},{12,4},... | collective-permute-start | bytes 6291464 | tf_op jit(solution)/shard_map/ppermute | solution.py:594
  173.3 3.7 %write_half.2.refs_0_ = f32[512,4096]{1,0:T(8,128)} custom-call(s32[1]{0:T(128)} %bitcast.16.place, bf16[64,16,1024]{2,1,0:T(8,128)(2,1)} %copy-done.1), custom_call_target="tpu_custom_call" | custom-call | flops 1000000 | bytes 6000000 | tf_op jit(solution)/shard_map/write_half/pallas_call | solution.py:536
  177.2 3.7 %write_half.3 = f32[512,4096]{1,0:T(8,128)} custom-call(s32[1]{0:T(128)S(6)} %sub.14.place, bf16[64,16,1024]{2,1,0:T(8,128)(2,1)} %collective-permute-done.22.mine, f32[512,4096]{1,0:T(8,128)} %write_half.2.refs_0_), custom_call_target="tpu_custom_call", output_to_operand_aliasing={{}: (2, {})} | custom-call | flops 1000000 | bytes 6000000 | tf_op jit(solution)/shard_map/write_half/pallas_call | solution.py:536
  (99 shorter events, 22.8 us)
Async XLA Ops:
  7.0 25.2 %all-to-all-start = ((bf16[8,320,256]{2,1,0:T(8,128)(2,1)}), bf16[8,320,256]{2,1,0:T(8,128)(2,1)S(1)}, u32[]{:S(2)}, u32[]{:S(2)}) async-start(bf16[8,320,256]{2,1,0:T(8,128)(2,1)} %pack.1), calls=%async_computation | async-start | bytes 2621440 | tf_op jit(solution)/shard_map/all_to_all | solution.py:590
  14.2 28.6 %collective-permute-start.2 = (bf16[256,1024]{1,0:T(8,128)(2,1)}, bf16[256,1024]{1,0:T(8,128)(2,1)S(1)}, u32[]{:S(2)}, u32[]{:S(2)}) collective-permute-start(bf16[256,1024]{1,0:T(8,128)(2,1)} %get-tuple-element.106), channel_id=1, source_target_pairs={{0,40},{8,32},{32,8},{40,0},{1,41},{9,33},{33,9},{41,1},{2,42},{10... | collective-permute-start | bytes 1572872 | tf_op jit(solution)/shard_map/ppermute | solution.py:602
  16.7 26.2 %collective-permute-start = (bf16[256,1024]{1,0:T(8,128)(2,1)}, bf16[256,1024]{1,0:T(8,128)(2,1)S(1)}, u32[]{:S(2)}, u32[]{:S(2)}) collective-permute-start(bf16[256,1024]{1,0:T(8,128)(2,1)} %get-tuple-element.107), channel_id=1, source_target_pairs={{0,32},{32,0},{1,33},{33,1},{2,34},{34,2},{3,35},{35,3},{4,36},{36... | collective-permute-start | bytes 1572872 | tf_op jit(solution)/shard_map/ppermute | solution.py:598
  16.7 26.2 %collective-permute-start.1 = (bf16[256,1024]{1,0:T(8,128)(2,1)}, bf16[256,1024]{1,0:T(8,128)(2,1)S(1)}, u32[]{:S(2)}, u32[]{:S(2)}) collective-permute-start(bf16[256,1024]{1,0:T(8,128)(2,1)} %get-tuple-element.108), channel_id=1, source_target_pairs={{0,8},{8,0},{1,9},{9,1},{2,10},{10,2},{3,11},{11,3},{4,12},{12,4},... | collective-permute-start | bytes 1572872 | tf_op jit(solution)/shard_map/ppermute | solution.py:594
  42.9 13.9 %all-to-all-start.1 = ((bf16[8,64,256]{2,1,0:T(8,128)(2,1)}), bf16[8,64,256]{2,1,0:T(8,128)(2,1)S(1)}, u32[]{:S(2)}, u32[]{:S(2)}) async-start(bf16[8,64,256]{2,1,0:T(8,128)(2,1)} %get-tuple-element.55), calls=%async_computation.1 | async-start | bytes 524288 | tf_op jit(solution)/shard_map/all_to_all | solution.py:590
  59.3 6.8 %collective-permute-start.3 = (bf16[256,512]{1,0:T(8,128)(2,1)}, bf16[256,512]{1,0:T(8,128)(2,1)S(1)}, u32[]{:S(2)}, u32[]{:S(2)}) collective-permute-start(bf16[256,512]{1,0:T(8,128)(2,1)} %unpack_mixed.1.m00), channel_id=1, source_target_pairs={{0,32},{32,0},{1,33},{33,1},{2,34},{34,2},{3,35},{35,3},{4,36},{36... | collective-permute-start | bytes 786440 | tf_op jit(solution)/shard_map/ppermute | solution.py:598
  60.9 12.6 %collective-permute-start.4 = (bf16[256,512]{1,0:T(8,128)(2,1)}, bf16[256,512]{1,0:T(8,128)(2,1)S(1)}, u32[]{:S(2)}, u32[]{:S(2)}) collective-permute-start(bf16[256,512]{1,0:T(8,128)(2,1)} %unpack_mixed.1.m00), channel_id=1, source_target_pairs={{0,8},{8,0},{1,9},{9,1},{2,10},{10,2},{3,11},{11,3},{4,12},{12,4},... | collective-permute-start | bytes 786440 | tf_op jit(solution)/shard_map/ppermute | solution.py:594
  66.0 7.5 %collective-permute-start.5 = (bf16[256,512]{1,0:T(8,128)(2,1)S(1)}, bf16[256,512]{1,0:T(8,128)(2,1)S(1)}, u32[]{:S(2)}, u32[]{:S(2)}) collective-permute-start(bf16[256,512]{1,0:T(8,128)(2,1)S(1)} %collective-permute-done.3.m01), channel_id=1, source_target_pairs={{0,8},{8,0},{1,9},{9,1},{2,10},{10,2},{3,11},{11,3},{4,12},{12,4},... | collective-permute-start | bytes 786440 | tf_op jit(solution)/shard_map/ppermute | solution.py:594
  68.4 5.1 %collective-permute-start.6 = (bf16[8,4,16,128]{3,2,1,0:T(8,128)(2,1)S(1)}, bf16[8,4,16,128]{3,2,1,0:T(8,128)(2,1)S(1)}, u32[]{:S(2)}, u32[]{:S(2)}) collective-permute-start(bf16[8,4,16,128]{3,2,1,0:T(8,128)(2,1)S(1)} %bitcast.33), channel_id=1, source_target_pairs={{0,32},{32,0},{1,33},{33,1},{2,34},{34,2},{3,35},{35,3},{4,36},{36... | collective-permute-start | bytes 393224 | tf_op jit(solution)/shard_map/ppermute | solution.py:598
  78.5 38.0 %all-to-all-start.2 = ((bf16[32,16,1152]{2,1,0:T(8,128)(2,1)}), bf16[32,16,1152]{2,1,0:T(8,128)(2,1)S(1)}, u32[]{:S(2)}, u32[]{:S(2)}) async-start(bf16[32,16,1152]{2,1,0:T(8,128)(2,1)} %partial.1), calls=%async_computation.2 | async-start | bytes 2359296 | tf_op jit(solution)/shard_map/all_to_all | solution.py:590
  92.4 11.5 %collective-permute-start.7 = (bf16[384,128]{1,0:T(8,128)(2,1)}, bf16[384,128]{1,0:T(8,128)(2,1)S(1)}, u32[]{:S(2)}, u32[]{:S(2)}) collective-permute-start(bf16[384,128]{1,0:T(8,128)(2,1)} %get-tuple-element.67), channel_id=1, source_target_pairs={{0,1},{1,0},{2,3},{3,2},{4,5},{5,4},{6,7},{7,6},{8,9},{9,8},{10,11... | collective-permute-start | bytes 294920 | tf_op jit(solution)/shard_map/ppermute | solution.py:651
  93.6 13.0 %collective-permute-start.8 = (bf16[384,128]{1,0:T(8,128)(2,1)}, bf16[384,128]{1,0:T(8,128)(2,1)S(1)}, u32[]{:S(2)}, u32[]{:S(2)}) collective-permute-start(bf16[384,128]{1,0:T(8,128)(2,1)} %get-tuple-element.68), channel_id=1, source_target_pairs={{0,2},{1,3},{2,0},{3,1},{4,6},{5,7},{6,4},{7,5},{8,10},{9,11},{10,... | collective-permute-start | bytes 294920 | tf_op jit(solution)/shard_map/ppermute | solution.py:651
  94.8 12.5 %collective-permute-start.9 = (bf16[384,128]{1,0:T(8,128)(2,1)}, bf16[384,128]{1,0:T(8,128)(2,1)S(1)}, u32[]{:S(2)}, u32[]{:S(2)}) collective-permute-start(bf16[384,128]{1,0:T(8,128)(2,1)} %get-tuple-element.69), channel_id=1, source_target_pairs={{0,3},{1,2},{2,1},{3,0},{4,7},{5,6},{6,5},{7,4},{8,11},{9,10},{10,... | collective-permute-start | bytes 294920 | tf_op jit(solution)/shard_map/ppermute | solution.py:651
  95.0 15.0 %collective-permute-start.10 = (bf16[384,128]{1,0:T(8,128)(2,1)}, bf16[384,128]{1,0:T(8,128)(2,1)S(1)}, u32[]{:S(2)}, u32[]{:S(2)}) collective-permute-start(bf16[384,128]{1,0:T(8,128)(2,1)} %get-tuple-element.70), channel_id=1, source_target_pairs={{0,4},{1,5},{2,6},{3,7},{4,0},{5,1},{6,2},{7,3},{8,12},{9,13},{10,... | collective-permute-start | bytes 294920 | tf_op jit(solution)/shard_map/ppermute | solution.py:651
  97.8 15.0 %collective-permute-start.11 = (bf16[384,128]{1,0:T(8,128)(2,1)}, bf16[384,128]{1,0:T(8,128)(2,1)S(1)}, u32[]{:S(2)}, u32[]{:S(2)}) collective-permute-start(bf16[384,128]{1,0:T(8,128)(2,1)} %get-tuple-element.71), channel_id=1, source_target_pairs={{0,5},{1,4},{2,7},{3,6},{4,1},{5,0},{6,3},{7,2},{8,13},{9,12},{10,... | collective-permute-start | bytes 294920 | tf_op jit(solution)/shard_map/ppermute | solution.py:651
  103.9 53.4 %copy-start.14 = (bf16[384,128]{1,0:T(8,128)(2,1)}, bf16[384,128]{1,0:T(8,128)(2,1)S(1)}, u32[]{:S(2)}) copy-start(bf16[384,128]{1,0:T(8,128)(2,1)S(1)} %collective-permute-done.7.refs_1_) | copy-start | bytes 294916
  103.9 8.9 %collective-permute-start.12 = (bf16[384,128]{1,0:T(8,128)(2,1)}, bf16[384,128]{1,0:T(8,128)(2,1)S(1)}, u32[]{:S(2)}, u32[]{:S(2)}) collective-permute-start(bf16[384,128]{1,0:T(8,128)(2,1)} %get-tuple-element.72), channel_id=1, source_target_pairs={{0,6},{1,7},{2,4},{3,5},{4,2},{5,3},{6,0},{7,1},{8,14},{9,15},{10,... | collective-permute-start | bytes 294920 | tf_op jit(solution)/shard_map/ppermute | solution.py:651
  106.6 50.7 %copy-start.15 = (bf16[384,128]{1,0:T(8,128)(2,1)}, bf16[384,128]{1,0:T(8,128)(2,1)S(1)}, u32[]{:S(2)}) copy-start(bf16[384,128]{1,0:T(8,128)(2,1)S(1)} %collective-permute-done.8.refs_2_) | copy-start | bytes 294916
  106.6 9.9 %collective-permute-start.13 = (bf16[384,128]{1,0:T(8,128)(2,1)}, bf16[384,128]{1,0:T(8,128)(2,1)S(1)}, u32[]{:S(2)}, u32[]{:S(2)}) collective-permute-start(bf16[384,128]{1,0:T(8,128)(2,1)} %get-tuple-element.73), channel_id=1, source_target_pairs={{0,7},{1,6},{2,5},{3,4},{4,3},{5,2},{6,1},{7,0},{8,15},{9,14},{10,... | collective-permute-start | bytes 294920 | tf_op jit(solution)/shard_map/ppermute | solution.py:651
  107.3 50.0 %copy-start.16 = (bf16[384,128]{1,0:T(8,128)(2,1)}, bf16[384,128]{1,0:T(8,128)(2,1)S(1)}, u32[]{:S(2)}) copy-start(bf16[384,128]{1,0:T(8,128)(2,1)S(1)} %collective-permute-done.9.refs_3_) | copy-start | bytes 294916
  110.0 47.3 %copy-start.17 = (bf16[384,128]{1,0:T(8,128)(2,1)}, bf16[384,128]{1,0:T(8,128)(2,1)S(1)}, u32[]{:S(2)}) copy-start(bf16[384,128]{1,0:T(8,128)(2,1)S(1)} %collective-permute-done.10.refs_4_) | copy-start | bytes 294916
  112.8 44.5 %copy-start.19 = (bf16[384,128]{1,0:T(8,128)(2,1)}, bf16[384,128]{1,0:T(8,128)(2,1)S(1)}, u32[]{:S(2)}) copy-start(bf16[384,128]{1,0:T(8,128)(2,1)S(1)} %collective-permute-done.12.refs_6_) | copy-start | bytes 294916
  120.5 43.1 %all-to-all-start.3 = ((bf16[64,16,1024]{2,1,0:T(8,128)(2,1)}), bf16[64,16,1024]{2,1,0:T(8,128)(2,1)S(1)}, u32[]{:S(2)}, u32[]{:S(2)}) async-start(bf16[64,16,1024]{2,1,0:T(8,128)(2,1)} %get-tuple-element.87), calls=%async_computation.3 | async-start | bytes 4194304 | tf_op jit(solution)/shard_map/all_to_all | solution.py:590
  130.2 1.8 collective-permute-start.14
  131.9 20.0 %collective-permute-start.20 = (bf16[16,1024]{1,0:T(8,128)(2,1)S(1)}, bf16[16,1024]{1,0:T(8,128)(2,1)S(1)}, u32[]{:S(2)}, u32[]{:S(2)}) collective-permute-start(bf16[16,1024]{1,0:T(8,128)(2,1)S(1)} %add_convert_fusion.refs_0_), channel_id=1, source_target_pairs={{0,96},{32,0},{64,32},{96,64},{1,97},{33,1},{65,33},{97,65},{2,98}... | collective-permute-start | bytes 98312 | tf_op jit(solution)/shard_map/ppermute | solution.py:610
  134.7 14.1 %collective-permute-start.15 = (bf16[16,1024]{1,0:T(8,128)(2,1)S(1)}, bf16[16,1024]{1,0:T(8,128)(2,1)S(1)}, u32[]{:S(2)}, u32[]{:S(2)}) collective-permute-start(bf16[16,1024]{1,0:T(8,128)(2,1)S(1)} %add_convert_fusion.refs_0_), channel_id=1, source_target_pairs={{0,16},{16,0},{1,17},{17,1},{2,18},{18,2},{3,19},{19,3},{4,20},{20... | collective-permute-start | bytes 98312 | tf_op jit(solution)/shard_map/ppermute | solution.py:606
  138.1 21.8 %collective-permute-start.18 = (bf16[16,1024]{1,0:T(8,128)(2,1)S(1)}, bf16[16,1024]{1,0:T(8,128)(2,1)S(1)}, u32[]{:S(2)}, u32[]{:S(2)}) collective-permute-start(bf16[16,1024]{1,0:T(8,128)(2,1)S(1)} %add_convert_fusion.refs_0_), channel_id=1, source_target_pairs={{0,64},{32,96},{64,0},{96,32},{1,65},{33,97},{65,1},{97,33},{2,66}... | collective-permute-start | bytes 98312 | tf_op jit(solution)/shard_map/ppermute | solution.py:610
  138.4 21.5 %collective-permute-start.16 = (bf16[16,1024]{1,0:T(8,128)(2,1)S(1)}, bf16[16,1024]{1,0:T(8,128)(2,1)S(1)}, u32[]{:S(2)}, u32[]{:S(2)}) collective-permute-start(bf16[16,1024]{1,0:T(8,128)(2,1)S(1)} %add_convert_fusion.refs_0_), channel_id=1, source_target_pairs={{0,32},{32,64},{64,96},{96,0},{1,33},{33,65},{65,97},{97,1},{2,34}... | collective-permute-start | bytes 98312 | tf_op jit(solution)/shard_map/ppermute | solution.py:610
  148.9 11.0 %collective-permute-start.21 = (bf16[16,1024]{1,0:T(8,128)(2,1)S(1)}, bf16[16,1024]{1,0:T(8,128)(2,1)S(1)}, u32[]{:S(2)}, u32[]{:S(2)}) collective-permute-start(bf16[16,1024]{1,0:T(8,128)(2,1)S(1)} %collective-permute-done.15.refs_1_), channel_id=1, source_target_pairs={{0,96},{32,0},{64,32},{96,64},{1,97},{33,1},{65,33},{97,65},{2,98}... | collective-permute-start | bytes 98312 | tf_op jit(solution)/shard_map/ppermute | solution.py:610
  151.6 8.3 %collective-permute-start.19 = (bf16[16,1024]{1,0:T(8,128)(2,1)S(1)}, bf16[16,1024]{1,0:T(8,128)(2,1)S(1)}, u32[]{:S(2)}, u32[]{:S(2)}) collective-permute-start(bf16[16,1024]{1,0:T(8,128)(2,1)S(1)} %collective-permute-done.15.refs_1_), channel_id=1, source_target_pairs={{0,64},{32,96},{64,0},{96,32},{1,65},{33,97},{65,1},{97,33},{2,66}... | collective-permute-start | bytes 98312 | tf_op jit(solution)/shard_map/ppermute | solution.py:610
  152.0 8.0 %collective-permute-start.17 = (bf16[16,1024]{1,0:T(8,128)(2,1)S(1)}, bf16[16,1024]{1,0:T(8,128)(2,1)S(1)}, u32[]{:S(2)}, u32[]{:S(2)}) collective-permute-start(bf16[16,1024]{1,0:T(8,128)(2,1)S(1)} %collective-permute-done.15.refs_1_), channel_id=1, source_target_pairs={{0,32},{32,64},{64,96},{96,0},{1,33},{33,65},{65,97},{97,1},{2,34}... | collective-permute-start | bytes 98312 | tf_op jit(solution)/shard_map/ppermute | solution.py:610
  163.6 13.6 %collective-permute-start.22 = (bf16[64,16,1024]{2,1,0:T(8,128)(2,1)S(1)}, bf16[64,16,1024]{2,1,0:T(8,128)(2,1)}, u32[]{:S(2)}, u32[]{:S(2)}) collective-permute-start(bf16[64,16,1024]{2,1,0:T(8,128)(2,1)S(1)} %all-to-all-done.3.mine), channel_id=1, source_target_pairs={{0,8},{8,0},{1,9},{9,1},{2,10},{10,2},{3,11},{11,3},{4,12},{12,4},... | collective-permute-start | bytes 6291464 | tf_op jit(solution)/shard_map/ppermute | solution.py:594
  (25 other events, 238.6 us)

commit v7 on v6

--- a/solution.py
+++ b/solution.py
@@ -205,8 +205,8 @@
 
 def conv_kernel(
     place, got, short, skip, ahead_h, ahead_l, back_h, back_l,
-    sent, whole,
-    sa_pad, sv_pad, sa, prod, spec, fspec, res, time,
+    sent,
+    sa_pad, sv_pad, sa, sv, prod, spec, fspec, res, time, u_pad, x_pad,
 ):
     low = low_lanes(BLOCK)
     low64 = low_lanes(64)
@@ -237,6 +237,7 @@
 
     def keep(b, a, v):
         sa[b] = a
+        sv[b] = v
         prod[b] = turned(a) * v
 
     shorten(got, pair, sa_pad, sv_pad, keep)
@@ -262,15 +263,21 @@
 
     def gate(b, carry):
         t = jnp.where(low, time[b], time[7 - b]) + gain * prod[b]
-        whole[b] = t
-        y = t * sa[b]
-        for n in range(2):
-            first, second = y[128 * n : 128 * n + 64], y[128 * n + 64 : 128 * n + 128]
-            there = slice(128 * n, 128 * n + 128)
-            sent[b, :, there] = jnp.where(low64, first, turned(second)).astype(BF)
+        rows = pl.ds(pl.multiple_of(BLOCK * b, 8), BLOCK)
+        u_pad[rows] = turned(t) * sv[b]
+        x_pad[rows] = t * sa[b]
         return carry
 
     lax.fori_loop(0, 8, gate, 0)
+    u_pad[8 * BLOCK :] = jnp.zeros((8, 128), F32)
+    x_pad[8 * BLOCK :] = jnp.zeros((8, 128), F32)
+    w_u, w_x = pair(1, 0), pair(None, 2)
+    for b in range(8):
+        start = BLOCK * b
+        y = sum(w_u[j] * u_pad[start + j : start + j + BLOCK] for j in range(3))
+        sent[b, :, 0:128] = y.astype(BF)
+        y = sum(w_x[j] * x_pad[start + j : start + j + BLOCK] for j in range(3))
+        sent[b, :, 128:256] = y.astype(BF)
 
 
 def lag_kernel(
@@ -319,30 +326,6 @@
         return carry
 
     lax.fori_loop(0, 2, invert, 0)
-
-
-def stream_kernel(place, got, short, skip, whole, *refs):
-    outs, (sa_pad, sv_pad, u_pad, x_pad, wide) = refs[:8], refs[8:]
-    pair, _ = weights(place, short, skip)
-
-    def keep(b, a, v):
-        t = whole[b]
-        u_pad[BLOCK * b : BLOCK * b + BLOCK] = turned(t) * v
-        x_pad[BLOCK * b : BLOCK * b + BLOCK] = t * a
-
-    shorten(got, pair, sa_pad, sv_pad, keep)
-    u_pad[8 * BLOCK :] = jnp.zeros((8, 128), F32)
-    x_pad[8 * BLOCK :] = jnp.zeros((8, 128), F32)
-    w_u, w_x = pair(1, 0), pair(None, 2)
-    low128 = low_lanes(128)
-    for b in range(8):
-        start = BLOCK * b
-        y = sum(w_u[j] * u_pad[start + j : start + j + BLOCK] for j in range(3))
-        wide[b, 0:BLOCK] = y.astype(BF)
-        y = sum(w_x[j] * x_pad[start + j : start + j + BLOCK] for j in range(3))
-        wide[b, BLOCK:] = jnp.where(low128, turned(y[:128]), y[128:]).astype(BF)
-    for n in range(8):
-        outs[n][...] = wide[place[0] ^ n]
 
 
 def on_channels(kernel, name, inputs, in_shapes, outputs, scratch, cost):
@@ -381,9 +364,10 @@
 
 def conv(place, got, short, skip):
     inputs = (place, got, short, skip, *(jnp.asarray(t) for t in tables()))
-    outputs = [((8, 64, 256), BF), BLOCKS]
-    scratch = [BLOCKS, BLOCKS, BINS, BINS, BINS, BLOCKS]
-    return on_channels(conv_kernel, "conv", inputs, TABLES, outputs, scratch, None)
+    outputs = [((8, BLOCK, 256), BF)]
+    pad = ((8 * BLOCK + 8, 128), F32)
+    scratch = [BLOCKS, BLOCKS, BLOCKS, BINS, BINS, BINS, BLOCKS, pad, pad]
+    return on_channels(conv_kernel, "conv", inputs, TABLES, outputs, scratch, None)[0]
 
 
 def lag_sums(place, got, short, skip):
@@ -394,66 +378,45 @@
     return on_channels(lag_kernel, "lag_sums", inputs, TABLES, outputs, scratch, cost)[0]
 
 
-def stream_grads(place, got, short, skip, whole):
-    outputs = [((384, 128), BF)] * 8
-    pad = ((8 * BLOCK + 8, 128), F32)
-    scratch = [pad, pad, ((8, 384, 128), BF)]
-    inputs = (place, got, short, skip, whole)
-    cost = spent(10**9)
-    return on_channels(
-        stream_kernel, "stream_grads", inputs, [BLOCKS[0]], outputs, scratch, cost
-    )
-
-
-def mixed_kernel(got, mixed):
-    low = low_lanes(64)
+def spread(got, there, first, second, low):
     for q in range(4):
         lanes = slice(128 * q, 128 * q + 128)
-        for t in range(2):
-            there = slice(128 * t, 128 * t + 128)
-            a = got[2 * q, :, there].astype(F32)
-            b = got[2 * q + 1, :, there].astype(F32)
-            mixed[128 * t : 128 * t + 64, lanes] = jnp.where(low, a, turned(b)).astype(BF)
-            mixed[128 * t + 64 : 128 * t + 128, lanes] = jnp.where(low, turned(a), b).astype(BF)
+        a = got[2 * q, 0:BLOCK, there].astype(F32)
+        b = got[2 * q + 1, 0:BLOCK, there].astype(F32)
+        if first is not None:
+            first[:, lanes] = jnp.where(low, a, turned(b)).astype(BF)
+        if second is not None:
+            second[:, lanes] = jnp.where(low, turned(a), b).astype(BF)
+
+
+def mixed_kernel(got, mixed):
+    spread(got, slice(0, 128), mixed, None, low_lanes(BLOCK))
 
 
 def unpack_mixed(got):
     return pl.pallas_call(
         mixed_kernel,
+        grid=(1,),
+        in_specs=[pl.BlockSpec((8, BLOCK, 128), lambda n: (0, 0, 1))],
+        out_specs=pl.BlockSpec((BLOCK, 512), lambda n: (0, 0)),
         out_shape=jax.ShapeDtypeStruct((BLOCK, 512), BF),
         name="unpack_mixed",
     )(got)
 
 
-def grads_kernel(place, *refs):
-    parts, grads = refs[:8], refs[8]
-    low, low128 = low_lanes(BLOCK), low_lanes(128)
-    even = place[0] % 2 == 0
-    for n in range(4):
-        lanes = pl.ds(pl.multiple_of(128 * ((place[0] // 2) ^ n), 128), 128)
-        first, second = parts[2 * n][...].astype(F32), parts[2 * n + 1][...].astype(F32)
-        a, b = jnp.where(even, first, second), jnp.where(even, second, first)
-        grads[1, :, lanes] = jnp.where(low, a[:BLOCK], turned(b[:BLOCK])).astype(BF)
-        grads[0, :, lanes] = jnp.where(low, turned(a[:BLOCK]), b[:BLOCK]).astype(BF)
-        a, b = a[BLOCK:], b[BLOCK:]
-        grads[2, 0:128, lanes] = jnp.where(low128, a, turned(b)).astype(BF)
-        grads[2, 128:256, lanes] = jnp.where(low128, turned(a), b).astype(BF)
-
-
-def unpack_grads(place, parts):
-    full = lambda *shape: pl.BlockSpec(shape, lambda n, p: (0,) * len(shape))
+def grads_kernel(got, grads):
+    low = low_lanes(BLOCK)
+    spread(got, slice(0, 128), grads.at[1], grads.at[0], low)
+    spread(got, slice(128, 256), None, grads.at[2], low)
+
+
+def unpack_grads(got):
     return pl.pallas_call(
         grads_kernel,
-        grid_spec=pltpu.PrefetchScalarGridSpec(
-            num_scalar_prefetch=1,
-            grid=(1,),
-            in_specs=[full(384, 128)] * 8,
-            out_specs=full(3, BLOCK, 512),
-        ),
         out_shape=jax.ShapeDtypeStruct((3, BLOCK, 512), BF),
         cost_estimate=pl.CostEstimate(flops=10**6, bytes_accessed=2 * 10**6, transcendentals=0),
         name="unpack_grads",
-    )(place, *parts)
+    )(got)
 
 
 def partial_kernel(place, m00, m01, m10, m11, g00, g01, g10, g11, lags, lags_z, packed):
@@ -628,8 +591,8 @@
     )
     got = exchange(pack(streams[:, 0], grad, out_weight, long_filter), SEQ)
     channels = (seq[None], got, short_filter.reshape(9, 512), skip_gain.reshape(1, 512))
-    sent, whole = conv(*channels)
-    sent, whole, got, grads = lax.optimization_barrier((sent, whole, got, grads))
+    sent = conv(*channels)
+    sent, got, grads = lax.optimization_barrier((sent, got, grads))
     channels = (channels[0], got) + channels[2:]
     lags = lag_sums(*channels).reshape(8, 2, 2, 2, 16, 128)
 
@@ -638,30 +601,23 @@
 
     lags_own, lags_z = of_side(side), above(of_side(1 - side))
     back = exchange(sent, SEQ)
-    back, lags_own = lax.optimization_barrier((back, lags_own))
+    back, lags_own, lags_z = lax.optimization_barrier((back, lags_own, lags_z))
     m00 = unpack_mixed(back)
     m01, m10 = above(m00), across(m00)
     mixed = (m00, m01, m10, across(m01))
     part = partial((2 * core + side)[None], mixed, grad, grads, lags_own, lags_z)
-    part, m00, whole, got = lax.optimization_barrier((part, m00, whole, got))
+    part, m00, back = lax.optimization_barrier((part, m00, back))
     part = exchange(part, MOST)
-    channels = (channels[0], got) + channels[2:]
-    parts = stream_grads(*channels, whole)
-    parts = [parts[0]] + [
-        lax.ppermute(parts[n], SEQ, [(i, i ^ n) for i in range(8)]) for n in range(1, 8)
-    ]
-    part, parts, m00 = lax.optimization_barrier((part, parts, m00))
+    layer_out = jnp.dot(m00, out_weight, preferred_element_type=F32).astype(BF)
+    grad_streams = unpack_grads(back)
+    part, layer_out, grad_streams = lax.optimization_barrier((part, layer_out, grad_streams))
     rows, lags = reduce(part, scale)
-    rows, lags, parts, m00 = lax.optimization_barrier((rows, lags, parts, m00))
+    rows, lags = lax.optimization_barrier((rows, lags))
     mine = exchange(rows, CHIPS)
-    layer_out = jnp.dot(m00, out_weight, preferred_element_type=F32).astype(BF)
-    grad_streams = unpack_grads(seq[None], parts)
     lags = (lags + across(lags)).astype(BF)
     place = jnp.stack([lax.axis_index(("zh", "zl")), lax.axis_index("yh")]).astype(jnp.int32)
     grad_filter = write_filter(place, gathered(lags))
-    mine, grad_filter, layer_out, grad_streams = lax.optimization_barrier(
-        (mine, grad_filter, layer_out, grad_streams)
-    )
+    mine, grad_filter = lax.optimization_barrier((mine, grad_filter))
     theirs = across(mine)
     grad_weight = write_half(core[None], mine)
     grad_weight = write_half(1 - core[None], theirs, grad_weight)

time: 182 us -> 167 us (0.918)
  the two profiles are of different devices: /device:TPU:1 before, /device:TPU:2 now
where the time goes in v7:
time: 167 us; the launch traced here: 166 us
  waiting for transfers between devices  57 us (34%)
  Pallas kernels  46.6 us (28%)
  starting transfers between devices  46.3 us (28%)
  local copies, waits for them, and re-layouts  9.44 us (6%)
  matrix products  4.77 us (3%)
    all_to_all x4, starting transfers between devices, exchange(): return lax.all_to_all(x, axes, 0, 0, tiled=True)  28 us
    all_to_all x4, waiting for transfers between devices, exchange(): return lax.all_to_all(x, axes, 0, 0, tiled=True)  26.6 us
    pallas_call x2, Pallas kernels, on_channels(): pl.pallas_call(kernel, grid_spec=pltpu.PrefetchScalarGridSpec(num_scalar_...  19 us
    ppermute x1, waiting for transfers between devices, gathered(): pair = (lags, lax.ppermute(lags, 'yh', [(0, 1), (1, 0)]))  16.3 us
    ppermute x6, starting transfers between devices, gathered(): out += [lax.ppermute(part, ('zh', 'zl'), route) for part in pair]  9.18 us
    ppermute x3, waiting for transfers between devices, above(): return lax.ppermute(x, 'zl', [(0, 1), (1, 0)])  7.7 us
    pallas_call x2, Pallas kernels, write_half(): pl.pallas_call(half_kernel, grid_spec=pltpu.PrefetchScalarGridSpec(num_sc...  7.39 us
    pallas_call x1, Pallas kernels, pack(): pl.pallas_call(pack_kernel, grid=(steps,), in_specs=[pl.BlockSpec((3, BLO...  6.38 us
  transfers between devices with their start and end apart: 20, of which 9 were waited for; matrix products, arithmetic and copies ran while one was open for 5% of the time, Pallas kernels for 17%

profile of v7, /device:TPU:2, one launch (start us, length us, event | category | flops | bytes accessed | tf_op | source)
XLA Modules:
  0.0 165.8 jit_solution(14580704260627111415)
XLA Ops:
  0.6 6.4 %pack.1 = bf16[8,320,256]{2,1,0:T(8,128)(2,1)} custom-call(bf16[3,256,512]{2,1,0:T(8,128)(2,1)} %bitcast.29, bf16[256,4096]{1,0:T(8,128)(2,1)} %bitcast.27, bf16[512,4096]{1,0:T(8,128)(2,1)} %weight.1, f32[256,512]{1,0:T(8,128)} %filt.1), custom_call_target="tpu_custom_call" | custom-call | tf_op jit(solution)/shard_map/pack/pallas_call | solution.py:90
  7.0 6.0 %all-to-all-start = ((bf16[8,320,256]{2,1,0:T(8,128)(2,1)}), bf16[8,320,256]{2,1,0:T(8,128)(2,1)S(1)}, u32[]{:S(2)}, u32[]{:S(2)}) async-start(bf16[8,320,256]{2,1,0:T(8,128)(2,1)} %pack.1), calls=%async_computation | async-start | bytes 2621440 | tf_op jit(solution)/shard_map/all_to_all | solution.py:553
  13.0 1.2 dynamic-slice_bitcast_fusion
  15.0 1.2 collective-permute-start
  16.9 14.0 %all-to-all-done.got = bf16[8,320,256]{2,1,0:T(8,128)(2,1)S(1)} async-done(((bf16[8,320,256]{2,1,0:T(8,128)(2,1)}), bf16[8,320,256]{2,1,0:T(8,128)(2,1)S(1)}, u32[]{:S(2)}, u32[]{:S(2)}) %all-to-all-start) | async-done | bytes 1310752 | tf_op jit(solution)/shard_map/all_to_all | solution.py:553
  31.9 10.2 %conv.1 = bf16[8,256,256]{2,1,0:T(8,128)(2,1)} custom-call(s32[1]{0:T(128)} %bitcast.1.place, bf16[8,320,256]{2,1,0:T(8,128)(2,1)} %copy-done.3, f32[9,512]{1,0:T(8,128)} %reshape.28.short, f32[1,512]{1,0:T(1,128)} %bitcast.34, bf16[512,256]{1,0:T(8,128)(2,1)} %constant.54.clone.ahead_h, bf16[512,256]{1,0:T(8,128)(2,1)} %constant.55.clone.ahead_l, ...), custom_call_target="tpu_custom_call" | custom-call | tf_op jit(solution)/shard_map/conv/pallas_call | solution.py:333
  42.1 5.5 %all-to-all-start.1 = ((bf16[8,256,256]{2,1,0:T(8,128)(2,1)}), bf16[8,256,256]{2,1,0:T(8,128)(2,1)S(1)}, u32[]{:S(2)}, u32[]{:S(2)}) async-start(bf16[8,256,256]{2,1,0:T(8,128)(2,1)} %conv.1), calls=%async_computation.1 | async-start | bytes 2097152 | tf_op jit(solution)/shard_map/all_to_all | solution.py:553
  47.7 8.8 %lag_sums.1 = bf16[8,8,16,128]{3,2,1,0:T(8,128)(2,1)} custom-call(s32[1]{0:T(128)} %bitcast.1.place, bf16[8,320,256]{2,1,0:T(8,128)(2,1)} %copy-done.3, f32[9,512]{1,0:T(8,128)} %reshape.28.short, f32[1,512]{1,0:T(1,128)} %bitcast.35, bf16[512,256]{1,0:T(8,128)(2,1)} %constant.54.clone.ahead_h, bf16[512,256]{1,0:T(8,128)(2,1)} %constant.55.clone.ahead_l, ...), custom_call_target="tpu_custom_call" | custom-call | flops 2000000000 | bytes 3000000 | tf_op jit(solution)/shard_map/lag_sums/pallas_call | solution.py:333
  56.5 1.6 constant_dynamic-slice_fusion
  58.1 1.9 %collective-permute-start.3 = (bf16[8,4,16,128]{3,2,1,0:T(8,128)(2,1)S(1)}, bf16[8,4,16,128]{3,2,1,0:T(8,128)(2,1)S(1)}, u32[]{:S(2)}, u32[]{:S(2)}) collective-permute-start(bf16[8,4,16,128]{3,2,1,0:T(8,128)(2,1)S(1)} %bitcast.33), channel_id=1, source_target_pairs={{0,32},{32,0},{1,33},{33,1},{2,34},{34,2},{3,35},{35,3},{4,36},{36... | collective-permute-start | bytes 393224 | tf_op jit(solution)/shard_map/ppermute | solution.py:561
  60.0 3.0 %collective-permute-done.3.lags_z = bf16[8,4,16,128]{3,2,1,0:T(8,128)(2,1)S(1)} collective-permute-done((bf16[8,4,16,128]{3,2,1,0:T(8,128)(2,1)S(1)}, bf16[8,4,16,128]{3,2,1,0:T(8,128)(2,1)S(1)}, u32[]{:S(2)}, u32[]{:S(2)}) %collective-permute-start.3) | collective-permute-done | bytes 131104 | tf_op jit(solution)/shard_map/ppermute | solution.py:561
  64.1 1.9 %unpack_mixed.1.m00 = bf16[256,512]{1,0:T(8,128)(2,1)} custom-call(bf16[8,256,256]{2,1,0:T(8,128)(2,1)} %copy-done.1), custom_call_target="tpu_custom_call" | custom-call | tf_op jit(solution)/shard_map/unpack_mixed/pallas_call | solution.py:397
  66.0 1.9 %collective-permute-start.4 = (bf16[256,512]{1,0:T(8,128)(2,1)}, bf16[256,512]{1,0:T(8,128)(2,1)S(1)}, u32[]{:S(2)}, u32[]{:S(2)}) collective-permute-start(bf16[256,512]{1,0:T(8,128)(2,1)} %unpack_mixed.1.m00), channel_id=1, source_target_pairs={{0,32},{32,0},{1,33},{33,1},{2,34},{34,2},{3,35},{35,3},{4,36},{36... | collective-permute-start | bytes 786440 | tf_op jit(solution)/shard_map/ppermute | solution.py:561
  67.9 4.7 %collective-permute-done.4.m01 = bf16[256,512]{1,0:T(8,128)(2,1)S(1)} collective-permute-done((bf16[256,512]{1,0:T(8,128)(2,1)}, bf16[256,512]{1,0:T(8,128)(2,1)S(1)}, u32[]{:S(2)}, u32[]{:S(2)}) %collective-permute-start.4) | collective-permute-done | bytes 262176 | tf_op jit(solution)/shard_map/ppermute | solution.py:561
  72.6 1.5 collective-permute-done.6.m11
  74.9 4.2 %partial.1 = bf16[32,16,1152]{2,1,0:T(8,128)(2,1)} custom-call(s32[1]{0:T(128)} %bitcast.place, bf16[256,512]{1,0:T(8,128)(2,1)} %unpack_mixed.1.m00, bf16[256,512]{1,0:T(8,128)(2,1)} %copy-done.9, bf16[256,512]{1,0:T(8,128)(2,1)} %copy-done.10, bf16[256,512]{1,0:T(8,128)(2,1)} %copy-done.11, bf16[256,4096]{1,0:T(8,128)(2,1)} %bitcast.28, ...), custom_call_target="tpu_custom_call" | custom-call | tf_op jit(solution)/shard_map/partial/pallas_call | solution.py:439
  79.0 10.8 %all-to-all-start.2 = ((bf16[32,16,1152]{2,1,0:T(8,128)(2,1)}), bf16[32,16,1152]{2,1,0:T(8,128)(2,1)S(1)}, u32[]{:S(2)}, u32[]{:S(2)}) async-start(bf16[32,16,1152]{2,1,0:T(8,128)(2,1)} %partial.1), calls=%async_computation.2 | async-start | bytes 2359296 | tf_op jit(solution)/shard_map/all_to_all | solution.py:553
  89.8 2.4 %unpack_grads.1 = bf16[3,256,512]{2,1,0:T(8,128)(2,1)} custom-call(bf16[8,256,256]{2,1,0:T(8,128)(2,1)} %copy-done.1), custom_call_target="tpu_custom_call" | custom-call | flops 1000000 | bytes 2000000 | tf_op jit(solution)/shard_map/unpack_grads/pallas_call | solution.py:414
  92.2 4.8 %convolution_convert_fusion = bf16[256,4096]{1,0:T(8,128)(2,1)} fusion(bf16[256,512]{1,0:T(8,128)(2,1)S(1)} %copy-done.5, bf16[512,4096]{1,0:T(8,128)(2,1)} %weight.1), kind=kOutput, calls=%fused_computation | convolution fusion | flops 1074790400 | bytes 6553600 | tf_op jit(solution)/shard_map/dot_general | solution.py:611
  97.0 12.6 %all-to-all-done.2.got = bf16[32,16,1152]{2,1,0:T(8,128)(2,1)S(1)} async-done(((bf16[32,16,1152]{2,1,0:T(8,128)(2,1)}), bf16[32,16,1152]{2,1,0:T(8,128)(2,1)S(1)}, u32[]{:S(2)}, u32[]{:S(2)}) %all-to-all-start.2) | async-done | bytes 1179680 | tf_op jit(solution)/shard_map/all_to_all | solution.py:553
  110.7 3.0 %reduce.1 = (bf16[64,16,1024]{2,1,0:T(8,128)(2,1)}, f32[16,1024]{1,0:T(8,128)}) custom-call(bf16[32,16,1152]{2,1,0:T(8,128)(2,1)} %copy-done.4), custom_call_target="tpu_custom_call" | custom-call | tf_op jit(solution)/shard_map/reduce/pallas_call | solution.py:470
  113.7 5.7 %all-to-all-start.3 = ((bf16[64,16,1024]{2,1,0:T(8,128)(2,1)}), bf16[64,16,1024]{2,1,0:T(8,128)(2,1)S(1)}, u32[]{:S(2)}, u32[]{:S(2)}) async-start(bf16[64,16,1024]{2,1,0:T(8,128)(2,1)} %get-tuple-element.36), calls=%async_computation.3 | async-start | bytes 4194304 | tf_op jit(solution)/shard_map/all_to_all | solution.py:553
  119.5 1.2 collective-permute-done.7
  120.7 3.1 %collective-permute-start.8 = (bf16[16,1024]{1,0:T(8,128)(2,1)S(1)}, bf16[16,1024]{1,0:T(8,128)(2,1)S(1)}, u32[]{:S(2)}, u32[]{:S(2)}) collective-permute-start(bf16[16,1024]{1,0:T(8,128)(2,1)S(1)} %add_convert_fusion.refs_0_), channel_id=1, source_target_pairs={{0,16},{16,0},{1,17},{17,1},{2,18},{18,2},{3,19},{19,3},{4,20},{20... | collective-permute-start | bytes 98312 | tf_op jit(solution)/shard_map/ppermute | solution.py:569
  123.9 3.0 %collective-permute-start.13 = (bf16[16,1024]{1,0:T(8,128)(2,1)S(1)}, bf16[16,1024]{1,0:T(8,128)(2,1)S(1)}, u32[]{:S(2)}, u32[]{:S(2)}) collective-permute-start(bf16[16,1024]{1,0:T(8,128)(2,1)S(1)} %add_convert_fusion.refs_0_), channel_id=1, source_target_pairs={{0,96},{32,0},{64,32},{96,64},{1,97},{33,1},{65,33},{97,65},{2,98}... | collective-permute-start | bytes 98312 | tf_op jit(solution)/shard_map/ppermute | solution.py:573
  128.5 16.3 %collective-permute-done.8.refs_1_ = bf16[16,1024]{1,0:T(8,128)(2,1)S(1)} collective-permute-done((bf16[16,1024]{1,0:T(8,128)(2,1)S(1)}, bf16[16,1024]{1,0:T(8,128)(2,1)S(1)}, u32[]{:S(2)}, u32[]{:S(2)}) %collective-permute-start.8) | collective-permute-done | bytes 32800 | tf_op jit(solution)/shard_map/ppermute | solution.py:569
  144.7 3.1 %collective-permute-start.14 = (bf16[16,1024]{1,0:T(8,128)(2,1)S(1)}, bf16[16,1024]{1,0:T(8,128)(2,1)S(1)}, u32[]{:S(2)}, u32[]{:S(2)}) collective-permute-start(bf16[16,1024]{1,0:T(8,128)(2,1)S(1)} %collective-permute-done.8.refs_1_), channel_id=1, source_target_pairs={{0,96},{32,0},{64,32},{96,64},{1,97},{33,1},{65,33},{97,65},{2,98}... | collective-permute-start | bytes 98312 | tf_op jit(solution)/shard_map/ppermute | solution.py:573
  150.0 3.3 %collective-permute-done.12.refs_5_ = bf16[16,1024]{1,0:T(8,128)(2,1)S(1)} collective-permute-done((bf16[16,1024]{1,0:T(8,128)(2,1)S(1)}, bf16[16,1024]{1,0:T(8,128)(2,1)S(1)}, u32[]{:S(2)}, u32[]{:S(2)}) %collective-permute-start.12) | collective-permute-done | bytes 32800 | tf_op jit(solution)/shard_map/ppermute | solution.py:573
  154.4 2.5 %write_filter.1 = f32[256,512]{1,0:T(8,128)} custom-call(s32[2]{0:T(128)} %pad_add_fusion.place, bf16[16,1024]{1,0:T(8,128)(2,1)} %copy-done.13, bf16[16,1024]{1,0:T(8,128)(2,1)} %copy-done.15, bf16[16,1024]{1,0:T(8,128)(2,1)} %copy-done.18, bf16[16,1024]{1,0:T(8,128)(2,1)} %copy-done.21, bf16[16,1024]{1,0:T(8,128)(2,1)} %copy-done.17, ...), custom_call_target="tpu_custom_call" | custom-call | flops 1000000 | bytes 2000000 | tf_op jit(solution)/shard_map/write_filter/pallas_call | solution.py:538
  157.0 1.2 copy-done.2
  158.2 3.7 %write_half.2.refs_0_ = f32[512,4096]{1,0:T(8,128)} custom-call(s32[1]{0:T(128)} %bitcast.16.place, bf16[64,16,1024]{2,1,0:T(8,128)(2,1)} %copy-done.2), custom_call_target="tpu_custom_call" | custom-call | flops 1000000 | bytes 6000000 | tf_op jit(solution)/shard_map/write_half/pallas_call | solution.py:499
  161.9 3.7 %write_half.3 = f32[512,4096]{1,0:T(8,128)} custom-call(s32[1]{0:T(128)S(6)} %sub.14.place, bf16[64,16,1024]{2,1,0:T(8,128)(2,1)} %collective-permute-done.15.mine, f32[512,4096]{1,0:T(8,128)} %write_half.2.refs_0_), custom_call_target="tpu_custom_call", output_to_operand_aliasing={{}: (2, {})} | custom-call | flops 1000000 | bytes 6000000 | tf_op jit(solution)/shard_map/write_half/pallas_call | solution.py:499
  (70 shorter events, 10.5 us)
Async XLA Ops:
  7.0 6.0 %copy-start = (bf16[1,256,4096]{2,1,0:T(8,128)(2,1)S(1)}, bf16[1,256,4096]{2,1,0:T(8,128)(2,1)}, u32[]{:S(2)}) copy-start(bf16[1,256,4096]{2,1,0:T(8,128)(2,1)} %param.15) | copy-start | bytes 6291460
  7.0 23.8 %all-to-all-start = ((bf16[8,320,256]{2,1,0:T(8,128)(2,1)}), bf16[8,320,256]{2,1,0:T(8,128)(2,1)S(1)}, u32[]{:S(2)}, u32[]{:S(2)}) async-start(bf16[8,320,256]{2,1,0:T(8,128)(2,1)} %pack.1), calls=%async_computation | async-start | bytes 2621440 | tf_op jit(solution)/shard_map/all_to_all | solution.py:553
  14.2 27.9 %collective-permute-start.2 = (bf16[256,1024]{1,0:T(8,128)(2,1)}, bf16[256,1024]{1,0:T(8,128)(2,1)S(1)}, u32[]{:S(2)}, u32[]{:S(2)}) collective-permute-start(bf16[256,1024]{1,0:T(8,128)(2,1)} %get-tuple-element.44), channel_id=1, source_target_pairs={{0,40},{8,32},{32,8},{40,0},{1,41},{9,33},{33,9},{41,1},{2,42},{10... | collective-permute-start | bytes 1572872 | tf_op jit(solution)/shard_map/ppermute | solution.py:565
  15.0 27.1 %collective-permute-start = (bf16[256,1024]{1,0:T(8,128)(2,1)}, bf16[256,1024]{1,0:T(8,128)(2,1)S(1)}, u32[]{:S(2)}, u32[]{:S(2)}) collective-permute-start(bf16[256,1024]{1,0:T(8,128)(2,1)} %get-tuple-element.45), channel_id=1, source_target_pairs={{0,32},{32,0},{1,33},{33,1},{2,34},{34,2},{3,35},{35,3},{4,36},{36... | collective-permute-start | bytes 1572872 | tf_op jit(solution)/shard_map/ppermute | solution.py:561
  16.2 26.0 %collective-permute-start.1 = (bf16[256,1024]{1,0:T(8,128)(2,1)}, bf16[256,1024]{1,0:T(8,128)(2,1)S(1)}, u32[]{:S(2)}, u32[]{:S(2)}) collective-permute-start(bf16[256,1024]{1,0:T(8,128)(2,1)} %get-tuple-element.46), channel_id=1, source_target_pairs={{0,8},{8,0},{1,9},{9,1},{2,10},{10,2},{3,11},{11,3},{4,12},{12,4},... | collective-permute-start | bytes 1572872 | tf_op jit(solution)/shard_map/ppermute | solution.py:557
  42.1 14.4 %copy-start.6 = (bf16[256,1024]{1,0:T(8,128)(2,1)}, bf16[256,1024]{1,0:T(8,128)(2,1)S(1)}, u32[]{:S(2)}) copy-start(bf16[256,1024]{1,0:T(8,128)(2,1)S(1)} %collective-permute-done.2.g11) | copy-start | bytes 1572868
  42.1 14.4 %copy-start.7 = (bf16[256,1024]{1,0:T(8,128)(2,1)}, bf16[256,1024]{1,0:T(8,128)(2,1)S(1)}, u32[]{:S(2)}) copy-start(bf16[256,1024]{1,0:T(8,128)(2,1)S(1)} %collective-permute-done.g01) | copy-start | bytes 1572868
  42.1 14.3 %copy-start.8 = (bf16[256,1024]{1,0:T(8,128)(2,1)}, bf16[256,1024]{1,0:T(8,128)(2,1)S(1)}, u32[]{:S(2)}) copy-start(bf16[256,1024]{1,0:T(8,128)(2,1)S(1)} %collective-permute-done.1.g10) | copy-start | bytes 1572868
  42.1 21.0 %all-to-all-start.1 = ((bf16[8,256,256]{2,1,0:T(8,128)(2,1)}), bf16[8,256,256]{2,1,0:T(8,128)(2,1)S(1)}, u32[]{:S(2)}, u32[]{:S(2)}) async-start(bf16[8,256,256]{2,1,0:T(8,128)(2,1)} %conv.1), calls=%async_computation.1 | async-start | bytes 2097152 | tf_op jit(solution)/shard_map/all_to_all | solution.py:553
  58.1 5.0 %collective-permute-start.3 = (bf16[8,4,16,128]{3,2,1,0:T(8,128)(2,1)S(1)}, bf16[8,4,16,128]{3,2,1,0:T(8,128)(2,1)S(1)}, u32[]{:S(2)}, u32[]{:S(2)}) collective-permute-start(bf16[8,4,16,128]{3,2,1,0:T(8,128)(2,1)S(1)} %bitcast.33), channel_id=1, source_target_pairs={{0,32},{32,0},{1,33},{33,1},{2,34},{34,2},{3,35},{35,3},{4,36},{36... | collective-permute-start | bytes 393224 | tf_op jit(solution)/shard_map/ppermute | solution.py:561
  63.1 11.0 %copy-start.12 = (bf16[8,4,16,128]{3,2,1,0:T(8,128)(2,1)}, bf16[8,4,16,128]{3,2,1,0:T(8,128)(2,1)S(1)}, u32[]{:S(2)}) copy-start(bf16[8,4,16,128]{3,2,1,0:T(8,128)(2,1)S(1)} %collective-permute-done.3.lags_z) | copy-start | bytes 393220
  66.0 6.6 %collective-permute-start.4 = (bf16[256,512]{1,0:T(8,128)(2,1)}, bf16[256,512]{1,0:T(8,128)(2,1)S(1)}, u32[]{:S(2)}, u32[]{:S(2)}) collective-permute-start(bf16[256,512]{1,0:T(8,128)(2,1)} %unpack_mixed.1.m00), channel_id=1, source_target_pairs={{0,32},{32,0},{1,33},{33,1},{2,34},{34,2},{3,35},{35,3},{4,36},{36... | collective-permute-start | bytes 786440 | tf_op jit(solution)/shard_map/ppermute | solution.py:561
  67.9 4.7 %collective-permute-start.5 = (bf16[256,512]{1,0:T(8,128)(2,1)}, bf16[256,512]{1,0:T(8,128)(2,1)S(1)}, u32[]{:S(2)}, u32[]{:S(2)}) collective-permute-start(bf16[256,512]{1,0:T(8,128)(2,1)} %unpack_mixed.1.m00), channel_id=1, source_target_pairs={{0,8},{8,0},{1,9},{9,1},{2,10},{10,2},{3,11},{11,3},{4,12},{12,4},... | collective-permute-start | bytes 786440 | tf_op jit(solution)/shard_map/ppermute | solution.py:557
  72.6 1.5 collective-permute-start.6
  79.0 13.2 %copy-start.5 = (bf16[256,512]{1,0:T(8,128)(2,1)S(1)}, bf16[256,512]{1,0:T(8,128)(2,1)}, u32[]{:S(2)}) copy-start(bf16[256,512]{1,0:T(8,128)(2,1)} %unpack_mixed.1.m00) | copy-start | bytes 786436
  79.0 30.6 %all-to-all-start.2 = ((bf16[32,16,1152]{2,1,0:T(8,128)(2,1)}), bf16[32,16,1152]{2,1,0:T(8,128)(2,1)S(1)}, u32[]{:S(2)}, u32[]{:S(2)}) async-start(bf16[32,16,1152]{2,1,0:T(8,128)(2,1)} %partial.1), calls=%async_computation.2 | async-start | bytes 2359296 | tf_op jit(solution)/shard_map/all_to_all | solution.py:553
  113.7 5.7 %copy-start.14 = (f32[16,1024]{1,0:T(8,128)S(1)}, f32[16,1024]{1,0:T(8,128)}, u32[]{:S(2)}) copy-start(f32[16,1024]{1,0:T(8,128)} %get-tuple-element.37) | copy-start | bytes 196612
  113.7 43.2 %all-to-all-start.3 = ((bf16[64,16,1024]{2,1,0:T(8,128)(2,1)}), bf16[64,16,1024]{2,1,0:T(8,128)(2,1)S(1)}, u32[]{:S(2)}, u32[]{:S(2)}) async-start(bf16[64,16,1024]{2,1,0:T(8,128)(2,1)} %get-tuple-element.36), calls=%async_computation.3 | async-start | bytes 4194304 | tf_op jit(solution)/shard_map/all_to_all | solution.py:553
  119.4 1.3 collective-permute-start.7
  120.7 32.8 %copy-start.13 = (bf16[16,1024]{1,0:T(8,128)(2,1)}, bf16[16,1024]{1,0:T(8,128)(2,1)S(1)}, u32[]{:S(2)}) copy-start(bf16[16,1024]{1,0:T(8,128)(2,1)S(1)} %add_convert_fusion.refs_0_) | copy-start | bytes 98308
  120.7 24.0 %collective-permute-start.8 = (bf16[16,1024]{1,0:T(8,128)(2,1)S(1)}, bf16[16,1024]{1,0:T(8,128)(2,1)S(1)}, u32[]{:S(2)}, u32[]{:S(2)}) collective-permute-start(bf16[16,1024]{1,0:T(8,128)(2,1)S(1)} %add_convert_fusion.refs_0_), channel_id=1, source_target_pairs={{0,16},{16,0},{1,17},{17,1},{2,18},{18,2},{3,19},{19,3},{4,20},{20... | collective-permute-start | bytes 98312 | tf_op jit(solution)/shard_map/ppermute | solution.py:569
  123.9 24.6 %collective-permute-start.13 = (bf16[16,1024]{1,0:T(8,128)(2,1)S(1)}, bf16[16,1024]{1,0:T(8,128)(2,1)S(1)}, u32[]{:S(2)}, u32[]{:S(2)}) collective-permute-start(bf16[16,1024]{1,0:T(8,128)(2,1)S(1)} %add_convert_fusion.refs_0_), channel_id=1, source_target_pairs={{0,96},{32,0},{64,32},{96,64},{1,97},{33,1},{65,33},{97,65},{2,98}... | collective-permute-start | bytes 98312 | tf_op jit(solution)/shard_map/ppermute | solution.py:573
  126.9 23.1 %collective-permute-start.11 = (bf16[16,1024]{1,0:T(8,128)(2,1)S(1)}, bf16[16,1024]{1,0:T(8,128)(2,1)S(1)}, u32[]{:S(2)}, u32[]{:S(2)}) collective-permute-start(bf16[16,1024]{1,0:T(8,128)(2,1)S(1)} %add_convert_fusion.refs_0_), channel_id=1, source_target_pairs={{0,64},{32,96},{64,0},{96,32},{1,65},{33,97},{65,1},{97,33},{2,66}... | collective-permute-start | bytes 98312 | tf_op jit(solution)/shard_map/ppermute | solution.py:573
  127.5 22.4 %collective-permute-start.9 = (bf16[16,1024]{1,0:T(8,128)(2,1)S(1)}, bf16[16,1024]{1,0:T(8,128)(2,1)S(1)}, u32[]{:S(2)}, u32[]{:S(2)}) collective-permute-start(bf16[16,1024]{1,0:T(8,128)(2,1)S(1)} %add_convert_fusion.refs_0_), channel_id=1, source_target_pairs={{0,32},{32,64},{64,96},{96,0},{1,33},{33,65},{65,97},{97,1},{2,34}... | collective-permute-start | bytes 98312 | tf_op jit(solution)/shard_map/ppermute | solution.py:573
  144.7 8.9 %copy-start.15 = (bf16[16,1024]{1,0:T(8,128)(2,1)}, bf16[16,1024]{1,0:T(8,128)(2,1)S(1)}, u32[]{:S(2)}) copy-start(bf16[16,1024]{1,0:T(8,128)(2,1)S(1)} %collective-permute-done.8.refs_1_) | copy-start | bytes 98308
  144.7 5.2 %collective-permute-start.14 = (bf16[16,1024]{1,0:T(8,128)(2,1)S(1)}, bf16[16,1024]{1,0:T(8,128)(2,1)S(1)}, u32[]{:S(2)}, u32[]{:S(2)}) collective-permute-start(bf16[16,1024]{1,0:T(8,128)(2,1)S(1)} %collective-permute-done.8.refs_1_), channel_id=1, source_target_pairs={{0,96},{32,0},{64,32},{96,64},{1,97},{33,1},{65,33},{97,65},{2,98}... | collective-permute-start | bytes 98312 | tf_op jit(solution)/shard_map/ppermute | solution.py:573
  147.8 5.4 %collective-permute-start.12 = (bf16[16,1024]{1,0:T(8,128)(2,1)S(1)}, bf16[16,1024]{1,0:T(8,128)(2,1)S(1)}, u32[]{:S(2)}, u32[]{:S(2)}) collective-permute-start(bf16[16,1024]{1,0:T(8,128)(2,1)S(1)} %collective-permute-done.8.refs_1_), channel_id=1, source_target_pairs={{0,64},{32,96},{64,0},{96,32},{1,65},{33,97},{65,1},{97,33},{2,66}... | collective-permute-start | bytes 98312 | tf_op jit(solution)/shard_map/ppermute | solution.py:573
  148.4 5.1 %copy-start.16 = (bf16[16,1024]{1,0:T(8,128)(2,1)}, bf16[16,1024]{1,0:T(8,128)(2,1)S(1)}, u32[]{:S(2)}) copy-start(bf16[16,1024]{1,0:T(8,128)(2,1)S(1)} %collective-permute-done.13.refs_6_) | copy-start | bytes 98308
  148.4 5.1 %collective-permute-start.10 = (bf16[16,1024]{1,0:T(8,128)(2,1)S(1)}, bf16[16,1024]{1,0:T(8,128)(2,1)S(1)}, u32[]{:S(2)}, u32[]{:S(2)}) collective-permute-start(bf16[16,1024]{1,0:T(8,128)(2,1)S(1)} %collective-permute-done.8.refs_1_), channel_id=1, source_target_pairs={{0,32},{32,64},{64,96},{96,0},{1,33},{33,65},{65,97},{97,1},{2,34}... | collective-permute-start | bytes 98312 | tf_op jit(solution)/shard_map/ppermute | solution.py:573
  149.9 3.7 %copy-start.17 = (bf16[16,1024]{1,0:T(8,128)(2,1)}, bf16[16,1024]{1,0:T(8,128)(2,1)S(1)}, u32[]{:S(2)}) copy-start(bf16[16,1024]{1,0:T(8,128)(2,1)S(1)} %collective-permute-done.11.refs_4_) | copy-start | bytes 98308
  149.9 3.7 %copy-start.18 = (bf16[16,1024]{1,0:T(8,128)(2,1)}, bf16[16,1024]{1,0:T(8,128)(2,1)S(1)}, u32[]{:S(2)}) copy-start(bf16[16,1024]{1,0:T(8,128)(2,1)S(1)} %collective-permute-done.9.refs_2_) | copy-start | bytes 98308
  156.9 5.0 %collective-permute-start.15 = (bf16[64,16,1024]{2,1,0:T(8,128)(2,1)S(1)}, bf16[64,16,1024]{2,1,0:T(8,128)(2,1)}, u32[]{:S(2)}, u32[]{:S(2)}) collective-permute-start(bf16[64,16,1024]{2,1,0:T(8,128)(2,1)S(1)} %all-to-all-done.3.mine), channel_id=1, source_target_pairs={{0,8},{8,0},{1,9},{9,1},{2,10},{10,2},{3,11},{11,3},{4,12},{12,4},... | collective-permute-start | bytes 6291464 | tf_op jit(solution)/shard_map/ppermute | solution.py:557
  (11 other events, 16.4 us)

commit v8 on v7

--- a/solution.py
+++ b/solution.py
@@ -13,7 +13,6 @@
 F32 = jnp.float32
 BLOCK = 256
 HALF = 64
-SENT_ROWS = BLOCK + 64
 SEQ = ("x", "yl")
 MOST = ("zh", "yh") + SEQ
 CHIPS = ("zh", "zl", "yh") + SEQ
@@ -46,11 +45,8 @@
     return pltpu.roll(x, HALF, 1)
 
 
-def pack_kernel(streams, out_grad, weight, filt, packed, total):
-    step = pl.program_id(0)
-    low = low_lanes(BLOCK)
-
-    @pl.when(step == 0)
+def grad_kernel(out_grad, weight, total):
+    @pl.when(pl.program_id(0) == 0)
     def _():
         total[...] = jnp.zeros_like(total)
 
@@ -58,49 +54,54 @@
         out_grad[...], weight[...], (((1,), (1,)), ((), ())), preferred_element_type=F32
     )
 
-    def put(q, tile, a, b):
-        lanes = slice(128 * tile, 128 * tile + 128)
-        packed[2 * q, 0:BLOCK, lanes] = jnp.where(low, a, turned(b)).astype(BF)
-        packed[2 * q + 1, 0:BLOCK, lanes] = jnp.where(low, turned(a), b).astype(BF)
-
+
+def grad_of_mixed(out_grad, weight):
+    steps = 4
+    wide = out_grad.shape[1] // steps
+    return pl.pallas_call(
+        grad_kernel,
+        grid=(steps,),
+        in_specs=[
+            pl.BlockSpec((BLOCK, wide), lambda k: (0, k)),
+            pl.BlockSpec((512, wide), lambda k: (0, k)),
+        ],
+        out_specs=pl.BlockSpec((BLOCK, 512), lambda k: (0, 0)),
+        out_shape=jax.ShapeDtypeStruct((BLOCK, 512), F32),
+        cost_estimate=pl.CostEstimate(flops=10**9, bytes_accessed=7 * 10**6, transcendentals=0),
+        name="grad_of_mixed",
+    )(out_grad, weight)
+
+
+def pack_kernel(streams, edge, grad, filt, short, packed, gate_out, pad):
+    low = low_lanes(BLOCK)
+    pad[0:8] = edge[...].astype(F32)
+    pad[8:] = streams[0].astype(F32)
     for q in range(4):
         lanes = slice(128 * q, 128 * q + 128)
-
-        @pl.when(step == q)
-        def _(q=q, lanes=lanes):
-            put(q, 0, streams[0, :, lanes].astype(F32), streams[1, :, lanes].astype(F32))
-            low64 = low_lanes(64)
-            for n in range(2):
-                a = filt[128 * n : 128 * n + 64, lanes]
-                b = filt[128 * n + 64 : 128 * n + 128, lanes]
-                there = slice(128 * n, 128 * n + 128)
-                packed[2 * q, BLOCK:, there] = jnp.where(low64, a, turned(b)).astype(BF)
-                packed[2 * q + 1, BLOCK:, there] = jnp.where(low64, turned(a), b).astype(BF)
-
-    @pl.when(step == pl.num_programs(0) - 1)
-    def _():
-        for q in range(4):
-            lanes = slice(128 * q, 128 * q + 128)
-            put(q, 1, streams[2, :, lanes].astype(F32), total[:, lanes])
-
-
-def pack(streams, out_grad, weight, filt):
-    steps = 4
-    wide = out_grad.shape[1] // steps
+        gate = sum(
+            short[j : j + 1, lanes] * pad[8 - j : 8 - j + BLOCK, lanes] for j in range(3)
+        )
+        gate_out[:, lanes] = gate
+        pairs = (
+            (streams[1, :, lanes].astype(F32), streams[2, :, lanes].astype(F32)),
+            (grad[:, lanes] * gate, filt[:, lanes]),
+        )
+        for n, (a, b) in enumerate(pairs):
+            there = slice(128 * n, 128 * n + 128)
+            packed[2 * q, :, there] = jnp.where(low, a, turned(b)).astype(BF)
+            packed[2 * q + 1, :, there] = jnp.where(low, turned(a), b).astype(BF)
+
+
+def pack(streams, edge, grad, filt, short):
     return pl.pallas_call(
         pack_kernel,
-        grid=(steps,),
-        in_specs=[
-            pl.BlockSpec((3, BLOCK, 512), lambda k: (0, 0, 0)),
-            pl.BlockSpec((BLOCK, wide), lambda k: (0, k)),
-            pl.BlockSpec((512, wide), lambda k: (0, k)),
-            pl.BlockSpec((BLOCK, 512), lambda k: (0, 0)),
+        out_shape=[
+            jax.ShapeDtypeStruct((8, BLOCK, 256), BF),
+            jax.ShapeDtypeStruct((BLOCK, 512), F32),
         ],
-        out_specs=pl.BlockSpec((8, SENT_ROWS, 256), lambda k: (0, 0, 0)),
-        out_shape=jax.ShapeDtypeStruct((8, SENT_ROWS, 256), BF),
-        scratch_shapes=[pltpu.VMEM((BLOCK, 512), F32)],
+        scratch_shapes=[pltpu.VMEM((8 + BLOCK, 512), F32)],
         name="pack",
-    )(streams, out_grad, weight, filt)
+    )(streams, edge, grad, filt, short)
 
 
 def split(x):
@@ -135,23 +136,23 @@
     return pair, gain
 
 
-def shorten(got, pair, sa_pad, sv_pad, use):
-    w_a, w_v = pair(0, 1), pair(2, None)
-    sa_pad[0:8] = jnp.zeros((8, 128), F32)
-    sv_pad[0:8] = jnp.zeros((8, 128), F32)
+def prepare(got, pair, pad, prod, gates=None):
+    taps = pair(1, 2)
+    low = low_lanes(BLOCK)
+    pad[0:8] = jnp.zeros((8, 128), F32)
 
     def load(b, carry):
         rows = pl.ds(pl.multiple_of(8 + BLOCK * b, 8), BLOCK)
-        sa_pad[rows] = got[b, 0:BLOCK, 0:128].astype(F32)
-        sv_pad[rows] = got[b, 0:BLOCK, 128:256].astype(F32)
+        pad[rows] = got[b, :, 0:128].astype(F32)
         return carry
 
     lax.fori_loop(0, 8, load, 0)
     for b in range(8):
         start = 8 + BLOCK * b
-        a = sum(w_a[j] * sa_pad[start - j : start - j + BLOCK] for j in range(3))
-        v = sum(w_v[j] * sv_pad[start - j : start - j + BLOCK] for j in range(3))
-        use(b, a, v)
+        s = sum(taps[j] * pad[start - j : start - j + BLOCK] for j in range(3))
+        if gates is not None:
+            gates[b] = s
+        prod[b] = jnp.where(low, s * turned(s), turned(got[b, :, 128:256].astype(F32)))
 
 
 def spectra(prod, ahead_h, ahead_l, spec):
@@ -206,22 +207,16 @@
 def conv_kernel(
     place, got, short, skip, ahead_h, ahead_l, back_h, back_l,
     sent,
-    sa_pad, sv_pad, sa, sv, prod, spec, fspec, res, time, u_pad, x_pad,
+    pad, prod, gates, spec, fspec, res, time, after,
 ):
     low = low_lanes(BLOCK)
-    low64 = low_lanes(64)
     sigma = jnp.where(low, 1.0, -1.0)
     pair, gain = weights(place, short, skip)
 
     def filters(n, carry):
         def blocks(b):
-            parts = []
-            for t in range(2):
-                x = got[b, BLOCK:, 128 * t : 128 * t + 128].astype(F32)
-                y = got[b + 1, BLOCK:, 128 * t : 128 * t + 128].astype(F32)
-                parts.append(jnp.where(low64, x, turned(y)))
-                parts.append(jnp.where(low64, turned(x), y))
-            return jnp.concatenate(parts, axis=0).astype(BF)
+            x, y = got[b, :, 128:256].astype(F32), got[b + 1, :, 128:256].astype(F32)
+            return jnp.where(low, turned(x), y).astype(BF)
 
         f = jnp.concatenate([blocks(4 * n), blocks(4 * n + 2)], axis=1)
         out = mm(ahead_h[...], f) + mm(ahead_l[...], f)
@@ -234,13 +229,7 @@
         return carry
 
     lax.fori_loop(0, 2, filters, 0)
-
-    def keep(b, a, v):
-        sa[b] = a
-        sv[b] = v
-        prod[b] = turned(a) * v
-
-    shorten(got, pair, sa_pad, sv_pad, keep)
+    prepare(got, pair, pad, prod, gates)
     spectra(prod, ahead_h, ahead_l, spec)
 
     def multiply(re, im, own, both):
@@ -261,36 +250,31 @@
 
     lax.fori_loop(0, 4, invert, 0)
 
+    low128 = low_lanes(128)
+
     def gate(b, carry):
         t = jnp.where(low, time[b], time[7 - b]) + gain * prod[b]
         rows = pl.ds(pl.multiple_of(BLOCK * b, 8), BLOCK)
-        u_pad[rows] = turned(t) * sv[b]
-        x_pad[rows] = t * sa[b]
+        after[rows] = jnp.where(low, turned(t), t) * turned(gates[b])
+        sent[b, BLOCK:] = jnp.where(low128, t[0:128], turned(t[128:256])).astype(BF)
         return carry
 
     lax.fori_loop(0, 8, gate, 0)
-    u_pad[8 * BLOCK :] = jnp.zeros((8, 128), F32)
-    x_pad[8 * BLOCK :] = jnp.zeros((8, 128), F32)
-    w_u, w_x = pair(1, 0), pair(None, 2)
+    after[8 * BLOCK :] = jnp.zeros((8, 128), F32)
+    taps = pair(1, 2)
     for b in range(8):
         start = BLOCK * b
-        y = sum(w_u[j] * u_pad[start + j : start + j + BLOCK] for j in range(3))
-        sent[b, :, 0:128] = y.astype(BF)
-        y = sum(w_x[j] * x_pad[start + j : start + j + BLOCK] for j in range(3))
-        sent[b, :, 128:256] = y.astype(BF)
+        y = sum(taps[j] * after[start + j : start + j + BLOCK] for j in range(3))
+        sent[b, 0:BLOCK] = y.astype(BF)
 
 
 def lag_kernel(
     place, got, short, skip, ahead_h, ahead_l, back_h, back_l,
     lags,
-    sa_pad, sv_pad, prod, spec, lres,
+    pad, prod, spec, lres,
 ):
     pair, _ = weights(place, short, skip)
-
-    def keep(b, a, v):
-        prod[b] = turned(a) * v
-
-    shorten(got, pair, sa_pad, sv_pad, keep)
+    prepare(got, pair, pad, prod)
     spectra(prod, ahead_h, ahead_l, spec)
     zero = jnp.zeros((8, 128), F32)
     low8 = low_lanes(8)
@@ -336,7 +320,7 @@
             num_scalar_prefetch=1,
             grid=(1,),
             in_specs=[
-                full(8, SENT_ROWS, 256),
+                full(8, BLOCK, 256),
                 pl.BlockSpec((9, 128), lambda n, p: (0, p[0] // 2)),
                 pl.BlockSpec((1, 128), lambda n, p: (0, p[0] // 2)),
             ]
@@ -344,7 +328,7 @@
             out_specs=[full(*shape) for shape, _ in outputs],
             scratch_shapes=[
                 pltpu.VMEM(shape, dtype)
-                for shape, dtype in [((8 + 8 * BLOCK, 128), F32)] * 2 + scratch
+                for shape, dtype in [((8 + 8 * BLOCK, 128), F32)] + scratch
             ],
         ),
         out_shape=[jax.ShapeDtypeStruct(shape, dtype) for shape, dtype in outputs],
@@ -364,9 +348,8 @@
 
 def conv(place, got, short, skip):
     inputs = (place, got, short, skip, *(jnp.asarray(t) for t in tables()))
-    outputs = [((8, BLOCK, 256), BF)]
-    pad = ((8 * BLOCK + 8, 128), F32)
-    scratch = [BLOCKS, BLOCKS, BLOCKS, BINS, BINS, BINS, BLOCKS, pad, pad]
+    outputs = [((8, 384, 128), BF)]
+    scratch = [BLOCKS, BLOCKS, BINS, BINS, BINS, BLOCKS, ((8 * BLOCK + 8, 128), F32)]
     return on_channels(conv_kernel, "conv", inputs, TABLES, outputs, scratch, None)[0]
 
 
@@ -378,45 +361,66 @@
     return on_channels(lag_kernel, "lag_sums", inputs, TABLES, outputs, scratch, cost)[0]
 
 
-def spread(got, there, first, second, low):
+def convolved(got, q, low128):
+    a, b = got[2 * q, -128:].astype(F32), got[2 * q + 1, -128:].astype(F32)
+    return jnp.where(low128, a, turned(b)), jnp.where(low128, turned(a), b)
+
+
+def mixed_kernel(got, gate_out, grad, mixed, head):
+    low128 = low_lanes(128)
     for q in range(4):
         lanes = slice(128 * q, 128 * q + 128)
-        a = got[2 * q, 0:BLOCK, there].astype(F32)
-        b = got[2 * q + 1, 0:BLOCK, there].astype(F32)
-        if first is not None:
-            first[:, lanes] = jnp.where(low, a, turned(b)).astype(BF)
-        if second is not None:
-            second[:, lanes] = jnp.where(low, turned(a), b).astype(BF)
-
-
-def mixed_kernel(got, mixed):
-    spread(got, slice(0, 128), mixed, None, low_lanes(BLOCK))
-
-
-def unpack_mixed(got):
+        first, second = convolved(got, q, low128)
+        mixed[0:128, lanes] = (gate_out[0:128, lanes] * first).astype(BF)
+        mixed[128:256, lanes] = (gate_out[128:256, lanes] * second).astype(BF)
+        head[:, lanes] = grad[:, lanes] * first[0:8]
+
+
+def unpack_mixed(got, gate_out, grad):
     return pl.pallas_call(
         mixed_kernel,
         grid=(1,),
-        in_specs=[pl.BlockSpec((8, BLOCK, 128), lambda n: (0, 0, 1))],
-        out_specs=pl.BlockSpec((BLOCK, 512), lambda n: (0, 0)),
-        out_shape=jax.ShapeDtypeStruct((BLOCK, 512), BF),
+        in_specs=[
+            pl.BlockSpec((8, 128, 128), lambda n: (0, 2, 0)),
+            pl.BlockSpec((BLOCK, 512), lambda n: (0, 0)),
+            pl.BlockSpec((8, 512), lambda n: (0, 0)),
+        ],
+        out_specs=[
+            pl.BlockSpec((BLOCK, 512), lambda n: (0, 0)),
+            pl.BlockSpec((8, 512), lambda n: (0, 0)),
+        ],
+        out_shape=[
+            jax.ShapeDtypeStruct((BLOCK, 512), BF),
+            jax.ShapeDtypeStruct((8, 512), F32),
+        ],
         name="unpack_mixed",
-    )(got)
-
-
-def grads_kernel(got, grads):
-    low = low_lanes(BLOCK)
-    spread(got, slice(0, 128), grads.at[1], grads.at[0], low)
-    spread(got, slice(128, 256), None, grads.at[2], low)
-
-
-def unpack_grads(got):
+    )(got, gate_out, grad)
+
+
+def grads_kernel(got, grad, tail, short, grads, pad):
+    low, low128 = low_lanes(BLOCK), low_lanes(128)
+    pad[BLOCK:] = tail[...]
+    for q in range(4):
+        lanes = slice(128 * q, 128 * q + 128)
+        first, second = convolved(got, q, low128)
+        pad[0:128, lanes] = grad[0:128, lanes] * first
+        pad[128:256, lanes] = grad[128:256, lanes] * second
+        a, b = got[2 * q, 0:BLOCK].astype(F32), got[2 * q + 1, 0:BLOCK].astype(F32)
+        grads[1, :, lanes] = jnp.where(low, a, turned(b)).astype(BF)
+        grads[2, :, lanes] = jnp.where(low, turned(a), b).astype(BF)
+        grads[0, :, lanes] = sum(
+            short[j : j + 1, lanes] * pad[j : j + BLOCK, lanes] for j in range(3)
+        ).astype(BF)
+
+
+def unpack_grads(got, grad, tail, short):
     return pl.pallas_call(
         grads_kernel,
         out_shape=jax.ShapeDtypeStruct((3, BLOCK, 512), BF),
+        scratch_shapes=[pltpu.VMEM((BLOCK + 8, 512), F32)],
         cost_estimate=pl.CostEstimate(flops=10**6, bytes_accessed=2 * 10**6, transcendentals=0),
         name="unpack_grads",
-    )(got)
+    )(got, grad, tail, short)
 
 
 def partial_kernel(place, m00, m01, m10, m11, g00, g01, g10, g11, lags, lags_z, packed):
@@ -557,6 +561,10 @@
     return lax.ppermute(x, "c", [(0, 1), (1, 0)])
 
 
+def along(x, step):
+    return lax.ppermute(x, SEQ, [(n, n + step) for n in range(8) if 0 <= n + step < 8])
+
+
 def above(x):
     return lax.ppermute(x, "zl", [(0, 1), (1, 0)])
 
@@ -589,8 +597,13 @@
         across(quarter(1 - core, side)),
         opposite(quarter(1 - core, 1 - side)),
     )
-    got = exchange(pack(streams[:, 0], grad, out_weight, long_filter), SEQ)
-    channels = (seq[None], got, short_filter.reshape(9, 512), skip_gain.reshape(1, 512))
+    short = short_filter.reshape(9, 512)
+    edge = along(streams[0, 0, BLOCK - 8 :], 1)
+    grad_mixed = grad_of_mixed(grad, out_weight)
+    edge, grad_mixed = lax.optimization_barrier((edge, grad_mixed))
+    packed, gate_out = pack(streams[:, 0], edge, grad_mixed, long_filter, short)
+    got = exchange(packed, SEQ)
+    channels = (seq[None], got, short, skip_gain.reshape(1, 512))
     sent = conv(*channels)
     sent, got, grads = lax.optimization_barrier((sent, got, grads))
     channels = (channels[0], got) + channels[2:]
@@ -602,14 +615,14 @@
     lags_own, lags_z = of_side(side), above(of_side(1 - side))
     back = exchange(sent, SEQ)
     back, lags_own, lags_z = lax.optimization_barrier((back, lags_own, lags_z))
-    m00 = unpack_mixed(back)
+    m00, head = unpack_mixed(back, gate_out, grad_mixed)
     m01, m10 = above(m00), across(m00)
     mixed = (m00, m01, m10, across(m01))
     part = partial((2 * core + side)[None], mixed, grad, grads, lags_own, lags_z)
-    part, m00, back = lax.optimization_barrier((part, m00, back))
+    part, m00, back, head = lax.optimization_barrier((part, m00, back, head))
     part = exchange(part, MOST)
     layer_out = jnp.dot(m00, out_weight, preferred_element_type=F32).astype(BF)
-    grad_streams = unpack_grads(back)
+    grad_streams = unpack_grads(back, grad_mixed, along(head, -1), short)
     part, layer_out, grad_streams = lax.optimization_barrier((part, layer_out, grad_streams))
     rows, lags = reduce(part, scale)
     rows, lags = lax.optimization_barrier((rows, lags))

time: 167 us -> 175 us (1.048)
  starting transfers between devices: 46.3 us -> 53.1 us
  waiting for transfers between devices: 57 us -> 54.3 us
  Pallas kernels: 46.6 us -> 48.6 us
  local copies, waits for them, and re-layouts: 9.44 us -> 11.2 us
    all_to_all x4, waiting for transfers between devices: 26.6 us -> 12.2 us  [exchange(): return lax.all_to_all(x, axes, 0, 0, tiled=True)]
    ppermute x0 -> x2, starting transfers between devices: none -> 6.84 us  [along(): lax.ppermute(x, SEQ, [(n, n + step) for n in range(8) if 0 <= n + step < 8])]
    ppermute x0 -> x2, waiting for transfers between devices: none -> 6.81 us  [along(): lax.ppermute(x, SEQ, [(n, n + step) for n in range(8) if 0 <= n + step < 8])]
    ppermute x3, waiting for transfers between devices: 7.7 us -> 12.7 us  [above(): return lax.ppermute(x, 'zl', [(0, 1), (1, 0)])]
    all_to_all x4, starting transfers between devices: 28 us -> 30.8 us  [exchange(): return lax.all_to_all(x, axes, 0, 0, tiled=True)]
    ppermute x3, starting transfers between devices: 5 us -> 2.51 us  [above(): return lax.ppermute(x, 'zl', [(0, 1), (1, 0)])]
    pallas_call x2 -> x3, Pallas kernels: 8.28 us -> 10.2 us  [the longest x1 5.17 us: grad_of_mixed(): pl.pallas_call(grad_kernel, grid=(steps,), in_specs=[pl.BlockSpec((BLOCK,...]
    unnamed x46 -> x52, local copies, waits for them, and re-layouts: 5.96 us -> 7.03 us
  transfers between devices with their start and end apart: 20 -> 22, of which waited for: 9 -> 11; matrix products, arithmetic and copies ran while one was open for 5% -> 5% of each run, Pallas kernels for 17% -> 19%
where the time goes in v8:
time: 175 us; the launch traced here: 174 us
  waiting for transfers between devices  54.3 us (31%)
  starting transfers between devices  53.1 us (30%)
  Pallas kernels  48.6 us (28%)
  local copies, waits for them, and re-layouts  11.2 us (6%)
  matrix products  4.77 us (3%)
    all_to_all x4, starting transfers between devices, exchange(): return lax.all_to_all(x, axes, 0, 0, tiled=True)  30.8 us
    pallas_call x2, Pallas kernels, on_channels(): pl.pallas_call(kernel, grid_spec=pltpu.PrefetchScalarGridSpec(num_scalar_...  18.6 us
    ppermute x1, waiting for transfers between devices, gathered(): pair = (lags, lax.ppermute(lags, 'yh', [(0, 1), (1, 0)]))  16.2 us
    ppermute x3, waiting for transfers between devices, above(): return lax.ppermute(x, 'zl', [(0, 1), (1, 0)])  12.7 us
    all_to_all x4, waiting for transfers between devices, exchange(): return lax.all_to_all(x, axes, 0, 0, tiled=True)  12.2 us
    ppermute x6, starting transfers between devices, gathered(): out += [lax.ppermute(part, ('zh', 'zl'), route) for part in pair]  9.1 us
    pallas_call x2, Pallas kernels, write_half(): pl.pallas_call(half_kernel, grid_spec=pltpu.PrefetchScalarGridSpec(num_sc...  7.39 us
    unnamed x52, local copies, waits for them, and re-layouts  7.03 us
  transfers between devices with their start and end apart: 22, of which 11 were waited for; matrix products, arithmetic and copies ran while one was open for 5% of the time, Pallas kernels for 19%

profile of v8, /device:TPU:2, one launch (start us, length us, event | category | flops | bytes accessed | tf_op | source)
XLA Modules:
  0.0 173.6 jit_solution(2332125332444179835)
XLA Ops:
  1.3 3.5 %collective-permute-start = (bf16[8,512]{1,0:T(8,128)(2,1)S(1)}, bf16[8,512]{1,0:T(8,128)(2,1)S(1)}, u32[]{:S(2)}, u32[]{:S(2)}) collective-permute-start(bf16[8,512]{1,0:T(8,128)(2,1)S(1)} %slice_bitcast_fusion), channel_id=1, source_target_pairs={{0,1},{1,2},{2,3},{3,4},{4,5},{5,6},{6,7},{8,9},{9,10},{10,11},{11... | collective-permute-start | bytes 24584 | tf_op jit(solution)/shard_map/ppermute | solution.py:565
  4.8 5.2 %grad_of_mixed.1.grad = f32[256,512]{1,0:T(8,128)} custom-call(bf16[256,4096]{1,0:T(8,128)(2,1)} %bitcast.29, bf16[512,4096]{1,0:T(8,128)(2,1)} %weight.1), custom_call_target="tpu_custom_call" | custom-call | flops 1000000000 | bytes 7000000 | tf_op jit(solution)/shard_map/grad_of_mixed/pallas_call | solution.py:61
  11.2 3.1 %pack.1 = (bf16[8,256,256]{2,1,0:T(8,128)(2,1)}, f32[256,512]{1,0:T(8,128)}) custom-call(bf16[3,256,512]{2,1,0:T(8,128)(2,1)} %bitcast.31, bf16[8,512]{1,0:T(8,128)(2,1)} %copy-done.24, f32[256,512]{1,0:T(8,128)} %grad_of_mixed.1.grad, f32[256,512]{1,0:T(8,128)} %filt.1, f32[9,512]{1,0:T(8,128)} %reshape.28.short), custom_call_target="tpu_custom_call" | custom-call | tf_op jit(solution)/shard_map/pack/pallas_call | solution.py:96
  14.3 5.3 %all-to-all-start = ((bf16[8,256,256]{2,1,0:T(8,128)(2,1)}), bf16[8,256,256]{2,1,0:T(8,128)(2,1)S(1)}, u32[]{:S(2)}, u32[]{:S(2)}) async-start(bf16[8,256,256]{2,1,0:T(8,128)(2,1)} %get-tuple-element.31), calls=%async_computation | async-start | bytes 2097152 | tf_op jit(solution)/shard_map/all_to_all | solution.py:557
  21.4 1.4 collective-permute-start.1
  23.0 10.6 %all-to-all-done.got = bf16[8,256,256]{2,1,0:T(8,128)(2,1)S(1)} async-done(((bf16[8,256,256]{2,1,0:T(8,128)(2,1)}), bf16[8,256,256]{2,1,0:T(8,128)(2,1)S(1)}, u32[]{:S(2)}, u32[]{:S(2)}) %all-to-all-start) | async-done | bytes 1048608 | tf_op jit(solution)/shard_map/all_to_all | solution.py:557
  34.5 10.0 %conv.1 = bf16[8,384,128]{2,1,0:T(8,128)(2,1)} custom-call(s32[1]{0:T(128)} %bitcast.1.place, bf16[8,256,256]{2,1,0:T(8,128)(2,1)} %copy-done.4, f32[9,512]{1,0:T(8,128)} %reshape.28.short, f32[1,512]{1,0:T(1,128)} %bitcast.36, bf16[512,256]{1,0:T(8,128)(2,1)} %constant.54.clone.ahead_h, bf16[512,256]{1,0:T(8,128)(2,1)} %constant.55.clone.ahead_l, ...), custom_call_target="tpu_custom_call" | custom-call | tf_op jit(solution)/shard_map/conv/pallas_call | solution.py:317
  44.5 2.1 %collective-permute-done.1.g01 = bf16[256,1024]{1,0:T(8,128)(2,1)S(1)} collective-permute-done((bf16[256,1024]{1,0:T(8,128)(2,1)}, bf16[256,1024]{1,0:T(8,128)(2,1)S(1)}, u32[]{:S(2)}, u32[]{:S(2)}) %collective-permute-start.1) | collective-permute-done | bytes 524320 | tf_op jit(solution)/shard_map/ppermute | solution.py:569
  46.6 5.7 %all-to-all-start.1 = ((bf16[8,384,128]{2,1,0:T(8,128)(2,1)}), bf16[8,384,128]{2,1,0:T(8,128)(2,1)S(1)}, u32[]{:S(2)}, u32[]{:S(2)}) async-start(bf16[8,384,128]{2,1,0:T(8,128)(2,1)} %conv.1), calls=%async_computation.1 | async-start | bytes 1572864 | tf_op jit(solution)/shard_map/all_to_all | solution.py:557
  52.3 8.7 %lag_sums.1 = bf16[8,8,16,128]{3,2,1,0:T(8,128)(2,1)} custom-call(s32[1]{0:T(128)} %bitcast.1.place, bf16[8,256,256]{2,1,0:T(8,128)(2,1)} %copy-done.4, f32[9,512]{1,0:T(8,128)} %reshape.28.short, f32[1,512]{1,0:T(1,128)} %bitcast.37, bf16[512,256]{1,0:T(8,128)(2,1)} %constant.54.clone.ahead_h, bf16[512,256]{1,0:T(8,128)(2,1)} %constant.55.clone.ahead_l, ...), custom_call_target="tpu_custom_call" | custom-call | flops 2000000000 | bytes 3000000 | tf_op jit(solution)/shard_map/lag_sums/pallas_call | solution.py:317
  61.0 1.6 constant_dynamic-slice_fusion
  62.9 4.7 %collective-permute-done.4.lags_z = bf16[8,4,16,128]{3,2,1,0:T(8,128)(2,1)S(1)} collective-permute-done((bf16[8,4,16,128]{3,2,1,0:T(8,128)(2,1)S(1)}, bf16[8,4,16,128]{3,2,1,0:T(8,128)(2,1)S(1)}, u32[]{:S(2)}, u32[]{:S(2)}) %collective-permute-start.4) | collective-permute-done | bytes 131104 | tf_op jit(solution)/shard_map/ppermute | solution.py:569
  68.6 2.0 %unpack_mixed.1 = (bf16[256,512]{1,0:T(8,128)(2,1)}, f32[8,512]{1,0:T(8,128)}) custom-call(bf16[8,384,128]{2,1,0:T(8,128)(2,1)} %copy-done.2, f32[256,512]{1,0:T(8,128)} %get-tuple-element.35.gate_out, f32[256,512]{1,0:T(8,128)} %grad_of_mixed.1.grad), custom_call_target="tpu_custom_call" | custom-call | tf_op jit(solution)/shard_map/unpack_mixed/pallas_call | solution.py:380
  71.3 5.9 %collective-permute-done.5.m01 = bf16[256,512]{1,0:T(8,128)(2,1)S(1)} collective-permute-done((bf16[256,512]{1,0:T(8,128)(2,1)}, bf16[256,512]{1,0:T(8,128)(2,1)S(1)}, u32[]{:S(2)}, u32[]{:S(2)}) %collective-permute-start.5) | collective-permute-done | bytes 262176 | tf_op jit(solution)/shard_map/ppermute | solution.py:569
  77.3 1.5 collective-permute-done.7.m11
  79.5 4.2 %partial.1 = bf16[32,16,1152]{2,1,0:T(8,128)(2,1)} custom-call(s32[1]{0:T(128)} %bitcast.place, bf16[256,512]{1,0:T(8,128)(2,1)} %get-tuple-element.44.m00, bf16[256,512]{1,0:T(8,128)(2,1)} %copy-done.9, bf16[256,512]{1,0:T(8,128)(2,1)} %copy-done.10, bf16[256,512]{1,0:T(8,128)(2,1)} %copy-done.11, bf16[256,4096]{1,0:T(8,128)(2,1)} %bitcast.30, ...), custom_call_target="tpu_custom_call" | custom-call | tf_op jit(solution)/shard_map/partial/pallas_call | solution.py:443
  83.7 11.0 %all-to-all-start.2 = ((bf16[32,16,1152]{2,1,0:T(8,128)(2,1)}), bf16[32,16,1152]{2,1,0:T(8,128)(2,1)S(1)}, u32[]{:S(2)}, u32[]{:S(2)}) async-start(bf16[32,16,1152]{2,1,0:T(8,128)(2,1)} %partial.1), calls=%async_computation.2 | async-start | bytes 2359296 | tf_op jit(solution)/shard_map/all_to_all | solution.py:557
  94.7 3.4 %collective-permute-start.8 = (f32[8,512]{1,0:T(8,128)S(1)}, f32[8,512]{1,0:T(8,128)S(1)}, u32[]{:S(2)}, u32[]{:S(2)}) collective-permute-start(f32[8,512]{1,0:T(8,128)S(1)} %copy-done.25), channel_id=1, source_target_pairs={{1,0},{2,1},{3,2},{4,3},{5,4},{6,5},{7,6},{9,8},{10,9},{11,10},{12... | collective-permute-start | bytes 49160 | tf_op jit(solution)/shard_map/ppermute | solution.py:565
  98.1 4.8 %convolution_convert_fusion = bf16[256,4096]{1,0:T(8,128)(2,1)} fusion(bf16[256,512]{1,0:T(8,128)(2,1)S(1)} %copy-done.8, bf16[512,4096]{1,0:T(8,128)(2,1)} %weight.1), kind=kOutput, calls=%fused_computation | convolution fusion | flops 1074790400 | bytes 6553600 | tf_op jit(solution)/shard_map/dot_general | solution.py:624
  102.8 6.8 %collective-permute-done.8.tail = f32[8,512]{1,0:T(8,128)S(1)} collective-permute-done((f32[8,512]{1,0:T(8,128)S(1)}, f32[8,512]{1,0:T(8,128)S(1)}, u32[]{:S(2)}, u32[]{:S(2)}) %collective-permute-start.8) | collective-permute-done | bytes 16416 | tf_op jit(solution)/shard_map/ppermute | solution.py:565
  110.3 2.7 %unpack_grads.1 = bf16[3,256,512]{2,1,0:T(8,128)(2,1)} custom-call(bf16[8,384,128]{2,1,0:T(8,128)(2,1)} %copy-done.2, f32[256,512]{1,0:T(8,128)} %grad_of_mixed.1.grad, f32[8,512]{1,0:T(8,128)} %copy-done.23, f32[9,512]{1,0:T(8,128)} %reshape.28.short), custom_call_target="tpu_custom_call" | custom-call | flops 1000000 | bytes 2000000 | tf_op jit(solution)/shard_map/unpack_grads/pallas_call | solution.py:417
  112.9 1.6 all-to-all-done.2.got
  115.6 3.0 %reduce.1 = (bf16[64,16,1024]{2,1,0:T(8,128)(2,1)}, f32[16,1024]{1,0:T(8,128)}) custom-call(bf16[32,16,1152]{2,1,0:T(8,128)(2,1)} %copy-done.3), custom_call_target="tpu_custom_call" | custom-call | tf_op jit(solution)/shard_map/reduce/pallas_call | solution.py:474
  118.5 8.7 %all-to-all-start.3 = ((bf16[64,16,1024]{2,1,0:T(8,128)(2,1)}), bf16[64,16,1024]{2,1,0:T(8,128)(2,1)S(1)}, u32[]{:S(2)}, u32[]{:S(2)}) async-start(bf16[64,16,1024]{2,1,0:T(8,128)(2,1)} %get-tuple-element.50), calls=%async_computation.3 | async-start | bytes 4194304 | tf_op jit(solution)/shard_map/all_to_all | solution.py:557
  128.6 3.1 %collective-permute-start.10 = (bf16[16,1024]{1,0:T(8,128)(2,1)S(1)}, bf16[16,1024]{1,0:T(8,128)(2,1)S(1)}, u32[]{:S(2)}, u32[]{:S(2)}) collective-permute-start(bf16[16,1024]{1,0:T(8,128)(2,1)S(1)} %add_convert_fusion.refs_0_), channel_id=1, source_target_pairs={{0,16},{16,0},{1,17},{17,1},{2,18},{18,2},{3,19},{19,3},{4,20},{20... | collective-permute-start | bytes 98312 | tf_op jit(solution)/shard_map/ppermute | solution.py:577
  131.7 2.9 %collective-permute-start.15 = (bf16[16,1024]{1,0:T(8,128)(2,1)S(1)}, bf16[16,1024]{1,0:T(8,128)(2,1)S(1)}, u32[]{:S(2)}, u32[]{:S(2)}) collective-permute-start(bf16[16,1024]{1,0:T(8,128)(2,1)S(1)} %add_convert_fusion.refs_0_), channel_id=1, source_target_pairs={{0,96},{32,0},{64,32},{96,64},{1,97},{33,1},{65,33},{97,65},{2,98}... | collective-permute-start | bytes 98312 | tf_op jit(solution)/shard_map/ppermute | solution.py:581
  136.3 16.2 %collective-permute-done.10.refs_1_ = bf16[16,1024]{1,0:T(8,128)(2,1)S(1)} collective-permute-done((bf16[16,1024]{1,0:T(8,128)(2,1)S(1)}, bf16[16,1024]{1,0:T(8,128)(2,1)S(1)}, u32[]{:S(2)}, u32[]{:S(2)}) %collective-permute-start.10) | collective-permute-done | bytes 32800 | tf_op jit(solution)/shard_map/ppermute | solution.py:577
  152.5 3.1 %collective-permute-start.16 = (bf16[16,1024]{1,0:T(8,128)(2,1)S(1)}, bf16[16,1024]{1,0:T(8,128)(2,1)S(1)}, u32[]{:S(2)}, u32[]{:S(2)}) collective-permute-start(bf16[16,1024]{1,0:T(8,128)(2,1)S(1)} %collective-permute-done.10.refs_1_), channel_id=1, source_target_pairs={{0,96},{32,0},{64,32},{96,64},{1,97},{33,1},{65,33},{97,65},{2,98}... | collective-permute-start | bytes 98312 | tf_op jit(solution)/shard_map/ppermute | solution.py:581
  157.7 3.3 %collective-permute-done.14.refs_5_ = bf16[16,1024]{1,0:T(8,128)(2,1)S(1)} collective-permute-done((bf16[16,1024]{1,0:T(8,128)(2,1)S(1)}, bf16[16,1024]{1,0:T(8,128)(2,1)S(1)}, u32[]{:S(2)}, u32[]{:S(2)}) %collective-permute-start.14) | collective-permute-done | bytes 32800 | tf_op jit(solution)/shard_map/ppermute | solution.py:581
  162.2 2.5 %write_filter.1 = f32[256,512]{1,0:T(8,128)} custom-call(s32[2]{0:T(128)} %pad_add_fusion.place, bf16[16,1024]{1,0:T(8,128)(2,1)} %copy-done.13, bf16[16,1024]{1,0:T(8,128)(2,1)} %copy-done.15, bf16[16,1024]{1,0:T(8,128)(2,1)} %copy-done.18, bf16[16,1024]{1,0:T(8,128)(2,1)} %copy-done.21, bf16[16,1024]{1,0:T(8,128)(2,1)} %copy-done.17, ...), custom_call_target="tpu_custom_call" | custom-call | flops 1000000 | bytes 2000000 | tf_op jit(solution)/shard_map/write_filter/pallas_call | solution.py:542
  166.0 3.7 %write_half.2.refs_0_ = f32[512,4096]{1,0:T(8,128)} custom-call(s32[1]{0:T(128)} %bitcast.17.place, bf16[64,16,1024]{2,1,0:T(8,128)(2,1)} %copy-done.1), custom_call_target="tpu_custom_call" | custom-call | flops 1000000 | bytes 6000000 | tf_op jit(solution)/shard_map/write_half/pallas_call | solution.py:503
  169.7 3.7 %write_half.3 = f32[512,4096]{1,0:T(8,128)} custom-call(s32[1]{0:T(128)S(6)} %sub.14.place, bf16[64,16,1024]{2,1,0:T(8,128)(2,1)} %collective-permute-done.17.mine, f32[512,4096]{1,0:T(8,128)} %write_half.2.refs_0_), custom_call_target="tpu_custom_call", output_to_operand_aliasing={{}: (2, {})} | custom-call | flops 1000000 | bytes 6000000 | tf_op jit(solution)/shard_map/write_half/pallas_call | solution.py:503
  (82 shorter events, 16.8 us)
Async XLA Ops:
  1.3 9.3 %collective-permute-start = (bf16[8,512]{1,0:T(8,128)(2,1)S(1)}, bf16[8,512]{1,0:T(8,128)(2,1)S(1)}, u32[]{:S(2)}, u32[]{:S(2)}) collective-permute-start(bf16[8,512]{1,0:T(8,128)(2,1)S(1)} %slice_bitcast_fusion), channel_id=1, source_target_pairs={{0,1},{1,2},{2,3},{3,4},{4,5},{5,6},{6,7},{8,9},{9,10},{10,11},{11... | collective-permute-start | bytes 24584 | tf_op jit(solution)/shard_map/ppermute | solution.py:565
  10.0 9.7 %copy-start = (bf16[1,256,4096]{2,1,0:T(8,128)(2,1)S(1)}, bf16[1,256,4096]{2,1,0:T(8,128)(2,1)}, u32[]{:S(2)}) copy-start(bf16[1,256,4096]{2,1,0:T(8,128)(2,1)} %param.15) | copy-start | bytes 6291460
  14.3 19.2 %all-to-all-start = ((bf16[8,256,256]{2,1,0:T(8,128)(2,1)}), bf16[8,256,256]{2,1,0:T(8,128)(2,1)S(1)}, u32[]{:S(2)}, u32[]{:S(2)}) async-start(bf16[8,256,256]{2,1,0:T(8,128)(2,1)} %get-tuple-element.31), calls=%async_computation | async-start | bytes 2097152 | tf_op jit(solution)/shard_map/all_to_all | solution.py:557
  20.9 23.6 %collective-permute-start.3 = (bf16[256,1024]{1,0:T(8,128)(2,1)}, bf16[256,1024]{1,0:T(8,128)(2,1)S(1)}, u32[]{:S(2)}, u32[]{:S(2)}) collective-permute-start(bf16[256,1024]{1,0:T(8,128)(2,1)} %get-tuple-element.58), channel_id=1, source_target_pairs={{0,40},{8,32},{32,8},{40,0},{1,41},{9,33},{33,9},{41,1},{2,42},{10... | collective-permute-start | bytes 1572872 | tf_op jit(solution)/shard_map/ppermute | solution.py:573
  21.4 25.2 %collective-permute-start.1 = (bf16[256,1024]{1,0:T(8,128)(2,1)}, bf16[256,1024]{1,0:T(8,128)(2,1)S(1)}, u32[]{:S(2)}, u32[]{:S(2)}) collective-permute-start(bf16[256,1024]{1,0:T(8,128)(2,1)} %get-tuple-element.59), channel_id=1, source_target_pairs={{0,32},{32,0},{1,33},{33,1},{2,34},{34,2},{3,35},{35,3},{4,36},{36... | collective-permute-start | bytes 1572872 | tf_op jit(solution)/shard_map/ppermute | solution.py:569
  22.9 23.7 %collective-permute-start.2 = (bf16[256,1024]{1,0:T(8,128)(2,1)}, bf16[256,1024]{1,0:T(8,128)(2,1)S(1)}, u32[]{:S(2)}, u32[]{:S(2)}) collective-permute-start(bf16[256,1024]{1,0:T(8,128)(2,1)} %get-tuple-element.60), channel_id=1, source_target_pairs={{0,8},{8,0},{1,9},{9,1},{2,10},{10,2},{3,11},{11,3},{4,12},{12,4},... | collective-permute-start | bytes 1572872 | tf_op jit(solution)/shard_map/ppermute | solution.py:561
  44.5 16.5 %copy-start.5 = (bf16[256,1024]{1,0:T(8,128)(2,1)}, bf16[256,1024]{1,0:T(8,128)(2,1)S(1)}, u32[]{:S(2)}) copy-start(bf16[256,1024]{1,0:T(8,128)(2,1)S(1)} %collective-permute-done.3.g11) | copy-start | bytes 1572868
  46.6 14.4 %copy-start.6 = (bf16[256,1024]{1,0:T(8,128)(2,1)}, bf16[256,1024]{1,0:T(8,128)(2,1)S(1)}, u32[]{:S(2)}) copy-start(bf16[256,1024]{1,0:T(8,128)(2,1)S(1)} %collective-permute-done.1.g01) | copy-start | bytes 1572868
  46.6 14.4 %copy-start.7 = (bf16[256,1024]{1,0:T(8,128)(2,1)}, bf16[256,1024]{1,0:T(8,128)(2,1)S(1)}, u32[]{:S(2)}) copy-start(bf16[256,1024]{1,0:T(8,128)(2,1)S(1)} %collective-permute-done.2.g10) | copy-start | bytes 1572868
  46.6 21.0 %all-to-all-start.1 = ((bf16[8,384,128]{2,1,0:T(8,128)(2,1)}), bf16[8,384,128]{2,1,0:T(8,128)(2,1)S(1)}, u32[]{:S(2)}, u32[]{:S(2)}) async-start(bf16[8,384,128]{2,1,0:T(8,128)(2,1)} %conv.1), calls=%async_computation.1 | async-start | bytes 1572864 | tf_op jit(solution)/shard_map/all_to_all | solution.py:557
  62.7 5.0 %collective-permute-start.4 = (bf16[8,4,16,128]{3,2,1,0:T(8,128)(2,1)S(1)}, bf16[8,4,16,128]{3,2,1,0:T(8,128)(2,1)S(1)}, u32[]{:S(2)}, u32[]{:S(2)}) collective-permute-start(bf16[8,4,16,128]{3,2,1,0:T(8,128)(2,1)S(1)} %bitcast.35), channel_id=1, source_target_pairs={{0,32},{32,0},{1,33},{33,1},{2,34},{34,2},{3,35},{35,3},{4,36},{36... | collective-permute-start | bytes 393224 | tf_op jit(solution)/shard_map/ppermute | solution.py:569
  67.6 11.2 %copy-start.12 = (bf16[8,4,16,128]{3,2,1,0:T(8,128)(2,1)}, bf16[8,4,16,128]{3,2,1,0:T(8,128)(2,1)S(1)}, u32[]{:S(2)}) copy-start(bf16[8,4,16,128]{3,2,1,0:T(8,128)(2,1)S(1)} %collective-permute-done.4.lags_z) | copy-start | bytes 393220
  70.5 6.7 %collective-permute-start.5 = (bf16[256,512]{1,0:T(8,128)(2,1)}, bf16[256,512]{1,0:T(8,128)(2,1)S(1)}, u32[]{:S(2)}, u32[]{:S(2)}) collective-permute-start(bf16[256,512]{1,0:T(8,128)(2,1)} %get-tuple-element.44.m00), channel_id=1, source_target_pairs={{0,32},{32,0},{1,33},{33,1},{2,34},{34,2},{3,35},{35,3},{4,36},{36... | collective-permute-start | bytes 786440 | tf_op jit(solution)/shard_map/ppermute | solution.py:569
  71.3 5.9 %collective-permute-start.6 = (bf16[256,512]{1,0:T(8,128)(2,1)}, bf16[256,512]{1,0:T(8,128)(2,1)S(1)}, u32[]{:S(2)}, u32[]{:S(2)}) collective-permute-start(bf16[256,512]{1,0:T(8,128)(2,1)} %get-tuple-element.44.m00), channel_id=1, source_target_pairs={{0,8},{8,0},{1,9},{9,1},{2,10},{10,2},{3,11},{11,3},{4,12},{12,4},... | collective-permute-start | bytes 786440 | tf_op jit(solution)/shard_map/ppermute | solution.py:561
  77.2 1.5 collective-permute-start.7
  83.7 11.0 %copy-start.25 = (f32[8,512]{1,0:T(8,128)S(1)}, f32[8,512]{1,0:T(8,128)}, u32[]{:S(2)}) copy-start(f32[8,512]{1,0:T(8,128)} %get-tuple-element.46) | copy-start | bytes 49156
  83.7 14.4 %copy-start.8 = (bf16[256,512]{1,0:T(8,128)(2,1)S(1)}, bf16[256,512]{1,0:T(8,128)(2,1)}, u32[]{:S(2)}) copy-start(bf16[256,512]{1,0:T(8,128)(2,1)} %get-tuple-element.44.m00) | copy-start | bytes 786436
  83.7 30.8 %all-to-all-start.2 = ((bf16[32,16,1152]{2,1,0:T(8,128)(2,1)}), bf16[32,16,1152]{2,1,0:T(8,128)(2,1)S(1)}, u32[]{:S(2)}, u32[]{:S(2)}) async-start(bf16[32,16,1152]{2,1,0:T(8,128)(2,1)} %partial.1), calls=%async_computation.2 | async-start | bytes 2359296 | tf_op jit(solution)/shard_map/all_to_all | solution.py:557
  94.7 15.0 %collective-permute-start.8 = (f32[8,512]{1,0:T(8,128)S(1)}, f32[8,512]{1,0:T(8,128)S(1)}, u32[]{:S(2)}, u32[]{:S(2)}) collective-permute-start(f32[8,512]{1,0:T(8,128)S(1)} %copy-done.25), channel_id=1, source_target_pairs={{1,0},{2,1},{3,2},{4,3},{5,4},{6,5},{7,6},{9,8},{10,9},{11,10},{12... | collective-permute-start | bytes 49160 | tf_op jit(solution)/shard_map/ppermute | solution.py:565
  118.5 8.7 %copy-start.14 = (f32[16,1024]{1,0:T(8,128)S(1)}, f32[16,1024]{1,0:T(8,128)}, u32[]{:S(2)}) copy-start(f32[16,1024]{1,0:T(8,128)} %get-tuple-element.51) | copy-start | bytes 196612
  118.5 46.1 %all-to-all-start.3 = ((bf16[64,16,1024]{2,1,0:T(8,128)(2,1)}), bf16[64,16,1024]{2,1,0:T(8,128)(2,1)S(1)}, u32[]{:S(2)}, u32[]{:S(2)}) async-start(bf16[64,16,1024]{2,1,0:T(8,128)(2,1)} %get-tuple-element.50), calls=%async_computation.3 | async-start | bytes 4194304 | tf_op jit(solution)/shard_map/all_to_all | solution.py:557
  127.3 1.3 collective-permute-start.9
  128.6 32.7 %copy-start.13 = (bf16[16,1024]{1,0:T(8,128)(2,1)}, bf16[16,1024]{1,0:T(8,128)(2,1)S(1)}, u32[]{:S(2)}) copy-start(bf16[16,1024]{1,0:T(8,128)(2,1)S(1)} %add_convert_fusion.refs_0_) | copy-start | bytes 98308
  128.6 23.8 %collective-permute-start.10 = (bf16[16,1024]{1,0:T(8,128)(2,1)S(1)}, bf16[16,1024]{1,0:T(8,128)(2,1)S(1)}, u32[]{:S(2)}, u32[]{:S(2)}) collective-permute-start(bf16[16,1024]{1,0:T(8,128)(2,1)S(1)} %add_convert_fusion.refs_0_), channel_id=1, source_target_pairs={{0,16},{16,0},{1,17},{17,1},{2,18},{18,2},{3,19},{19,3},{4,20},{20... | collective-permute-start | bytes 98312 | tf_op jit(solution)/shard_map/ppermute | solution.py:577
  131.7 24.5 %collective-permute-start.15 = (bf16[16,1024]{1,0:T(8,128)(2,1)S(1)}, bf16[16,1024]{1,0:T(8,128)(2,1)S(1)}, u32[]{:S(2)}, u32[]{:S(2)}) collective-permute-start(bf16[16,1024]{1,0:T(8,128)(2,1)S(1)} %add_convert_fusion.refs_0_), channel_id=1, source_target_pairs={{0,96},{32,0},{64,32},{96,64},{1,97},{33,1},{65,33},{97,65},{2,98}... | collective-permute-start | bytes 98312 | tf_op jit(solution)/shard_map/ppermute | solution.py:581
  134.6 23.0 %collective-permute-start.13 = (bf16[16,1024]{1,0:T(8,128)(2,1)S(1)}, bf16[16,1024]{1,0:T(8,128)(2,1)S(1)}, u32[]{:S(2)}, u32[]{:S(2)}) collective-permute-start(bf16[16,1024]{1,0:T(8,128)(2,1)S(1)} %add_convert_fusion.refs_0_), channel_id=1, source_target_pairs={{0,64},{32,96},{64,0},{96,32},{1,65},{33,97},{65,1},{97,33},{2,66}... | collective-permute-start | bytes 98312 | tf_op jit(solution)/shard_map/ppermute | solution.py:581
  135.3 22.4 %collective-permute-start.11 = (bf16[16,1024]{1,0:T(8,128)(2,1)S(1)}, bf16[16,1024]{1,0:T(8,128)(2,1)S(1)}, u32[]{:S(2)}, u32[]{:S(2)}) collective-permute-start(bf16[16,1024]{1,0:T(8,128)(2,1)S(1)} %add_convert_fusion.refs_0_), channel_id=1, source_target_pairs={{0,32},{32,64},{64,96},{96,0},{1,33},{33,65},{65,97},{97,1},{2,34}... | collective-permute-start | bytes 98312 | tf_op jit(solution)/shard_map/ppermute | solution.py:581
  152.5 8.9 %copy-start.15 = (bf16[16,1024]{1,0:T(8,128)(2,1)}, bf16[16,1024]{1,0:T(8,128)(2,1)S(1)}, u32[]{:S(2)}) copy-start(bf16[16,1024]{1,0:T(8,128)(2,1)S(1)} %collective-permute-done.10.refs_1_) | copy-start | bytes 98308
  152.5 5.2 %collective-permute-start.16 = (bf16[16,1024]{1,0:T(8,128)(2,1)S(1)}, bf16[16,1024]{1,0:T(8,128)(2,1)S(1)}, u32[]{:S(2)}, u32[]{:S(2)}) collective-permute-start(bf16[16,1024]{1,0:T(8,128)(2,1)S(1)} %collective-permute-done.10.refs_1_), channel_id=1, source_target_pairs={{0,96},{32,0},{64,32},{96,64},{1,97},{33,1},{65,33},{97,65},{2,98}... | collective-permute-start | bytes 98312 | tf_op jit(solution)/shard_map/ppermute | solution.py:581
  155.6 5.4 %collective-permute-start.14 = (bf16[16,1024]{1,0:T(8,128)(2,1)S(1)}, bf16[16,1024]{1,0:T(8,128)(2,1)S(1)}, u32[]{:S(2)}, u32[]{:S(2)}) collective-permute-start(bf16[16,1024]{1,0:T(8,128)(2,1)S(1)} %collective-permute-done.10.refs_1_), channel_id=1, source_target_pairs={{0,64},{32,96},{64,0},{96,32},{1,65},{33,97},{65,1},{97,33},{2,66}... | collective-permute-start | bytes 98312 | tf_op jit(solution)/shard_map/ppermute | solution.py:581
  156.2 5.1 %collective-permute-start.12 = (bf16[16,1024]{1,0:T(8,128)(2,1)S(1)}, bf16[16,1024]{1,0:T(8,128)(2,1)S(1)}, u32[]{:S(2)}, u32[]{:S(2)}) collective-permute-start(bf16[16,1024]{1,0:T(8,128)(2,1)S(1)} %collective-permute-done.10.refs_1_), channel_id=1, source_target_pairs={{0,32},{32,64},{64,96},{96,0},{1,33},{33,65},{65,97},{97,1},{2,34}... | collective-permute-start | bytes 98312 | tf_op jit(solution)/shard_map/ppermute | solution.py:581
  164.7 5.1 %collective-permute-start.17 = (bf16[64,16,1024]{2,1,0:T(8,128)(2,1)S(1)}, bf16[64,16,1024]{2,1,0:T(8,128)(2,1)}, u32[]{:S(2)}, u32[]{:S(2)}) collective-permute-start(bf16[64,16,1024]{2,1,0:T(8,128)(2,1)S(1)} %all-to-all-done.3.mine), channel_id=1, source_target_pairs={{0,8},{8,0},{1,9},{9,1},{2,10},{10,2},{3,11},{11,3},{4,12},{12,4},... | collective-permute-start | bytes 6291464 | tf_op jit(solution)/shard_map/ppermute | solution.py:561
  (16 other events, 32.0 us)

commit v9 on v8

--- a/solution.py
+++ b/solution.py
@@ -13,9 +13,11 @@
 F32 = jnp.float32
 BLOCK = 256
 HALF = 64
+SENT_ROWS = BLOCK + 16
 SEQ = ("x", "yl")
 MOST = ("zh", "yh") + SEQ
-CHIPS = ("zh", "zl", "yh") + SEQ
+DEPTH = ("zh", "zl", "yh")
+CHIPS = DEPTH + SEQ
 
 
 @functools.lru_cache(maxsize=None)
@@ -45,63 +47,71 @@
     return pltpu.roll(x, HALF, 1)
 
 
-def grad_kernel(out_grad, weight, total):
-    @pl.when(pl.program_id(0) == 0)
+def pack_kernel(streams, out_grad, weight, filt, short, packed, grad, gate_out, pad):
+    step = pl.program_id(0)
+    low, low16 = low_lanes(BLOCK), low_lanes(16)
+
+    @pl.when(step == 0)
     def _():
-        total[...] = jnp.zeros_like(total)
-
-    total[...] += lax.dot_general(
+        grad[...] = jnp.zeros_like(grad)
+
+    grad[...] += lax.dot_general(
         out_grad[...], weight[...], (((1,), (1,)), ((), ())), preferred_element_type=F32
     )
 
-
-def grad_of_mixed(out_grad, weight):
+    for q in range(4):
+
+        @pl.when(step == q)
+        def _(q=q):
+            lanes = slice(128 * q, 128 * q + 128)
+            a, b = streams[1, :, lanes].astype(F32), streams[2, :, lanes].astype(F32)
+            packed[2 * q, 0:BLOCK, 0:128] = jnp.where(low, a, turned(b)).astype(BF)
+            packed[2 * q + 1, 0:BLOCK, 0:128] = jnp.where(low, turned(a), b).astype(BF)
+            pad[0:8] = jnp.zeros((8, 128), F32)
+            pad[8:] = streams[0, :, lanes].astype(F32)
+            gate_out[:, lanes] = sum(
+                short[j : j + 1, lanes] * pad[8 - j : 8 - j + BLOCK] for j in range(3)
+            )
+
+    @pl.when(step == pl.num_programs(0) - 1)
+    def _():
+        for q in range(4):
+            lanes = slice(128 * q, 128 * q + 128)
+            a, b = grad[:, lanes] * gate_out[:, lanes], filt[:, lanes]
+            packed[2 * q, 0:BLOCK, 128:256] = jnp.where(low, a, turned(b)).astype(BF)
+            packed[2 * q + 1, 0:BLOCK, 128:256] = jnp.where(low, turned(a), b).astype(BF)
+            ends = streams[0, :, lanes].astype(F32)
+            a = jnp.concatenate([ends[0:8], ends[BLOCK - 8 :]], axis=0)
+            b = grad[0:16, lanes]
+            packed[2 * q, BLOCK:, 0:128] = jnp.where(low16, a, turned(b)).astype(BF)
+            packed[2 * q + 1, BLOCK:, 0:128] = jnp.where(low16, turned(a), b).astype(BF)
+            packed[2 * q, BLOCK:, 128:256] = jnp.zeros((16, 128), BF)
+            packed[2 * q + 1, BLOCK:, 128:256] = jnp.zeros((16, 128), BF)
+
+
+def pack(streams, out_grad, weight, filt, short):
     steps = 4
     wide = out_grad.shape[1] // steps
-    return pl.pallas_call(
-        grad_kernel,
+    full = lambda *shape: pl.BlockSpec(shape, lambda k: (0,) * len(shape))
+    return pl.pallas_call(
+        pack_kernel,
         grid=(steps,),
         in_specs=[
+            full(3, BLOCK, 512),
             pl.BlockSpec((BLOCK, wide), lambda k: (0, k)),
             pl.BlockSpec((512, wide), lambda k: (0, k)),
+            full(BLOCK, 512),
+            full(9, 512),
         ],
-        out_specs=pl.BlockSpec((BLOCK, 512), lambda k: (0, 0)),
-        out_shape=jax.ShapeDtypeStruct((BLOCK, 512), F32),
-        cost_estimate=pl.CostEstimate(flops=10**9, bytes_accessed=7 * 10**6, transcendentals=0),
-        name="grad_of_mixed",
-    )(out_grad, weight)
-
-
-def pack_kernel(streams, edge, grad, filt, short, packed, gate_out, pad):
-    low = low_lanes(BLOCK)
-    pad[0:8] = edge[...].astype(F32)
-    pad[8:] = streams[0].astype(F32)
-    for q in range(4):
-        lanes = slice(128 * q, 128 * q + 128)
-        gate = sum(
-            short[j : j + 1, lanes] * pad[8 - j : 8 - j + BLOCK, lanes] for j in range(3)
-        )
-        gate_out[:, lanes] = gate
-        pairs = (
-            (streams[1, :, lanes].astype(F32), streams[2, :, lanes].astype(F32)),
-            (grad[:, lanes] * gate, filt[:, lanes]),
-        )
-        for n, (a, b) in enumerate(pairs):
-            there = slice(128 * n, 128 * n + 128)
-            packed[2 * q, :, there] = jnp.where(low, a, turned(b)).astype(BF)
-            packed[2 * q + 1, :, there] = jnp.where(low, turned(a), b).astype(BF)
-
-
-def pack(streams, edge, grad, filt, short):
-    return pl.pallas_call(
-        pack_kernel,
+        out_specs=[full(8, SENT_ROWS, 256), full(BLOCK, 512), full(BLOCK, 512)],
         out_shape=[
-            jax.ShapeDtypeStruct((8, BLOCK, 256), BF),
+            jax.ShapeDtypeStruct((8, SENT_ROWS, 256), BF),
+            jax.ShapeDtypeStruct((BLOCK, 512), F32),
             jax.ShapeDtypeStruct((BLOCK, 512), F32),
         ],
-        scratch_shapes=[pltpu.VMEM((8 + BLOCK, 512), F32)],
+        scratch_shapes=[pltpu.VMEM((8 + BLOCK, 128), F32)],
         name="pack",
-    )(streams, edge, grad, filt, short)
+    )(streams, out_grad, weight, filt, short)
 
 
 def split(x):
@@ -143,7 +153,7 @@
 
     def load(b, carry):
         rows = pl.ds(pl.multiple_of(8 + BLOCK * b, 8), BLOCK)
-        pad[rows] = got[b, :, 0:128].astype(F32)
+        pad[rows] = got[b, 0:BLOCK, 0:128].astype(F32)
         return carry
 
     lax.fori_loop(0, 8, load, 0)
@@ -152,7 +162,16 @@
         s = sum(taps[j] * pad[start - j : start - j + BLOCK] for j in range(3))
         if gates is not None:
             gates[b] = s
-        prod[b] = jnp.where(low, s * turned(s), turned(got[b, :, 128:256].astype(F32)))
+        prod[b] = jnp.where(low, s * turned(s), turned(got[b, 0:BLOCK, 128:256].astype(F32)))
+    low8 = low_lanes(8)
+    gate = pair(0, None)
+    for b in range(8):
+        ends = got[b, BLOCK:, 0:128].astype(F32)
+        first = got[b - 1, BLOCK:, 0:128].astype(F32)[8:] if b else jnp.zeros((8, 128), F32)
+        pad[0:8] = first
+        pad[8:16] = ends[0:8]
+        out = sum(gate[j] * pad[8 - j : 16 - j] for j in range(3))
+        prod[b, 0:8] = jnp.where(low8, prod[b, 0:8], turned(out) * ends[0:8])
 
 
 def spectra(prod, ahead_h, ahead_l, spec):
@@ -215,7 +234,7 @@
 
     def filters(n, carry):
         def blocks(b):
-            x, y = got[b, :, 128:256].astype(F32), got[b + 1, :, 128:256].astype(F32)
+            x, y = (got[n, 0:BLOCK, 128:256].astype(F32) for n in (b, b + 1))
             return jnp.where(low, turned(x), y).astype(BF)
 
         f = jnp.concatenate([blocks(4 * n), blocks(4 * n + 2)], axis=1)
@@ -320,7 +339,7 @@
             num_scalar_prefetch=1,
             grid=(1,),
             in_specs=[
-                full(8, BLOCK, 256),
+                full(8, SENT_ROWS, 256),
                 pl.BlockSpec((9, 128), lambda n, p: (0, p[0] // 2)),
                 pl.BlockSpec((1, 128), lambda n, p: (0, p[0] // 2)),
             ]
@@ -366,17 +385,22 @@
     return jnp.where(low128, a, turned(b)), jnp.where(low128, turned(a), b)
 
 
-def mixed_kernel(got, gate_out, grad, mixed, head):
+def mixed_kernel(got, gate_out, grad, edge, short, mixed, head, pad):
     low128 = low_lanes(128)
+    pad[0:8] = edge[...].astype(F32)
+    pad[8:] = jnp.zeros((8, 512), F32)
+    more = sum(short[j : j + 1] * pad[8 - j : 16 - j] for j in (1, 2))
     for q in range(4):
         lanes = slice(128 * q, 128 * q + 128)
         first, second = convolved(got, q, low128)
-        mixed[0:128, lanes] = (gate_out[0:128, lanes] * first).astype(BF)
+        gate = gate_out[0:128, lanes]
+        gate = jnp.concatenate([gate[0:8] + more[:, lanes], gate[8:]], axis=0)
+        mixed[0:128, lanes] = (gate * first).astype(BF)
         mixed[128:256, lanes] = (gate_out[128:256, lanes] * second).astype(BF)
         head[:, lanes] = grad[:, lanes] * first[0:8]
 
 
-def unpack_mixed(got, gate_out, grad):
+def unpack_mixed(got, gate_out, grad, edge, short):
     return pl.pallas_call(
         mixed_kernel,
         grid=(1,),
@@ -384,17 +408,20 @@
             pl.BlockSpec((8, 128, 128), lambda n: (0, 2, 0)),
             pl.BlockSpec((BLOCK, 512), lambda n: (0, 0)),
             pl.BlockSpec((8, 512), lambda n: (0, 0)),
+            pl.BlockSpec((8, 512), lambda n: (0, 0)),
+            pl.BlockSpec((9, 512), lambda n: (0, 0)),
         ],
         out_specs=[
             pl.BlockSpec((BLOCK, 512), lambda n: (0, 0)),
             pl.BlockSpec((8, 512), lambda n: (0, 0)),
         ],
+        scratch_shapes=[pltpu.VMEM((16, 512), F32)],
         out_shape=[
             jax.ShapeDtypeStruct((BLOCK, 512), BF),
             jax.ShapeDtypeStruct((8, 512), F32),
         ],
         name="unpack_mixed",
-    )(got, gate_out, grad)
+    )(got, gate_out, grad, edge, short)
 
 
 def grads_kernel(got, grad, tail, short, grads, pad):
@@ -523,18 +550,14 @@
 def filter_kernel(place, *refs):
     grad_filter = refs[-1]
     low = low_lanes(16)
-    for d in range(4):
-        z = (place[0] + 4 - d) % 4
-        for n in range(2):
-            yh = place[1] if n == 0 else 1 - place[1]
-            row = pl.multiple_of(32 * (2 * z + yh), 32)
-            lags = refs[2 * d + n]
-            for q in range(4):
-                a = lags[:, 256 * q : 256 * q + 128].astype(F32)
-                b = lags[:, 256 * q + 128 : 256 * q + 256].astype(F32)
-                lanes = slice(128 * q, 128 * q + 128)
-                grad_filter[pl.ds(row, 16), lanes] = jnp.where(low, a, turned(b))
-                grad_filter[pl.ds(row + 16, 16), lanes] = jnp.where(low, turned(a), b)
+    for n in range(8):
+        row = pl.multiple_of(32 * (place[0] ^ n), 32)
+        for q in range(4):
+            a = refs[n][:, 256 * q : 256 * q + 128].astype(F32)
+            b = refs[n][:, 256 * q + 128 : 256 * q + 256].astype(F32)
+            lanes = slice(128 * q, 128 * q + 128)
+            grad_filter[pl.ds(row, 16), lanes] = jnp.where(low, a, turned(b))
+            grad_filter[pl.ds(row + 16, 16), lanes] = jnp.where(low, turned(a), b)
 
 
 def write_filter(place, lags):
@@ -574,12 +597,9 @@
 
 
 def gathered(lags):
-    pair = (lags, lax.ppermute(lags, "yh", [(0, 1), (1, 0)]))
-    out = list(pair)
-    for d in range(1, 4):
-        route = [(n, (n + d) % 4) for n in range(4)]
-        out += [lax.ppermute(part, ("zh", "zl"), route) for part in pair]
-    return out
+    return [lags] + [
+        lax.ppermute(lags, DEPTH, [(i, i ^ n) for i in range(8)]) for n in range(1, 8)
+    ]
 
 
 def on_device(streams, short_filter, long_filter, skip_gain, out_weight, out_grad):
@@ -598,14 +618,12 @@
         opposite(quarter(1 - core, 1 - side)),
     )
     short = short_filter.reshape(9, 512)
+    packed, grad_mixed, gate_out = pack(streams[:, 0], grad, out_weight, long_filter, short)
+    got = exchange(packed, SEQ)
     edge = along(streams[0, 0, BLOCK - 8 :], 1)
-    grad_mixed = grad_of_mixed(grad, out_weight)
-    edge, grad_mixed = lax.optimization_barrier((edge, grad_mixed))
-    packed, gate_out = pack(streams[:, 0], edge, grad_mixed, long_filter, short)
-    got = exchange(packed, SEQ)
     channels = (seq[None], got, short, skip_gain.reshape(1, 512))
     sent = conv(*channels)
-    sent, got, grads = lax.optimization_barrier((sent, got, grads))
+    sent, got, grads, edge = lax.optimization_barrier((sent, got, grads, edge))
     channels = (channels[0], got) + channels[2:]
     lags = lag_sums(*channels).reshape(8, 2, 2, 2, 16, 128)
 
@@ -614,22 +632,23 @@
 
     lags_own, lags_z = of_side(side), above(of_side(1 - side))
     back = exchange(sent, SEQ)
-    back, lags_own, lags_z = lax.optimization_barrier((back, lags_own, lags_z))
-    m00, head = unpack_mixed(back, gate_out, grad_mixed)
+    back, lags_own = lax.optimization_barrier((back, lags_own))
+    m00, head = unpack_mixed(back, gate_out, grad_mixed, edge, short)
     m01, m10 = above(m00), across(m00)
     mixed = (m00, m01, m10, across(m01))
+    tail = along(head, -1)
     part = partial((2 * core + side)[None], mixed, grad, grads, lags_own, lags_z)
-    part, m00, back, head = lax.optimization_barrier((part, m00, back, head))
+    part, m00, back, tail = lax.optimization_barrier((part, m00, back, tail))
     part = exchange(part, MOST)
     layer_out = jnp.dot(m00, out_weight, preferred_element_type=F32).astype(BF)
-    grad_streams = unpack_grads(back, grad_mixed, along(head, -1), short)
+    grad_streams = unpack_grads(back, grad_mixed, tail, short)
     part, layer_out, grad_streams = lax.optimization_barrier((part, layer_out, grad_streams))
     rows, lags = reduce(part, scale)
     rows, lags = lax.optimization_barrier((rows, lags))
     mine = exchange(rows, CHIPS)
     lags = (lags + across(lags)).astype(BF)
-    place = jnp.stack([lax.axis_index(("zh", "zl")), lax.axis_index("yh")]).astype(jnp.int32)
-    grad_filter = write_filter(place, gathered(lags))
+    depth = lax.axis_index(DEPTH).astype(jnp.int32)
+    grad_filter = write_filter(depth[None], gathered(lags))
     mine, grad_filter = lax.optimization_barrier((mine, grad_filter))
     theirs = across(mine)
     grad_weight = write_half(core[None], mine)

time: 175 us -> 167 us (0.954)
  the two profiles are of different devices: /device:TPU:2 before, /device:TPU:1 now
where the time goes in v9:
time: 167 us; the launch traced here: 165 us
  starting transfers between devices  63 us (38%)
  Pallas kernels  46.5 us (28%)
  waiting for transfers between devices  40 us (24%)
  local copies, waits for them, and re-layouts  9.31 us (6%)
  matrix products  4.77 us (3%)
    all_to_all x4, starting transfers between devices, exchange(): return lax.all_to_all(x, axes, 0, 0, tiled=True)  25.6 us
    all_to_all x4, waiting for transfers between devices, exchange(): return lax.all_to_all(x, axes, 0, 0, tiled=True)  21.2 us
    pallas_call x2, Pallas kernels, on_channels(): pl.pallas_call(kernel, grid_spec=pltpu.PrefetchScalarGridSpec(num_scalar_...  18.7 us
    ppermute x7, starting transfers between devices, gathered(): lax.ppermute(lags, DEPTH, [(i, i ^ n) for i in range(8)])  18.2 us
    ppermute x7, waiting for transfers between devices, gathered(): lax.ppermute(lags, DEPTH, [(i, i ^ n) for i in range(8)])  11.8 us
    ppermute x5, starting transfers between devices, across(): return lax.ppermute(x, 'c', [(0, 1), (1, 0)])  8.49 us
    pallas_call x2, Pallas kernels, write_half(): pl.pallas_call(half_kernel, grid_spec=pltpu.PrefetchScalarGridSpec(num_sc...  7.39 us
    pallas_call x1, Pallas kernels, pack(): pl.pallas_call(pack_kernel, grid=(steps,), in_specs=[full(3, BLOCK, 512),...  6.77 us
  transfers between devices with their start and end apart: 22, of which 10 were waited for; matrix products, arithmetic and copies ran while one was open for 5% of the time, Pallas kernels for 19%

profile of v9, /device:TPU:1, one launch (start us, length us, event | category | flops | bytes accessed | tf_op | source)
XLA Modules:
  0.0 164.7 jit_solution(6900390096667629809)
XLA Ops:
  2.0 6.8 %pack.1 = (bf16[8,272,256]{2,1,0:T(8,128)(2,1)}, f32[256,512]{1,0:T(8,128)}, f32[256,512]{1,0:T(8,128)}) custom-call(bf16[3,256,512]{2,1,0:T(8,128)(2,1)} %bitcast.30, bf16[256,4096]{1,0:T(8,128)(2,1)} %bitcast.28, bf16[512,4096]{1,0:T(8,128)(2,1)} %weight.1, f32[256,512]{1,0:T(8,128)} %filt.1, f32[9,512]{1,0:T(8,128)} %reshape.28.short), custom_call_target="tpu_custom_call" | custom-call | tf_op jit(solution)/shard_map/pack/pallas_call | solution.py:96
  8.8 6.0 %all-to-all-start = ((bf16[8,272,256]{2,1,0:T(8,128)(2,1)}), bf16[8,272,256]{2,1,0:T(8,128)(2,1)S(1)}, u32[]{:S(2)}, u32[]{:S(2)}) async-start(bf16[8,272,256]{2,1,0:T(8,128)(2,1)} %get-tuple-element.28), calls=%async_computation | async-start | bytes 2228224 | tf_op jit(solution)/shard_map/all_to_all | solution.py:580
  16.0 2.5 %collective-permute-start.2 = (bf16[256,1024]{1,0:T(8,128)(2,1)}, bf16[256,1024]{1,0:T(8,128)(2,1)S(1)}, u32[]{:S(2)}, u32[]{:S(2)}) collective-permute-start(bf16[256,1024]{1,0:T(8,128)(2,1)} %get-tuple-element.56), channel_id=1, source_target_pairs={{0,40},{8,32},{32,8},{40,0},{1,41},{9,33},{33,9},{41,1},{2,42},{10... | collective-permute-start | bytes 1572872 | tf_op jit(solution)/shard_map/ppermute | solution.py:596
  19.6 3.6 %collective-permute-start.3 = (bf16[8,512]{1,0:T(8,128)(2,1)S(1)}, bf16[8,512]{1,0:T(8,128)(2,1)S(1)}, u32[]{:S(2)}, u32[]{:S(2)}) collective-permute-start(bf16[8,512]{1,0:T(8,128)(2,1)S(1)} %slice_bitcast_fusion), channel_id=1, source_target_pairs={{0,1},{1,2},{2,3},{3,4},{4,5},{5,6},{6,7},{8,9},{9,10},{10,11},{11... | collective-permute-start | bytes 24584 | tf_op jit(solution)/shard_map/ppermute | solution.py:588
  23.2 7.7 %all-to-all-done.got = bf16[8,272,256]{2,1,0:T(8,128)(2,1)S(1)} async-done(((bf16[8,272,256]{2,1,0:T(8,128)(2,1)}), bf16[8,272,256]{2,1,0:T(8,128)(2,1)S(1)}, u32[]{:S(2)}, u32[]{:S(2)}) %all-to-all-start) | async-done | bytes 1114144 | tf_op jit(solution)/shard_map/all_to_all | solution.py:580
  31.9 10.0 %conv.1 = bf16[8,384,128]{2,1,0:T(8,128)(2,1)} custom-call(s32[1]{0:T(128)} %bitcast.1.place, bf16[8,272,256]{2,1,0:T(8,128)(2,1)} %copy-done.4, f32[9,512]{1,0:T(8,128)} %reshape.28.short, f32[1,512]{1,0:T(1,128)} %bitcast.35, bf16[512,256]{1,0:T(8,128)(2,1)} %constant.56.clone.ahead_h, bf16[512,256]{1,0:T(8,128)(2,1)} %constant.57.clone.ahead_l, ...), custom_call_target="tpu_custom_call" | custom-call | tf_op jit(solution)/shard_map/conv/pallas_call | solution.py:336
  42.0 5.2 %all-to-all-start.1 = ((bf16[8,384,128]{2,1,0:T(8,128)(2,1)}), bf16[8,384,128]{2,1,0:T(8,128)(2,1)S(1)}, u32[]{:S(2)}, u32[]{:S(2)}) async-start(bf16[8,384,128]{2,1,0:T(8,128)(2,1)} %conv.1), calls=%async_computation.1 | async-start | bytes 1572864 | tf_op jit(solution)/shard_map/all_to_all | solution.py:580
  47.2 8.7 %lag_sums.1 = bf16[8,8,16,128]{3,2,1,0:T(8,128)(2,1)} custom-call(s32[1]{0:T(128)} %bitcast.1.place, bf16[8,272,256]{2,1,0:T(8,128)(2,1)} %copy-done.4, f32[9,512]{1,0:T(8,128)} %reshape.28.short, f32[1,512]{1,0:T(1,128)} %bitcast.36, bf16[512,256]{1,0:T(8,128)(2,1)} %constant.56.clone.ahead_h, bf16[512,256]{1,0:T(8,128)(2,1)} %constant.57.clone.ahead_l, ...), custom_call_target="tpu_custom_call" | custom-call | flops 2000000000 | bytes 3000000 | tf_op jit(solution)/shard_map/lag_sums/pallas_call | solution.py:336
  56.0 1.6 constant_dynamic-slice_fusion
  59.6 2.0 %unpack_mixed.1 = (bf16[256,512]{1,0:T(8,128)(2,1)}, f32[8,512]{1,0:T(8,128)}) custom-call(bf16[8,384,128]{2,1,0:T(8,128)(2,1)} %copy-done.2, f32[256,512]{1,0:T(8,128)} %get-tuple-element.32.gate_out, f32[256,512]{1,0:T(8,128)} %get-tuple-element.33.grad, bf16[8,512]{1,0:T(8,128)(2,1)} %copy-done.23, f32[9,512]{1,0:T(8,128)} %reshape.28.short), custom_call_target="tpu_custom_call" | custom-call | tf_op jit(solution)/shard_map/unpack_mixed/pallas_call | solution.py:404
  61.6 1.9 %collective-permute-start.4 = (bf16[256,512]{1,0:T(8,128)(2,1)}, bf16[256,512]{1,0:T(8,128)(2,1)S(1)}, u32[]{:S(2)}, u32[]{:S(2)}) collective-permute-start(bf16[256,512]{1,0:T(8,128)(2,1)} %get-tuple-element.42.m00), channel_id=1, source_target_pairs={{0,32},{32,0},{1,33},{33,1},{2,34},{34,2},{3,35},{35,3},{4,36},{36... | collective-permute-start | bytes 786440 | tf_op jit(solution)/shard_map/ppermute | solution.py:592
  63.5 1.6 collective-permute-start.5
  65.1 3.5 %collective-permute-done.4.m01 = bf16[256,512]{1,0:T(8,128)(2,1)S(1)} collective-permute-done((bf16[256,512]{1,0:T(8,128)(2,1)}, bf16[256,512]{1,0:T(8,128)(2,1)S(1)}, u32[]{:S(2)}, u32[]{:S(2)}) %collective-permute-start.4) | collective-permute-done | bytes 262176 | tf_op jit(solution)/shard_map/ppermute | solution.py:592
  68.6 2.4 %collective-permute-start.6 = (bf16[256,512]{1,0:T(8,128)(2,1)S(1)}, bf16[256,512]{1,0:T(8,128)(2,1)S(1)}, u32[]{:S(2)}, u32[]{:S(2)}) collective-permute-start(bf16[256,512]{1,0:T(8,128)(2,1)S(1)} %collective-permute-done.4.m01), channel_id=1, source_target_pairs={{0,8},{8,0},{1,9},{9,1},{2,10},{10,2},{3,11},{11,3},{4,12},{12,4},... | collective-permute-start | bytes 786440 | tf_op jit(solution)/shard_map/ppermute | solution.py:584
  73.7 2.4 %collective-permute-done.7.lags_z = bf16[8,4,16,128]{3,2,1,0:T(8,128)(2,1)S(1)} collective-permute-done((bf16[8,4,16,128]{3,2,1,0:T(8,128)(2,1)S(1)}, bf16[8,4,16,128]{3,2,1,0:T(8,128)(2,1)S(1)}, u32[]{:S(2)}, u32[]{:S(2)}) %collective-permute-start.7) | collective-permute-done | bytes 131104 | tf_op jit(solution)/shard_map/ppermute | solution.py:592
  76.9 4.2 %partial.1 = bf16[32,16,1152]{2,1,0:T(8,128)(2,1)} custom-call(s32[1]{0:T(128)} %bitcast.place, bf16[256,512]{1,0:T(8,128)(2,1)} %get-tuple-element.42.m00, bf16[256,512]{1,0:T(8,128)(2,1)} %copy-done.9, bf16[256,512]{1,0:T(8,128)(2,1)} %copy-done.10, bf16[256,512]{1,0:T(8,128)(2,1)} %copy-done.11, bf16[256,4096]{1,0:T(8,128)(2,1)} %bitcast.29, ...), custom_call_target="tpu_custom_call" | custom-call | tf_op jit(solution)/shard_map/partial/pallas_call | solution.py:470
  81.1 9.5 %all-to-all-start.2 = ((bf16[32,16,1152]{2,1,0:T(8,128)(2,1)}), bf16[32,16,1152]{2,1,0:T(8,128)(2,1)S(1)}, u32[]{:S(2)}, u32[]{:S(2)}) async-start(bf16[32,16,1152]{2,1,0:T(8,128)(2,1)} %partial.1), calls=%async_computation.2 | async-start | bytes 2359296 | tf_op jit(solution)/shard_map/all_to_all | solution.py:580
  90.7 2.7 %unpack_grads.1 = bf16[3,256,512]{2,1,0:T(8,128)(2,1)} custom-call(bf16[8,384,128]{2,1,0:T(8,128)(2,1)} %copy-done.2, f32[256,512]{1,0:T(8,128)} %get-tuple-element.33.grad, f32[8,512]{1,0:T(8,128)} %copy-done.22, f32[9,512]{1,0:T(8,128)} %reshape.28.short), custom_call_target="tpu_custom_call" | custom-call | flops 1000000 | bytes 2000000 | tf_op jit(solution)/shard_map/unpack_grads/pallas_call | solution.py:444
  93.4 4.8 %convolution_convert_fusion = bf16[256,4096]{1,0:T(8,128)(2,1)} fusion(bf16[256,512]{1,0:T(8,128)(2,1)S(1)} %copy-done.8, bf16[512,4096]{1,0:T(8,128)(2,1)} %weight.1), kind=kOutput, calls=%fused_computation | convolution fusion | flops 1074790400 | bytes 6553600 | tf_op jit(solution)/shard_map/dot_general | solution.py:643
  98.1 12.4 %all-to-all-done.2.got = bf16[32,16,1152]{2,1,0:T(8,128)(2,1)S(1)} async-done(((bf16[32,16,1152]{2,1,0:T(8,128)(2,1)}), bf16[32,16,1152]{2,1,0:T(8,128)(2,1)S(1)}, u32[]{:S(2)}, u32[]{:S(2)}) %all-to-all-start.2) | async-done | bytes 1179680 | tf_op jit(solution)/shard_map/all_to_all | solution.py:580
  111.6 3.0 %reduce.1 = (bf16[64,16,1024]{2,1,0:T(8,128)(2,1)}, f32[16,1024]{1,0:T(8,128)}) custom-call(bf16[32,16,1152]{2,1,0:T(8,128)(2,1)} %copy-done.3), custom_call_target="tpu_custom_call" | custom-call | tf_op jit(solution)/shard_map/reduce/pallas_call | solution.py:501
  114.5 4.8 %all-to-all-start.3 = ((bf16[64,16,1024]{2,1,0:T(8,128)(2,1)}), bf16[64,16,1024]{2,1,0:T(8,128)(2,1)S(1)}, u32[]{:S(2)}, u32[]{:S(2)}) async-start(bf16[64,16,1024]{2,1,0:T(8,128)(2,1)} %get-tuple-element.48), calls=%async_computation.3 | async-start | bytes 4194304 | tf_op jit(solution)/shard_map/all_to_all | solution.py:580
  119.4 1.9 %collective-permute-start.9 = (f32[16,1024]{1,0:T(8,128)S(1)}, f32[16,1024]{1,0:T(8,128)S(1)}, u32[]{:S(2)}, u32[]{:S(2)}) collective-permute-start(f32[16,1024]{1,0:T(8,128)S(1)} %copy-done.14), channel_id=1, source_target_pairs={{0,8},{8,0},{1,9},{9,1},{2,10},{10,2},{3,11},{11,3},{4,12},{12,4},... | collective-permute-start | bytes 196616 | tf_op jit(solution)/shard_map/ppermute | solution.py:584
  122.3 5.4 %collective-permute-start.16 = (bf16[16,1024]{1,0:T(8,128)(2,1)S(1)}, bf16[16,1024]{1,0:T(8,128)(2,1)S(1)}, u32[]{:S(2)}, u32[]{:S(2)}) collective-permute-start(bf16[16,1024]{1,0:T(8,128)(2,1)S(1)} %add_convert_fusion.refs_0_), channel_id=1, source_target_pairs={{0,112},{16,96},{32,80},{48,64},{64,48},{80,32},{96,16},{112,0},{1... | collective-permute-start | bytes 98312 | tf_op jit(solution)/shard_map/ppermute | solution.py:601
  130.7 2.6 %collective-permute-start.12 = (bf16[16,1024]{1,0:T(8,128)(2,1)S(1)}, bf16[16,1024]{1,0:T(8,128)(2,1)S(1)}, u32[]{:S(2)}, u32[]{:S(2)}) collective-permute-start(bf16[16,1024]{1,0:T(8,128)(2,1)S(1)} %add_convert_fusion.refs_0_), channel_id=1, source_target_pairs={{0,48},{16,32},{32,16},{48,0},{64,112},{80,96},{96,80},{112,64},{1... | collective-permute-start | bytes 98312 | tf_op jit(solution)/shard_map/ppermute | solution.py:601
  133.3 2.4 %collective-permute-done.16.refs_7_ = bf16[16,1024]{1,0:T(8,128)(2,1)S(1)} collective-permute-done((bf16[16,1024]{1,0:T(8,128)(2,1)S(1)}, bf16[16,1024]{1,0:T(8,128)(2,1)S(1)}, u32[]{:S(2)}, u32[]{:S(2)}) %collective-permute-start.16) | collective-permute-done | bytes 32800 | tf_op jit(solution)/shard_map/ppermute | solution.py:601
  136.2 8.2 %collective-permute-done.15.refs_6_ = bf16[16,1024]{1,0:T(8,128)(2,1)S(1)} collective-permute-done((bf16[16,1024]{1,0:T(8,128)(2,1)S(1)}, bf16[16,1024]{1,0:T(8,128)(2,1)S(1)}, u32[]{:S(2)}, u32[]{:S(2)}) %collective-permute-start.15) | collective-permute-done | bytes 32800 | tf_op jit(solution)/shard_map/ppermute | solution.py:601
  144.4 6.6 %collective-permute-start.10 = (bf16[16,1024]{1,0:T(8,128)(2,1)S(1)}, bf16[16,1024]{1,0:T(8,128)(2,1)S(1)}, u32[]{:S(2)}, u32[]{:S(2)}) collective-permute-start(bf16[16,1024]{1,0:T(8,128)(2,1)S(1)} %add_convert_fusion.refs_0_), channel_id=1, source_target_pairs={{0,16},{16,0},{32,48},{48,32},{64,80},{80,64},{96,112},{112,96},{1... | collective-permute-start | bytes 98312 | tf_op jit(solution)/shard_map/ppermute | solution.py:601
  152.9 1.8 %write_filter.1 = f32[256,512]{1,0:T(8,128)} custom-call(s32[1]{0:T(128)} %bitcast.15.place, bf16[16,1024]{1,0:T(8,128)(2,1)} %copy-done.13, bf16[16,1024]{1,0:T(8,128)(2,1)} %copy-done.21, bf16[16,1024]{1,0:T(8,128)(2,1)} %copy-done.20, bf16[16,1024]{1,0:T(8,128)(2,1)} %copy-done.19, bf16[16,1024]{1,0:T(8,128)(2,1)} %copy-done.18, ...), custom_call_target="tpu_custom_call" | custom-call | flops 1000000 | bytes 2000000 | tf_op jit(solution)/shard_map/write_filter/pallas_call | solution.py:565
  154.8 2.1 %collective-permute-start.17 = (bf16[64,16,1024]{2,1,0:T(8,128)(2,1)S(1)}, bf16[64,16,1024]{2,1,0:T(8,128)(2,1)}, u32[]{:S(2)}, u32[]{:S(2)}) collective-permute-start(bf16[64,16,1024]{2,1,0:T(8,128)(2,1)S(1)} %all-to-all-done.3.mine), channel_id=1, source_target_pairs={{0,8},{8,0},{1,9},{9,1},{2,10},{10,2},{3,11},{11,3},{4,12},{12,4},... | collective-permute-start | bytes 6291464 | tf_op jit(solution)/shard_map/ppermute | solution.py:584
  156.9 3.7 %write_half.2.refs_0_ = f32[512,4096]{1,0:T(8,128)} custom-call(s32[1]{0:T(128)} %bitcast.16.place, bf16[64,16,1024]{2,1,0:T(8,128)(2,1)} %copy-done.1), custom_call_target="tpu_custom_call" | custom-call | flops 1000000 | bytes 6000000 | tf_op jit(solution)/shard_map/write_half/pallas_call | solution.py:530
  160.8 3.7 %write_half.3 = f32[512,4096]{1,0:T(8,128)} custom-call(s32[1]{0:T(128)S(6)} %sub.14.place, bf16[64,16,1024]{2,1,0:T(8,128)(2,1)} %collective-permute-done.17.mine, f32[512,4096]{1,0:T(8,128)} %write_half.2.refs_0_), custom_call_target="tpu_custom_call", output_to_operand_aliasing={{}: (2, {})} | custom-call | flops 1000000 | bytes 6000000 | tf_op jit(solution)/shard_map/write_half/pallas_call | solution.py:530
  (76 shorter events, 17.8 us)
Async XLA Ops:
  8.8 22.2 %all-to-all-start = ((bf16[8,272,256]{2,1,0:T(8,128)(2,1)}), bf16[8,272,256]{2,1,0:T(8,128)(2,1)S(1)}, u32[]{:S(2)}, u32[]{:S(2)}) async-start(bf16[8,272,256]{2,1,0:T(8,128)(2,1)} %get-tuple-element.28), calls=%async_computation | async-start | bytes 2228224 | tf_op jit(solution)/shard_map/all_to_all | solution.py:580
  16.0 26.0 %collective-permute-start.2 = (bf16[256,1024]{1,0:T(8,128)(2,1)}, bf16[256,1024]{1,0:T(8,128)(2,1)S(1)}, u32[]{:S(2)}, u32[]{:S(2)}) collective-permute-start(bf16[256,1024]{1,0:T(8,128)(2,1)} %get-tuple-element.56), channel_id=1, source_target_pairs={{0,40},{8,32},{32,8},{40,0},{1,41},{9,33},{33,9},{41,1},{2,42},{10... | collective-permute-start | bytes 1572872 | tf_op jit(solution)/shard_map/ppermute | solution.py:596
  18.4 23.5 %collective-permute-start = (bf16[256,1024]{1,0:T(8,128)(2,1)}, bf16[256,1024]{1,0:T(8,128)(2,1)S(1)}, u32[]{:S(2)}, u32[]{:S(2)}) collective-permute-start(bf16[256,1024]{1,0:T(8,128)(2,1)} %get-tuple-element.57), channel_id=1, source_target_pairs={{0,32},{32,0},{1,33},{33,1},{2,34},{34,2},{3,35},{35,3},{4,36},{36... | collective-permute-start | bytes 1572872 | tf_op jit(solution)/shard_map/ppermute | solution.py:592
  18.4 23.5 %collective-permute-start.1 = (bf16[256,1024]{1,0:T(8,128)(2,1)}, bf16[256,1024]{1,0:T(8,128)(2,1)S(1)}, u32[]{:S(2)}, u32[]{:S(2)}) collective-permute-start(bf16[256,1024]{1,0:T(8,128)(2,1)} %get-tuple-element.58), channel_id=1, source_target_pairs={{0,8},{8,0},{1,9},{9,1},{2,10},{10,2},{3,11},{11,3},{4,12},{12,4},... | collective-permute-start | bytes 1572872 | tf_op jit(solution)/shard_map/ppermute | solution.py:584
  19.6 22.4 %collective-permute-start.3 = (bf16[8,512]{1,0:T(8,128)(2,1)S(1)}, bf16[8,512]{1,0:T(8,128)(2,1)S(1)}, u32[]{:S(2)}, u32[]{:S(2)}) collective-permute-start(bf16[8,512]{1,0:T(8,128)(2,1)S(1)} %slice_bitcast_fusion), channel_id=1, source_target_pairs={{0,1},{1,2},{2,3},{3,4},{4,5},{5,6},{6,7},{8,9},{9,10},{10,11},{11... | collective-permute-start | bytes 24584 | tf_op jit(solution)/shard_map/ppermute | solution.py:588
  41.9 14.0 %copy-start.23 = (bf16[8,512]{1,0:T(8,128)(2,1)}, bf16[8,512]{1,0:T(8,128)(2,1)S(1)}, u32[]{:S(2)}) copy-start(bf16[8,512]{1,0:T(8,128)(2,1)S(1)} %collective-permute-done.3.edge) | copy-start | bytes 24580
  41.9 14.0 %copy-start.5 = (bf16[256,1024]{1,0:T(8,128)(2,1)}, bf16[256,1024]{1,0:T(8,128)(2,1)S(1)}, u32[]{:S(2)}) copy-start(bf16[256,1024]{1,0:T(8,128)(2,1)S(1)} %collective-permute-done.2.g11) | copy-start | bytes 1572868
  42.0 14.0 %copy-start.6 = (bf16[256,1024]{1,0:T(8,128)(2,1)}, bf16[256,1024]{1,0:T(8,128)(2,1)S(1)}, u32[]{:S(2)}) copy-start(bf16[256,1024]{1,0:T(8,128)(2,1)S(1)} %collective-permute-done.g01) | copy-start | bytes 1572868
  42.0 14.0 %copy-start.7 = (bf16[256,1024]{1,0:T(8,128)(2,1)}, bf16[256,1024]{1,0:T(8,128)(2,1)S(1)}, u32[]{:S(2)}) copy-start(bf16[256,1024]{1,0:T(8,128)(2,1)S(1)} %collective-permute-done.1.g10) | copy-start | bytes 1572868
  42.0 16.7 %all-to-all-start.1 = ((bf16[8,384,128]{2,1,0:T(8,128)(2,1)}), bf16[8,384,128]{2,1,0:T(8,128)(2,1)S(1)}, u32[]{:S(2)}, u32[]{:S(2)}) async-start(bf16[8,384,128]{2,1,0:T(8,128)(2,1)} %conv.1), calls=%async_computation.1 | async-start | bytes 1572864 | tf_op jit(solution)/shard_map/all_to_all | solution.py:580
  61.6 7.0 %collective-permute-start.4 = (bf16[256,512]{1,0:T(8,128)(2,1)}, bf16[256,512]{1,0:T(8,128)(2,1)S(1)}, u32[]{:S(2)}, u32[]{:S(2)}) collective-permute-start(bf16[256,512]{1,0:T(8,128)(2,1)} %get-tuple-element.42.m00), channel_id=1, source_target_pairs={{0,32},{32,0},{1,33},{33,1},{2,34},{34,2},{3,35},{35,3},{4,36},{36... | collective-permute-start | bytes 786440 | tf_op jit(solution)/shard_map/ppermute | solution.py:592
  63.5 12.6 %collective-permute-start.5 = (bf16[256,512]{1,0:T(8,128)(2,1)}, bf16[256,512]{1,0:T(8,128)(2,1)S(1)}, u32[]{:S(2)}, u32[]{:S(2)}) collective-permute-start(bf16[256,512]{1,0:T(8,128)(2,1)} %get-tuple-element.42.m00), channel_id=1, source_target_pairs={{0,8},{8,0},{1,9},{9,1},{2,10},{10,2},{3,11},{11,3},{4,12},{12,4},... | collective-permute-start | bytes 786440 | tf_op jit(solution)/shard_map/ppermute | solution.py:584
  68.6 7.5 %copy-start.9 = (bf16[256,512]{1,0:T(8,128)(2,1)}, bf16[256,512]{1,0:T(8,128)(2,1)S(1)}, u32[]{:S(2)}) copy-start(bf16[256,512]{1,0:T(8,128)(2,1)S(1)} %collective-permute-done.4.m01) | copy-start | bytes 786436
  68.6 7.5 %collective-permute-start.6 = (bf16[256,512]{1,0:T(8,128)(2,1)S(1)}, bf16[256,512]{1,0:T(8,128)(2,1)S(1)}, u32[]{:S(2)}, u32[]{:S(2)}) collective-permute-start(bf16[256,512]{1,0:T(8,128)(2,1)S(1)} %collective-permute-done.4.m01), channel_id=1, source_target_pairs={{0,8},{8,0},{1,9},{9,1},{2,10},{10,2},{3,11},{11,3},{4,12},{12,4},... | collective-permute-start | bytes 786440 | tf_op jit(solution)/shard_map/ppermute | solution.py:584
  70.9 5.1 %collective-permute-start.7 = (bf16[8,4,16,128]{3,2,1,0:T(8,128)(2,1)S(1)}, bf16[8,4,16,128]{3,2,1,0:T(8,128)(2,1)S(1)}, u32[]{:S(2)}, u32[]{:S(2)}) collective-permute-start(bf16[8,4,16,128]{3,2,1,0:T(8,128)(2,1)S(1)} %bitcast.34), channel_id=1, source_target_pairs={{0,32},{32,0},{1,33},{33,1},{2,34},{34,2},{3,35},{35,3},{4,36},{36... | collective-permute-start | bytes 393224 | tf_op jit(solution)/shard_map/ppermute | solution.py:592
  72.4 8.7 %collective-permute-start.8 = (f32[8,512]{1,0:T(8,128)}, f32[8,512]{1,0:T(8,128)S(1)}, u32[]{:S(2)}, u32[]{:S(2)}) collective-permute-start(f32[8,512]{1,0:T(8,128)} %get-tuple-element.40), channel_id=1, source_target_pairs={{1,0},{2,1},{3,2},{4,3},{5,4},{6,5},{7,6},{9,8},{10,9},{11,10},{12... | collective-permute-start | bytes 49160 | tf_op jit(solution)/shard_map/ppermute | solution.py:588
  81.1 12.3 %copy-start.8 = (bf16[256,512]{1,0:T(8,128)(2,1)S(1)}, bf16[256,512]{1,0:T(8,128)(2,1)}, u32[]{:S(2)}) copy-start(bf16[256,512]{1,0:T(8,128)(2,1)} %get-tuple-element.42.m00) | copy-start | bytes 786436
  81.1 9.6 %copy-start.22 = (f32[8,512]{1,0:T(8,128)}, f32[8,512]{1,0:T(8,128)S(1)}, u32[]{:S(2)}) copy-start(f32[8,512]{1,0:T(8,128)S(1)} %collective-permute-done.8.tail) | copy-start | bytes 49156
  81.1 29.4 %all-to-all-start.2 = ((bf16[32,16,1152]{2,1,0:T(8,128)(2,1)}), bf16[32,16,1152]{2,1,0:T(8,128)(2,1)S(1)}, u32[]{:S(2)}, u32[]{:S(2)}) async-start(bf16[32,16,1152]{2,1,0:T(8,128)(2,1)} %partial.1), calls=%async_computation.2 | async-start | bytes 2359296 | tf_op jit(solution)/shard_map/all_to_all | solution.py:580
  114.5 40.2 %all-to-all-start.3 = ((bf16[64,16,1024]{2,1,0:T(8,128)(2,1)}), bf16[64,16,1024]{2,1,0:T(8,128)(2,1)S(1)}, u32[]{:S(2)}, u32[]{:S(2)}) async-start(bf16[64,16,1024]{2,1,0:T(8,128)(2,1)} %get-tuple-element.48), calls=%async_computation.3 | async-start | bytes 4194304 | tf_op jit(solution)/shard_map/all_to_all | solution.py:580
  119.4 2.9 %collective-permute-start.9 = (f32[16,1024]{1,0:T(8,128)S(1)}, f32[16,1024]{1,0:T(8,128)S(1)}, u32[]{:S(2)}, u32[]{:S(2)}) collective-permute-start(f32[16,1024]{1,0:T(8,128)S(1)} %copy-done.14), channel_id=1, source_target_pairs={{0,8},{8,0},{1,9},{9,1},{2,10},{10,2},{3,11},{11,3},{4,12},{12,4},... | collective-permute-start | bytes 196616 | tf_op jit(solution)/shard_map/ppermute | solution.py:584
  122.2 30.1 %copy-start.13 = (bf16[16,1024]{1,0:T(8,128)(2,1)}, bf16[16,1024]{1,0:T(8,128)(2,1)S(1)}, u32[]{:S(2)}) copy-start(bf16[16,1024]{1,0:T(8,128)(2,1)S(1)} %add_convert_fusion.refs_0_) | copy-start | bytes 98308
  122.3 13.5 %collective-permute-start.16 = (bf16[16,1024]{1,0:T(8,128)(2,1)S(1)}, bf16[16,1024]{1,0:T(8,128)(2,1)S(1)}, u32[]{:S(2)}, u32[]{:S(2)}) collective-permute-start(bf16[16,1024]{1,0:T(8,128)(2,1)S(1)} %add_convert_fusion.refs_0_), channel_id=1, source_target_pairs={{0,112},{16,96},{32,80},{48,64},{64,48},{80,32},{96,16},{112,0},{1... | collective-permute-start | bytes 98312 | tf_op jit(solution)/shard_map/ppermute | solution.py:601
  127.7 16.7 %collective-permute-start.15 = (bf16[16,1024]{1,0:T(8,128)(2,1)S(1)}, bf16[16,1024]{1,0:T(8,128)(2,1)S(1)}, u32[]{:S(2)}, u32[]{:S(2)}) collective-permute-start(bf16[16,1024]{1,0:T(8,128)(2,1)S(1)} %add_convert_fusion.refs_0_), channel_id=1, source_target_pairs={{0,96},{16,112},{32,64},{48,80},{64,32},{80,48},{96,0},{112,16},{1... | collective-permute-start | bytes 98312 | tf_op jit(solution)/shard_map/ppermute | solution.py:601
  127.7 23.3 %collective-permute-start.14 = (bf16[16,1024]{1,0:T(8,128)(2,1)S(1)}, bf16[16,1024]{1,0:T(8,128)(2,1)S(1)}, u32[]{:S(2)}, u32[]{:S(2)}) collective-permute-start(bf16[16,1024]{1,0:T(8,128)(2,1)S(1)} %add_convert_fusion.refs_0_), channel_id=1, source_target_pairs={{0,80},{16,64},{32,112},{48,96},{64,16},{80,0},{96,48},{112,32},{1... | collective-permute-start | bytes 98312 | tf_op jit(solution)/shard_map/ppermute | solution.py:601
  129.3 21.8 %collective-permute-start.13 = (bf16[16,1024]{1,0:T(8,128)(2,1)S(1)}, bf16[16,1024]{1,0:T(8,128)(2,1)S(1)}, u32[]{:S(2)}, u32[]{:S(2)}) collective-permute-start(bf16[16,1024]{1,0:T(8,128)(2,1)S(1)} %add_convert_fusion.refs_0_), channel_id=1, source_target_pairs={{0,64},{16,80},{32,96},{48,112},{64,0},{80,16},{96,32},{112,48},{1... | collective-permute-start | bytes 98312 | tf_op jit(solution)/shard_map/ppermute | solution.py:601
  130.7 20.3 %collective-permute-start.12 = (bf16[16,1024]{1,0:T(8,128)(2,1)S(1)}, bf16[16,1024]{1,0:T(8,128)(2,1)S(1)}, u32[]{:S(2)}, u32[]{:S(2)}) collective-permute-start(bf16[16,1024]{1,0:T(8,128)(2,1)S(1)} %add_convert_fusion.refs_0_), channel_id=1, source_target_pairs={{0,48},{16,32},{32,16},{48,0},{64,112},{80,96},{96,80},{112,64},{1... | collective-permute-start | bytes 98312 | tf_op jit(solution)/shard_map/ppermute | solution.py:601
  135.7 16.6 %copy-start.15 = (bf16[16,1024]{1,0:T(8,128)(2,1)}, bf16[16,1024]{1,0:T(8,128)(2,1)S(1)}, u32[]{:S(2)}) copy-start(bf16[16,1024]{1,0:T(8,128)(2,1)S(1)} %collective-permute-done.16.refs_7_) | copy-start | bytes 98308
  135.7 15.4 %collective-permute-start.11 = (bf16[16,1024]{1,0:T(8,128)(2,1)S(1)}, bf16[16,1024]{1,0:T(8,128)(2,1)S(1)}, u32[]{:S(2)}, u32[]{:S(2)}) collective-permute-start(bf16[16,1024]{1,0:T(8,128)(2,1)S(1)} %add_convert_fusion.refs_0_), channel_id=1, source_target_pairs={{0,32},{16,48},{32,0},{48,16},{64,96},{80,112},{96,64},{112,80},{1... | collective-permute-start | bytes 98312 | tf_op jit(solution)/shard_map/ppermute | solution.py:601
  144.4 8.0 %copy-start.16 = (bf16[16,1024]{1,0:T(8,128)(2,1)}, bf16[16,1024]{1,0:T(8,128)(2,1)S(1)}, u32[]{:S(2)}) copy-start(bf16[16,1024]{1,0:T(8,128)(2,1)S(1)} %collective-permute-done.15.refs_6_) | copy-start | bytes 98308
  144.4 7.9 %collective-permute-start.10 = (bf16[16,1024]{1,0:T(8,128)(2,1)S(1)}, bf16[16,1024]{1,0:T(8,128)(2,1)S(1)}, u32[]{:S(2)}, u32[]{:S(2)}) collective-permute-start(bf16[16,1024]{1,0:T(8,128)(2,1)S(1)} %add_convert_fusion.refs_0_), channel_id=1, source_target_pairs={{0,16},{16,0},{32,48},{48,32},{64,80},{80,64},{96,112},{112,96},{1... | collective-permute-start | bytes 98312 | tf_op jit(solution)/shard_map/ppermute | solution.py:601
  154.8 6.1 %collective-permute-start.17 = (bf16[64,16,1024]{2,1,0:T(8,128)(2,1)S(1)}, bf16[64,16,1024]{2,1,0:T(8,128)(2,1)}, u32[]{:S(2)}, u32[]{:S(2)}) collective-permute-start(bf16[64,16,1024]{2,1,0:T(8,128)(2,1)S(1)} %all-to-all-done.3.mine), channel_id=1, source_target_pairs={{0,8},{8,0},{1,9},{9,1},{2,10},{10,2},{3,11},{11,3},{4,12},{12,4},... | collective-permute-start | bytes 6291464 | tf_op jit(solution)/shard_map/ppermute | solution.py:584
  (14 other events, 24.1 us)

commit v10 on v9

--- a/solution.py
+++ b/solution.py
@@ -275,10 +275,17 @@
         t = jnp.where(low, time[b], time[7 - b]) + gain * prod[b]
         rows = pl.ds(pl.multiple_of(BLOCK * b, 8), BLOCK)
         after[rows] = jnp.where(low, turned(t), t) * turned(gates[b])
-        sent[b, BLOCK:] = jnp.where(low128, t[0:128], turned(t[128:256])).astype(BF)
+        sent[b, BLOCK:384] = jnp.where(low128, t[0:128], turned(t[128:256])).astype(BF)
         return carry
 
     lax.fori_loop(0, 8, gate, 0)
+    low8 = low_lanes(8)
+    for b in range(8):
+        if b < 7:
+            t = jnp.where(low8, time[b + 1, 0:8], time[6 - b, 0:8]) + gain * prod[b + 1, 0:8]
+        else:
+            t = jnp.zeros((8, 128), F32)
+        sent[b, 384:400] = jnp.concatenate([t, t], axis=0).astype(BF)
     after[8 * BLOCK :] = jnp.zeros((8, 128), F32)
     taps = pair(1, 2)
     for b in range(8):
@@ -289,8 +296,8 @@
 
 def lag_kernel(
     place, got, short, skip, ahead_h, ahead_l, back_h, back_l,
-    lags,
-    pad, prod, spec, lres,
+    lags, lags_z,
+    pad, prod, spec, lres, rows,
 ):
     pair, _ = weights(place, short, skip)
     prepare(got, pair, pad, prod)
@@ -318,17 +325,18 @@
     def invert(n, carry):
         x = jnp.concatenate([flipped(lres[a], -1.0) for a in (2 * n, 2 * n + 1)], axis=1)
         out = apply(back_h, back_l, *split(x))
-        low16 = low_lanes(16)
         for t in range(2):
-            for k in range(8):
-                x = out[32 * k : 32 * k + 16, 128 * t : 128 * t + 128]
-                y = out[32 * k + 16 : 32 * k + 32, 128 * t : 128 * t + 128]
-                m = 4 * n + 2 * t
-                lags[m, k] = jnp.where(low16, turned(x), y).astype(BF)
-                lags[m + 1, k] = jnp.where(low16, x, turned(y)).astype(BF)
+            for k in range(4):
+                there = pl.ds(8 * n + 4 * t + k, 64, stride=16)
+                rows[there, :] = out[64 * k : 64 * k + 64, 128 * t : 128 * t + 128]
         return carry
 
-    lax.fori_loop(0, 2, invert, 0)
+    for n in range(2):
+        invert(n, 0)
+    for z in range(2):
+        for ref, side in ((lags, place[1]), (lags_z, 1 - place[1])):
+            part = rows[pl.ds(pl.multiple_of(512 * z + 256 * side, 256), 256), :]
+            ref[16 * z : 16 * z + 16] = part.reshape(16, 16, 128).astype(BF)
 
 
 def on_channels(kernel, name, inputs, in_shapes, outputs, scratch, cost):
@@ -367,71 +375,66 @@
 
 def conv(place, got, short, skip):
     inputs = (place, got, short, skip, *(jnp.asarray(t) for t in tables()))
-    outputs = [((8, 384, 128), BF)]
+    outputs = [((8, 400, 128), BF)]
     scratch = [BLOCKS, BLOCKS, BINS, BINS, BINS, BLOCKS, ((8 * BLOCK + 8, 128), F32)]
     return on_channels(conv_kernel, "conv", inputs, TABLES, outputs, scratch, None)[0]
 
 
 def lag_sums(place, got, short, skip):
     inputs = (place, got, short, skip, *(jnp.asarray(t) for t in tables()))
-    outputs = [((8, 8, 16, 128), BF)]
-    scratch = [BLOCKS, BINS, ((4, 512, 128), F32)]
+    outputs = [((32, 16, 128), BF)] * 2
+    scratch = [BLOCKS, BINS, ((4, 512, 128), F32), ((1024, 128), F32)]
     cost = spent(2 * 10**9)
-    return on_channels(lag_kernel, "lag_sums", inputs, TABLES, outputs, scratch, cost)[0]
-
-
-def convolved(got, q, low128):
-    a, b = got[2 * q, -128:].astype(F32), got[2 * q + 1, -128:].astype(F32)
+    return on_channels(lag_kernel, "lag_sums", inputs, TABLES, outputs, scratch, cost)
+
+
+def convolved(got, q, start, low128):
+    there = slice(start, start + 128)
+    a, b = got[2 * q, there].astype(F32), got[2 * q + 1, there].astype(F32)
     return jnp.where(low128, a, turned(b)), jnp.where(low128, turned(a), b)
 
 
-def mixed_kernel(got, gate_out, grad, edge, short, mixed, head, pad):
+def mixed_kernel(got, gate_out, edge, short, mixed, pad):
     low128 = low_lanes(128)
     pad[0:8] = edge[...].astype(F32)
     pad[8:] = jnp.zeros((8, 512), F32)
     more = sum(short[j : j + 1] * pad[8 - j : 16 - j] for j in (1, 2))
     for q in range(4):
         lanes = slice(128 * q, 128 * q + 128)
-        first, second = convolved(got, q, low128)
+        first, second = convolved(got, q, 0, low128)
         gate = gate_out[0:128, lanes]
         gate = jnp.concatenate([gate[0:8] + more[:, lanes], gate[8:]], axis=0)
         mixed[0:128, lanes] = (gate * first).astype(BF)
         mixed[128:256, lanes] = (gate_out[128:256, lanes] * second).astype(BF)
-        head[:, lanes] = grad[:, lanes] * first[0:8]
-
-
-def unpack_mixed(got, gate_out, grad, edge, short):
+
+
+def unpack_mixed(got, gate_out, edge, short):
+    full = lambda *shape: pl.BlockSpec(shape, lambda n: (0,) * len(shape))
     return pl.pallas_call(
         mixed_kernel,
         grid=(1,),
         in_specs=[
             pl.BlockSpec((8, 128, 128), lambda n: (0, 2, 0)),
-            pl.BlockSpec((BLOCK, 512), lambda n: (0, 0)),
-            pl.BlockSpec((8, 512), lambda n: (0, 0)),
-            pl.BlockSpec((8, 512), lambda n: (0, 0)),
-            pl.BlockSpec((9, 512), lambda n: (0, 0)),
+            full(BLOCK, 512),
+            full(8, 512),
+            full(9, 512),
         ],
-        out_specs=[
-            pl.BlockSpec((BLOCK, 512), lambda n: (0, 0)),
-            pl.BlockSpec((8, 512), lambda n: (0, 0)),
-        ],
+        out_specs=full(BLOCK, 512),
+        out_shape=jax.ShapeDtypeStruct((BLOCK, 512), BF),
         scratch_shapes=[pltpu.VMEM((16, 512), F32)],
-        out_shape=[
-            jax.ShapeDtypeStruct((BLOCK, 512), BF),
-            jax.ShapeDtypeStruct((8, 512), F32),
-        ],
         name="unpack_mixed",
-    )(got, gate_out, grad, edge, short)
-
-
-def grads_kernel(got, grad, tail, short, grads, pad):
-    low, low128 = low_lanes(BLOCK), low_lanes(128)
-    pad[BLOCK:] = tail[...]
+    )(got, gate_out, edge, short)
+
+
+def grads_kernel(got, grad, later, short, grads, pad):
+    low, low128, low8 = low_lanes(BLOCK), low_lanes(128), low_lanes(8)
     for q in range(4):
         lanes = slice(128 * q, 128 * q + 128)
-        first, second = convolved(got, q, low128)
+        first, second = convolved(got, q, BLOCK, low128)
         pad[0:128, lanes] = grad[0:128, lanes] * first
         pad[128:256, lanes] = grad[128:256, lanes] * second
+        a, b = (got[2 * q + n, 384:400].astype(F32)[0:8] for n in range(2))
+        pad[256:264, lanes] = later[:, lanes] * jnp.where(low8, a, turned(b))
         a, b = got[2 * q, 0:BLOCK].astype(F32), got[2 * q + 1, 0:BLOCK].astype(F32)
         grads[1, :, lanes] = jnp.where(low, a, turned(b)).astype(BF)
         grads[2, :, lanes] = jnp.where(low, turned(a), b).astype(BF)
@@ -440,14 +443,14 @@
         ).astype(BF)
 
 
-def unpack_grads(got, grad, tail, short):
+def unpack_grads(got, grad, later, short):
     return pl.pallas_call(
         grads_kernel,
         out_shape=jax.ShapeDtypeStruct((3, BLOCK, 512), BF),
         scratch_shapes=[pltpu.VMEM((BLOCK + 8, 512), F32)],
         cost_estimate=pl.CostEstimate(flops=10**6, bytes_accessed=2 * 10**6, transcendentals=0),
         name="unpack_grads",
-    )(got, grad, tail, short)
+    )(got, grad, later, short)
 
 
 def partial_kernel(place, m00, m01, m10, m11, g00, g01, g10, g11, lags, lags_z, packed):
@@ -460,8 +463,7 @@
     part = part.astype(BF)
     for n in range(32):
         packed[n, :, 0:1024] = part[16 * n : 16 * n + 16]
-        s, k = n % 8, n // 8
-        lag = lags[s, k].astype(F32) + lags_z[s, k].astype(F32)
+        lag = lags[n].astype(F32) + lags_z[n].astype(F32)
         packed[n, :, 1024:1152] = lag.astype(BF)
 
 
@@ -475,7 +477,7 @@
             in_specs=[full(BLOCK, 512)] * 4
             + [pl.BlockSpec((BLOCK, 1024), lambda n, p: (0, p[0]))]
             + [full(BLOCK, 1024)] * 3
-            + [full(8, 4, 16, 128)] * 2,
+            + [full(32, 16, 128)] * 2,
             out_specs=full(32, 16, 1152),
         ),
         out_shape=jax.ShapeDtypeStruct((32, 16, 1152), BF),
@@ -488,92 +490,86 @@
     for n in range(32):
         total = total + got[n, :, 0:1024].astype(F32)
     total = (total * scale).astype(BF)
+    low = low_lanes(16)
+    for q in range(4):
+        a, b = (
+            sum(got[8 * k + s, :, 1024:1152].astype(F32) for k in range(4))
+            for s in (2 * q, 2 * q + 1)
+        )
+        sides = (jnp.where(low, turned(a), b), jnp.where(low, a, turned(b)))
+        for s in range(8):
+            start = 4 * (s // 2)
+            lags[s, 4 * q : 4 * q + 4] = sides[s % 2][start : start + 4] * scale
     for n in range(64):
-        shared[n] = total
-    for s in range(8):
-        lag = jnp.zeros((16, 128), F32)
-        for k in range(4):
-            lag = lag + got[8 * k + s, :, 1024:1152].astype(F32)
-        lags[:, 128 * s : 128 * s + 128] = lag * scale
+        shared[n, :, 0:1024] = total
+        shared[n, :, 1024:1152] = lags[n % 8].astype(BF)
 
 
 def reduce(got, scale):
     return pl.pallas_call(
         functools.partial(reduce_kernel, scale),
-        out_shape=[
-            jax.ShapeDtypeStruct((64, 16, 1024), BF),
-            jax.ShapeDtypeStruct((16, 1024), F32),
-        ],
+        out_shape=jax.ShapeDtypeStruct((64, 16, 1152), BF),
+        scratch_shapes=[pltpu.VMEM((8, 16, 128), F32)],
         name="reduce",
     )(got)
 
 
-def half_kernel(place, mine, *refs):
-    grad_weight, wide, sems = refs[-3:]
-
-    def copy(n):
+def start_writes(place, rows, grad_weight, wide, sems):
+    copies = []
+    for n in range(8):
         zh, zl, yh = n // 4, n // 2 % 2, n % 2
-        rows = slice(128 * (2 * zh + yh), 128 * (2 * zh + yh) + 128)
+        for k in range(8):
+            wide[n, 16 * k : 16 * k + 16] = rows[8 * n + k].astype(F32)
+        there = slice(128 * (2 * zh + yh), 128 * (2 * zh + yh) + 128)
         lanes = pl.ds(pl.multiple_of(2048 * place[0] + 1024 * zl, 1024), 1024)
-        return pltpu.make_async_copy(wide.at[n], grad_weight.at[rows, lanes], sems.at[n])
-
-    for n in range(8):
-        for k in range(8):
-            wide[n, 16 * k : 16 * k + 16] = mine[8 * n + k].astype(F32)
-        copy(n).start()
-    for n in range(8):
-        copy(n).wait()
-
-
-def write_half(half, rows, whole=None):
-    more = [] if whole is None else [whole]
+        copies.append(
+            pltpu.make_async_copy(wide.at[n], grad_weight.at[there, lanes], sems.at[n])
+        )
+        copies[-1].start()
+    return copies
+
+
+def first_kernel(place, rows, grad_weight, wide, sems):
+    for copy in start_writes(place, rows, grad_weight, wide, sems):
+        copy.wait()
+
+
+def last_kernel(place, rows, lags, lags_c, whole, grad_weight, grad_filter, wide, sems, sums):
+    copies = start_writes(place, rows, grad_weight, wide, sems)
+    total = lags[...].astype(F32) + lags_c[...].astype(F32)
+    sums[...] = total.reshape(1024, 128)
+    for q in range(4):
+        for k in range(4):
+            part = sums[pl.ds(4 * q + k, 64, stride=16), :]
+            grad_filter[64 * k : 64 * k + 64, 128 * q : 128 * q + 128] = part
+    for copy in copies:
+        copy.wait()
+
+
+def write_half(half, rows, mine=None, whole=None):
+    last = whole is not None
+    rows_spec = pl.BlockSpec((64, 16, 1024), lambda n, p: (0, 0, 0))
+    lags_spec = pl.BlockSpec((64, 16, 128), lambda n, p: (0, 0, 8))
+    hbm = pl.BlockSpec(memory_space=pltpu.HBM)
+    shapes = [jax.ShapeDtypeStruct((512, 4096), F32)]
+    scratch = [pltpu.VMEM((8, 128, 1024), F32), pltpu.SemaphoreType.DMA((8,))]
+    if last:
+        shapes.append(jax.ShapeDtypeStruct((BLOCK, 512), F32))
+        scratch.append(pltpu.VMEM((1024, 128), F32))
     return pl.pallas_call(
-        half_kernel,
+        last_kernel if last else first_kernel,
         grid_spec=pltpu.PrefetchScalarGridSpec(
             num_scalar_prefetch=1,
             grid=(1,),
-            in_specs=[pl.BlockSpec((64, 16, 1024), lambda n, p: (0, 0, 0))]
-            + [pl.BlockSpec(memory_space=pltpu.HBM)] * len(more),
-            out_specs=pl.BlockSpec(memory_space=pltpu.HBM),
-            scratch_shapes=[
-                pltpu.VMEM((8, 128, 1024), F32),
-                pltpu.SemaphoreType.DMA((8,)),
-            ],
+            in_specs=[rows_spec] + [lags_spec, lags_spec, hbm] * last,
+            out_specs=[hbm] + [pl.BlockSpec((BLOCK, 512), lambda n, p: (0, 0))] * last,
+            scratch_shapes=scratch,
         ),
-        out_shape=jax.ShapeDtypeStruct((512, 4096), F32),
-        input_output_aliases={2: 0} if more else {},
+        out_shape=shapes,
+        input_output_aliases={4: 0} if last else {},
         cost_estimate=pl.CostEstimate(flops=10**6, bytes_accessed=6 * 10**6, transcendentals=0),
-        name="write_half",
-    )(half, rows, *more)
-
-
-def filter_kernel(place, *refs):
-    grad_filter = refs[-1]
-    low = low_lanes(16)
-    for n in range(8):
-        row = pl.multiple_of(32 * (place[0] ^ n), 32)
-        for q in range(4):
-            a = refs[n][:, 256 * q : 256 * q + 128].astype(F32)
-            b = refs[n][:, 256 * q + 128 : 256 * q + 256].astype(F32)
-            lanes = slice(128 * q, 128 * q + 128)
-            grad_filter[pl.ds(row, 16), lanes] = jnp.where(low, a, turned(b))
-            grad_filter[pl.ds(row + 16, 16), lanes] = jnp.where(low, turned(a), b)
-
-
-def write_filter(place, lags):
-    full = lambda *shape: pl.BlockSpec(shape, lambda n, p: (0,) * len(shape))
-    return pl.pallas_call(
-        filter_kernel,
-        grid_spec=pltpu.PrefetchScalarGridSpec(
-            num_scalar_prefetch=1,
-            grid=(1,),
-            in_specs=[full(16, 1024)] * 8,
-            out_specs=full(BLOCK, 512),
-        ),
-        out_shape=jax.ShapeDtypeStruct((BLOCK, 512), F32),
-        cost_estimate=pl.CostEstimate(flops=10**6, bytes_accessed=2 * 10**6, transcendentals=0),
-        name="write_filter",
-    )(place, *lags)
+        name="write_last" if last else "write_first",
+    )(half, rows, *([rows, mine, whole] if last else []))
 
 
 def exchange(x, axes):
@@ -594,12 +590,6 @@
 
 def opposite(x):
     return lax.ppermute(x, ("zl", "c"), [(n, 3 - n) for n in range(4)])
-
-
-def gathered(lags):
-    return [lags] + [
-        lax.ppermute(lags, DEPTH, [(i, i ^ n) for i in range(8)]) for n in range(1, 8)
-    ]
 
 
 def on_device(streams, short_filter, long_filter, skip_gain, out_weight, out_grad):
@@ -621,38 +611,30 @@
     packed, grad_mixed, gate_out = pack(streams[:, 0], grad, out_weight, long_filter, short)
     got = exchange(packed, SEQ)
     edge = along(streams[0, 0, BLOCK - 8 :], 1)
-    channels = (seq[None], got, short, skip_gain.reshape(1, 512))
-    sent = conv(*channels)
-    sent, got, grads, edge = lax.optimization_barrier((sent, got, grads, edge))
-    channels = (channels[0], got) + channels[2:]
-    lags = lag_sums(*channels).reshape(8, 2, 2, 2, 16, 128)
-
-    def of_side(z):
-        return lax.dynamic_index_in_dim(lags, z, 2, False).reshape(8, 4, 16, 128)
-
-    lags_own, lags_z = of_side(side), above(of_side(1 - side))
+    later = along(grad_mixed[:8], -1)
+    place = jnp.stack([seq, side])
+    gain = skip_gain.reshape(1, 512)
+    sent = conv(place, got, short, gain)
+    sent, got, grads, edge, later = lax.optimization_barrier((sent, got, grads, edge, later))
+    lags_own, lags = lag_sums(place, got, short, gain)
+    lags_z = above(lags)
     back = exchange(sent, SEQ)
-    back, lags_own = lax.optimization_barrier((back, lags_own))
-    m00, head = unpack_mixed(back, gate_out, grad_mixed, edge, short)
+    back, lags_own, lags_z = lax.optimization_barrier((back, lags_own, lags_z))
+    m00 = unpack_mixed(back, gate_out, edge, short)
     m01, m10 = above(m00), across(m00)
     mixed = (m00, m01, m10, across(m01))
-    tail = along(head, -1)
     part = partial((2 * core + side)[None], mixed, grad, grads, lags_own, lags_z)
-    part, m00, back, tail = lax.optimization_barrier((part, m00, back, tail))
+    part, m00, back = lax.optimization_barrier((part, m00, back))
     part = exchange(part, MOST)
     layer_out = jnp.dot(m00, out_weight, preferred_element_type=F32).astype(BF)
-    grad_streams = unpack_grads(back, grad_mixed, tail, short)
-    part, layer_out, grad_streams = lax.optimization_barrier((part, layer_out, grad_streams))
-    rows, lags = reduce(part, scale)
-    rows, lags = lax.optimization_barrier((rows, lags))
+    part, m00, layer_out = lax.optimization_barrier((part, m00, layer_out))
+    rows, back = lax.optimization_barrier((reduce(part, scale), back))
     mine = exchange(rows, CHIPS)
-    lags = (lags + across(lags)).astype(BF)
-    depth = lax.axis_index(DEPTH).astype(jnp.int32)
-    grad_filter = write_filter(depth[None], gathered(lags))
-    mine, grad_filter = lax.optimization_barrier((mine, grad_filter))
+    grad_streams = unpack_grads(back, grad_mixed, later, short)
+    mine, grad_streams = lax.optimization_barrier((mine, grad_streams))
     theirs = across(mine)
-    grad_weight = write_half(core[None], mine)
-    grad_weight = write_half(1 - core[None], theirs, grad_weight)
+    grad_weight = write_half(core[None], mine)[0]
+    grad_weight, grad_filter = write_half(1 - core[None], theirs, mine, grad_weight)
     return layer_out[None], grad_streams[:, None], grad_filter, grad_weight
 
 

time: 167 us -> 162 us (0.970)
  starting transfers between devices: 63 us -> 45.5 us
  waiting for transfers between devices: 40 us -> 54.7 us
    all_to_all x4, waiting for transfers between devices: 21.2 us -> 48.1 us  [exchange(): return lax.all_to_all(x, axes, 0, 0, tiled=True)]
    ppermute x7 -> x0, starting transfers between devices: 18.2 us -> none  [gathered(): lax.ppermute(lags, DEPTH, [(i, i ^ n) for i in range(8)])]
    ppermute x7 -> x0, waiting for transfers between devices: 11.8 us -> none  [gathered(): lax.ppermute(lags, DEPTH, [(i, i ^ n) for i in range(8)])]
    ppermute x5 -> x4, starting transfers between devices: 8.49 us -> 9.78 us  [across(): return lax.ppermute(x, 'c', [(0, 1), (1, 0)])]
    pallas_call x4 -> x3, Pallas kernels: 12.1 us -> 11.3 us  [the longest x2 8.29 us: write_half(): pl.pallas_call(last_kernel if last else first_kernel, grid_spec=pltpu.Pre...]
    unnamed x48 -> x30, local copies, waits for them, and re-layouts: 4.41 us -> 3.67 us
  transfers between devices with their start and end apart: 22 -> 14, of which waited for: 10 -> 7; matrix products, arithmetic and copies ran while one was open for 5% -> 5% of each run, Pallas kernels for 19% -> 16%
where the time goes in v10:
time: 162 us; the launch traced here: 161 us
  waiting for transfers between devices  54.7 us (34%)
  Pallas kernels  46.8 us (29%)
  starting transfers between devices  45.5 us (28%)
  local copies, waits for them, and re-layouts  7.65 us (5%)
  matrix products  4.77 us (3%)
    all_to_all x4, waiting for transfers between devices, exchange(): return lax.all_to_all(x, axes, 0, 0, tiled=True)  48.1 us
    all_to_all x4, starting transfers between devices, exchange(): return lax.all_to_all(x, axes, 0, 0, tiled=True)  25.8 us
    pallas_call x2, Pallas kernels, on_channels(): pl.pallas_call(kernel, grid_spec=pltpu.PrefetchScalarGridSpec(num_scalar_...  19.9 us
    ppermute x4, starting transfers between devices, across(): return lax.ppermute(x, 'c', [(0, 1), (1, 0)])  9.78 us
    pallas_call x2, Pallas kernels, write_half(): pl.pallas_call(last_kernel if last else first_kernel, grid_spec=pltpu.Pre...  8.29 us
    pallas_call x1, Pallas kernels, pack(): pl.pallas_call(pack_kernel, grid=(steps,), in_specs=[full(3, BLOCK, 512),...  6.77 us
    ppermute x2, starting transfers between devices, along(): lax.ppermute(x, SEQ, [(n, n + step) for n in range(8) if 0 <= n + step < 8])  4.92 us
    ppermute x3, waiting for transfers between devices, above(): return lax.ppermute(x, 'zl', [(0, 1), (1, 0)])  4.87 us
  transfers between devices with their start and end apart: 14, of which 7 were waited for; matrix products, arithmetic and copies ran while one was open for 5% of the time, Pallas kernels for 16%

profile of v10, /device:TPU:1, one launch (start us, length us, event | category | flops | bytes accessed | tf_op | source)
XLA Modules:
  0.0 160.9 jit_solution(5784645332645634460)
XLA Ops:
  0.6 1.4 reshape.17.short
  2.0 6.8 %pack.1 = (bf16[8,272,256]{2,1,0:T(8,128)(2,1)}, f32[256,512]{1,0:T(8,128)}, f32[256,512]{1,0:T(8,128)}) custom-call(bf16[3,256,512]{2,1,0:T(8,128)(2,1)} %bitcast.23, bf16[256,4096]{1,0:T(8,128)(2,1)} %bitcast.21, bf16[512,4096]{1,0:T(8,128)(2,1)} %weight.1, f32[256,512]{1,0:T(8,128)} %filt.1, f32[9,512]{1,0:T(8,128)} %reshape.17.short), custom_call_target="tpu_custom_call" | custom-call | tf_op jit(solution)/shard_map/pack/pallas_call | solution.py:96
  8.8 6.0 %all-to-all-start = ((bf16[8,272,256]{2,1,0:T(8,128)(2,1)}), bf16[8,272,256]{2,1,0:T(8,128)(2,1)S(1)}, u32[]{:S(2)}, u32[]{:S(2)}) async-start(bf16[8,272,256]{2,1,0:T(8,128)(2,1)} %get-tuple-element.30), calls=%async_computation | async-start | bytes 2228224 | tf_op jit(solution)/shard_map/all_to_all | solution.py:576
  14.8 1.2 dynamic-slice_bitcast_fusion
  16.0 2.5 %collective-permute-start.2 = (bf16[256,1024]{1,0:T(8,128)(2,1)}, bf16[256,1024]{1,0:T(8,128)(2,1)S(1)}, u32[]{:S(2)}, u32[]{:S(2)}) collective-permute-start(bf16[256,1024]{1,0:T(8,128)(2,1)} %get-tuple-element.60), channel_id=1, source_target_pairs={{0,40},{8,32},{32,8},{40,0},{1,41},{9,33},{33,9},{41,1},{2,42},{10... | collective-permute-start | bytes 1572872 | tf_op jit(solution)/shard_map/ppermute | solution.py:592
  19.6 3.6 %collective-permute-start.3 = (bf16[8,512]{1,0:T(8,128)(2,1)S(1)}, bf16[8,512]{1,0:T(8,128)(2,1)S(1)}, u32[]{:S(2)}, u32[]{:S(2)}) collective-permute-start(bf16[8,512]{1,0:T(8,128)(2,1)S(1)} %slice_bitcast_fusion), channel_id=1, source_target_pairs={{0,1},{1,2},{2,3},{3,4},{4,5},{5,6},{6,7},{8,9},{9,10},{10,11},{11... | collective-permute-start | bytes 24584 | tf_op jit(solution)/shard_map/ppermute | solution.py:584
  23.9 1.3 collective-permute-start.4
  25.8 5.1 %all-to-all-done.got = bf16[8,272,256]{2,1,0:T(8,128)(2,1)S(1)} async-done(((bf16[8,272,256]{2,1,0:T(8,128)(2,1)}), bf16[8,272,256]{2,1,0:T(8,128)(2,1)S(1)}, u32[]{:S(2)}, u32[]{:S(2)}) %all-to-all-start) | async-done | bytes 1114144 | tf_op jit(solution)/shard_map/all_to_all | solution.py:576
  31.0 1.0 copy-done.4
  31.9 10.7 %conv.1 = bf16[8,400,128]{2,1,0:T(8,128)(2,1)} custom-call(s32[2]{0:T(128)} %pad_add_fusion.place, bf16[8,272,256]{2,1,0:T(8,128)(2,1)} %copy-done.4, f32[9,512]{1,0:T(8,128)} %reshape.17.short, f32[1,512]{1,0:T(1,128)} %bitcast.25, bf16[512,256]{1,0:T(8,128)(2,1)} %constant.38.clone.ahead_h, bf16[512,256]{1,0:T(8,128)(2,1)} %constant.39.clone.ahead_l, ...), custom_call_target="tpu_custom_call" | custom-call | tf_op jit(solution)/shard_map/conv/pallas_call | solution.py:344
  42.7 4.5 %all-to-all-start.1 = ((bf16[8,400,128]{2,1,0:T(8,128)(2,1)}), bf16[8,400,128]{2,1,0:T(8,128)(2,1)S(1)}, u32[]{:S(2)}, u32[]{:S(2)}) async-start(bf16[8,400,128]{2,1,0:T(8,128)(2,1)} %conv.1), calls=%async_computation.1 | async-start | bytes 1638400 | tf_op jit(solution)/shard_map/all_to_all | solution.py:576
  47.2 9.2 %lag_sums.1 = (bf16[32,16,128]{2,1,0:T(8,128)(2,1)}, bf16[32,16,128]{2,1,0:T(8,128)(2,1)}) custom-call(s32[2]{0:T(128)} %pad_add_fusion.place, bf16[8,272,256]{2,1,0:T(8,128)(2,1)} %copy-done.4, f32[9,512]{1,0:T(8,128)} %reshape.17.short, f32[1,512]{1,0:T(1,128)} %bitcast.26, bf16[512,256]{1,0:T(8,128)(2,1)} %constant.38.clone.ahead_h, ...), custom_call_target="tpu_custom_call" | custom-call | flops 2000000000 | bytes 3000000 | tf_op jit(solution)/shard_map/lag_sums/pallas_call | solution.py:344
  56.5 1.3 collective-permute-start.5
  57.7 2.8 %collective-permute-done.5.lags_z = bf16[32,16,128]{2,1,0:T(8,128)(2,1)S(1)} collective-permute-done((bf16[32,16,128]{2,1,0:T(8,128)(2,1)}, bf16[32,16,128]{2,1,0:T(8,128)(2,1)S(1)}, u32[]{:S(2)}, u32[]{:S(2)}) %collective-permute-start.5) | collective-permute-done | bytes 131104 | tf_op jit(solution)/shard_map/ppermute | solution.py:588
  61.5 2.0 %unpack_mixed.1.m00 = bf16[256,512]{1,0:T(8,128)(2,1)} custom-call(bf16[8,400,128]{2,1,0:T(8,128)(2,1)} %copy-done.2, f32[256,512]{1,0:T(8,128)} %get-tuple-element.37.gate_out, bf16[8,512]{1,0:T(8,128)(2,1)} %copy-done.14, f32[9,512]{1,0:T(8,128)} %reshape.17.short), custom_call_target="tpu_custom_call" | custom-call | tf_op jit(solution)/shard_map/unpack_mixed/pallas_call | solution.py:413
  63.5 1.2 collective-permute-start.6
  64.7 2.5 %collective-permute-start.7 = (bf16[256,512]{1,0:T(8,128)(2,1)}, bf16[256,512]{1,0:T(8,128)(2,1)S(1)}, u32[]{:S(2)}, u32[]{:S(2)}) collective-permute-start(bf16[256,512]{1,0:T(8,128)(2,1)} %unpack_mixed.1.m00), channel_id=1, source_target_pairs={{0,8},{8,0},{1,9},{9,1},{2,10},{10,2},{3,11},{11,3},{4,12},{12,4},... | collective-permute-start | bytes 786440 | tf_op jit(solution)/shard_map/ppermute | solution.py:580
  67.2 2.0 %collective-permute-done.6.m01 = bf16[256,512]{1,0:T(8,128)(2,1)S(1)} collective-permute-done((bf16[256,512]{1,0:T(8,128)(2,1)}, bf16[256,512]{1,0:T(8,128)(2,1)S(1)}, u32[]{:S(2)}, u32[]{:S(2)}) %collective-permute-start.6) | collective-permute-done | bytes 262176 | tf_op jit(solution)/shard_map/ppermute | solution.py:588
  69.3 3.1 %collective-permute-start.8 = (bf16[256,512]{1,0:T(8,128)(2,1)S(1)}, bf16[256,512]{1,0:T(8,128)(2,1)S(1)}, u32[]{:S(2)}, u32[]{:S(2)}) collective-permute-start(bf16[256,512]{1,0:T(8,128)(2,1)S(1)} %collective-permute-done.6.m01), channel_id=1, source_target_pairs={{0,8},{8,0},{1,9},{9,1},{2,10},{10,2},{3,11},{11,3},{4,12},{12,4},... | collective-permute-start | bytes 786440 | tf_op jit(solution)/shard_map/ppermute | solution.py:580
  72.4 1.2 collective-permute-done.8.m11
  74.3 4.2 %partial.1 = bf16[32,16,1152]{2,1,0:T(8,128)(2,1)} custom-call(s32[1]{0:T(128)} %bitcast.place, bf16[256,512]{1,0:T(8,128)(2,1)} %unpack_mixed.1.m00, bf16[256,512]{1,0:T(8,128)(2,1)} %copy-done.9, bf16[256,512]{1,0:T(8,128)(2,1)} %copy-done.10, bf16[256,512]{1,0:T(8,128)(2,1)} %copy-done.11, bf16[256,4096]{1,0:T(8,128)(2,1)} %bitcast.22, ...), custom_call_target="tpu_custom_call" | custom-call | tf_op jit(solution)/shard_map/partial/pallas_call | solution.py:472
  78.5 10.6 %all-to-all-start.2 = ((bf16[32,16,1152]{2,1,0:T(8,128)(2,1)}), bf16[32,16,1152]{2,1,0:T(8,128)(2,1)S(1)}, u32[]{:S(2)}, u32[]{:S(2)}) async-start(bf16[32,16,1152]{2,1,0:T(8,128)(2,1)} %partial.1), calls=%async_computation.2 | async-start | bytes 2359296 | tf_op jit(solution)/shard_map/all_to_all | solution.py:576
  89.1 4.8 %convolution_convert_fusion = bf16[256,4096]{1,0:T(8,128)(2,1)} fusion(bf16[256,512]{1,0:T(8,128)(2,1)S(1)} %copy-done.5, bf16[512,4096]{1,0:T(8,128)(2,1)} %weight.1), kind=kOutput, calls=%fused_computation | convolution fusion | flops 1074790400 | bytes 6553600 | tf_op jit(solution)/shard_map/dot_general | solution.py:629
  93.9 15.1 %all-to-all-done.2.got = bf16[32,16,1152]{2,1,0:T(8,128)(2,1)S(1)} async-done(((bf16[32,16,1152]{2,1,0:T(8,128)(2,1)}), bf16[32,16,1152]{2,1,0:T(8,128)(2,1)S(1)}, u32[]{:S(2)}, u32[]{:S(2)}) %all-to-all-start.2) | async-done | bytes 1179680 | tf_op jit(solution)/shard_map/all_to_all | solution.py:576
  109.0 1.0 copy-done.3
  110.0 3.0 %reduce.1 = bf16[64,16,1152]{2,1,0:T(8,128)(2,1)} custom-call(bf16[32,16,1152]{2,1,0:T(8,128)(2,1)} %copy-done.3), custom_call_target="tpu_custom_call" | custom-call | tf_op jit(solution)/shard_map/reduce/pallas_call | solution.py:509
  113.0 4.7 %all-to-all-start.3 = ((bf16[64,16,1152]{2,1,0:T(8,128)(2,1)}), bf16[64,16,1152]{2,1,0:T(8,128)(2,1)S(1)}, u32[]{:S(2)}, u32[]{:S(2)}) async-start(bf16[64,16,1152]{2,1,0:T(8,128)(2,1)} %reduce.1), calls=%async_computation.3 | async-start | bytes 4718592 | tf_op jit(solution)/shard_map/all_to_all | solution.py:576
  117.7 2.7 %unpack_grads.1 = bf16[3,256,512]{2,1,0:T(8,128)(2,1)} custom-call(bf16[8,400,128]{2,1,0:T(8,128)(2,1)} %copy-done.2, f32[256,512]{1,0:T(8,128)} %get-tuple-element.31.grad, f32[8,512]{1,0:T(8,128)} %copy-done.13, f32[9,512]{1,0:T(8,128)} %reshape.17.short), custom_call_target="tpu_custom_call" | custom-call | flops 1000000 | bytes 2000000 | tf_op jit(solution)/shard_map/unpack_grads/pallas_call | solution.py:447
  120.4 27.9 %all-to-all-done.3.rows.lags_c = bf16[64,16,1152]{2,1,0:T(8,128)(2,1)S(1)} async-done(((bf16[64,16,1152]{2,1,0:T(8,128)(2,1)}), bf16[64,16,1152]{2,1,0:T(8,128)(2,1)S(1)}, u32[]{:S(2)}, u32[]{:S(2)}) %all-to-all-start.3) | async-done | bytes 2359328 | tf_op jit(solution)/shard_map/all_to_all | solution.py:576
  148.3 3.7 %collective-permute-start.9 = (bf16[64,16,1152]{2,1,0:T(8,128)(2,1)S(1)}, bf16[64,16,1152]{2,1,0:T(8,128)(2,1)}, u32[]{:S(2)}, u32[]{:S(2)}) collective-permute-start(bf16[64,16,1152]{2,1,0:T(8,128)(2,1)S(1)} %all-to-all-done.3.rows.lags_c), channel_id=1, source_target_pairs={{0,8},{8,0},{1,9},{9,1},{2,10},{10,2},{3,11},{11,3},{4,12},{12,4},... | collective-permute-start | bytes 7077896 | tf_op jit(solution)/shard_map/ppermute | solution.py:580
  152.0 3.7 %write_first.1.whole = f32[512,4096]{1,0:T(8,128)} custom-call(s32[1]{0:T(128)} %bitcast.13.place, bf16[64,16,1152]{2,1,0:T(8,128)(2,1)} %copy-done), custom_call_target="tpu_custom_call" | custom-call | flops 1000000 | bytes 6000000 | tf_op jit(solution)/shard_map/write_first/pallas_call | solution.py:559
  156.3 4.6 %write_last.1 = (f32[512,4096]{1,0:T(8,128)}, f32[256,512]{1,0:T(8,128)}) custom-call(s32[1]{0:T(128)S(6)} %sub.13.place, bf16[64,16,1152]{2,1,0:T(8,128)(2,1)} %collective-permute-done.9.rows.lags, bf16[64,16,1152]{2,1,0:T(8,128)(2,1)} %collective-permute-done.9.rows.lags, bf16[64,16,1152]{2,1,0:T(8,128)(2,1)} %copy-done, ...), custom_call_target="tpu_custom_call", output_to_operand_aliasing={{0}: (4, {})} | custom-call | flops 1000000 | bytes 6000000 | tf_op jit(solution)/shard_map/write_last/pallas_call | solution.py:559
  (41 shorter events, 4.7 us)
Async XLA Ops:
  8.8 6.0 %copy-start.1 = (bf16[1,256,4096]{2,1,0:T(8,128)(2,1)S(1)}, bf16[1,256,4096]{2,1,0:T(8,128)(2,1)}, u32[]{:S(2)}) copy-start(bf16[1,256,4096]{2,1,0:T(8,128)(2,1)} %param.15) | copy-start | bytes 6291460
  8.8 22.2 %all-to-all-start = ((bf16[8,272,256]{2,1,0:T(8,128)(2,1)}), bf16[8,272,256]{2,1,0:T(8,128)(2,1)S(1)}, u32[]{:S(2)}, u32[]{:S(2)}) async-start(bf16[8,272,256]{2,1,0:T(8,128)(2,1)} %get-tuple-element.30), calls=%async_computation | async-start | bytes 2228224 | tf_op jit(solution)/shard_map/all_to_all | solution.py:576
  16.0 26.7 %collective-permute-start.2 = (bf16[256,1024]{1,0:T(8,128)(2,1)}, bf16[256,1024]{1,0:T(8,128)(2,1)S(1)}, u32[]{:S(2)}, u32[]{:S(2)}) collective-permute-start(bf16[256,1024]{1,0:T(8,128)(2,1)} %get-tuple-element.60), channel_id=1, source_target_pairs={{0,40},{8,32},{32,8},{40,0},{1,41},{9,33},{33,9},{41,1},{2,42},{10... | collective-permute-start | bytes 1572872 | tf_op jit(solution)/shard_map/ppermute | solution.py:592
  18.4 24.2 %collective-permute-start = (bf16[256,1024]{1,0:T(8,128)(2,1)}, bf16[256,1024]{1,0:T(8,128)(2,1)S(1)}, u32[]{:S(2)}, u32[]{:S(2)}) collective-permute-start(bf16[256,1024]{1,0:T(8,128)(2,1)} %get-tuple-element.61), channel_id=1, source_target_pairs={{0,32},{32,0},{1,33},{33,1},{2,34},{34,2},{3,35},{35,3},{4,36},{36... | collective-permute-start | bytes 1572872 | tf_op jit(solution)/shard_map/ppermute | solution.py:588
  18.5 24.2 %collective-permute-start.1 = (bf16[256,1024]{1,0:T(8,128)(2,1)}, bf16[256,1024]{1,0:T(8,128)(2,1)S(1)}, u32[]{:S(2)}, u32[]{:S(2)}) collective-permute-start(bf16[256,1024]{1,0:T(8,128)(2,1)} %get-tuple-element.62), channel_id=1, source_target_pairs={{0,8},{8,0},{1,9},{9,1},{2,10},{10,2},{3,11},{11,3},{4,12},{12,4},... | collective-permute-start | bytes 1572872 | tf_op jit(solution)/shard_map/ppermute | solution.py:580
  19.6 23.0 %collective-permute-start.3 = (bf16[8,512]{1,0:T(8,128)(2,1)S(1)}, bf16[8,512]{1,0:T(8,128)(2,1)S(1)}, u32[]{:S(2)}, u32[]{:S(2)}) collective-permute-start(bf16[8,512]{1,0:T(8,128)(2,1)S(1)} %slice_bitcast_fusion), channel_id=1, source_target_pairs={{0,1},{1,2},{2,3},{3,4},{4,5},{5,6},{6,7},{8,9},{9,10},{10,11},{11... | collective-permute-start | bytes 24584 | tf_op jit(solution)/shard_map/ppermute | solution.py:584
  23.9 18.7 %collective-permute-start.4 = (f32[8,512]{1,0:T(8,128)S(1)}, f32[8,512]{1,0:T(8,128)S(1)}, u32[]{:S(2)}, u32[]{:S(2)}) collective-permute-start(f32[8,512]{1,0:T(8,128)S(1)} %slice.7), channel_id=1, source_target_pairs={{1,0},{2,1},{3,2},{4,3},{5,4},{6,5},{7,6},{9,8},{10,9},{11,10},{12... | collective-permute-start | bytes 49160 | tf_op jit(solution)/shard_map/ppermute | solution.py:584
  30.9 1.0 copy-start.4
  42.6 13.8 %copy-start.14 = (bf16[8,512]{1,0:T(8,128)(2,1)}, bf16[8,512]{1,0:T(8,128)(2,1)S(1)}, u32[]{:S(2)}) copy-start(bf16[8,512]{1,0:T(8,128)(2,1)S(1)} %collective-permute-done.3.edge) | copy-start | bytes 24580
  42.6 13.8 %copy-start.13 = (f32[8,512]{1,0:T(8,128)}, f32[8,512]{1,0:T(8,128)S(1)}, u32[]{:S(2)}) copy-start(f32[8,512]{1,0:T(8,128)S(1)} %collective-permute-done.4.later) | copy-start | bytes 49156
  42.7 13.8 %copy-start.6 = (bf16[256,1024]{1,0:T(8,128)(2,1)}, bf16[256,1024]{1,0:T(8,128)(2,1)S(1)}, u32[]{:S(2)}) copy-start(bf16[256,1024]{1,0:T(8,128)(2,1)S(1)} %collective-permute-done.2.g11) | copy-start | bytes 1572868
  42.7 13.8 %copy-start.7 = (bf16[256,1024]{1,0:T(8,128)(2,1)}, bf16[256,1024]{1,0:T(8,128)(2,1)S(1)}, u32[]{:S(2)}) copy-start(bf16[256,1024]{1,0:T(8,128)(2,1)S(1)} %collective-permute-done.g01) | copy-start | bytes 1572868
  42.7 13.8 %copy-start.8 = (bf16[256,1024]{1,0:T(8,128)(2,1)}, bf16[256,1024]{1,0:T(8,128)(2,1)S(1)}, u32[]{:S(2)}) copy-start(bf16[256,1024]{1,0:T(8,128)(2,1)S(1)} %collective-permute-done.1.g10) | copy-start | bytes 1572868
  42.7 17.9 %all-to-all-start.1 = ((bf16[8,400,128]{2,1,0:T(8,128)(2,1)}), bf16[8,400,128]{2,1,0:T(8,128)(2,1)S(1)}, u32[]{:S(2)}, u32[]{:S(2)}) async-start(bf16[8,400,128]{2,1,0:T(8,128)(2,1)} %conv.1), calls=%async_computation.1 | async-start | bytes 1638400 | tf_op jit(solution)/shard_map/all_to_all | solution.py:576
  56.5 4.1 %collective-permute-start.5 = (bf16[32,16,128]{2,1,0:T(8,128)(2,1)}, bf16[32,16,128]{2,1,0:T(8,128)(2,1)S(1)}, u32[]{:S(2)}, u32[]{:S(2)}) collective-permute-start(bf16[32,16,128]{2,1,0:T(8,128)(2,1)} %get-tuple-element.35), channel_id=1, source_target_pairs={{0,32},{32,0},{1,33},{33,1},{2,34},{34,2},{3,35},{35,3},{4,36},{36... | collective-permute-start | bytes 393224 | tf_op jit(solution)/shard_map/ppermute | solution.py:588
  60.6 13.0 %copy-start.12 = (bf16[32,16,128]{2,1,0:T(8,128)(2,1)}, bf16[32,16,128]{2,1,0:T(8,128)(2,1)S(1)}, u32[]{:S(2)}) copy-start(bf16[32,16,128]{2,1,0:T(8,128)(2,1)S(1)} %collective-permute-done.5.lags_z) | copy-start | bytes 393220
  60.6 0.9 copy-start.2
  63.5 5.8 %collective-permute-start.6 = (bf16[256,512]{1,0:T(8,128)(2,1)}, bf16[256,512]{1,0:T(8,128)(2,1)S(1)}, u32[]{:S(2)}, u32[]{:S(2)}) collective-permute-start(bf16[256,512]{1,0:T(8,128)(2,1)} %unpack_mixed.1.m00), channel_id=1, source_target_pairs={{0,32},{32,0},{1,33},{33,1},{2,34},{34,2},{3,35},{35,3},{4,36},{36... | collective-permute-start | bytes 786440 | tf_op jit(solution)/shard_map/ppermute | solution.py:588
  64.7 7.7 %collective-permute-start.7 = (bf16[256,512]{1,0:T(8,128)(2,1)}, bf16[256,512]{1,0:T(8,128)(2,1)S(1)}, u32[]{:S(2)}, u32[]{:S(2)}) collective-permute-start(bf16[256,512]{1,0:T(8,128)(2,1)} %unpack_mixed.1.m00), channel_id=1, source_target_pairs={{0,8},{8,0},{1,9},{9,1},{2,10},{10,2},{3,11},{11,3},{4,12},{12,4},... | collective-permute-start | bytes 786440 | tf_op jit(solution)/shard_map/ppermute | solution.py:580
  69.3 4.3 %copy-start.9 = (bf16[256,512]{1,0:T(8,128)(2,1)}, bf16[256,512]{1,0:T(8,128)(2,1)S(1)}, u32[]{:S(2)}) copy-start(bf16[256,512]{1,0:T(8,128)(2,1)S(1)} %collective-permute-done.6.m01) | copy-start | bytes 786436
  69.3 4.3 %collective-permute-start.8 = (bf16[256,512]{1,0:T(8,128)(2,1)S(1)}, bf16[256,512]{1,0:T(8,128)(2,1)S(1)}, u32[]{:S(2)}, u32[]{:S(2)}) collective-permute-start(bf16[256,512]{1,0:T(8,128)(2,1)S(1)} %collective-permute-done.6.m01), channel_id=1, source_target_pairs={{0,8},{8,0},{1,9},{9,1},{2,10},{10,2},{3,11},{11,3},{4,12},{12,4},... | collective-permute-start | bytes 786440 | tf_op jit(solution)/shard_map/ppermute | solution.py:580
  72.4 1.2 copy-start.10
  73.6 0.7 copy-start.11
  78.5 10.6 %copy-start.5 = (bf16[256,512]{1,0:T(8,128)(2,1)S(1)}, bf16[256,512]{1,0:T(8,128)(2,1)}, u32[]{:S(2)}) copy-start(bf16[256,512]{1,0:T(8,128)(2,1)} %unpack_mixed.1.m00) | copy-start | bytes 786436
  78.5 30.5 %all-to-all-start.2 = ((bf16[32,16,1152]{2,1,0:T(8,128)(2,1)}), bf16[32,16,1152]{2,1,0:T(8,128)(2,1)S(1)}, u32[]{:S(2)}, u32[]{:S(2)}) async-start(bf16[32,16,1152]{2,1,0:T(8,128)(2,1)} %partial.1), calls=%async_computation.2 | async-start | bytes 2359296 | tf_op jit(solution)/shard_map/all_to_all | solution.py:576
  109.0 1.0 copy-start.3
  113.0 35.3 %all-to-all-start.3 = ((bf16[64,16,1152]{2,1,0:T(8,128)(2,1)}), bf16[64,16,1152]{2,1,0:T(8,128)(2,1)S(1)}, u32[]{:S(2)}, u32[]{:S(2)}) async-start(bf16[64,16,1152]{2,1,0:T(8,128)(2,1)} %reduce.1), calls=%async_computation.3 | async-start | bytes 4718592 | tf_op jit(solution)/shard_map/all_to_all | solution.py:576
  148.3 3.7 %copy-start = (bf16[64,16,1152]{2,1,0:T(8,128)(2,1)}, bf16[64,16,1152]{2,1,0:T(8,128)(2,1)S(1)}, u32[]{:S(2)}) copy-start(bf16[64,16,1152]{2,1,0:T(8,128)(2,1)S(1)} %all-to-all-done.3.rows.lags_c) | copy-start | bytes 7077892
  148.3 8.0 %collective-permute-start.9 = (bf16[64,16,1152]{2,1,0:T(8,128)(2,1)S(1)}, bf16[64,16,1152]{2,1,0:T(8,128)(2,1)}, u32[]{:S(2)}, u32[]{:S(2)}) collective-permute-start(bf16[64,16,1152]{2,1,0:T(8,128)(2,1)S(1)} %all-to-all-done.3.rows.lags_c), channel_id=1, source_target_pairs={{0,8},{8,0},{1,9},{9,1},{2,10},{10,2},{3,11},{11,3},{4,12},{12,4},... | collective-permute-start | bytes 7077896 | tf_op jit(solution)/shard_map/ppermute | solution.py:580

commit v11 on v10

--- a/solution.py
+++ b/solution.py
@@ -70,7 +70,7 @@
             pad[0:8] = jnp.zeros((8, 128), F32)
             pad[8:] = streams[0, :, lanes].astype(F32)
             gate_out[:, lanes] = sum(
-                short[j : j + 1, lanes] * pad[8 - j : 8 - j + BLOCK] for j in range(3)
+                short[0, j : j + 1, lanes] * pad[8 - j : 8 - j + BLOCK] for j in range(3)
             )
 
     @pl.when(step == pl.num_programs(0) - 1)
@@ -101,7 +101,7 @@
             pl.BlockSpec((BLOCK, wide), lambda k: (0, k)),
             pl.BlockSpec((512, wide), lambda k: (0, k)),
             full(BLOCK, 512),
-            full(9, 512),
+            full(3, 3, 512),
         ],
         out_specs=[full(8, SENT_ROWS, 256), full(BLOCK, 512), full(BLOCK, 512)],
         out_shape=[
@@ -126,7 +126,7 @@
 def weights(place, short, skip):
     low1 = low_lanes(1)
     odd = place[0] % 2 == 1
-    taps = short[...]
+    taps = jnp.concatenate([short[n] for n in range(3)], axis=0)
     taps = jnp.where(odd, turned(taps), taps)
     taps_up = turned(taps)
     gain = skip[...]
@@ -348,7 +348,7 @@
             grid=(1,),
             in_specs=[
                 full(8, SENT_ROWS, 256),
-                pl.BlockSpec((9, 128), lambda n, p: (0, p[0] // 2)),
+                pl.BlockSpec((3, 3, 128), lambda n, p: (0, 0, p[0] // 2)),
                 pl.BlockSpec((1, 128), lambda n, p: (0, p[0] // 2)),
             ]
             + [full(*shape) for shape in in_shapes],
@@ -394,21 +394,25 @@
     return jnp.where(low128, a, turned(b)), jnp.where(low128, turned(a), b)
 
 
-def mixed_kernel(got, gate_out, edge, short, mixed, pad):
+def mixed_kernel(got, gate_out, edge, short, lags, mixed, joined, pad):
     low128 = low_lanes(128)
     pad[0:8] = edge[...].astype(F32)
     pad[8:] = jnp.zeros((8, 512), F32)
-    more = sum(short[j : j + 1] * pad[8 - j : 16 - j] for j in (1, 2))
+    more = sum(short[0, j : j + 1] * pad[8 - j : 16 - j] for j in (1, 2))
     for q in range(4):
         lanes = slice(128 * q, 128 * q + 128)
         first, second = convolved(got, q, 0, low128)
         gate = gate_out[0:128, lanes]
         gate = jnp.concatenate([gate[0:8] + more[:, lanes], gate[8:]], axis=0)
-        mixed[0:128, lanes] = (gate * first).astype(BF)
-        mixed[128:256, lanes] = (gate_out[128:256, lanes] * second).astype(BF)
-
-
-def unpack_mixed(got, gate_out, edge, short):
+        for ref in (mixed, joined):
+            ref[0:128, lanes] = (gate * first).astype(BF)
+            ref[128:256, lanes] = (gate_out[128:256, lanes] * second).astype(BF)
+    for n in range(32):
+        start, lane = 16 * (n % 16), 512 + 128 * (n // 16)
+        joined[start : start + 16, lane : lane + 128] = lags[n]
+
+
+def unpack_mixed(got, gate_out, edge, short, lags):
     full = lambda *shape: pl.BlockSpec(shape, lambda n: (0,) * len(shape))
     return pl.pallas_call(
         mixed_kernel,
@@ -417,13 +421,17 @@
             pl.BlockSpec((8, 128, 128), lambda n: (0, 2, 0)),
             full(BLOCK, 512),
             full(8, 512),
-            full(9, 512),
+            full(3, 3, 512),
+            full(32, 16, 128),
         ],
-        out_specs=full(BLOCK, 512),
-        out_shape=jax.ShapeDtypeStruct((BLOCK, 512), BF),
+        out_specs=[full(BLOCK, 512), full(BLOCK, 768)],
+        out_shape=[
+            jax.ShapeDtypeStruct((BLOCK, 512), BF),
+            jax.ShapeDtypeStruct((BLOCK, 768), BF),
+        ],
         scratch_shapes=[pltpu.VMEM((16, 512), F32)],
         name="unpack_mixed",
-    )(got, gate_out, edge, short)
+    )(got, gate_out, edge, short, lags)
 
 
 def grads_kernel(got, grad, later, short, grads, pad):
@@ -439,7 +447,7 @@
         grads[1, :, lanes] = jnp.where(low, a, turned(b)).astype(BF)
         grads[2, :, lanes] = jnp.where(low, turned(a), b).astype(BF)
         grads[0, :, lanes] = sum(
-            short[j : j + 1, lanes] * pad[j : j + BLOCK, lanes] for j in range(3)
+            short[0, j : j + 1, lanes] * pad[j : j + BLOCK, lanes] for j in range(3)
         ).astype(BF)
 
 
@@ -453,89 +461,125 @@
     )(got, grad, later, short)
 
 
-def partial_kernel(place, m00, m01, m10, m11, g00, g01, g10, g11, lags, lags_z, packed):
+def partial_kernel(place, m00, m01, m10, m11, g00, g01, g10, g11, lags, packed):
     def term(mixed, grad):
         return lax.dot_general(
-            mixed[...], grad[...], (((0,), (0,)), ((), ())), preferred_element_type=F32
+            mixed[:, 0:512], grad[...], (((0,), (0,)), ((), ())), preferred_element_type=F32
         )
 
     part = term(m00, g00) + term(m01, g01) + term(m10, g10) + term(m11, g11)
     part = part.astype(BF)
     for n in range(32):
         packed[n, :, 0:1024] = part[16 * n : 16 * n + 16]
-        lag = lags[n].astype(F32) + lags_z[n].astype(F32)
+        start, lane = 16 * (n % 16), 512 + 128 * (n // 16)
+        lag_z = m01[start : start + 16, lane : lane + 128]
+        lag = lags[n].astype(F32) + lag_z.astype(F32)
         packed[n, :, 1024:1152] = lag.astype(BF)
 
 
-def partial(place, mixed, grad, grads, lags, lags_z):
+def partial(place, mixed, grad, grads, lags):
     full = lambda *shape: pl.BlockSpec(shape, lambda n, p: (0,) * len(shape))
     return pl.pallas_call(
         partial_kernel,
         grid_spec=pltpu.PrefetchScalarGridSpec(
             num_scalar_prefetch=1,
             grid=(1,),
-            in_specs=[full(BLOCK, 512)] * 4
+            in_specs=[full(BLOCK, 512), full(BLOCK, 768), full(BLOCK, 512), full(BLOCK, 512)]
             + [pl.BlockSpec((BLOCK, 1024), lambda n, p: (0, p[0]))]
             + [full(BLOCK, 1024)] * 3
-            + [full(32, 16, 128)] * 2,
+            + [full(32, 16, 128)],
             out_specs=full(32, 16, 1152),
         ),
         out_shape=jax.ShapeDtypeStruct((32, 16, 1152), BF),
         name="partial",
-    )(place, *mixed, grad, *grads, lags, lags_z)
-
-
-def reduce_kernel(scale, got, shared, lags):
+    )(place, *mixed, grad, *grads, lags)
+
+
+def reduce_kernel(scale, got, shared, held, lags, wide, in_sems, out_sems):
+    copies = [
+        pltpu.make_async_copy(
+            got.at[8 * k : 8 * k + 8], held.at[8 * k : 8 * k + 8], in_sems.at[k]
+        )
+        for k in range(4)
+    ]
+    for copy in copies:
+        copy.start()
     total = jnp.zeros((16, 1024), F32)
-    for n in range(32):
-        total = total + got[n, :, 0:1024].astype(F32)
+    sums = [jnp.zeros((16, 128), F32) for _ in range(8)]
+    for k in range(4):
+        copies[k].wait()
+        for s in range(8):
+            total = total + held[8 * k + s, :, 0:1024].astype(F32)
+            sums[s] = sums[s] + held[8 * k + s, :, 1024:1152].astype(F32)
     total = (total * scale).astype(BF)
     low = low_lanes(16)
     for q in range(4):
-        a, b = (
-            sum(got[8 * k + s, :, 1024:1152].astype(F32) for k in range(4))
-            for s in (2 * q, 2 * q + 1)
-        )
+        a, b = sums[2 * q] * scale, sums[2 * q + 1] * scale
         sides = (jnp.where(low, turned(a), b), jnp.where(low, a, turned(b)))
         for s in range(8):
             start = 4 * (s // 2)
-            lags[s, 4 * q : 4 * q + 4] = sides[s % 2][start : start + 4] * scale
-    for n in range(64):
-        shared[n, :, 0:1024] = total
-        shared[n, :, 1024:1152] = lags[n % 8].astype(BF)
+            lags[s, 4 * q : 4 * q + 4] = sides[s % 2][start : start + 4]
+    for s in range(8):
+        wide[s, :, 0:1024] = total
+        wide[s, :, 1024:1152] = lags[s].astype(BF)
+    copies = [
+        pltpu.make_async_copy(wide, shared.at[8 * k : 8 * k + 8], out_sems.at[k])
+        for k in range(8)
+    ]
+    for copy in copies:
+        copy.start()
+    for copy in copies:
+        copy.wait()
 
 
 def reduce(got, scale):
     return pl.pallas_call(
         functools.partial(reduce_kernel, scale),
+        in_specs=[pl.BlockSpec(memory_space=pltpu.HBM)],
+        out_specs=pl.BlockSpec(memory_space=pltpu.HBM),
         out_shape=jax.ShapeDtypeStruct((64, 16, 1152), BF),
-        scratch_shapes=[pltpu.VMEM((8, 16, 128), F32)],
+        scratch_shapes=[
+            pltpu.VMEM((32, 16, 1152), BF),
+            pltpu.VMEM((8, 16, 128), F32),
+            pltpu.VMEM((8, 16, 1152), BF),
+            pltpu.SemaphoreType.DMA((4,)),
+            pltpu.SemaphoreType.DMA((8,)),
+        ],
         name="reduce",
     )(got)
 
 
-def start_writes(place, rows, grad_weight, wide, sems):
+def start_writes(place, rows, grad_weight, held, wide, in_sems, out_sems):
+    reads = [
+        pltpu.make_async_copy(
+            rows.at[8 * n : 8 * n + 8, :, 0:1024], held.at[n], in_sems.at[n]
+        )
+        for n in range(8)
+    ]
+    for copy in reads:
+        copy.start()
     copies = []
     for n in range(8):
+        reads[n].wait()
         zh, zl, yh = n // 4, n // 2 % 2, n % 2
         for k in range(8):
-            wide[n, 16 * k : 16 * k + 16] = rows[8 * n + k].astype(F32)
+            wide[n, 16 * k : 16 * k + 16] = held[n, k].astype(F32)
         there = slice(128 * (2 * zh + yh), 128 * (2 * zh + yh) + 128)
         lanes = pl.ds(pl.multiple_of(2048 * place[0] + 1024 * zl, 1024), 1024)
         copies.append(
-            pltpu.make_async_copy(wide.at[n], grad_weight.at[there, lanes], sems.at[n])
+            pltpu.make_async_copy(wide.at[n], grad_weight.at[there, lanes], out_sems.at[n])
         )
         copies[-1].start()
     return copies
 
 
-def first_kernel(place, rows, grad_weight, wide, sems):
-    for copy in start_writes(place, rows, grad_weight, wide, sems):
+def first_kernel(place, rows, grad_weight, *scratch):
+    for copy in start_writes(place, rows, grad_weight, *scratch):
         copy.wait()
 
 
-def last_kernel(place, rows, lags, lags_c, whole, grad_weight, grad_filter, wide, sems, sums):
-    copies = start_writes(place, rows, grad_weight, wide, sems)
+def last_kernel(place, rows, lags, lags_c, whole, grad_weight, grad_filter, sums, *scratch):
+    copies = start_writes(place, rows, grad_weight, *scratch)
     total = lags[...].astype(F32) + lags_c[...].astype(F32)
     sums[...] = total.reshape(1024, 128)
     for q in range(4):
@@ -548,22 +592,25 @@
 
 def write_half(half, rows, mine=None, whole=None):
     last = whole is not None
-    rows_spec = pl.BlockSpec((64, 16, 1024), lambda n, p: (0, 0, 0))
     lags_spec = pl.BlockSpec((64, 16, 128), lambda n, p: (0, 0, 8))
     hbm = pl.BlockSpec(memory_space=pltpu.HBM)
     shapes = [jax.ShapeDtypeStruct((512, 4096), F32)]
-    scratch = [pltpu.VMEM((8, 128, 1024), F32), pltpu.SemaphoreType.DMA((8,))]
     if last:
         shapes.append(jax.ShapeDtypeStruct((BLOCK, 512), F32))
-        scratch.append(pltpu.VMEM((1024, 128), F32))
     return pl.pallas_call(
         last_kernel if last else first_kernel,
         grid_spec=pltpu.PrefetchScalarGridSpec(
             num_scalar_prefetch=1,
             grid=(1,),
-            in_specs=[rows_spec] + [lags_spec, lags_spec, hbm] * last,
+            in_specs=[hbm] + [lags_spec, lags_spec, hbm] * last,
             out_specs=[hbm] + [pl.BlockSpec((BLOCK, 512), lambda n, p: (0, 0))] * last,
-            scratch_shapes=scratch,
+            scratch_shapes=[pltpu.VMEM((1024, 128), F32)] * last
+            + [
+                pltpu.VMEM((8, 8, 16, 1024), BF),
+                pltpu.VMEM((8, 128, 1024), F32),
+                pltpu.SemaphoreType.DMA((8,)),
+                pltpu.SemaphoreType.DMA((8,)),
+            ],
         ),
         out_shape=shapes,
         input_output_aliases={4: 0} if last else {},
@@ -607,7 +654,7 @@
         across(quarter(1 - core, side)),
         opposite(quarter(1 - core, 1 - side)),
     )
-    short = short_filter.reshape(9, 512)
+    short = short_filter
     packed, grad_mixed, gate_out = pack(streams[:, 0], grad, out_weight, long_filter, short)
     got = exchange(packed, SEQ)
     edge = along(streams[0, 0, BLOCK - 8 :], 1)
@@ -617,13 +664,12 @@
     sent = conv(place, got, short, gain)
     sent, got, grads, edge, later = lax.optimization_barrier((sent, got, grads, edge, later))
     lags_own, lags = lag_sums(place, got, short, gain)
-    lags_z = above(lags)
     back = exchange(sent, SEQ)
-    back, lags_own, lags_z = lax.optimization_barrier((back, lags_own, lags_z))
-    m00 = unpack_mixed(back, gate_out, edge, short)
-    m01, m10 = above(m00), across(m00)
-    mixed = (m00, m01, m10, across(m01))
-    part = partial((2 * core + side)[None], mixed, grad, grads, lags_own, lags_z)
+    back, lags_own, lags = lax.optimization_barrier((back, lags_own, lags))
+    m00, joined = unpack_mixed(back, gate_out, edge, short, lags)
+    m01, m10 = above(joined), across(m00)
+    mixed = (m00, m01, m10, across(m01[:, :512]))
+    part = partial((2 * core + side)[None], mixed, grad, grads, lags_own)
     part, m00, back = lax.optimization_barrier((part, m00, back))
     part = exchange(part, MOST)
     layer_out = jnp.dot(m00, out_weight, preferred_element_type=F32).astype(BF)

time: 162 us -> 162 us (level)
  waiting for transfers between devices: 54.7 us -> 58.7 us
  starting transfers between devices: 45.5 us -> 42.8 us
    all_to_all x4, waiting for transfers between devices: 48.1 us -> 50.8 us  [exchange(): return lax.all_to_all(x, axes, 0, 0, tiled=True)]
    ppermute x3 -> x2, waiting for transfers between devices: 4.87 us -> 5.63 us  [above(): return lax.ppermute(x, 'zl', [(0, 1), (1, 0)])]
    unnamed x30 -> x28, local copies, waits for them, and re-layouts: 3.67 us -> 3.64 us
  transfers between devices with their start and end apart: 14 -> 13, of which waited for: 7 -> 7; matrix products, arithmetic and copies ran while one was open for 5% -> 5% of each run, Pallas kernels for 16% -> 16%
where the time goes in v11:
time: 162 us; the launch traced here: 161 us
  waiting for transfers between devices  58.7 us (36%)
  Pallas kernels  46.6 us (29%)
  starting transfers between devices  42.8 us (26%)
  local copies, waits for them, and re-layouts  6.26 us (4%)
  matrix products  4.77 us (3%)
    all_to_all x4, waiting for transfers between devices, exchange(): return lax.all_to_all(x, axes, 0, 0, tiled=True)  50.8 us
    all_to_all x4, starting transfers between devices, exchange(): return lax.all_to_all(x, axes, 0, 0, tiled=True)  25.1 us
    pallas_call x2, Pallas kernels, on_channels(): pl.pallas_call(kernel, grid_spec=pltpu.PrefetchScalarGridSpec(num_scalar_...  19.9 us
    ppermute x4, starting transfers between devices, across(): return lax.ppermute(x, 'c', [(0, 1), (1, 0)])  9.06 us
    pallas_call x2, Pallas kernels, write_half(): pl.pallas_call(last_kernel if last else first_kernel, grid_spec=pltpu.Pre...  8.07 us
    pallas_call x1, Pallas kernels, pack(): pl.pallas_call(pack_kernel, grid=(steps,), in_specs=[full(3, BLOCK, 512),...  6.77 us
    ppermute x2, waiting for transfers between devices, above(): return lax.ppermute(x, 'zl', [(0, 1), (1, 0)])  5.63 us
    ppermute x2, starting transfers between devices, along(): lax.ppermute(x, SEQ, [(n, n + step) for n in range(8) if 0 <= n + step < 8])  4.92 us
  transfers between devices with their start and end apart: 13, of which 7 were waited for; matrix products, arithmetic and copies ran while one was open for 5% of the time, Pallas kernels for 16%

profile of v11, /device:TPU:1, one launch (start us, length us, event | category | flops | bytes accessed | tf_op | source)
XLA Modules:
  0.0 160.6 jit_solution(4251785506931825136)
XLA Ops:
  0.6 6.8 %pack.1 = (bf16[8,272,256]{2,1,0:T(8,128)(2,1)}, f32[256,512]{1,0:T(8,128)}, f32[256,512]{1,0:T(8,128)}) custom-call(bf16[3,256,512]{2,1,0:T(8,128)(2,1)} %bitcast.23, bf16[256,4096]{1,0:T(8,128)(2,1)} %bitcast.21, bf16[512,4096]{1,0:T(8,128)(2,1)} %weight.1, f32[256,512]{1,0:T(8,128)} %filt.1, f32[3,3,512]{2,1,0:T(4,128)} %short.9), custom_call_target="tpu_custom_call" | custom-call | tf_op jit(solution)/shard_map/pack/pallas_call | solution.py:96
  7.4 6.0 %all-to-all-start = ((bf16[8,272,256]{2,1,0:T(8,128)(2,1)}), bf16[8,272,256]{2,1,0:T(8,128)(2,1)S(1)}, u32[]{:S(2)}, u32[]{:S(2)}) async-start(bf16[8,272,256]{2,1,0:T(8,128)(2,1)} %get-tuple-element.32), calls=%async_computation | async-start | bytes 2228224 | tf_op jit(solution)/shard_map/all_to_all | solution.py:623
  13.4 1.2 dynamic-slice_bitcast_fusion
  14.6 2.5 %collective-permute-start.2 = (bf16[256,1024]{1,0:T(8,128)(2,1)}, bf16[256,1024]{1,0:T(8,128)(2,1)S(1)}, u32[]{:S(2)}, u32[]{:S(2)}) collective-permute-start(bf16[256,1024]{1,0:T(8,128)(2,1)} %get-tuple-element.64), channel_id=1, source_target_pairs={{0,40},{8,32},{32,8},{40,0},{1,41},{9,33},{33,9},{41,1},{2,42},{10... | collective-permute-start | bytes 1572872 | tf_op jit(solution)/shard_map/ppermute | solution.py:639
  18.2 3.6 %collective-permute-start.3 = (bf16[8,512]{1,0:T(8,128)(2,1)S(1)}, bf16[8,512]{1,0:T(8,128)(2,1)S(1)}, u32[]{:S(2)}, u32[]{:S(2)}) collective-permute-start(bf16[8,512]{1,0:T(8,128)(2,1)S(1)} %slice_bitcast_fusion), channel_id=1, source_target_pairs={{0,1},{1,2},{2,3},{3,4},{4,5},{5,6},{6,7},{8,9},{9,10},{10,11},{11... | collective-permute-start | bytes 24584 | tf_op jit(solution)/shard_map/ppermute | solution.py:631
  22.6 1.3 collective-permute-start.4
  24.5 5.1 %all-to-all-done.got = bf16[8,272,256]{2,1,0:T(8,128)(2,1)S(1)} async-done(((bf16[8,272,256]{2,1,0:T(8,128)(2,1)}), bf16[8,272,256]{2,1,0:T(8,128)(2,1)S(1)}, u32[]{:S(2)}, u32[]{:S(2)}) %all-to-all-start) | async-done | bytes 1114144 | tf_op jit(solution)/shard_map/all_to_all | solution.py:623
  29.6 1.0 copy-done.4
  30.6 10.7 %conv.1 = bf16[8,400,128]{2,1,0:T(8,128)(2,1)} custom-call(s32[2]{0:T(128)} %pad_add_fusion.place, bf16[8,272,256]{2,1,0:T(8,128)(2,1)} %copy-done.4, f32[3,3,512]{2,1,0:T(4,128)} %short.9, f32[1,512]{1,0:T(1,128)} %bitcast.25, bf16[512,256]{1,0:T(8,128)(2,1)} %constant.38.clone.ahead_h, bf16[512,256]{1,0:T(8,128)(2,1)} %constant.39.clone.ahead_l, ...), custom_call_target="tpu_custom_call" | custom-call | tf_op jit(solution)/shard_map/conv/pallas_call | solution.py:344
  41.4 4.5 %all-to-all-start.1 = ((bf16[8,400,128]{2,1,0:T(8,128)(2,1)}), bf16[8,400,128]{2,1,0:T(8,128)(2,1)S(1)}, u32[]{:S(2)}, u32[]{:S(2)}) async-start(bf16[8,400,128]{2,1,0:T(8,128)(2,1)} %conv.1), calls=%async_computation.1 | async-start | bytes 1638400 | tf_op jit(solution)/shard_map/all_to_all | solution.py:623
  45.8 9.2 %lag_sums.1 = (bf16[32,16,128]{2,1,0:T(8,128)(2,1)}, bf16[32,16,128]{2,1,0:T(8,128)(2,1)}) custom-call(s32[2]{0:T(128)} %pad_add_fusion.place, bf16[8,272,256]{2,1,0:T(8,128)(2,1)} %copy-done.4, f32[3,3,512]{2,1,0:T(4,128)} %short.9, f32[1,512]{1,0:T(1,128)} %bitcast.26, bf16[512,256]{1,0:T(8,128)(2,1)} %constant.38.clone.ahead_h, ...), custom_call_target="tpu_custom_call" | custom-call | flops 2000000000 | bytes 3000000 | tf_op jit(solution)/shard_map/lag_sums/pallas_call | solution.py:344
  55.1 2.6 %all-to-all-done.1.got = bf16[8,400,128]{2,1,0:T(8,128)(2,1)S(1)} async-done(((bf16[8,400,128]{2,1,0:T(8,128)(2,1)}), bf16[8,400,128]{2,1,0:T(8,128)(2,1)S(1)}, u32[]{:S(2)}, u32[]{:S(2)}) %all-to-all-start.1) | async-done | bytes 819232 | tf_op jit(solution)/shard_map/all_to_all | solution.py:623
  57.7 0.9 copy-done.2
  58.6 2.2 %unpack_mixed.1 = (bf16[256,512]{1,0:T(8,128)(2,1)}, bf16[256,768]{1,0:T(8,128)(2,1)}) custom-call(bf16[8,400,128]{2,1,0:T(8,128)(2,1)} %copy-done.2, f32[256,512]{1,0:T(8,128)} %get-tuple-element.39.gate_out, bf16[8,512]{1,0:T(8,128)(2,1)} %copy-done.13, f32[3,3,512]{2,1,0:T(4,128)} %short.9, bf16[32,16,128]{2,1,0:T(8,128)(2,1)} %get-tuple-element.41.lags), custom_call_target="tpu_custom_call" | custom-call | tf_op jit(solution)/shard_map/unpack_mixed/pallas_call | solution.py:417
  60.8 1.2 collective-permute-start.5
  62.0 2.1 %collective-permute-start.6 = (bf16[256,512]{1,0:T(8,128)(2,1)}, bf16[256,512]{1,0:T(8,128)(2,1)S(1)}, u32[]{:S(2)}, u32[]{:S(2)}) collective-permute-start(bf16[256,512]{1,0:T(8,128)(2,1)} %get-tuple-element.49.m00), channel_id=1, source_target_pairs={{0,8},{8,0},{1,9},{9,1},{2,10},{10,2},{3,11},{11,3},{4,12},{12,4},... | collective-permute-start | bytes 786440 | tf_op jit(solution)/shard_map/ppermute | solution.py:627
  64.1 5.6 %collective-permute-done.5.m01 = bf16[256,768]{1,0:T(8,128)(2,1)S(1)} collective-permute-done((bf16[256,768]{1,0:T(8,128)(2,1)}, bf16[256,768]{1,0:T(8,128)(2,1)S(1)}, u32[]{:S(2)}, u32[]{:S(2)}) %collective-permute-start.5) | collective-permute-done | bytes 393248 | tf_op jit(solution)/shard_map/ppermute | solution.py:635
  69.8 2.9 %collective-permute-start.7 = (bf16[256,512]{1,0:T(8,128)(2,1)S(1)}, bf16[256,512]{1,0:T(8,128)(2,1)S(1)}, u32[]{:S(2)}, u32[]{:S(2)}) collective-permute-start(bf16[256,512]{1,0:T(8,128)(2,1)S(1)} %slice.12), channel_id=1, source_target_pairs={{0,8},{8,0},{1,9},{9,1},{2,10},{10,2},{3,11},{11,3},{4,12},{12,4},... | collective-permute-start | bytes 786440 | tf_op jit(solution)/shard_map/ppermute | solution.py:627
  72.6 1.2 collective-permute-done.7.m11
  74.5 4.2 %partial.1 = bf16[32,16,1152]{2,1,0:T(8,128)(2,1)} custom-call(s32[1]{0:T(128)} %bitcast.place, bf16[256,512]{1,0:T(8,128)(2,1)} %get-tuple-element.49.m00, bf16[256,768]{1,0:T(8,128)(2,1)} %copy-done.5, bf16[256,512]{1,0:T(8,128)(2,1)} %copy-done.10, bf16[256,512]{1,0:T(8,128)(2,1)} %copy-done.11, bf16[256,4096]{1,0:T(8,128)(2,1)} %bitcast.22, ...), custom_call_target="tpu_custom_call" | custom-call | tf_op jit(solution)/shard_map/partial/pallas_call | solution.py:482
  78.7 9.9 %all-to-all-start.2 = ((bf16[32,16,1152]{2,1,0:T(8,128)(2,1)}), bf16[32,16,1152]{2,1,0:T(8,128)(2,1)S(1)}, u32[]{:S(2)}, u32[]{:S(2)}) async-start(bf16[32,16,1152]{2,1,0:T(8,128)(2,1)} %partial.1), calls=%async_computation.2 | async-start | bytes 2359296 | tf_op jit(solution)/shard_map/all_to_all | solution.py:623
  88.6 4.8 %convolution_convert_fusion = bf16[256,4096]{1,0:T(8,128)(2,1)} fusion(bf16[256,512]{1,0:T(8,128)(2,1)S(1)} %copy-done.9, bf16[512,4096]{1,0:T(8,128)(2,1)} %weight.1), kind=kOutput, calls=%fused_computation | convolution fusion | flops 1074790400 | bytes 6553600 | tf_op jit(solution)/shard_map/dot_general | solution.py:675
  93.4 15.1 %all-to-all-done.2.got = bf16[32,16,1152]{2,1,0:T(8,128)(2,1)S(1)} async-done(((bf16[32,16,1152]{2,1,0:T(8,128)(2,1)}), bf16[32,16,1152]{2,1,0:T(8,128)(2,1)S(1)}, u32[]{:S(2)}, u32[]{:S(2)}) %all-to-all-start.2) | async-done | bytes 1179680 | tf_op jit(solution)/shard_map/all_to_all | solution.py:623
  108.5 1.0 copy-done.3
  109.5 2.8 %reduce.1 = bf16[64,16,1152]{2,1,0:T(8,128)(2,1)} custom-call(bf16[32,16,1152]{2,1,0:T(8,128)(2,1)} %copy-done.3), custom_call_target="tpu_custom_call" | custom-call | tf_op jit(solution)/shard_map/reduce/pallas_call | solution.py:536
  112.4 4.7 %all-to-all-start.3 = ((bf16[64,16,1152]{2,1,0:T(8,128)(2,1)}), bf16[64,16,1152]{2,1,0:T(8,128)(2,1)S(1)}, u32[]{:S(2)}, u32[]{:S(2)}) async-start(bf16[64,16,1152]{2,1,0:T(8,128)(2,1)} %reduce.1), calls=%async_computation.3 | async-start | bytes 4718592 | tf_op jit(solution)/shard_map/all_to_all | solution.py:623
  117.1 2.7 %unpack_grads.1 = bf16[3,256,512]{2,1,0:T(8,128)(2,1)} custom-call(bf16[8,400,128]{2,1,0:T(8,128)(2,1)} %copy-done.2, f32[256,512]{1,0:T(8,128)} %get-tuple-element.33.grad, f32[8,512]{1,0:T(8,128)} %copy-done.12, f32[3,3,512]{2,1,0:T(4,128)} %short.9), custom_call_target="tpu_custom_call" | custom-call | flops 1000000 | bytes 2000000 | tf_op jit(solution)/shard_map/unpack_grads/pallas_call | solution.py:455
  119.8 27.9 %all-to-all-done.3.rows.lags_c = bf16[64,16,1152]{2,1,0:T(8,128)(2,1)S(1)} async-done(((bf16[64,16,1152]{2,1,0:T(8,128)(2,1)}), bf16[64,16,1152]{2,1,0:T(8,128)(2,1)S(1)}, u32[]{:S(2)}, u32[]{:S(2)}) %all-to-all-start.3) | async-done | bytes 2359328 | tf_op jit(solution)/shard_map/all_to_all | solution.py:623
  147.7 3.7 %collective-permute-start.8 = (bf16[64,16,1152]{2,1,0:T(8,128)(2,1)S(1)}, bf16[64,16,1152]{2,1,0:T(8,128)(2,1)}, u32[]{:S(2)}, u32[]{:S(2)}) collective-permute-start(bf16[64,16,1152]{2,1,0:T(8,128)(2,1)S(1)} %all-to-all-done.3.rows.lags_c), channel_id=1, source_target_pairs={{0,8},{8,0},{1,9},{9,1},{2,10},{10,2},{3,11},{11,3},{4,12},{12,4},... | collective-permute-start | bytes 7077896 | tf_op jit(solution)/shard_map/ppermute | solution.py:627
  151.3 3.1 %write_first.1.whole = f32[512,4096]{1,0:T(8,128)} custom-call(s32[1]{0:T(128)} %bitcast.13.place, bf16[64,16,1152]{2,1,0:T(8,128)(2,1)} %copy-done), custom_call_target="tpu_custom_call" | custom-call | flops 1000000 | bytes 6000000 | tf_op jit(solution)/shard_map/write_first/pallas_call | solution.py:600
  154.5 1.2 collective-permute-done.8.rows.lags
  155.6 5.0 %write_last.1 = (f32[512,4096]{1,0:T(8,128)}, f32[256,512]{1,0:T(8,128)}) custom-call(s32[1]{0:T(128)S(6)} %sub.13.place, bf16[64,16,1152]{2,1,0:T(8,128)(2,1)} %collective-permute-done.8.rows.lags, bf16[64,16,1152]{2,1,0:T(8,128)(2,1)} %collective-permute-done.8.rows.lags, bf16[64,16,1152]{2,1,0:T(8,128)(2,1)} %copy-done, ...), custom_call_target="tpu_custom_call", output_to_operand_aliasing={{0}: (4, {})} | custom-call | flops 1000000 | bytes 6000000 | tf_op jit(solution)/shard_map/write_last/pallas_call | solution.py:600
  (37 shorter events, 3.2 us)
Async XLA Ops:
  7.4 6.0 %copy-start.1 = (bf16[1,256,4096]{2,1,0:T(8,128)(2,1)S(1)}, bf16[1,256,4096]{2,1,0:T(8,128)(2,1)}, u32[]{:S(2)}) copy-start(bf16[1,256,4096]{2,1,0:T(8,128)(2,1)} %param.15) | copy-start | bytes 6291460
  7.4 22.2 %all-to-all-start = ((bf16[8,272,256]{2,1,0:T(8,128)(2,1)}), bf16[8,272,256]{2,1,0:T(8,128)(2,1)S(1)}, u32[]{:S(2)}, u32[]{:S(2)}) async-start(bf16[8,272,256]{2,1,0:T(8,128)(2,1)} %get-tuple-element.32), calls=%async_computation | async-start | bytes 2228224 | tf_op jit(solution)/shard_map/all_to_all | solution.py:623
  14.6 26.7 %collective-permute-start.2 = (bf16[256,1024]{1,0:T(8,128)(2,1)}, bf16[256,1024]{1,0:T(8,128)(2,1)S(1)}, u32[]{:S(2)}, u32[]{:S(2)}) collective-permute-start(bf16[256,1024]{1,0:T(8,128)(2,1)} %get-tuple-element.64), channel_id=1, source_target_pairs={{0,40},{8,32},{32,8},{40,0},{1,41},{9,33},{33,9},{41,1},{2,42},{10... | collective-permute-start | bytes 1572872 | tf_op jit(solution)/shard_map/ppermute | solution.py:639
  17.1 24.2 %collective-permute-start = (bf16[256,1024]{1,0:T(8,128)(2,1)}, bf16[256,1024]{1,0:T(8,128)(2,1)S(1)}, u32[]{:S(2)}, u32[]{:S(2)}) collective-permute-start(bf16[256,1024]{1,0:T(8,128)(2,1)} %get-tuple-element.65), channel_id=1, source_target_pairs={{0,32},{32,0},{1,33},{33,1},{2,34},{34,2},{3,35},{35,3},{4,36},{36... | collective-permute-start | bytes 1572872 | tf_op jit(solution)/shard_map/ppermute | solution.py:635
  17.1 24.3 %collective-permute-start.1 = (bf16[256,1024]{1,0:T(8,128)(2,1)}, bf16[256,1024]{1,0:T(8,128)(2,1)S(1)}, u32[]{:S(2)}, u32[]{:S(2)}) collective-permute-start(bf16[256,1024]{1,0:T(8,128)(2,1)} %get-tuple-element.66), channel_id=1, source_target_pairs={{0,8},{8,0},{1,9},{9,1},{2,10},{10,2},{3,11},{11,3},{4,12},{12,4},... | collective-permute-start | bytes 1572872 | tf_op jit(solution)/shard_map/ppermute | solution.py:627
  18.2 23.1 %collective-permute-start.3 = (bf16[8,512]{1,0:T(8,128)(2,1)S(1)}, bf16[8,512]{1,0:T(8,128)(2,1)S(1)}, u32[]{:S(2)}, u32[]{:S(2)}) collective-permute-start(bf16[8,512]{1,0:T(8,128)(2,1)S(1)} %slice_bitcast_fusion), channel_id=1, source_target_pairs={{0,1},{1,2},{2,3},{3,4},{4,5},{5,6},{6,7},{8,9},{9,10},{10,11},{11... | collective-permute-start | bytes 24584 | tf_op jit(solution)/shard_map/ppermute | solution.py:631
  22.6 18.7 %collective-permute-start.4 = (f32[8,512]{1,0:T(8,128)S(1)}, f32[8,512]{1,0:T(8,128)S(1)}, u32[]{:S(2)}, u32[]{:S(2)}) collective-permute-start(f32[8,512]{1,0:T(8,128)S(1)} %slice.10), channel_id=1, source_target_pairs={{1,0},{2,1},{3,2},{4,3},{5,4},{6,5},{7,6},{9,8},{10,9},{11,10},{12... | collective-permute-start | bytes 49160 | tf_op jit(solution)/shard_map/ppermute | solution.py:631
  29.6 1.0 copy-start.4
  41.3 13.8 %copy-start.13 = (bf16[8,512]{1,0:T(8,128)(2,1)}, bf16[8,512]{1,0:T(8,128)(2,1)S(1)}, u32[]{:S(2)}) copy-start(bf16[8,512]{1,0:T(8,128)(2,1)S(1)} %collective-permute-done.3.edge) | copy-start | bytes 24580
  41.3 13.8 %copy-start.12 = (f32[8,512]{1,0:T(8,128)}, f32[8,512]{1,0:T(8,128)S(1)}, u32[]{:S(2)}) copy-start(f32[8,512]{1,0:T(8,128)S(1)} %collective-permute-done.4.later) | copy-start | bytes 49156
  41.3 13.8 %copy-start.6 = (bf16[256,1024]{1,0:T(8,128)(2,1)}, bf16[256,1024]{1,0:T(8,128)(2,1)S(1)}, u32[]{:S(2)}) copy-start(bf16[256,1024]{1,0:T(8,128)(2,1)S(1)} %collective-permute-done.2.g11) | copy-start | bytes 1572868
  41.3 13.7 %copy-start.7 = (bf16[256,1024]{1,0:T(8,128)(2,1)}, bf16[256,1024]{1,0:T(8,128)(2,1)S(1)}, u32[]{:S(2)}) copy-start(bf16[256,1024]{1,0:T(8,128)(2,1)S(1)} %collective-permute-done.g01) | copy-start | bytes 1572868
  41.3 13.7 %copy-start.8 = (bf16[256,1024]{1,0:T(8,128)(2,1)}, bf16[256,1024]{1,0:T(8,128)(2,1)S(1)}, u32[]{:S(2)}) copy-start(bf16[256,1024]{1,0:T(8,128)(2,1)S(1)} %collective-permute-done.1.g10) | copy-start | bytes 1572868
  41.4 16.4 %all-to-all-start.1 = ((bf16[8,400,128]{2,1,0:T(8,128)(2,1)}), bf16[8,400,128]{2,1,0:T(8,128)(2,1)S(1)}, u32[]{:S(2)}, u32[]{:S(2)}) async-start(bf16[8,400,128]{2,1,0:T(8,128)(2,1)} %conv.1), calls=%async_computation.1 | async-start | bytes 1638400 | tf_op jit(solution)/shard_map/all_to_all | solution.py:623
  57.7 0.9 copy-start.2
  60.8 9.0 %collective-permute-start.5 = (bf16[256,768]{1,0:T(8,128)(2,1)}, bf16[256,768]{1,0:T(8,128)(2,1)S(1)}, u32[]{:S(2)}, u32[]{:S(2)}) collective-permute-start(bf16[256,768]{1,0:T(8,128)(2,1)} %get-tuple-element.43), channel_id=1, source_target_pairs={{0,32},{32,0},{1,33},{33,1},{2,34},{34,2},{3,35},{35,3},{4,36},{36... | collective-permute-start | bytes 1179656 | tf_op jit(solution)/shard_map/ppermute | solution.py:635
  62.0 10.6 %collective-permute-start.6 = (bf16[256,512]{1,0:T(8,128)(2,1)}, bf16[256,512]{1,0:T(8,128)(2,1)S(1)}, u32[]{:S(2)}, u32[]{:S(2)}) collective-permute-start(bf16[256,512]{1,0:T(8,128)(2,1)} %get-tuple-element.49.m00), channel_id=1, source_target_pairs={{0,8},{8,0},{1,9},{9,1},{2,10},{10,2},{3,11},{11,3},{4,12},{12,4},... | collective-permute-start | bytes 786440 | tf_op jit(solution)/shard_map/ppermute | solution.py:627
  69.8 4.0 %copy-start.5 = (bf16[256,768]{1,0:T(8,128)(2,1)}, bf16[256,768]{1,0:T(8,128)(2,1)S(1)}, u32[]{:S(2)}) copy-start(bf16[256,768]{1,0:T(8,128)(2,1)S(1)} %collective-permute-done.5.m01) | copy-start | bytes 1179652
  69.8 4.0 %collective-permute-start.7 = (bf16[256,512]{1,0:T(8,128)(2,1)S(1)}, bf16[256,512]{1,0:T(8,128)(2,1)S(1)}, u32[]{:S(2)}, u32[]{:S(2)}) collective-permute-start(bf16[256,512]{1,0:T(8,128)(2,1)S(1)} %slice.12), channel_id=1, source_target_pairs={{0,8},{8,0},{1,9},{9,1},{2,10},{10,2},{3,11},{11,3},{4,12},{12,4},... | collective-permute-start | bytes 786440 | tf_op jit(solution)/shard_map/ppermute | solution.py:627
  72.6 1.2 copy-start.10
  73.8 0.7 copy-start.11
  78.7 10.0 %copy-start.9 = (bf16[256,512]{1,0:T(8,128)(2,1)S(1)}, bf16[256,512]{1,0:T(8,128)(2,1)}, u32[]{:S(2)}) copy-start(bf16[256,512]{1,0:T(8,128)(2,1)} %get-tuple-element.49.m00) | copy-start | bytes 786436
  78.7 29.8 %all-to-all-start.2 = ((bf16[32,16,1152]{2,1,0:T(8,128)(2,1)}), bf16[32,16,1152]{2,1,0:T(8,128)(2,1)S(1)}, u32[]{:S(2)}, u32[]{:S(2)}) async-start(bf16[32,16,1152]{2,1,0:T(8,128)(2,1)} %partial.1), calls=%async_computation.2 | async-start | bytes 2359296 | tf_op jit(solution)/shard_map/all_to_all | solution.py:623
  108.5 1.0 copy-start.3
  112.4 35.3 %all-to-all-start.3 = ((bf16[64,16,1152]{2,1,0:T(8,128)(2,1)}), bf16[64,16,1152]{2,1,0:T(8,128)(2,1)S(1)}, u32[]{:S(2)}, u32[]{:S(2)}) async-start(bf16[64,16,1152]{2,1,0:T(8,128)(2,1)} %reduce.1), calls=%async_computation.3 | async-start | bytes 4718592 | tf_op jit(solution)/shard_map/all_to_all | solution.py:623
  147.7 3.7 %copy-start = (bf16[64,16,1152]{2,1,0:T(8,128)(2,1)}, bf16[64,16,1152]{2,1,0:T(8,128)(2,1)S(1)}, u32[]{:S(2)}) copy-start(bf16[64,16,1152]{2,1,0:T(8,128)(2,1)S(1)} %all-to-all-done.3.rows.lags_c) | copy-start | bytes 7077892
  147.7 8.0 %collective-permute-start.8 = (bf16[64,16,1152]{2,1,0:T(8,128)(2,1)S(1)}, bf16[64,16,1152]{2,1,0:T(8,128)(2,1)}, u32[]{:S(2)}, u32[]{:S(2)}) collective-permute-start(bf16[64,16,1152]{2,1,0:T(8,128)(2,1)S(1)} %all-to-all-done.3.rows.lags_c), channel_id=1, source_target_pairs={{0,8},{8,0},{1,9},{9,1},{2,10},{10,2},{3,11},{11,3},{4,12},{12,4},... | collective-permute-start | bytes 7077896 | tf_op jit(solution)/shard_map/ppermute | solution.py:627

commit v12 on v11

--- a/solution.py
+++ b/solution.py
@@ -461,38 +461,41 @@
     )(got, grad, later, short)
 
 
-def partial_kernel(place, m00, m01, m10, m11, g00, g01, g10, g11, lags, packed):
+def partial_kernel(place, m00, m01, m10, m11, g00, g01, g10, g11, lags, lags_z, packed):
     def term(mixed, grad):
         return lax.dot_general(
-            mixed[:, 0:512], grad[...], (((0,), (0,)), ((), ())), preferred_element_type=F32
+            mixed[...], grad[...], (((0,), (0,)), ((), ())), preferred_element_type=F32
         )
 
     part = term(m00, g00) + term(m01, g01) + term(m10, g10) + term(m11, g11)
     part = part.astype(BF)
-    for n in range(32):
+    first = pl.multiple_of(128 * (pl.program_id(0) % 2), 128)
+    for n in range(8):
         packed[n, :, 0:1024] = part[16 * n : 16 * n + 16]
-        start, lane = 16 * (n % 16), 512 + 128 * (n // 16)
-        lag_z = m01[start : start + 16, lane : lane + 128]
-        lag = lags[n].astype(F32) + lag_z.astype(F32)
+        lag = lags[n].astype(F32) + lags_z[pl.ds(first + 16 * n, 16), :].astype(F32)
         packed[n, :, 1024:1152] = lag.astype(BF)
 
 
 def partial(place, mixed, grad, grads, lags):
     full = lambda *shape: pl.BlockSpec(shape, lambda n, p: (0,) * len(shape))
+    tall = pl.BlockSpec((BLOCK, 128), lambda n, p: (0, n))
     return pl.pallas_call(
         partial_kernel,
         grid_spec=pltpu.PrefetchScalarGridSpec(
             num_scalar_prefetch=1,
-            grid=(1,),
-            in_specs=[full(BLOCK, 512), full(BLOCK, 768), full(BLOCK, 512), full(BLOCK, 512)]
+            grid=(4,),
+            in_specs=[tall] * 4
             + [pl.BlockSpec((BLOCK, 1024), lambda n, p: (0, p[0]))]
             + [full(BLOCK, 1024)] * 3
-            + [full(32, 16, 128)],
-            out_specs=full(32, 16, 1152),
+            + [
+                pl.BlockSpec((8, 16, 128), lambda n, p: (n, 0, 0)),
+                pl.BlockSpec((BLOCK, 128), lambda n, p: (0, 4 + n // 2)),
+            ],
+            out_specs=pl.BlockSpec((8, 16, 1152), lambda n, p: (n, 0, 0)),
         ),
         out_shape=jax.ShapeDtypeStruct((32, 16, 1152), BF),
         name="partial",
-    )(place, *mixed, grad, *grads, lags)
+    )(place, *mixed, grad, *grads, lags, mixed[1])
 
 
 def reduce_kernel(scale, got, shared, held, lags, wide, in_sems, out_sems):
@@ -549,14 +552,14 @@
     )(got)
 
 
-def start_writes(place, rows, grad_weight, held, wide, in_sems, out_sems):
+def start_writes(place, rows, grad_weight, held, wide, in_sems, out_sems, more=()):
     reads = [
         pltpu.make_async_copy(
             rows.at[8 * n : 8 * n + 8, :, 0:1024], held.at[n], in_sems.at[n]
         )
         for n in range(8)
     ]
-    for copy in reads:
+    for copy in reads + list(more):
         copy.start()
     copies = []
     for n in range(8):
@@ -578,21 +581,29 @@
         copy.wait()
 
 
-def last_kernel(place, rows, lags, lags_c, whole, grad_weight, grad_filter, sums, *scratch):
-    copies = start_writes(place, rows, grad_weight, *scratch)
-    total = lags[...].astype(F32) + lags_c[...].astype(F32)
-    sums[...] = total.reshape(1024, 128)
+def last_kernel(
+    place, rows, mine, whole, grad_weight, grad_filter, lags, sums, filt, lag_sems, *scratch
+):
+    reads = [
+        pltpu.make_async_copy(src.at[:, :, 1024:1152], lags.at[n], lag_sems.at[n])
+        for n, src in enumerate((rows, mine))
+    ]
+    copies = start_writes(place, rows, grad_weight, *scratch, more=reads)
+    for copy in reads:
+        copy.wait()
+    sums[...] = (lags[0].astype(F32) + lags[1].astype(F32)).reshape(1024, 128)
     for q in range(4):
         for k in range(4):
             part = sums[pl.ds(4 * q + k, 64, stride=16), :]
-            grad_filter[64 * k : 64 * k + 64, 128 * q : 128 * q + 128] = part
+            filt[64 * k : 64 * k + 64, 128 * q : 128 * q + 128] = part
+    copies.append(pltpu.make_async_copy(filt, grad_filter, lag_sems.at[2]))
+    copies[-1].start()
     for copy in copies:
         copy.wait()
 
 
 def write_half(half, rows, mine=None, whole=None):
     last = whole is not None
-    lags_spec = pl.BlockSpec((64, 16, 128), lambda n, p: (0, 0, 8))
     hbm = pl.BlockSpec(memory_space=pltpu.HBM)
     shapes = [jax.ShapeDtypeStruct((512, 4096), F32)]
     if last:
@@ -602,9 +613,15 @@
         grid_spec=pltpu.PrefetchScalarGridSpec(
             num_scalar_prefetch=1,
             grid=(1,),
-            in_specs=[hbm] + [lags_spec, lags_spec, hbm] * last,
-            out_specs=[hbm] + [pl.BlockSpec((BLOCK, 512), lambda n, p: (0, 0))] * last,
-            scratch_shapes=[pltpu.VMEM((1024, 128), F32)] * last
+            in_specs=[hbm] + [hbm, hbm] * last,
+            out_specs=[hbm] + [hbm] * last,
+            scratch_shapes=[
+                pltpu.VMEM((2, 64, 16, 128), BF),
+                pltpu.VMEM((1024, 128), F32),
+                pltpu.VMEM((BLOCK, 512), F32),
+                pltpu.SemaphoreType.DMA((3,)),
+            ]
+            * last
             + [
                 pltpu.VMEM((8, 8, 16, 1024), BF),
                 pltpu.VMEM((8, 128, 1024), F32),
@@ -613,10 +630,10 @@
             ],
         ),
         out_shape=shapes,
-        input_output_aliases={4: 0} if last else {},
+        input_output_aliases={3: 0} if last else {},
         cost_estimate=pl.CostEstimate(flops=10**6, bytes_accessed=6 * 10**6, transcendentals=0),
         name="write_last" if last else "write_first",
-    )(half, rows, *([rows, mine, whole] if last else []))
+    )(half, rows, *([mine, whole] if last else []))
 
 
 def exchange(x, axes):

time: 162 us -> 161 us (level)
    pallas_call x2, Pallas kernels: 8.07 us -> 6.44 us  [write_half(): pl.pallas_call(last_kernel if last else first_kernel, grid_spec=pltpu.Pre...]
where the time goes in v12:
time: 161 us; the launch traced here: 160 us
  waiting for transfers between devices  58.7 us (36%)
  Pallas kernels  46 us (29%)
  starting transfers between devices  42.8 us (27%)
  local copies, waits for them, and re-layouts  6.26 us (4%)
  matrix products  4.77 us (3%)
    all_to_all x4, waiting for transfers between devices, exchange(): return lax.all_to_all(x, axes, 0, 0, tiled=True)  50.7 us
    all_to_all x4, starting transfers between devices, exchange(): return lax.all_to_all(x, axes, 0, 0, tiled=True)  25.2 us
    pallas_call x2, Pallas kernels, on_channels(): pl.pallas_call(kernel, grid_spec=pltpu.PrefetchScalarGridSpec(num_scalar_...  19.9 us
    ppermute x4, starting transfers between devices, across(): return lax.ppermute(x, 'c', [(0, 1), (1, 0)])  9.06 us
    pallas_call x1, Pallas kernels, pack(): pl.pallas_call(pack_kernel, grid=(steps,), in_specs=[full(3, BLOCK, 512),...  6.77 us
    pallas_call x2, Pallas kernels, write_half(): pl.pallas_call(last_kernel if last else first_kernel, grid_spec=pltpu.Pre...  6.44 us
    ppermute x2, waiting for transfers between devices, above(): return lax.ppermute(x, 'zl', [(0, 1), (1, 0)])  5.63 us
    pallas_call x1, Pallas kernels, partial(): pl.pallas_call(partial_kernel, grid_spec=pltpu.PrefetchScalarGridSpec(num...  5.14 us
  transfers between devices with their start and end apart: 13, of which 7 were waited for; matrix products, arithmetic and copies ran while one was open for 5% of the time, Pallas kernels for 16%

profile of v12, /device:TPU:1, one launch (start us, length us, event | category | flops | bytes accessed | tf_op | source)
XLA Modules:
  0.0 159.9 jit_solution(12635404809212679082)
XLA Ops:
  0.6 6.8 %pack.1 = (bf16[8,272,256]{2,1,0:T(8,128)(2,1)}, f32[256,512]{1,0:T(8,128)}, f32[256,512]{1,0:T(8,128)}) custom-call(bf16[3,256,512]{2,1,0:T(8,128)(2,1)} %bitcast.23, bf16[256,4096]{1,0:T(8,128)(2,1)} %bitcast.21, bf16[512,4096]{1,0:T(8,128)(2,1)} %weight.1, f32[256,512]{1,0:T(8,128)} %filt.1, f32[3,3,512]{2,1,0:T(4,128)} %short.9), custom_call_target="tpu_custom_call" | custom-call | tf_op jit(solution)/shard_map/pack/pallas_call | solution.py:96
  7.4 6.0 %all-to-all-start = ((bf16[8,272,256]{2,1,0:T(8,128)(2,1)}), bf16[8,272,256]{2,1,0:T(8,128)(2,1)S(1)}, u32[]{:S(2)}, u32[]{:S(2)}) async-start(bf16[8,272,256]{2,1,0:T(8,128)(2,1)} %get-tuple-element.32), calls=%async_computation | async-start | bytes 2228224 | tf_op jit(solution)/shard_map/all_to_all | solution.py:640
  13.4 1.2 dynamic-slice_bitcast_fusion
  14.6 2.5 %collective-permute-start.2 = (bf16[256,1024]{1,0:T(8,128)(2,1)}, bf16[256,1024]{1,0:T(8,128)(2,1)S(1)}, u32[]{:S(2)}, u32[]{:S(2)}) collective-permute-start(bf16[256,1024]{1,0:T(8,128)(2,1)} %get-tuple-element.64), channel_id=1, source_target_pairs={{0,40},{8,32},{32,8},{40,0},{1,41},{9,33},{33,9},{41,1},{2,42},{10... | collective-permute-start | bytes 1572872 | tf_op jit(solution)/shard_map/ppermute | solution.py:656
  18.2 3.6 %collective-permute-start.3 = (bf16[8,512]{1,0:T(8,128)(2,1)S(1)}, bf16[8,512]{1,0:T(8,128)(2,1)S(1)}, u32[]{:S(2)}, u32[]{:S(2)}) collective-permute-start(bf16[8,512]{1,0:T(8,128)(2,1)S(1)} %slice_bitcast_fusion), channel_id=1, source_target_pairs={{0,1},{1,2},{2,3},{3,4},{4,5},{5,6},{6,7},{8,9},{9,10},{10,11},{11... | collective-permute-start | bytes 24584 | tf_op jit(solution)/shard_map/ppermute | solution.py:648
  22.6 1.3 collective-permute-start.4
  24.5 5.1 %all-to-all-done.got = bf16[8,272,256]{2,1,0:T(8,128)(2,1)S(1)} async-done(((bf16[8,272,256]{2,1,0:T(8,128)(2,1)}), bf16[8,272,256]{2,1,0:T(8,128)(2,1)S(1)}, u32[]{:S(2)}, u32[]{:S(2)}) %all-to-all-start) | async-done | bytes 1114144 | tf_op jit(solution)/shard_map/all_to_all | solution.py:640
  29.6 1.0 copy-done.4
  30.6 10.7 %conv.1 = bf16[8,400,128]{2,1,0:T(8,128)(2,1)} custom-call(s32[2]{0:T(128)} %pad_add_fusion.place, bf16[8,272,256]{2,1,0:T(8,128)(2,1)} %copy-done.4, f32[3,3,512]{2,1,0:T(4,128)} %short.9, f32[1,512]{1,0:T(1,128)} %bitcast.25, bf16[512,256]{1,0:T(8,128)(2,1)} %constant.38.clone.ahead_h, bf16[512,256]{1,0:T(8,128)(2,1)} %constant.39.clone.ahead_l, ...), custom_call_target="tpu_custom_call" | custom-call | tf_op jit(solution)/shard_map/conv/pallas_call | solution.py:344
  41.4 4.5 %all-to-all-start.1 = ((bf16[8,400,128]{2,1,0:T(8,128)(2,1)}), bf16[8,400,128]{2,1,0:T(8,128)(2,1)S(1)}, u32[]{:S(2)}, u32[]{:S(2)}) async-start(bf16[8,400,128]{2,1,0:T(8,128)(2,1)} %conv.1), calls=%async_computation.1 | async-start | bytes 1638400 | tf_op jit(solution)/shard_map/all_to_all | solution.py:640
  45.8 9.2 %lag_sums.1 = (bf16[32,16,128]{2,1,0:T(8,128)(2,1)}, bf16[32,16,128]{2,1,0:T(8,128)(2,1)}) custom-call(s32[2]{0:T(128)} %pad_add_fusion.place, bf16[8,272,256]{2,1,0:T(8,128)(2,1)} %copy-done.4, f32[3,3,512]{2,1,0:T(4,128)} %short.9, f32[1,512]{1,0:T(1,128)} %bitcast.26, bf16[512,256]{1,0:T(8,128)(2,1)} %constant.38.clone.ahead_h, ...), custom_call_target="tpu_custom_call" | custom-call | flops 2000000000 | bytes 3000000 | tf_op jit(solution)/shard_map/lag_sums/pallas_call | solution.py:344
  55.1 2.6 %all-to-all-done.1.got = bf16[8,400,128]{2,1,0:T(8,128)(2,1)S(1)} async-done(((bf16[8,400,128]{2,1,0:T(8,128)(2,1)}), bf16[8,400,128]{2,1,0:T(8,128)(2,1)S(1)}, u32[]{:S(2)}, u32[]{:S(2)}) %all-to-all-start.1) | async-done | bytes 819232 | tf_op jit(solution)/shard_map/all_to_all | solution.py:640
  57.7 0.9 copy-done.2
  58.6 2.2 %unpack_mixed.1 = (bf16[256,512]{1,0:T(8,128)(2,1)}, bf16[256,768]{1,0:T(8,128)(2,1)}) custom-call(bf16[8,400,128]{2,1,0:T(8,128)(2,1)} %copy-done.2, f32[256,512]{1,0:T(8,128)} %get-tuple-element.39.gate_out, bf16[8,512]{1,0:T(8,128)(2,1)} %copy-done.13, f32[3,3,512]{2,1,0:T(4,128)} %short.9, bf16[32,16,128]{2,1,0:T(8,128)(2,1)} %get-tuple-element.41.lags), custom_call_target="tpu_custom_call" | custom-call | tf_op jit(solution)/shard_map/unpack_mixed/pallas_call | solution.py:417
  60.8 1.2 collective-permute-start.5
  62.0 2.1 %collective-permute-start.6 = (bf16[256,512]{1,0:T(8,128)(2,1)}, bf16[256,512]{1,0:T(8,128)(2,1)S(1)}, u32[]{:S(2)}, u32[]{:S(2)}) collective-permute-start(bf16[256,512]{1,0:T(8,128)(2,1)} %get-tuple-element.49.m00), channel_id=1, source_target_pairs={{0,8},{8,0},{1,9},{9,1},{2,10},{10,2},{3,11},{11,3},{4,12},{12,4},... | collective-permute-start | bytes 786440 | tf_op jit(solution)/shard_map/ppermute | solution.py:644
  64.1 5.6 %collective-permute-done.5.m01.lags_z = bf16[256,768]{1,0:T(8,128)(2,1)S(1)} collective-permute-done((bf16[256,768]{1,0:T(8,128)(2,1)}, bf16[256,768]{1,0:T(8,128)(2,1)S(1)}, u32[]{:S(2)}, u32[]{:S(2)}) %collective-permute-start.5) | collective-permute-done | bytes 393248 | tf_op jit(solution)/shard_map/ppermute | solution.py:652
  69.8 2.9 %collective-permute-start.7 = (bf16[256,512]{1,0:T(8,128)(2,1)S(1)}, bf16[256,512]{1,0:T(8,128)(2,1)S(1)}, u32[]{:S(2)}, u32[]{:S(2)}) collective-permute-start(bf16[256,512]{1,0:T(8,128)(2,1)S(1)} %slice.12), channel_id=1, source_target_pairs={{0,8},{8,0},{1,9},{9,1},{2,10},{10,2},{3,11},{11,3},{4,12},{12,4},... | collective-permute-start | bytes 786440 | tf_op jit(solution)/shard_map/ppermute | solution.py:644
  72.6 1.2 collective-permute-done.7.m11
  74.5 5.1 %partial.1 = bf16[32,16,1152]{2,1,0:T(8,128)(2,1)} custom-call(s32[1]{0:T(128)} %bitcast.place, bf16[256,512]{1,0:T(8,128)(2,1)} %get-tuple-element.49.m00, bf16[256,768]{1,0:T(8,128)(2,1)} %copy-done.5, bf16[256,512]{1,0:T(8,128)(2,1)} %copy-done.10, bf16[256,512]{1,0:T(8,128)(2,1)} %copy-done.11, bf16[256,4096]{1,0:T(8,128)(2,1)} %bitcast.22, ...), custom_call_target="tpu_custom_call" | custom-call | tf_op jit(solution)/shard_map/partial/pallas_call | solution.py:482
  79.6 10.0 %all-to-all-start.2 = ((bf16[32,16,1152]{2,1,0:T(8,128)(2,1)}), bf16[32,16,1152]{2,1,0:T(8,128)(2,1)S(1)}, u32[]{:S(2)}, u32[]{:S(2)}) async-start(bf16[32,16,1152]{2,1,0:T(8,128)(2,1)} %partial.1), calls=%async_computation.2 | async-start | bytes 2359296 | tf_op jit(solution)/shard_map/all_to_all | solution.py:640
  89.6 4.8 %convolution_convert_fusion = bf16[256,4096]{1,0:T(8,128)(2,1)} fusion(bf16[256,512]{1,0:T(8,128)(2,1)S(1)} %copy-done.9, bf16[512,4096]{1,0:T(8,128)(2,1)} %weight.1), kind=kOutput, calls=%fused_computation | convolution fusion | flops 1074790400 | bytes 6553600 | tf_op jit(solution)/shard_map/dot_general | solution.py:692
  94.4 15.1 %all-to-all-done.2.got = bf16[32,16,1152]{2,1,0:T(8,128)(2,1)S(1)} async-done(((bf16[32,16,1152]{2,1,0:T(8,128)(2,1)}), bf16[32,16,1152]{2,1,0:T(8,128)(2,1)S(1)}, u32[]{:S(2)}, u32[]{:S(2)}) %all-to-all-start.2) | async-done | bytes 1179680 | tf_op jit(solution)/shard_map/all_to_all | solution.py:640
  109.5 1.0 copy-done.3
  110.5 2.8 %reduce.1 = bf16[64,16,1152]{2,1,0:T(8,128)(2,1)} custom-call(bf16[32,16,1152]{2,1,0:T(8,128)(2,1)} %copy-done.3), custom_call_target="tpu_custom_call" | custom-call | tf_op jit(solution)/shard_map/reduce/pallas_call | solution.py:539
  113.4 4.7 %all-to-all-start.3 = ((bf16[64,16,1152]{2,1,0:T(8,128)(2,1)}), bf16[64,16,1152]{2,1,0:T(8,128)(2,1)S(1)}, u32[]{:S(2)}, u32[]{:S(2)}) async-start(bf16[64,16,1152]{2,1,0:T(8,128)(2,1)} %reduce.1), calls=%async_computation.3 | async-start | bytes 4718592 | tf_op jit(solution)/shard_map/all_to_all | solution.py:640
  118.1 2.7 %unpack_grads.1 = bf16[3,256,512]{2,1,0:T(8,128)(2,1)} custom-call(bf16[8,400,128]{2,1,0:T(8,128)(2,1)} %copy-done.2, f32[256,512]{1,0:T(8,128)} %get-tuple-element.33.grad, f32[8,512]{1,0:T(8,128)} %copy-done.12, f32[3,3,512]{2,1,0:T(4,128)} %short.9), custom_call_target="tpu_custom_call" | custom-call | flops 1000000 | bytes 2000000 | tf_op jit(solution)/shard_map/unpack_grads/pallas_call | solution.py:455
  120.8 27.9 %all-to-all-done.3.rows.mine = bf16[64,16,1152]{2,1,0:T(8,128)(2,1)S(1)} async-done(((bf16[64,16,1152]{2,1,0:T(8,128)(2,1)}), bf16[64,16,1152]{2,1,0:T(8,128)(2,1)S(1)}, u32[]{:S(2)}, u32[]{:S(2)}) %all-to-all-start.3) | async-done | bytes 2359328 | tf_op jit(solution)/shard_map/all_to_all | solution.py:640
  148.7 3.7 %collective-permute-start.8 = (bf16[64,16,1152]{2,1,0:T(8,128)(2,1)S(1)}, bf16[64,16,1152]{2,1,0:T(8,128)(2,1)}, u32[]{:S(2)}, u32[]{:S(2)}) collective-permute-start(bf16[64,16,1152]{2,1,0:T(8,128)(2,1)S(1)} %all-to-all-done.3.rows.mine), channel_id=1, source_target_pairs={{0,8},{8,0},{1,9},{9,1},{2,10},{10,2},{3,11},{11,3},{4,12},{12,4},... | collective-permute-start | bytes 7077896 | tf_op jit(solution)/shard_map/ppermute | solution.py:644
  152.3 3.1 %write_first.1.whole = f32[512,4096]{1,0:T(8,128)} custom-call(s32[1]{0:T(128)} %bitcast.13.place, bf16[64,16,1152]{2,1,0:T(8,128)(2,1)} %copy-done), custom_call_target="tpu_custom_call" | custom-call | flops 1000000 | bytes 6000000 | tf_op jit(solution)/shard_map/write_first/pallas_call | solution.py:611
  155.5 1.2 collective-permute-done.8.rows
  156.6 3.3 %write_last.1 = (f32[512,4096]{1,0:T(8,128)}, f32[256,512]{1,0:T(8,128)}) custom-call(s32[1]{0:T(128)S(6)} %sub.13.place, bf16[64,16,1152]{2,1,0:T(8,128)(2,1)} %collective-permute-done.8.rows, bf16[64,16,1152]{2,1,0:T(8,128)(2,1)} %copy-done, f32[512,4096]{1,0:T(8,128)} %write_first.1.whole), custom_call_target="tpu_custom_call", output_to_operand_aliasing={{0}: (3, {})} | custom-call | flops 1000000 | bytes 6000000 | tf_op jit(solution)/shard_map/write_last/pallas_call | solution.py:611
  (37 shorter events, 3.2 us)
Async XLA Ops:
  7.4 6.0 %copy-start.1 = (bf16[1,256,4096]{2,1,0:T(8,128)(2,1)S(1)}, bf16[1,256,4096]{2,1,0:T(8,128)(2,1)}, u32[]{:S(2)}) copy-start(bf16[1,256,4096]{2,1,0:T(8,128)(2,1)} %param.15) | copy-start | bytes 6291460
  7.4 22.2 %all-to-all-start = ((bf16[8,272,256]{2,1,0:T(8,128)(2,1)}), bf16[8,272,256]{2,1,0:T(8,128)(2,1)S(1)}, u32[]{:S(2)}, u32[]{:S(2)}) async-start(bf16[8,272,256]{2,1,0:T(8,128)(2,1)} %get-tuple-element.32), calls=%async_computation | async-start | bytes 2228224 | tf_op jit(solution)/shard_map/all_to_all | solution.py:640
  14.6 26.7 %collective-permute-start.2 = (bf16[256,1024]{1,0:T(8,128)(2,1)}, bf16[256,1024]{1,0:T(8,128)(2,1)S(1)}, u32[]{:S(2)}, u32[]{:S(2)}) collective-permute-start(bf16[256,1024]{1,0:T(8,128)(2,1)} %get-tuple-element.64), channel_id=1, source_target_pairs={{0,40},{8,32},{32,8},{40,0},{1,41},{9,33},{33,9},{41,1},{2,42},{10... | collective-permute-start | bytes 1572872 | tf_op jit(solution)/shard_map/ppermute | solution.py:656
  17.1 24.2 %collective-permute-start = (bf16[256,1024]{1,0:T(8,128)(2,1)}, bf16[256,1024]{1,0:T(8,128)(2,1)S(1)}, u32[]{:S(2)}, u32[]{:S(2)}) collective-permute-start(bf16[256,1024]{1,0:T(8,128)(2,1)} %get-tuple-element.65), channel_id=1, source_target_pairs={{0,32},{32,0},{1,33},{33,1},{2,34},{34,2},{3,35},{35,3},{4,36},{36... | collective-permute-start | bytes 1572872 | tf_op jit(solution)/shard_map/ppermute | solution.py:652
  17.1 24.3 %collective-permute-start.1 = (bf16[256,1024]{1,0:T(8,128)(2,1)}, bf16[256,1024]{1,0:T(8,128)(2,1)S(1)}, u32[]{:S(2)}, u32[]{:S(2)}) collective-permute-start(bf16[256,1024]{1,0:T(8,128)(2,1)} %get-tuple-element.66), channel_id=1, source_target_pairs={{0,8},{8,0},{1,9},{9,1},{2,10},{10,2},{3,11},{11,3},{4,12},{12,4},... | collective-permute-start | bytes 1572872 | tf_op jit(solution)/shard_map/ppermute | solution.py:644
  18.2 23.1 %collective-permute-start.3 = (bf16[8,512]{1,0:T(8,128)(2,1)S(1)}, bf16[8,512]{1,0:T(8,128)(2,1)S(1)}, u32[]{:S(2)}, u32[]{:S(2)}) collective-permute-start(bf16[8,512]{1,0:T(8,128)(2,1)S(1)} %slice_bitcast_fusion), channel_id=1, source_target_pairs={{0,1},{1,2},{2,3},{3,4},{4,5},{5,6},{6,7},{8,9},{9,10},{10,11},{11... | collective-permute-start | bytes 24584 | tf_op jit(solution)/shard_map/ppermute | solution.py:648
  22.6 18.7 %collective-permute-start.4 = (f32[8,512]{1,0:T(8,128)S(1)}, f32[8,512]{1,0:T(8,128)S(1)}, u32[]{:S(2)}, u32[]{:S(2)}) collective-permute-start(f32[8,512]{1,0:T(8,128)S(1)} %slice.10), channel_id=1, source_target_pairs={{1,0},{2,1},{3,2},{4,3},{5,4},{6,5},{7,6},{9,8},{10,9},{11,10},{12... | collective-permute-start | bytes 49160 | tf_op jit(solution)/shard_map/ppermute | solution.py:648
  29.6 1.0 copy-start.4
  41.3 13.8 %copy-start.13 = (bf16[8,512]{1,0:T(8,128)(2,1)}, bf16[8,512]{1,0:T(8,128)(2,1)S(1)}, u32[]{:S(2)}) copy-start(bf16[8,512]{1,0:T(8,128)(2,1)S(1)} %collective-permute-done.3.edge) | copy-start | bytes 24580
  41.3 13.8 %copy-start.12 = (f32[8,512]{1,0:T(8,128)}, f32[8,512]{1,0:T(8,128)S(1)}, u32[]{:S(2)}) copy-start(f32[8,512]{1,0:T(8,128)S(1)} %collective-permute-done.4.later) | copy-start | bytes 49156
  41.3 13.8 %copy-start.6 = (bf16[256,1024]{1,0:T(8,128)(2,1)}, bf16[256,1024]{1,0:T(8,128)(2,1)S(1)}, u32[]{:S(2)}) copy-start(bf16[256,1024]{1,0:T(8,128)(2,1)S(1)} %collective-permute-done.2.g11) | copy-start | bytes 1572868
  41.3 13.7 %copy-start.7 = (bf16[256,1024]{1,0:T(8,128)(2,1)}, bf16[256,1024]{1,0:T(8,128)(2,1)S(1)}, u32[]{:S(2)}) copy-start(bf16[256,1024]{1,0:T(8,128)(2,1)S(1)} %collective-permute-done.g01) | copy-start | bytes 1572868
  41.3 13.7 %copy-start.8 = (bf16[256,1024]{1,0:T(8,128)(2,1)}, bf16[256,1024]{1,0:T(8,128)(2,1)S(1)}, u32[]{:S(2)}) copy-start(bf16[256,1024]{1,0:T(8,128)(2,1)S(1)} %collective-permute-done.1.g10) | copy-start | bytes 1572868
  41.4 16.4 %all-to-all-start.1 = ((bf16[8,400,128]{2,1,0:T(8,128)(2,1)}), bf16[8,400,128]{2,1,0:T(8,128)(2,1)S(1)}, u32[]{:S(2)}, u32[]{:S(2)}) async-start(bf16[8,400,128]{2,1,0:T(8,128)(2,1)} %conv.1), calls=%async_computation.1 | async-start | bytes 1638400 | tf_op jit(solution)/shard_map/all_to_all | solution.py:640
  57.7 0.9 copy-start.2
  60.8 9.0 %collective-permute-start.5 = (bf16[256,768]{1,0:T(8,128)(2,1)}, bf16[256,768]{1,0:T(8,128)(2,1)S(1)}, u32[]{:S(2)}, u32[]{:S(2)}) collective-permute-start(bf16[256,768]{1,0:T(8,128)(2,1)} %get-tuple-element.43), channel_id=1, source_target_pairs={{0,32},{32,0},{1,33},{33,1},{2,34},{34,2},{3,35},{35,3},{4,36},{36... | collective-permute-start | bytes 1179656 | tf_op jit(solution)/shard_map/ppermute | solution.py:652
  62.0 10.6 %collective-permute-start.6 = (bf16[256,512]{1,0:T(8,128)(2,1)}, bf16[256,512]{1,0:T(8,128)(2,1)S(1)}, u32[]{:S(2)}, u32[]{:S(2)}) collective-permute-start(bf16[256,512]{1,0:T(8,128)(2,1)} %get-tuple-element.49.m00), channel_id=1, source_target_pairs={{0,8},{8,0},{1,9},{9,1},{2,10},{10,2},{3,11},{11,3},{4,12},{12,4},... | collective-permute-start | bytes 786440 | tf_op jit(solution)/shard_map/ppermute | solution.py:644
  69.8 4.0 %copy-start.5 = (bf16[256,768]{1,0:T(8,128)(2,1)}, bf16[256,768]{1,0:T(8,128)(2,1)S(1)}, u32[]{:S(2)}) copy-start(bf16[256,768]{1,0:T(8,128)(2,1)S(1)} %collective-permute-done.5.m01.lags_z) | copy-start | bytes 1179652
  69.8 4.0 %collective-permute-start.7 = (bf16[256,512]{1,0:T(8,128)(2,1)S(1)}, bf16[256,512]{1,0:T(8,128)(2,1)S(1)}, u32[]{:S(2)}, u32[]{:S(2)}) collective-permute-start(bf16[256,512]{1,0:T(8,128)(2,1)S(1)} %slice.12), channel_id=1, source_target_pairs={{0,8},{8,0},{1,9},{9,1},{2,10},{10,2},{3,11},{11,3},{4,12},{12,4},... | collective-permute-start | bytes 786440 | tf_op jit(solution)/shard_map/ppermute | solution.py:644
  72.6 1.2 copy-start.10
  73.8 0.7 copy-start.11
  79.6 10.0 %copy-start.9 = (bf16[256,512]{1,0:T(8,128)(2,1)S(1)}, bf16[256,512]{1,0:T(8,128)(2,1)}, u32[]{:S(2)}) copy-start(bf16[256,512]{1,0:T(8,128)(2,1)} %get-tuple-element.49.m00) | copy-start | bytes 786436
  79.6 29.9 %all-to-all-start.2 = ((bf16[32,16,1152]{2,1,0:T(8,128)(2,1)}), bf16[32,16,1152]{2,1,0:T(8,128)(2,1)S(1)}, u32[]{:S(2)}, u32[]{:S(2)}) async-start(bf16[32,16,1152]{2,1,0:T(8,128)(2,1)} %partial.1), calls=%async_computation.2 | async-start | bytes 2359296 | tf_op jit(solution)/shard_map/all_to_all | solution.py:640
  109.5 1.0 copy-start.3
  113.4 35.3 %all-to-all-start.3 = ((bf16[64,16,1152]{2,1,0:T(8,128)(2,1)}), bf16[64,16,1152]{2,1,0:T(8,128)(2,1)S(1)}, u32[]{:S(2)}, u32[]{:S(2)}) async-start(bf16[64,16,1152]{2,1,0:T(8,128)(2,1)} %reduce.1), calls=%async_computation.3 | async-start | bytes 4718592 | tf_op jit(solution)/shard_map/all_to_all | solution.py:640
  148.7 3.7 %copy-start = (bf16[64,16,1152]{2,1,0:T(8,128)(2,1)}, bf16[64,16,1152]{2,1,0:T(8,128)(2,1)S(1)}, u32[]{:S(2)}) copy-start(bf16[64,16,1152]{2,1,0:T(8,128)(2,1)S(1)} %all-to-all-done.3.rows.mine) | copy-start | bytes 7077892
  148.7 8.0 %collective-permute-start.8 = (bf16[64,16,1152]{2,1,0:T(8,128)(2,1)S(1)}, bf16[64,16,1152]{2,1,0:T(8,128)(2,1)}, u32[]{:S(2)}, u32[]{:S(2)}) collective-permute-start(bf16[64,16,1152]{2,1,0:T(8,128)(2,1)S(1)} %all-to-all-done.3.rows.mine), channel_id=1, source_target_pairs={{0,8},{8,0},{1,9},{9,1},{2,10},{10,2},{3,11},{11,3},{4,12},{12,4},... | collective-permute-start | bytes 7077896 | tf_op jit(solution)/shard_map/ppermute | solution.py:644

commit v13 on v12

--- a/solution.py
+++ b/solution.py
@@ -14,6 +14,7 @@
 BLOCK = 256
 HALF = 64
 SENT_ROWS = BLOCK + 16
+KEEP_OUT = 63 * 2**20
 SEQ = ("x", "yl")
 MOST = ("zh", "yh") + SEQ
 DEPTH = ("zh", "zl", "yh")
@@ -430,6 +431,7 @@
             jax.ShapeDtypeStruct((BLOCK, 768), BF),
         ],
         scratch_shapes=[pltpu.VMEM((16, 512), F32)],
+        compiler_params=pltpu.CompilerParams(vmem_limit_bytes=KEEP_OUT),
         name="unpack_mixed",
     )(got, gate_out, edge, short, lags)
 
@@ -457,45 +459,43 @@
         out_shape=jax.ShapeDtypeStruct((3, BLOCK, 512), BF),
         scratch_shapes=[pltpu.VMEM((BLOCK + 8, 512), F32)],
         cost_estimate=pl.CostEstimate(flops=10**6, bytes_accessed=2 * 10**6, transcendentals=0),
+        compiler_params=pltpu.CompilerParams(vmem_limit_bytes=KEEP_OUT),
         name="unpack_grads",
     )(got, grad, later, short)
 
 
-def partial_kernel(place, m00, m01, m10, m11, g00, g01, g10, g11, lags, lags_z, packed):
+def partial_kernel(place, m00, m01, m10, m11, g00, g01, g10, g11, lags, packed):
     def term(mixed, grad):
         return lax.dot_general(
-            mixed[...], grad[...], (((0,), (0,)), ((), ())), preferred_element_type=F32
+            mixed[:, 0:512], grad[...], (((0,), (0,)), ((), ())), preferred_element_type=F32
         )
 
     part = term(m00, g00) + term(m01, g01) + term(m10, g10) + term(m11, g11)
     part = part.astype(BF)
-    first = pl.multiple_of(128 * (pl.program_id(0) % 2), 128)
-    for n in range(8):
+    for n in range(32):
         packed[n, :, 0:1024] = part[16 * n : 16 * n + 16]
-        lag = lags[n].astype(F32) + lags_z[pl.ds(first + 16 * n, 16), :].astype(F32)
+        start, lane = 16 * (n % 16), 512 + 128 * (n // 16)
+        lag_z = m01[start : start + 16, lane : lane + 128]
+        lag = lags[n].astype(F32) + lag_z.astype(F32)
         packed[n, :, 1024:1152] = lag.astype(BF)
 
 
 def partial(place, mixed, grad, grads, lags):
     full = lambda *shape: pl.BlockSpec(shape, lambda n, p: (0,) * len(shape))
-    tall = pl.BlockSpec((BLOCK, 128), lambda n, p: (0, n))
     return pl.pallas_call(
         partial_kernel,
         grid_spec=pltpu.PrefetchScalarGridSpec(
             num_scalar_prefetch=1,
-            grid=(4,),
-            in_specs=[tall] * 4
+            grid=(1,),
+            in_specs=[full(BLOCK, 512), full(BLOCK, 768), full(BLOCK, 512), full(BLOCK, 512)]
             + [pl.BlockSpec((BLOCK, 1024), lambda n, p: (0, p[0]))]
             + [full(BLOCK, 1024)] * 3
-            + [
-                pl.BlockSpec((8, 16, 128), lambda n, p: (n, 0, 0)),
-                pl.BlockSpec((BLOCK, 128), lambda n, p: (0, 4 + n // 2)),
-            ],
-            out_specs=pl.BlockSpec((8, 16, 1152), lambda n, p: (n, 0, 0)),
+            + [full(32, 16, 128)],
+            out_specs=full(32, 16, 1152),
         ),
         out_shape=jax.ShapeDtypeStruct((32, 16, 1152), BF),
         name="partial",
-    )(place, *mixed, grad, *grads, lags, mixed[1])
+    )(place, *mixed, grad, *grads, lags)
 
 
 def reduce_kernel(scale, got, shared, held, lags, wide, in_sems, out_sems):
@@ -548,6 +548,7 @@
             pltpu.SemaphoreType.DMA((4,)),
             pltpu.SemaphoreType.DMA((8,)),
         ],
+        compiler_params=pltpu.CompilerParams(vmem_limit_bytes=KEEP_OUT),
         name="reduce",
     )(got)
 
@@ -632,6 +633,7 @@
         out_shape=shapes,
         input_output_aliases={3: 0} if last else {},
         cost_estimate=pl.CostEstimate(flops=10**6, bytes_accessed=6 * 10**6, transcendentals=0),
+        compiler_params=pltpu.CompilerParams(vmem_limit_bytes=KEEP_OUT),
         name="write_last" if last else "write_first",
     )(half, rows, *([mine, whole] if last else []))
 

time: 161 us -> 161 us (level)
    unnamed x28 -> x24, local copies, waits for them, and re-layouts: 3.64 us -> 3.46 us
where the time goes in v13:
time: 161 us; the launch traced here: 160 us
  waiting for transfers between devices  58.8 us (37%)
  Pallas kernels  45 us (28%)
  starting transfers between devices  43.8 us (27%)
  local copies, waits for them, and re-layouts  6.11 us (4%)
  matrix products  4.77 us (3%)
    all_to_all x4, waiting for transfers between devices, exchange(): return lax.all_to_all(x, axes, 0, 0, tiled=True)  50.6 us
    all_to_all x4, starting transfers between devices, exchange(): return lax.all_to_all(x, axes, 0, 0, tiled=True)  26.1 us
    pallas_call x2, Pallas kernels, on_channels(): pl.pallas_call(kernel, grid_spec=pltpu.PrefetchScalarGridSpec(num_scalar_...  19.9 us
    ppermute x4, starting transfers between devices, across(): return lax.ppermute(x, 'c', [(0, 1), (1, 0)])  9.04 us
    pallas_call x1, Pallas kernels, pack(): pl.pallas_call(pack_kernel, grid=(steps,), in_specs=[full(3, BLOCK, 512),...  6.77 us
    pallas_call x2, Pallas kernels, write_half(): pl.pallas_call(last_kernel if last else first_kernel, grid_spec=pltpu.Pre...  6.44 us
    ppermute x2, waiting for transfers between devices, above(): return lax.ppermute(x, 'zl', [(0, 1), (1, 0)])  5.63 us
    ppermute x2, starting transfers between devices, along(): lax.ppermute(x, SEQ, [(n, n + step) for n in range(8) if 0 <= n + step < 8])  4.92 us
  transfers between devices with their start and end apart: 13, of which 7 were waited for; matrix products, arithmetic and copies ran while one was open for 5% of the time, Pallas kernels for 16%

profile of v13, /device:TPU:1, one launch (start us, length us, event | category | flops | bytes accessed | tf_op | source)
XLA Modules:
  0.0 159.8 jit_solution(10031250463275000939)
XLA Ops:
  0.6 6.8 %pack.1 = (bf16[8,272,256]{2,1,0:T(8,128)(2,1)}, f32[256,512]{1,0:T(8,128)}, f32[256,512]{1,0:T(8,128)}) custom-call(bf16[3,256,512]{2,1,0:T(8,128)(2,1)} %bitcast.23, bf16[256,4096]{1,0:T(8,128)(2,1)} %bitcast.21, bf16[512,4096]{1,0:T(8,128)(2,1)} %weight.1, f32[256,512]{1,0:T(8,128)} %filt.1, f32[3,3,512]{2,1,0:T(4,128)} %short.9), custom_call_target="tpu_custom_call" | custom-call | tf_op jit(solution)/shard_map/pack/pallas_call | solution.py:97
  7.4 6.0 %all-to-all-start = ((bf16[8,272,256]{2,1,0:T(8,128)(2,1)}), bf16[8,272,256]{2,1,0:T(8,128)(2,1)S(1)}, u32[]{:S(2)}, u32[]{:S(2)}) async-start(bf16[8,272,256]{2,1,0:T(8,128)(2,1)} %get-tuple-element.32), calls=%async_computation | async-start | bytes 2228224 | tf_op jit(solution)/shard_map/all_to_all | solution.py:642
  13.4 1.2 dynamic-slice_bitcast_fusion
  14.6 2.5 %collective-permute-start.2 = (bf16[256,1024]{1,0:T(8,128)(2,1)}, bf16[256,1024]{1,0:T(8,128)(2,1)S(1)}, u32[]{:S(2)}, u32[]{:S(2)}) collective-permute-start(bf16[256,1024]{1,0:T(8,128)(2,1)} %get-tuple-element.64), channel_id=1, source_target_pairs={{0,40},{8,32},{32,8},{40,0},{1,41},{9,33},{33,9},{41,1},{2,42},{10... | collective-permute-start | bytes 1572872 | tf_op jit(solution)/shard_map/ppermute | solution.py:658
  18.2 3.6 %collective-permute-start.3 = (bf16[8,512]{1,0:T(8,128)(2,1)S(1)}, bf16[8,512]{1,0:T(8,128)(2,1)S(1)}, u32[]{:S(2)}, u32[]{:S(2)}) collective-permute-start(bf16[8,512]{1,0:T(8,128)(2,1)S(1)} %slice_bitcast_fusion), channel_id=1, source_target_pairs={{0,1},{1,2},{2,3},{3,4},{4,5},{5,6},{6,7},{8,9},{9,10},{10,11},{11... | collective-permute-start | bytes 24584 | tf_op jit(solution)/shard_map/ppermute | solution.py:650
  22.6 1.3 collective-permute-start.4
  24.5 5.1 %all-to-all-done.got = bf16[8,272,256]{2,1,0:T(8,128)(2,1)S(1)} async-done(((bf16[8,272,256]{2,1,0:T(8,128)(2,1)}), bf16[8,272,256]{2,1,0:T(8,128)(2,1)S(1)}, u32[]{:S(2)}, u32[]{:S(2)}) %all-to-all-start) | async-done | bytes 1114144 | tf_op jit(solution)/shard_map/all_to_all | solution.py:642
  29.6 1.0 copy-done.2
  30.6 10.7 %conv.1 = bf16[8,400,128]{2,1,0:T(8,128)(2,1)} custom-call(s32[2]{0:T(128)} %pad_add_fusion.place, bf16[8,272,256]{2,1,0:T(8,128)(2,1)} %copy-done.2, f32[3,3,512]{2,1,0:T(4,128)} %short.9, f32[1,512]{1,0:T(1,128)} %bitcast.25, bf16[512,256]{1,0:T(8,128)(2,1)} %constant.38.clone.ahead_h, bf16[512,256]{1,0:T(8,128)(2,1)} %constant.39.clone.ahead_l, ...), custom_call_target="tpu_custom_call" | custom-call | tf_op jit(solution)/shard_map/conv/pallas_call | solution.py:345
  41.4 0.8 copy-done.6
  42.2 4.5 %all-to-all-start.1 = ((bf16[8,400,128]{2,1,0:T(8,128)(2,1)}), bf16[8,400,128]{2,1,0:T(8,128)(2,1)S(1)}, u32[]{:S(2)}, u32[]{:S(2)}) async-start(bf16[8,400,128]{2,1,0:T(8,128)(2,1)} %conv.1), calls=%async_computation.1 | async-start | bytes 1638400 | tf_op jit(solution)/shard_map/all_to_all | solution.py:642
  46.7 9.2 %lag_sums.1 = (bf16[32,16,128]{2,1,0:T(8,128)(2,1)}, bf16[32,16,128]{2,1,0:T(8,128)(2,1)}) custom-call(s32[2]{0:T(128)} %pad_add_fusion.place, bf16[8,272,256]{2,1,0:T(8,128)(2,1)} %copy-done.2, f32[3,3,512]{2,1,0:T(4,128)} %short.9, f32[1,512]{1,0:T(1,128)} %bitcast.26, bf16[512,256]{1,0:T(8,128)(2,1)} %constant.38.clone.ahead_h, ...), custom_call_target="tpu_custom_call" | custom-call | flops 2000000000 | bytes 3000000 | tf_op jit(solution)/shard_map/lag_sums/pallas_call | solution.py:345
  55.9 2.7 %all-to-all-done.1.got = bf16[8,400,128]{2,1,0:T(8,128)(2,1)S(1)} async-done(((bf16[8,400,128]{2,1,0:T(8,128)(2,1)}), bf16[8,400,128]{2,1,0:T(8,128)(2,1)S(1)}, u32[]{:S(2)}, u32[]{:S(2)}) %all-to-all-start.1) | async-done | bytes 819232 | tf_op jit(solution)/shard_map/all_to_all | solution.py:642
  58.6 0.9 copy-done.1
  59.5 2.2 %unpack_mixed.1 = (bf16[256,512]{1,0:T(8,128)(2,1)}, bf16[256,768]{1,0:T(8,128)(2,1)}) custom-call(bf16[8,400,128]{2,1,0:T(8,128)(2,1)} %copy-done.1, f32[256,512]{1,0:T(8,128)} %get-tuple-element.39.gate_out, bf16[8,512]{1,0:T(8,128)(2,1)} %copy-done.11, f32[3,3,512]{2,1,0:T(4,128)} %short.9, bf16[32,16,128]{2,1,0:T(8,128)(2,1)} %get-tuple-element.41.lags), custom_call_target="tpu_custom_call" | custom-call | tf_op jit(solution)/shard_map/unpack_mixed/pallas_call | solution.py:418
  61.6 1.2 collective-permute-start.5
  62.9 2.1 %collective-permute-start.6 = (bf16[256,512]{1,0:T(8,128)(2,1)}, bf16[256,512]{1,0:T(8,128)(2,1)S(1)}, u32[]{:S(2)}, u32[]{:S(2)}) collective-permute-start(bf16[256,512]{1,0:T(8,128)(2,1)} %get-tuple-element.49.m00), channel_id=1, source_target_pairs={{0,8},{8,0},{1,9},{9,1},{2,10},{10,2},{3,11},{11,3},{4,12},{12,4},... | collective-permute-start | bytes 786440 | tf_op jit(solution)/shard_map/ppermute | solution.py:646
  65.0 5.6 %collective-permute-done.5.m01 = bf16[256,768]{1,0:T(8,128)(2,1)S(1)} collective-permute-done((bf16[256,768]{1,0:T(8,128)(2,1)}, bf16[256,768]{1,0:T(8,128)(2,1)S(1)}, u32[]{:S(2)}, u32[]{:S(2)}) %collective-permute-start.5) | collective-permute-done | bytes 393248 | tf_op jit(solution)/shard_map/ppermute | solution.py:654
  70.6 2.9 %collective-permute-start.7 = (bf16[256,512]{1,0:T(8,128)(2,1)S(1)}, bf16[256,512]{1,0:T(8,128)(2,1)S(1)}, u32[]{:S(2)}, u32[]{:S(2)}) collective-permute-start(bf16[256,512]{1,0:T(8,128)(2,1)S(1)} %slice.12), channel_id=1, source_target_pairs={{0,8},{8,0},{1,9},{9,1},{2,10},{10,2},{3,11},{11,3},{4,12},{12,4},... | collective-permute-start | bytes 786440 | tf_op jit(solution)/shard_map/ppermute | solution.py:646
  73.5 1.2 collective-permute-done.7.m11
  75.4 4.2 %partial.1 = bf16[32,16,1152]{2,1,0:T(8,128)(2,1)} custom-call(s32[1]{0:T(128)} %bitcast.place, bf16[256,512]{1,0:T(8,128)(2,1)} %get-tuple-element.49.m00, bf16[256,768]{1,0:T(8,128)(2,1)} %copy-done.3, bf16[256,512]{1,0:T(8,128)(2,1)} %copy-done.8, bf16[256,512]{1,0:T(8,128)(2,1)} %copy-done.9, bf16[256,4096]{1,0:T(8,128)(2,1)} %bitcast.22, ...), custom_call_target="tpu_custom_call" | custom-call | tf_op jit(solution)/shard_map/partial/pallas_call | solution.py:485
  79.5 10.1 %all-to-all-start.2 = ((bf16[32,16,1152]{2,1,0:T(8,128)(2,1)}), bf16[32,16,1152]{2,1,0:T(8,128)(2,1)}, u32[]{:S(2)}, u32[]{:S(2)}) async-start(bf16[32,16,1152]{2,1,0:T(8,128)(2,1)} %partial.1), calls=%async_computation.2 | async-start | bytes 2359296 | tf_op jit(solution)/shard_map/all_to_all | solution.py:642
  89.6 4.8 %convolution_convert_fusion = bf16[256,4096]{1,0:T(8,128)(2,1)} fusion(bf16[256,512]{1,0:T(8,128)(2,1)S(1)} %copy-done.7, bf16[512,4096]{1,0:T(8,128)(2,1)} %weight.1), kind=kOutput, calls=%fused_computation | convolution fusion | flops 1074790400 | bytes 6553600 | tf_op jit(solution)/shard_map/dot_general | solution.py:694
  94.4 15.1 %all-to-all-done.2.got = bf16[32,16,1152]{2,1,0:T(8,128)(2,1)} async-done(((bf16[32,16,1152]{2,1,0:T(8,128)(2,1)}), bf16[32,16,1152]{2,1,0:T(8,128)(2,1)}, u32[]{:S(2)}, u32[]{:S(2)}) %all-to-all-start.2) | async-done | bytes 1179680 | tf_op jit(solution)/shard_map/all_to_all | solution.py:642
  109.5 2.8 %reduce.1 = bf16[64,16,1152]{2,1,0:T(8,128)(2,1)} custom-call(bf16[32,16,1152]{2,1,0:T(8,128)(2,1)} %all-to-all-done.2.got), custom_call_target="tpu_custom_call" | custom-call | tf_op jit(solution)/shard_map/reduce/pallas_call | solution.py:539
  112.3 5.6 %all-to-all-start.3 = ((bf16[64,16,1152]{2,1,0:T(8,128)(2,1)}), bf16[64,16,1152]{2,1,0:T(8,128)(2,1)}, u32[]{:S(2)}, u32[]{:S(2)}) async-start(bf16[64,16,1152]{2,1,0:T(8,128)(2,1)} %reduce.1), calls=%async_computation.3 | async-start | bytes 4718592 | tf_op jit(solution)/shard_map/all_to_all | solution.py:642
  117.9 2.7 %unpack_grads.1 = bf16[3,256,512]{2,1,0:T(8,128)(2,1)} custom-call(bf16[8,400,128]{2,1,0:T(8,128)(2,1)} %copy-done.1, f32[256,512]{1,0:T(8,128)} %get-tuple-element.33.grad, f32[8,512]{1,0:T(8,128)} %copy-done.10, f32[3,3,512]{2,1,0:T(4,128)} %short.9), custom_call_target="tpu_custom_call" | custom-call | flops 1000000 | bytes 2000000 | tf_op jit(solution)/shard_map/unpack_grads/pallas_call | solution.py:457
  120.6 27.7 %all-to-all-done.3.rows.mine = bf16[64,16,1152]{2,1,0:T(8,128)(2,1)} async-done(((bf16[64,16,1152]{2,1,0:T(8,128)(2,1)}), bf16[64,16,1152]{2,1,0:T(8,128)(2,1)}, u32[]{:S(2)}, u32[]{:S(2)}) %all-to-all-start.3) | async-done | bytes 2359328 | tf_op jit(solution)/shard_map/all_to_all | solution.py:642
  148.4 3.7 %collective-permute-start.8 = (bf16[64,16,1152]{2,1,0:T(8,128)(2,1)}, bf16[64,16,1152]{2,1,0:T(8,128)(2,1)}, u32[]{:S(2)}, u32[]{:S(2)}) collective-permute-start(bf16[64,16,1152]{2,1,0:T(8,128)(2,1)} %all-to-all-done.3.rows.mine), channel_id=1, source_target_pairs={{0,8},{8,0},{1,9},{9,1},{2,10},{10,2},{3,11},{11,3},{4,12},{12,4},... | collective-permute-start | bytes 7077896 | tf_op jit(solution)/shard_map/ppermute | solution.py:646
  152.0 3.1 %write_first.1.whole = f32[512,4096]{1,0:T(8,128)} custom-call(s32[1]{0:T(128)} %bitcast.13.place, bf16[64,16,1152]{2,1,0:T(8,128)(2,1)} %all-to-all-done.3.rows.mine), custom_call_target="tpu_custom_call" | custom-call | flops 1000000 | bytes 6000000 | tf_op jit(solution)/shard_map/write_first/pallas_call | solution.py:612
  155.2 1.4 collective-permute-done.8.rows
  156.5 3.3 %write_last.1 = (f32[512,4096]{1,0:T(8,128)}, f32[256,512]{1,0:T(8,128)}) custom-call(s32[1]{0:T(128)S(6)} %sub.13.place, bf16[64,16,1152]{2,1,0:T(8,128)(2,1)} %collective-permute-done.8.rows, bf16[64,16,1152]{2,1,0:T(8,128)(2,1)} %all-to-all-done.3.rows.mine, f32[512,4096]{1,0:T(8,128)} %write_first.1.whole), custom_call_target="tpu_custom_call", output_to_operand_aliasing={{0}: (3, {})} | custom-call | flops 1000000 | bytes 6000000 | tf_op jit(solution)/shard_map/write_last/pallas_call | solution.py:612
  (33 shorter events, 3.2 us)
Async XLA Ops:
  7.4 6.0 %copy-start = (bf16[1,256,4096]{2,1,0:T(8,128)(2,1)S(1)}, bf16[1,256,4096]{2,1,0:T(8,128)(2,1)}, u32[]{:S(2)}) copy-start(bf16[1,256,4096]{2,1,0:T(8,128)(2,1)} %param.15) | copy-start | bytes 6291460
  7.4 22.2 %all-to-all-start = ((bf16[8,272,256]{2,1,0:T(8,128)(2,1)}), bf16[8,272,256]{2,1,0:T(8,128)(2,1)S(1)}, u32[]{:S(2)}, u32[]{:S(2)}) async-start(bf16[8,272,256]{2,1,0:T(8,128)(2,1)} %get-tuple-element.32), calls=%async_computation | async-start | bytes 2228224 | tf_op jit(solution)/shard_map/all_to_all | solution.py:642
  14.6 26.7 %collective-permute-start.2 = (bf16[256,1024]{1,0:T(8,128)(2,1)}, bf16[256,1024]{1,0:T(8,128)(2,1)S(1)}, u32[]{:S(2)}, u32[]{:S(2)}) collective-permute-start(bf16[256,1024]{1,0:T(8,128)(2,1)} %get-tuple-element.64), channel_id=1, source_target_pairs={{0,40},{8,32},{32,8},{40,0},{1,41},{9,33},{33,9},{41,1},{2,42},{10... | collective-permute-start | bytes 1572872 | tf_op jit(solution)/shard_map/ppermute | solution.py:658
  17.1 24.2 %collective-permute-start = (bf16[256,1024]{1,0:T(8,128)(2,1)}, bf16[256,1024]{1,0:T(8,128)(2,1)S(1)}, u32[]{:S(2)}, u32[]{:S(2)}) collective-permute-start(bf16[256,1024]{1,0:T(8,128)(2,1)} %get-tuple-element.65), channel_id=1, source_target_pairs={{0,32},{32,0},{1,33},{33,1},{2,34},{34,2},{3,35},{35,3},{4,36},{36... | collective-permute-start | bytes 1572872 | tf_op jit(solution)/shard_map/ppermute | solution.py:654
  17.1 24.2 %collective-permute-start.1 = (bf16[256,1024]{1,0:T(8,128)(2,1)}, bf16[256,1024]{1,0:T(8,128)(2,1)S(1)}, u32[]{:S(2)}, u32[]{:S(2)}) collective-permute-start(bf16[256,1024]{1,0:T(8,128)(2,1)} %get-tuple-element.66), channel_id=1, source_target_pairs={{0,8},{8,0},{1,9},{9,1},{2,10},{10,2},{3,11},{11,3},{4,12},{12,4},... | collective-permute-start | bytes 1572872 | tf_op jit(solution)/shard_map/ppermute | solution.py:646
  18.2 23.1 %collective-permute-start.3 = (bf16[8,512]{1,0:T(8,128)(2,1)S(1)}, bf16[8,512]{1,0:T(8,128)(2,1)S(1)}, u32[]{:S(2)}, u32[]{:S(2)}) collective-permute-start(bf16[8,512]{1,0:T(8,128)(2,1)S(1)} %slice_bitcast_fusion), channel_id=1, source_target_pairs={{0,1},{1,2},{2,3},{3,4},{4,5},{5,6},{6,7},{8,9},{9,10},{10,11},{11... | collective-permute-start | bytes 24584 | tf_op jit(solution)/shard_map/ppermute | solution.py:650
  22.6 18.7 %collective-permute-start.4 = (f32[8,512]{1,0:T(8,128)S(1)}, f32[8,512]{1,0:T(8,128)S(1)}, u32[]{:S(2)}, u32[]{:S(2)}) collective-permute-start(f32[8,512]{1,0:T(8,128)S(1)} %slice.10), channel_id=1, source_target_pairs={{1,0},{2,1},{3,2},{4,3},{5,4},{6,5},{7,6},{9,8},{10,9},{11,10},{12... | collective-permute-start | bytes 49160 | tf_op jit(solution)/shard_map/ppermute | solution.py:650
  29.6 1.0 copy-start.2
  41.3 17.3 %copy-start.11 = (bf16[8,512]{1,0:T(8,128)(2,1)}, bf16[8,512]{1,0:T(8,128)(2,1)S(1)}, u32[]{:S(2)}) copy-start(bf16[8,512]{1,0:T(8,128)(2,1)S(1)} %collective-permute-done.3.edge) | copy-start | bytes 24580
  41.3 38.3 %copy-start.10 = (f32[8,512]{1,0:T(8,128)}, f32[8,512]{1,0:T(8,128)S(1)}, u32[]{:S(2)}) copy-start(f32[8,512]{1,0:T(8,128)S(1)} %collective-permute-done.4.later) | copy-start | bytes 49156
  41.3 14.6 %copy-start.4 = (bf16[256,1024]{1,0:T(8,128)(2,1)}, bf16[256,1024]{1,0:T(8,128)(2,1)S(1)}, u32[]{:S(2)}) copy-start(bf16[256,1024]{1,0:T(8,128)(2,1)S(1)} %collective-permute-done.2.g11) | copy-start | bytes 1572868
  41.3 14.6 %copy-start.5 = (bf16[256,1024]{1,0:T(8,128)(2,1)}, bf16[256,1024]{1,0:T(8,128)(2,1)S(1)}, u32[]{:S(2)}) copy-start(bf16[256,1024]{1,0:T(8,128)(2,1)S(1)} %collective-permute-done.g01) | copy-start | bytes 1572868
  41.3 0.8 copy-start.6
  42.2 16.4 %all-to-all-start.1 = ((bf16[8,400,128]{2,1,0:T(8,128)(2,1)}), bf16[8,400,128]{2,1,0:T(8,128)(2,1)S(1)}, u32[]{:S(2)}, u32[]{:S(2)}) async-start(bf16[8,400,128]{2,1,0:T(8,128)(2,1)} %conv.1), calls=%async_computation.1 | async-start | bytes 1638400 | tf_op jit(solution)/shard_map/all_to_all | solution.py:642
  58.6 0.9 copy-start.1
  61.6 9.0 %collective-permute-start.5 = (bf16[256,768]{1,0:T(8,128)(2,1)}, bf16[256,768]{1,0:T(8,128)(2,1)S(1)}, u32[]{:S(2)}, u32[]{:S(2)}) collective-permute-start(bf16[256,768]{1,0:T(8,128)(2,1)} %get-tuple-element.43), channel_id=1, source_target_pairs={{0,32},{32,0},{1,33},{33,1},{2,34},{34,2},{3,35},{35,3},{4,36},{36... | collective-permute-start | bytes 1179656 | tf_op jit(solution)/shard_map/ppermute | solution.py:654
  62.9 10.6 %collective-permute-start.6 = (bf16[256,512]{1,0:T(8,128)(2,1)}, bf16[256,512]{1,0:T(8,128)(2,1)S(1)}, u32[]{:S(2)}, u32[]{:S(2)}) collective-permute-start(bf16[256,512]{1,0:T(8,128)(2,1)} %get-tuple-element.49.m00), channel_id=1, source_target_pairs={{0,8},{8,0},{1,9},{9,1},{2,10},{10,2},{3,11},{11,3},{4,12},{12,4},... | collective-permute-start | bytes 786440 | tf_op jit(solution)/shard_map/ppermute | solution.py:646
  70.6 4.0 %copy-start.3 = (bf16[256,768]{1,0:T(8,128)(2,1)}, bf16[256,768]{1,0:T(8,128)(2,1)S(1)}, u32[]{:S(2)}) copy-start(bf16[256,768]{1,0:T(8,128)(2,1)S(1)} %collective-permute-done.5.m01) | copy-start | bytes 1179652
  70.6 4.0 %collective-permute-start.7 = (bf16[256,512]{1,0:T(8,128)(2,1)S(1)}, bf16[256,512]{1,0:T(8,128)(2,1)S(1)}, u32[]{:S(2)}, u32[]{:S(2)}) collective-permute-start(bf16[256,512]{1,0:T(8,128)(2,1)S(1)} %slice.12), channel_id=1, source_target_pairs={{0,8},{8,0},{1,9},{9,1},{2,10},{10,2},{3,11},{11,3},{4,12},{12,4},... | collective-permute-start | bytes 786440 | tf_op jit(solution)/shard_map/ppermute | solution.py:646
  73.5 1.2 copy-start.8
  74.7 0.7 copy-start.9
  79.5 10.1 %copy-start.7 = (bf16[256,512]{1,0:T(8,128)(2,1)S(1)}, bf16[256,512]{1,0:T(8,128)(2,1)}, u32[]{:S(2)}) copy-start(bf16[256,512]{1,0:T(8,128)(2,1)} %get-tuple-element.49.m00) | copy-start | bytes 786436
  79.5 29.9 %all-to-all-start.2 = ((bf16[32,16,1152]{2,1,0:T(8,128)(2,1)}), bf16[32,16,1152]{2,1,0:T(8,128)(2,1)}, u32[]{:S(2)}, u32[]{:S(2)}) async-start(bf16[32,16,1152]{2,1,0:T(8,128)(2,1)} %partial.1), calls=%async_computation.2 | async-start | bytes 2359296 | tf_op jit(solution)/shard_map/all_to_all | solution.py:642
  112.3 36.0 %all-to-all-start.3 = ((bf16[64,16,1152]{2,1,0:T(8,128)(2,1)}), bf16[64,16,1152]{2,1,0:T(8,128)(2,1)}, u32[]{:S(2)}, u32[]{:S(2)}) async-start(bf16[64,16,1152]{2,1,0:T(8,128)(2,1)} %reduce.1), calls=%async_computation.3 | async-start | bytes 4718592 | tf_op jit(solution)/shard_map/all_to_all | solution.py:642
  148.4 8.2 %collective-permute-start.8 = (bf16[64,16,1152]{2,1,0:T(8,128)(2,1)}, bf16[64,16,1152]{2,1,0:T(8,128)(2,1)}, u32[]{:S(2)}, u32[]{:S(2)}) collective-permute-start(bf16[64,16,1152]{2,1,0:T(8,128)(2,1)} %all-to-all-done.3.rows.mine), channel_id=1, source_target_pairs={{0,8},{8,0},{1,9},{9,1},{2,10},{10,2},{3,11},{11,3},{4,12},{12,4},... | collective-permute-start | bytes 7077896 | tf_op jit(solution)/shard_map/ppermute | solution.py:646

commit v14 on v13

--- a/solution.py
+++ b/solution.py
@@ -431,7 +431,6 @@
             jax.ShapeDtypeStruct((BLOCK, 768), BF),
         ],
         scratch_shapes=[pltpu.VMEM((16, 512), F32)],
-        compiler_params=pltpu.CompilerParams(vmem_limit_bytes=KEEP_OUT),
         name="unpack_mixed",
     )(got, gate_out, edge, short, lags)
 
@@ -459,7 +458,6 @@
         out_shape=jax.ShapeDtypeStruct((3, BLOCK, 512), BF),
         scratch_shapes=[pltpu.VMEM((BLOCK + 8, 512), F32)],
         cost_estimate=pl.CostEstimate(flops=10**6, bytes_accessed=2 * 10**6, transcendentals=0),
-        compiler_params=pltpu.CompilerParams(vmem_limit_bytes=KEEP_OUT),
         name="unpack_grads",
     )(got, grad, later, short)
 
@@ -633,7 +631,6 @@
         out_shape=shapes,
         input_output_aliases={3: 0} if last else {},
         cost_estimate=pl.CostEstimate(flops=10**6, bytes_accessed=6 * 10**6, transcendentals=0),
-        compiler_params=pltpu.CompilerParams(vmem_limit_bytes=KEEP_OUT),
         name="write_last" if last else "write_first",
     )(half, rows, *([mine, whole] if last else []))
 

time: 161 us -> 159 us (0.988)
    unnamed x24 -> x26, local copies, waits for them, and re-layouts: 3.46 us -> 2.62 us
where the time goes in v14:
time: 159 us; the launch traced here: 158 us
  waiting for transfers between devices  58.7 us (37%)
  Pallas kernels  45 us (28%)
  starting transfers between devices  42.9 us (27%)
  local copies, waits for them, and re-layouts  5.25 us (3%)
  matrix products  4.77 us (3%)
    all_to_all x4, waiting for transfers between devices, exchange(): return lax.all_to_all(x, axes, 0, 0, tiled=True)  50.7 us
    all_to_all x4, starting transfers between devices, exchange(): return lax.all_to_all(x, axes, 0, 0, tiled=True)  25.3 us
    pallas_call x2, Pallas kernels, on_channels(): pl.pallas_call(kernel, grid_spec=pltpu.PrefetchScalarGridSpec(num_scalar_...  19.9 us
    ppermute x4, starting transfers between devices, across(): return lax.ppermute(x, 'c', [(0, 1), (1, 0)])  9.06 us
    pallas_call x1, Pallas kernels, pack(): pl.pallas_call(pack_kernel, grid=(steps,), in_specs=[full(3, BLOCK, 512),...  6.77 us
    pallas_call x2, Pallas kernels, write_half(): pl.pallas_call(last_kernel if last else first_kernel, grid_spec=pltpu.Pre...  6.44 us
    ppermute x2, waiting for transfers between devices, above(): return lax.ppermute(x, 'zl', [(0, 1), (1, 0)])  5.63 us
    ppermute x2, starting transfers between devices, along(): lax.ppermute(x, SEQ, [(n, n + step) for n in range(8) if 0 <= n + step < 8])  4.92 us
  transfers between devices with their start and end apart: 13, of which 7 were waited for; matrix products, arithmetic and copies ran while one was open for 5% of the time, Pallas kernels for 16%

profile of v14, /device:TPU:1, one launch (start us, length us, event | category | flops | bytes accessed | tf_op | source)
XLA Modules:
  0.0 158.0 jit_solution(14707837108425753416)
XLA Ops:
  0.6 6.8 %pack.1 = (bf16[8,272,256]{2,1,0:T(8,128)(2,1)}, f32[256,512]{1,0:T(8,128)}, f32[256,512]{1,0:T(8,128)}) custom-call(bf16[3,256,512]{2,1,0:T(8,128)(2,1)} %bitcast.23, bf16[256,4096]{1,0:T(8,128)(2,1)} %bitcast.21, bf16[512,4096]{1,0:T(8,128)(2,1)} %weight.1, f32[256,512]{1,0:T(8,128)} %filt.1, f32[3,3,512]{2,1,0:T(4,128)} %short.9), custom_call_target="tpu_custom_call" | custom-call | tf_op jit(solution)/shard_map/pack/pallas_call | solution.py:97
  7.4 6.0 %all-to-all-start = ((bf16[8,272,256]{2,1,0:T(8,128)(2,1)}), bf16[8,272,256]{2,1,0:T(8,128)(2,1)S(1)}, u32[]{:S(2)}, u32[]{:S(2)}) async-start(bf16[8,272,256]{2,1,0:T(8,128)(2,1)} %get-tuple-element.32), calls=%async_computation | async-start | bytes 2228224 | tf_op jit(solution)/shard_map/all_to_all | solution.py:639
  13.4 1.2 dynamic-slice_bitcast_fusion
  14.6 2.5 %collective-permute-start.2 = (bf16[256,1024]{1,0:T(8,128)(2,1)}, bf16[256,1024]{1,0:T(8,128)(2,1)S(1)}, u32[]{:S(2)}, u32[]{:S(2)}) collective-permute-start(bf16[256,1024]{1,0:T(8,128)(2,1)} %get-tuple-element.64), channel_id=1, source_target_pairs={{0,40},{8,32},{32,8},{40,0},{1,41},{9,33},{33,9},{41,1},{2,42},{10... | collective-permute-start | bytes 1572872 | tf_op jit(solution)/shard_map/ppermute | solution.py:655
  18.2 3.6 %collective-permute-start.3 = (bf16[8,512]{1,0:T(8,128)(2,1)S(1)}, bf16[8,512]{1,0:T(8,128)(2,1)S(1)}, u32[]{:S(2)}, u32[]{:S(2)}) collective-permute-start(bf16[8,512]{1,0:T(8,128)(2,1)S(1)} %slice_bitcast_fusion), channel_id=1, source_target_pairs={{0,1},{1,2},{2,3},{3,4},{4,5},{5,6},{6,7},{8,9},{9,10},{10,11},{11... | collective-permute-start | bytes 24584 | tf_op jit(solution)/shard_map/ppermute | solution.py:647
  21.8 0.7 slice.10
  22.6 1.3 collective-permute-start.4
  24.5 5.1 %all-to-all-done.got = bf16[8,272,256]{2,1,0:T(8,128)(2,1)S(1)} async-done(((bf16[8,272,256]{2,1,0:T(8,128)(2,1)}), bf16[8,272,256]{2,1,0:T(8,128)(2,1)S(1)}, u32[]{:S(2)}, u32[]{:S(2)}) %all-to-all-start) | async-done | bytes 1114144 | tf_op jit(solution)/shard_map/all_to_all | solution.py:639
  29.6 1.0 copy-done.3
  30.6 10.7 %conv.1 = bf16[8,400,128]{2,1,0:T(8,128)(2,1)} custom-call(s32[2]{0:T(128)} %pad_add_fusion.place, bf16[8,272,256]{2,1,0:T(8,128)(2,1)} %copy-done.3, f32[3,3,512]{2,1,0:T(4,128)} %short.9, f32[1,512]{1,0:T(1,128)} %bitcast.25, bf16[512,256]{1,0:T(8,128)(2,1)} %constant.38.clone.ahead_h, bf16[512,256]{1,0:T(8,128)(2,1)} %constant.39.clone.ahead_l, ...), custom_call_target="tpu_custom_call" | custom-call | tf_op jit(solution)/shard_map/conv/pallas_call | solution.py:345
  41.4 4.5 %all-to-all-start.1 = ((bf16[8,400,128]{2,1,0:T(8,128)(2,1)}), bf16[8,400,128]{2,1,0:T(8,128)(2,1)S(1)}, u32[]{:S(2)}, u32[]{:S(2)}) async-start(bf16[8,400,128]{2,1,0:T(8,128)(2,1)} %conv.1), calls=%async_computation.1 | async-start | bytes 1638400 | tf_op jit(solution)/shard_map/all_to_all | solution.py:639
  45.8 9.2 %lag_sums.1 = (bf16[32,16,128]{2,1,0:T(8,128)(2,1)}, bf16[32,16,128]{2,1,0:T(8,128)(2,1)}) custom-call(s32[2]{0:T(128)} %pad_add_fusion.place, bf16[8,272,256]{2,1,0:T(8,128)(2,1)} %copy-done.3, f32[3,3,512]{2,1,0:T(4,128)} %short.9, f32[1,512]{1,0:T(1,128)} %bitcast.26, bf16[512,256]{1,0:T(8,128)(2,1)} %constant.38.clone.ahead_h, ...), custom_call_target="tpu_custom_call" | custom-call | flops 2000000000 | bytes 3000000 | tf_op jit(solution)/shard_map/lag_sums/pallas_call | solution.py:345
  55.1 2.6 %all-to-all-done.1.got = bf16[8,400,128]{2,1,0:T(8,128)(2,1)S(1)} async-done(((bf16[8,400,128]{2,1,0:T(8,128)(2,1)}), bf16[8,400,128]{2,1,0:T(8,128)(2,1)S(1)}, u32[]{:S(2)}, u32[]{:S(2)}) %all-to-all-start.1) | async-done | bytes 819232 | tf_op jit(solution)/shard_map/all_to_all | solution.py:639
  57.7 0.9 copy-done.2
  58.6 2.2 %unpack_mixed.1 = (bf16[256,512]{1,0:T(8,128)(2,1)}, bf16[256,768]{1,0:T(8,128)(2,1)}) custom-call(bf16[8,400,128]{2,1,0:T(8,128)(2,1)} %copy-done.2, f32[256,512]{1,0:T(8,128)} %get-tuple-element.39.gate_out, bf16[8,512]{1,0:T(8,128)(2,1)} %copy-done.12, f32[3,3,512]{2,1,0:T(4,128)} %short.9, bf16[32,16,128]{2,1,0:T(8,128)(2,1)} %get-tuple-element.41.lags), custom_call_target="tpu_custom_call" | custom-call | tf_op jit(solution)/shard_map/unpack_mixed/pallas_call | solution.py:418
  60.8 1.2 collective-permute-start.5
  62.0 2.1 %collective-permute-start.6 = (bf16[256,512]{1,0:T(8,128)(2,1)}, bf16[256,512]{1,0:T(8,128)(2,1)S(1)}, u32[]{:S(2)}, u32[]{:S(2)}) collective-permute-start(bf16[256,512]{1,0:T(8,128)(2,1)} %get-tuple-element.49.m00), channel_id=1, source_target_pairs={{0,8},{8,0},{1,9},{9,1},{2,10},{10,2},{3,11},{11,3},{4,12},{12,4},... | collective-permute-start | bytes 786440 | tf_op jit(solution)/shard_map/ppermute | solution.py:643
  64.1 5.6 %collective-permute-done.5.m01 = bf16[256,768]{1,0:T(8,128)(2,1)S(1)} collective-permute-done((bf16[256,768]{1,0:T(8,128)(2,1)}, bf16[256,768]{1,0:T(8,128)(2,1)S(1)}, u32[]{:S(2)}, u32[]{:S(2)}) %collective-permute-start.5) | collective-permute-done | bytes 393248 | tf_op jit(solution)/shard_map/ppermute | solution.py:651
  69.8 2.9 %collective-permute-start.7 = (bf16[256,512]{1,0:T(8,128)(2,1)S(1)}, bf16[256,512]{1,0:T(8,128)(2,1)S(1)}, u32[]{:S(2)}, u32[]{:S(2)}) collective-permute-start(bf16[256,512]{1,0:T(8,128)(2,1)S(1)} %slice.12), channel_id=1, source_target_pairs={{0,8},{8,0},{1,9},{9,1},{2,10},{10,2},{3,11},{11,3},{4,12},{12,4},... | collective-permute-start | bytes 786440 | tf_op jit(solution)/shard_map/ppermute | solution.py:643
  72.6 1.2 collective-permute-done.7.m11
  74.5 4.2 %partial.1 = bf16[32,16,1152]{2,1,0:T(8,128)(2,1)} custom-call(s32[1]{0:T(128)} %bitcast.place, bf16[256,512]{1,0:T(8,128)(2,1)} %get-tuple-element.49.m00, bf16[256,768]{1,0:T(8,128)(2,1)} %copy-done.4, bf16[256,512]{1,0:T(8,128)(2,1)} %copy-done.9, bf16[256,512]{1,0:T(8,128)(2,1)} %copy-done.10, bf16[256,4096]{1,0:T(8,128)(2,1)} %bitcast.22, ...), custom_call_target="tpu_custom_call" | custom-call | tf_op jit(solution)/shard_map/partial/pallas_call | solution.py:483
  78.7 10.1 %all-to-all-start.2 = ((bf16[32,16,1152]{2,1,0:T(8,128)(2,1)}), bf16[32,16,1152]{2,1,0:T(8,128)(2,1)}, u32[]{:S(2)}, u32[]{:S(2)}) async-start(bf16[32,16,1152]{2,1,0:T(8,128)(2,1)} %partial.1), calls=%async_computation.2 | async-start | bytes 2359296 | tf_op jit(solution)/shard_map/all_to_all | solution.py:639
  88.8 4.8 %convolution_convert_fusion = bf16[256,4096]{1,0:T(8,128)(2,1)} fusion(bf16[256,512]{1,0:T(8,128)(2,1)S(1)} %copy-done.8, bf16[512,4096]{1,0:T(8,128)(2,1)} %weight.1), kind=kOutput, calls=%fused_computation | convolution fusion | flops 1074790400 | bytes 6553600 | tf_op jit(solution)/shard_map/dot_general | solution.py:691
  93.5 15.1 %all-to-all-done.2.got = bf16[32,16,1152]{2,1,0:T(8,128)(2,1)} async-done(((bf16[32,16,1152]{2,1,0:T(8,128)(2,1)}), bf16[32,16,1152]{2,1,0:T(8,128)(2,1)}, u32[]{:S(2)}, u32[]{:S(2)}) %all-to-all-start.2) | async-done | bytes 1179680 | tf_op jit(solution)/shard_map/all_to_all | solution.py:639
  108.6 2.8 %reduce.1 = bf16[64,16,1152]{2,1,0:T(8,128)(2,1)} custom-call(bf16[32,16,1152]{2,1,0:T(8,128)(2,1)} %all-to-all-done.2.got), custom_call_target="tpu_custom_call" | custom-call | tf_op jit(solution)/shard_map/reduce/pallas_call | solution.py:537
  111.5 4.7 %all-to-all-start.3 = ((bf16[64,16,1152]{2,1,0:T(8,128)(2,1)}), bf16[64,16,1152]{2,1,0:T(8,128)(2,1)S(1)}, u32[]{:S(2)}, u32[]{:S(2)}) async-start(bf16[64,16,1152]{2,1,0:T(8,128)(2,1)} %reduce.1), calls=%async_computation.3 | async-start | bytes 4718592 | tf_op jit(solution)/shard_map/all_to_all | solution.py:639
  116.2 2.7 %unpack_grads.1 = bf16[3,256,512]{2,1,0:T(8,128)(2,1)} custom-call(bf16[8,400,128]{2,1,0:T(8,128)(2,1)} %copy-done.2, f32[256,512]{1,0:T(8,128)} %get-tuple-element.33.grad, f32[8,512]{1,0:T(8,128)} %copy-done.11, f32[3,3,512]{2,1,0:T(4,128)} %short.9), custom_call_target="tpu_custom_call" | custom-call | flops 1000000 | bytes 2000000 | tf_op jit(solution)/shard_map/unpack_grads/pallas_call | solution.py:456
  118.9 27.9 %all-to-all-done.3.rows.mine = bf16[64,16,1152]{2,1,0:T(8,128)(2,1)S(1)} async-done(((bf16[64,16,1152]{2,1,0:T(8,128)(2,1)}), bf16[64,16,1152]{2,1,0:T(8,128)(2,1)S(1)}, u32[]{:S(2)}, u32[]{:S(2)}) %all-to-all-start.3) | async-done | bytes 2359328 | tf_op jit(solution)/shard_map/all_to_all | solution.py:639
  146.8 3.7 %collective-permute-start.8 = (bf16[64,16,1152]{2,1,0:T(8,128)(2,1)S(1)}, bf16[64,16,1152]{2,1,0:T(8,128)(2,1)}, u32[]{:S(2)}, u32[]{:S(2)}) collective-permute-start(bf16[64,16,1152]{2,1,0:T(8,128)(2,1)S(1)} %all-to-all-done.3.rows.mine), channel_id=1, source_target_pairs={{0,8},{8,0},{1,9},{9,1},{2,10},{10,2},{3,11},{11,3},{4,12},{12,4},... | collective-permute-start | bytes 7077896 | tf_op jit(solution)/shard_map/ppermute | solution.py:643
  150.4 3.1 %write_first.1.whole = f32[512,4096]{1,0:T(8,128)} custom-call(s32[1]{0:T(128)} %bitcast.13.place, bf16[64,16,1152]{2,1,0:T(8,128)(2,1)} %copy-done), custom_call_target="tpu_custom_call" | custom-call | flops 1000000 | bytes 6000000 | tf_op jit(solution)/shard_map/write_first/pallas_call | solution.py:610
  153.6 1.2 collective-permute-done.8.rows
  154.7 3.3 %write_last.1 = (f32[512,4096]{1,0:T(8,128)}, f32[256,512]{1,0:T(8,128)}) custom-call(s32[1]{0:T(128)S(6)} %sub.13.place, bf16[64,16,1152]{2,1,0:T(8,128)(2,1)} %collective-permute-done.8.rows, bf16[64,16,1152]{2,1,0:T(8,128)(2,1)} %copy-done, f32[512,4096]{1,0:T(8,128)} %write_first.1.whole), custom_call_target="tpu_custom_call", output_to_operand_aliasing={{0}: (3, {})} | custom-call | flops 1000000 | bytes 6000000 | tf_op jit(solution)/shard_map/write_last/pallas_call | solution.py:610
  (35 shorter events, 2.6 us)
Async XLA Ops:
  7.4 6.0 %copy-start.1 = (bf16[1,256,4096]{2,1,0:T(8,128)(2,1)S(1)}, bf16[1,256,4096]{2,1,0:T(8,128)(2,1)}, u32[]{:S(2)}) copy-start(bf16[1,256,4096]{2,1,0:T(8,128)(2,1)} %param.15) | copy-start | bytes 6291460
  7.4 22.2 %all-to-all-start = ((bf16[8,272,256]{2,1,0:T(8,128)(2,1)}), bf16[8,272,256]{2,1,0:T(8,128)(2,1)S(1)}, u32[]{:S(2)}, u32[]{:S(2)}) async-start(bf16[8,272,256]{2,1,0:T(8,128)(2,1)} %get-tuple-element.32), calls=%async_computation | async-start | bytes 2228224 | tf_op jit(solution)/shard_map/all_to_all | solution.py:639
  14.6 26.7 %collective-permute-start.2 = (bf16[256,1024]{1,0:T(8,128)(2,1)}, bf16[256,1024]{1,0:T(8,128)(2,1)S(1)}, u32[]{:S(2)}, u32[]{:S(2)}) collective-permute-start(bf16[256,1024]{1,0:T(8,128)(2,1)} %get-tuple-element.64), channel_id=1, source_target_pairs={{0,40},{8,32},{32,8},{40,0},{1,41},{9,33},{33,9},{41,1},{2,42},{10... | collective-permute-start | bytes 1572872 | tf_op jit(solution)/shard_map/ppermute | solution.py:655
  17.1 24.2 %collective-permute-start = (bf16[256,1024]{1,0:T(8,128)(2,1)}, bf16[256,1024]{1,0:T(8,128)(2,1)S(1)}, u32[]{:S(2)}, u32[]{:S(2)}) collective-permute-start(bf16[256,1024]{1,0:T(8,128)(2,1)} %get-tuple-element.65), channel_id=1, source_target_pairs={{0,32},{32,0},{1,33},{33,1},{2,34},{34,2},{3,35},{35,3},{4,36},{36... | collective-permute-start | bytes 1572872 | tf_op jit(solution)/shard_map/ppermute | solution.py:651
  17.1 24.3 %collective-permute-start.1 = (bf16[256,1024]{1,0:T(8,128)(2,1)}, bf16[256,1024]{1,0:T(8,128)(2,1)S(1)}, u32[]{:S(2)}, u32[]{:S(2)}) collective-permute-start(bf16[256,1024]{1,0:T(8,128)(2,1)} %get-tuple-element.66), channel_id=1, source_target_pairs={{0,8},{8,0},{1,9},{9,1},{2,10},{10,2},{3,11},{11,3},{4,12},{12,4},... | collective-permute-start | bytes 1572872 | tf_op jit(solution)/shard_map/ppermute | solution.py:643
  18.2 23.1 %collective-permute-start.3 = (bf16[8,512]{1,0:T(8,128)(2,1)S(1)}, bf16[8,512]{1,0:T(8,128)(2,1)S(1)}, u32[]{:S(2)}, u32[]{:S(2)}) collective-permute-start(bf16[8,512]{1,0:T(8,128)(2,1)S(1)} %slice_bitcast_fusion), channel_id=1, source_target_pairs={{0,1},{1,2},{2,3},{3,4},{4,5},{5,6},{6,7},{8,9},{9,10},{10,11},{11... | collective-permute-start | bytes 24584 | tf_op jit(solution)/shard_map/ppermute | solution.py:647
  22.6 18.7 %collective-permute-start.4 = (f32[8,512]{1,0:T(8,128)S(1)}, f32[8,512]{1,0:T(8,128)S(1)}, u32[]{:S(2)}, u32[]{:S(2)}) collective-permute-start(f32[8,512]{1,0:T(8,128)S(1)} %slice.10), channel_id=1, source_target_pairs={{1,0},{2,1},{3,2},{4,3},{5,4},{6,5},{7,6},{9,8},{10,9},{11,10},{12... | collective-permute-start | bytes 49160 | tf_op jit(solution)/shard_map/ppermute | solution.py:647
  29.6 1.0 copy-start.3
  41.3 13.8 %copy-start.12 = (bf16[8,512]{1,0:T(8,128)(2,1)}, bf16[8,512]{1,0:T(8,128)(2,1)S(1)}, u32[]{:S(2)}) copy-start(bf16[8,512]{1,0:T(8,128)(2,1)S(1)} %collective-permute-done.3.edge) | copy-start | bytes 24580
  41.3 13.8 %copy-start.11 = (f32[8,512]{1,0:T(8,128)}, f32[8,512]{1,0:T(8,128)S(1)}, u32[]{:S(2)}) copy-start(f32[8,512]{1,0:T(8,128)S(1)} %collective-permute-done.4.later) | copy-start | bytes 49156
  41.3 13.8 %copy-start.5 = (bf16[256,1024]{1,0:T(8,128)(2,1)}, bf16[256,1024]{1,0:T(8,128)(2,1)S(1)}, u32[]{:S(2)}) copy-start(bf16[256,1024]{1,0:T(8,128)(2,1)S(1)} %collective-permute-done.2.g11) | copy-start | bytes 1572868
  41.3 13.7 %copy-start.6 = (bf16[256,1024]{1,0:T(8,128)(2,1)}, bf16[256,1024]{1,0:T(8,128)(2,1)S(1)}, u32[]{:S(2)}) copy-start(bf16[256,1024]{1,0:T(8,128)(2,1)S(1)} %collective-permute-done.g01) | copy-start | bytes 1572868
  41.3 13.7 %copy-start.7 = (bf16[256,1024]{1,0:T(8,128)(2,1)}, bf16[256,1024]{1,0:T(8,128)(2,1)S(1)}, u32[]{:S(2)}) copy-start(bf16[256,1024]{1,0:T(8,128)(2,1)S(1)} %collective-permute-done.1.g10) | copy-start | bytes 1572868
  41.4 16.4 %all-to-all-start.1 = ((bf16[8,400,128]{2,1,0:T(8,128)(2,1)}), bf16[8,400,128]{2,1,0:T(8,128)(2,1)S(1)}, u32[]{:S(2)}, u32[]{:S(2)}) async-start(bf16[8,400,128]{2,1,0:T(8,128)(2,1)} %conv.1), calls=%async_computation.1 | async-start | bytes 1638400 | tf_op jit(solution)/shard_map/all_to_all | solution.py:639
  57.7 0.9 copy-start.2
  60.8 9.0 %collective-permute-start.5 = (bf16[256,768]{1,0:T(8,128)(2,1)}, bf16[256,768]{1,0:T(8,128)(2,1)S(1)}, u32[]{:S(2)}, u32[]{:S(2)}) collective-permute-start(bf16[256,768]{1,0:T(8,128)(2,1)} %get-tuple-element.43), channel_id=1, source_target_pairs={{0,32},{32,0},{1,33},{33,1},{2,34},{34,2},{3,35},{35,3},{4,36},{36... | collective-permute-start | bytes 1179656 | tf_op jit(solution)/shard_map/ppermute | solution.py:651
  62.0 10.6 %collective-permute-start.6 = (bf16[256,512]{1,0:T(8,128)(2,1)}, bf16[256,512]{1,0:T(8,128)(2,1)S(1)}, u32[]{:S(2)}, u32[]{:S(2)}) collective-permute-start(bf16[256,512]{1,0:T(8,128)(2,1)} %get-tuple-element.49.m00), channel_id=1, source_target_pairs={{0,8},{8,0},{1,9},{9,1},{2,10},{10,2},{3,11},{11,3},{4,12},{12,4},... | collective-permute-start | bytes 786440 | tf_op jit(solution)/shard_map/ppermute | solution.py:643
  69.8 4.0 %copy-start.4 = (bf16[256,768]{1,0:T(8,128)(2,1)}, bf16[256,768]{1,0:T(8,128)(2,1)S(1)}, u32[]{:S(2)}) copy-start(bf16[256,768]{1,0:T(8,128)(2,1)S(1)} %collective-permute-done.5.m01) | copy-start | bytes 1179652
  69.8 4.0 %collective-permute-start.7 = (bf16[256,512]{1,0:T(8,128)(2,1)S(1)}, bf16[256,512]{1,0:T(8,128)(2,1)S(1)}, u32[]{:S(2)}, u32[]{:S(2)}) collective-permute-start(bf16[256,512]{1,0:T(8,128)(2,1)S(1)} %slice.12), channel_id=1, source_target_pairs={{0,8},{8,0},{1,9},{9,1},{2,10},{10,2},{3,11},{11,3},{4,12},{12,4},... | collective-permute-start | bytes 786440 | tf_op jit(solution)/shard_map/ppermute | solution.py:643
  72.6 1.2 copy-start.9
  73.8 0.7 copy-start.10
  78.7 10.1 %copy-start.8 = (bf16[256,512]{1,0:T(8,128)(2,1)S(1)}, bf16[256,512]{1,0:T(8,128)(2,1)}, u32[]{:S(2)}) copy-start(bf16[256,512]{1,0:T(8,128)(2,1)} %get-tuple-element.49.m00) | copy-start | bytes 786436
  78.7 29.9 %all-to-all-start.2 = ((bf16[32,16,1152]{2,1,0:T(8,128)(2,1)}), bf16[32,16,1152]{2,1,0:T(8,128)(2,1)}, u32[]{:S(2)}, u32[]{:S(2)}) async-start(bf16[32,16,1152]{2,1,0:T(8,128)(2,1)} %partial.1), calls=%async_computation.2 | async-start | bytes 2359296 | tf_op jit(solution)/shard_map/all_to_all | solution.py:639
  111.5 35.3 %all-to-all-start.3 = ((bf16[64,16,1152]{2,1,0:T(8,128)(2,1)}), bf16[64,16,1152]{2,1,0:T(8,128)(2,1)S(1)}, u32[]{:S(2)}, u32[]{:S(2)}) async-start(bf16[64,16,1152]{2,1,0:T(8,128)(2,1)} %reduce.1), calls=%async_computation.3 | async-start | bytes 4718592 | tf_op jit(solution)/shard_map/all_to_all | solution.py:639
  146.8 3.7 %copy-start = (bf16[64,16,1152]{2,1,0:T(8,128)(2,1)}, bf16[64,16,1152]{2,1,0:T(8,128)(2,1)S(1)}, u32[]{:S(2)}) copy-start(bf16[64,16,1152]{2,1,0:T(8,128)(2,1)S(1)} %all-to-all-done.3.rows.mine) | copy-start | bytes 7077892
  146.8 8.0 %collective-permute-start.8 = (bf16[64,16,1152]{2,1,0:T(8,128)(2,1)S(1)}, bf16[64,16,1152]{2,1,0:T(8,128)(2,1)}, u32[]{:S(2)}, u32[]{:S(2)}) collective-permute-start(bf16[64,16,1152]{2,1,0:T(8,128)(2,1)S(1)} %all-to-all-done.3.rows.mine), channel_id=1, source_target_pairs={{0,8},{8,0},{1,9},{9,1},{2,10},{10,2},{3,11},{11,3},{4,12},{12,4},... | collective-permute-start | bytes 7077896 | tf_op jit(solution)/shard_map/ppermute | solution.py:643

commit v15 on v14

--- a/solution.py
+++ b/solution.py
@@ -361,6 +361,7 @@
         ),
         out_shape=[jax.ShapeDtypeStruct(shape, dtype) for shape, dtype in outputs],
         cost_estimate=cost,
+        compiler_params=pltpu.CompilerParams(vmem_limit_bytes=KEEP_OUT if cost is None else None),
         name=name,
     )(*inputs)
 

time: 159 us -> 159 us (level)
  transfers between devices with their start and end apart: 13 -> 13, of which waited for: 7 -> 8; matrix products, arithmetic and copies ran while one was open for 5% -> 5% of each run, Pallas kernels for 16% -> 16%
where the time goes in v15:
time: 159 us; the launch traced here: 158 us
  waiting for transfers between devices  59.7 us (38%)
  Pallas kernels  45 us (28%)
  starting transfers between devices  43.1 us (27%)
  matrix products  4.77 us (3%)
  local copies, waits for them, and re-layouts  4.23 us (3%)
    all_to_all x4, waiting for transfers between devices, exchange(): return lax.all_to_all(x, axes, 0, 0, tiled=True)  50.8 us
    all_to_all x4, starting transfers between devices, exchange(): return lax.all_to_all(x, axes, 0, 0, tiled=True)  25.7 us
    pallas_call x2, Pallas kernels, on_channels(): pl.pallas_call(kernel, grid_spec=pltpu.PrefetchScalarGridSpec(num_scalar_...  19.9 us
    ppermute x4, starting transfers between devices, across(): return lax.ppermute(x, 'c', [(0, 1), (1, 0)])  8.05 us
    pallas_call x1, Pallas kernels, pack(): pl.pallas_call(pack_kernel, grid=(steps,), in_specs=[full(3, BLOCK, 512),...  6.77 us
    ppermute x2, waiting for transfers between devices, above(): return lax.ppermute(x, 'zl', [(0, 1), (1, 0)])  6.5 us
    pallas_call x2, Pallas kernels, write_half(): pl.pallas_call(last_kernel if last else first_kernel, grid_spec=pltpu.Pre...  6.44 us
    ppermute x2, starting transfers between devices, along(): lax.ppermute(x, SEQ, [(n, n + step) for n in range(8) if 0 <= n + step < 8])  4.92 us
  transfers between devices with their start and end apart: 13, of which 8 were waited for; matrix products, arithmetic and copies ran while one was open for 5% of the time, Pallas kernels for 16%

profile of v15, /device:TPU:1, one launch (start us, length us, event | category | flops | bytes accessed | tf_op | source)
XLA Modules:
  0.0 158.1 jit_solution(7269559378226037847)
XLA Ops:
  0.6 6.8 %pack.1 = (bf16[8,272,256]{2,1,0:T(8,128)(2,1)}, f32[256,512]{1,0:T(8,128)}, f32[256,512]{1,0:T(8,128)}) custom-call(bf16[3,256,512]{2,1,0:T(8,128)(2,1)} %bitcast.23, bf16[256,4096]{1,0:T(8,128)(2,1)} %bitcast.21, bf16[512,4096]{1,0:T(8,128)(2,1)} %weight.1, f32[256,512]{1,0:T(8,128)} %filt.1, f32[3,3,512]{2,1,0:T(4,128)} %short.9), custom_call_target="tpu_custom_call" | custom-call | tf_op jit(solution)/shard_map/pack/pallas_call | solution.py:97
  7.4 6.0 %all-to-all-start = ((bf16[8,272,256]{2,1,0:T(8,128)(2,1)}), bf16[8,272,256]{2,1,0:T(8,128)(2,1)}, u32[]{:S(2)}, u32[]{:S(2)}) async-start(bf16[8,272,256]{2,1,0:T(8,128)(2,1)} %get-tuple-element.32), calls=%async_computation | async-start | bytes 2228224 | tf_op jit(solution)/shard_map/all_to_all | solution.py:640
  13.4 1.2 dynamic-slice_bitcast_fusion
  14.6 2.5 %collective-permute-start.2 = (bf16[256,1024]{1,0:T(8,128)(2,1)}, bf16[256,1024]{1,0:T(8,128)(2,1)S(1)}, u32[]{:S(2)}, u32[]{:S(2)}) collective-permute-start(bf16[256,1024]{1,0:T(8,128)(2,1)} %get-tuple-element.64), channel_id=1, source_target_pairs={{0,40},{8,32},{32,8},{40,0},{1,41},{9,33},{33,9},{41,1},{2,42},{10... | collective-permute-start | bytes 1572872 | tf_op jit(solution)/shard_map/ppermute | solution.py:656
  17.5 0.7 slice_bitcast_fusion
  18.2 3.6 %collective-permute-start.3 = (bf16[8,512]{1,0:T(8,128)(2,1)S(1)}, bf16[8,512]{1,0:T(8,128)(2,1)S(1)}, u32[]{:S(2)}, u32[]{:S(2)}) collective-permute-start(bf16[8,512]{1,0:T(8,128)(2,1)S(1)} %slice_bitcast_fusion), channel_id=1, source_target_pairs={{0,1},{1,2},{2,3},{3,4},{4,5},{5,6},{6,7},{8,9},{9,10},{10,11},{11... | collective-permute-start | bytes 24584 | tf_op jit(solution)/shard_map/ppermute | solution.py:648
  21.8 0.7 slice.10
  22.6 1.3 collective-permute-start.4
  24.5 5.2 %all-to-all-done.got = bf16[8,272,256]{2,1,0:T(8,128)(2,1)} async-done(((bf16[8,272,256]{2,1,0:T(8,128)(2,1)}), bf16[8,272,256]{2,1,0:T(8,128)(2,1)}, u32[]{:S(2)}, u32[]{:S(2)}) %all-to-all-start) | async-done | bytes 1114144 | tf_op jit(solution)/shard_map/all_to_all | solution.py:640
  29.7 10.7 %conv.1 = bf16[8,400,128]{2,1,0:T(8,128)(2,1)} custom-call(s32[2]{0:T(128)} %pad_add_fusion.place, bf16[8,272,256]{2,1,0:T(8,128)(2,1)} %all-to-all-done.got, f32[3,3,512]{2,1,0:T(4,128)} %short.9, f32[1,512]{1,0:T(1,128)} %bitcast.25, bf16[512,256]{1,0:T(8,128)(2,1)} %constant.38.clone.ahead_h, bf16[512,256]{1,0:T(8,128)(2,1)} %constant.39.clone.ahead_l, ...), custom_call_target="tpu_custom_call" | custom-call | tf_op jit(solution)/shard_map/conv/pallas_call | solution.py:345
  40.5 5.4 %all-to-all-start.1 = ((bf16[8,400,128]{2,1,0:T(8,128)(2,1)}), bf16[8,400,128]{2,1,0:T(8,128)(2,1)S(1)}, u32[]{:S(2)}, u32[]{:S(2)}) async-start(bf16[8,400,128]{2,1,0:T(8,128)(2,1)} %conv.1), calls=%async_computation.1 | async-start | bytes 1638400 | tf_op jit(solution)/shard_map/all_to_all | solution.py:640
  45.9 9.2 %lag_sums.1 = (bf16[32,16,128]{2,1,0:T(8,128)(2,1)}, bf16[32,16,128]{2,1,0:T(8,128)(2,1)}) custom-call(s32[2]{0:T(128)} %pad_add_fusion.place, bf16[8,272,256]{2,1,0:T(8,128)(2,1)} %all-to-all-done.got, f32[3,3,512]{2,1,0:T(4,128)} %short.9, f32[1,512]{1,0:T(1,128)} %bitcast.26, bf16[512,256]{1,0:T(8,128)(2,1)} %constant.38.clone.ahead_h, ...), custom_call_target="tpu_custom_call" | custom-call | flops 2000000000 | bytes 3000000 | tf_op jit(solution)/shard_map/lag_sums/pallas_call | solution.py:345
  55.2 2.7 %all-to-all-done.1.got = bf16[8,400,128]{2,1,0:T(8,128)(2,1)S(1)} async-done(((bf16[8,400,128]{2,1,0:T(8,128)(2,1)}), bf16[8,400,128]{2,1,0:T(8,128)(2,1)S(1)}, u32[]{:S(2)}, u32[]{:S(2)}) %all-to-all-start.1) | async-done | bytes 819232 | tf_op jit(solution)/shard_map/all_to_all | solution.py:640
  57.8 0.9 copy-done.2
  58.7 2.2 %unpack_mixed.1 = (bf16[256,512]{1,0:T(8,128)(2,1)}, bf16[256,768]{1,0:T(8,128)(2,1)}) custom-call(bf16[8,400,128]{2,1,0:T(8,128)(2,1)} %copy-done.2, f32[256,512]{1,0:T(8,128)} %get-tuple-element.39.gate_out, bf16[8,512]{1,0:T(8,128)(2,1)} %copy-done.9, f32[3,3,512]{2,1,0:T(4,128)} %short.9, bf16[32,16,128]{2,1,0:T(8,128)(2,1)} %get-tuple-element.41.lags), custom_call_target="tpu_custom_call" | custom-call | tf_op jit(solution)/shard_map/unpack_mixed/pallas_call | solution.py:419
  60.9 2.0 %collective-permute-start.5 = (bf16[256,768]{1,0:T(8,128)(2,1)}, bf16[256,768]{1,0:T(8,128)(2,1)S(1)}, u32[]{:S(2)}, u32[]{:S(2)}) collective-permute-start(bf16[256,768]{1,0:T(8,128)(2,1)} %get-tuple-element.43), channel_id=1, source_target_pairs={{0,32},{32,0},{1,33},{33,1},{2,34},{34,2},{3,35},{35,3},{4,36},{36... | collective-permute-start | bytes 1179656 | tf_op jit(solution)/shard_map/ppermute | solution.py:652
  62.8 1.6 %collective-permute-start.6 = (bf16[256,512]{1,0:T(8,128)(2,1)}, bf16[256,512]{1,0:T(8,128)(2,1)S(1)}, u32[]{:S(2)}, u32[]{:S(2)}) collective-permute-start(bf16[256,512]{1,0:T(8,128)(2,1)} %get-tuple-element.49.m00), channel_id=1, source_target_pairs={{0,8},{8,0},{1,9},{9,1},{2,10},{10,2},{3,11},{11,3},{4,12},{12,4},... | collective-permute-start | bytes 786440 | tf_op jit(solution)/shard_map/ppermute | solution.py:644
  64.5 6.4 %collective-permute-done.5.m01 = bf16[256,768]{1,0:T(8,128)(2,1)S(1)} collective-permute-done((bf16[256,768]{1,0:T(8,128)(2,1)}, bf16[256,768]{1,0:T(8,128)(2,1)S(1)}, u32[]{:S(2)}, u32[]{:S(2)}) %collective-permute-start.5) | collective-permute-done | bytes 393248 | tf_op jit(solution)/shard_map/ppermute | solution.py:652
  70.9 2.4 %collective-permute-start.7 = (bf16[256,512]{1,0:T(8,128)(2,1)S(1)}, bf16[256,512]{1,0:T(8,128)(2,1)S(1)}, u32[]{:S(2)}, u32[]{:S(2)}) collective-permute-start(bf16[256,512]{1,0:T(8,128)(2,1)S(1)} %slice.12), channel_id=1, source_target_pairs={{0,8},{8,0},{1,9},{9,1},{2,10},{10,2},{3,11},{11,3},{4,12},{12,4},... | collective-permute-start | bytes 786440 | tf_op jit(solution)/shard_map/ppermute | solution.py:644
  73.2 1.2 collective-permute-done.7.m11
  75.1 4.2 %partial.1 = bf16[32,16,1152]{2,1,0:T(8,128)(2,1)} custom-call(s32[1]{0:T(128)} %bitcast.place, bf16[256,512]{1,0:T(8,128)(2,1)} %get-tuple-element.49.m00, bf16[256,768]{1,0:T(8,128)(2,1)} %copy-done.3, bf16[256,512]{1,0:T(8,128)(2,1)} %copy-done.6, bf16[256,512]{1,0:T(8,128)(2,1)} %copy-done.7, bf16[256,4096]{1,0:T(8,128)(2,1)} %bitcast.22, ...), custom_call_target="tpu_custom_call" | custom-call | tf_op jit(solution)/shard_map/partial/pallas_call | solution.py:484
  79.3 9.5 %all-to-all-start.2 = ((bf16[32,16,1152]{2,1,0:T(8,128)(2,1)}), bf16[32,16,1152]{2,1,0:T(8,128)(2,1)}, u32[]{:S(2)}, u32[]{:S(2)}) async-start(bf16[32,16,1152]{2,1,0:T(8,128)(2,1)} %partial.1), calls=%async_computation.2 | async-start | bytes 2359296 | tf_op jit(solution)/shard_map/all_to_all | solution.py:640
  88.8 4.8 %convolution_convert_fusion = bf16[256,4096]{1,0:T(8,128)(2,1)} fusion(bf16[256,512]{1,0:T(8,128)(2,1)S(1)} %copy-done.5, bf16[512,4096]{1,0:T(8,128)(2,1)} %weight.1), kind=kOutput, calls=%fused_computation | convolution fusion | flops 1074790400 | bytes 6553600 | tf_op jit(solution)/shard_map/dot_general | solution.py:692
  93.6 15.1 %all-to-all-done.2.got = bf16[32,16,1152]{2,1,0:T(8,128)(2,1)} async-done(((bf16[32,16,1152]{2,1,0:T(8,128)(2,1)}), bf16[32,16,1152]{2,1,0:T(8,128)(2,1)}, u32[]{:S(2)}, u32[]{:S(2)}) %all-to-all-start.2) | async-done | bytes 1179680 | tf_op jit(solution)/shard_map/all_to_all | solution.py:640
  108.7 2.8 %reduce.1 = bf16[64,16,1152]{2,1,0:T(8,128)(2,1)} custom-call(bf16[32,16,1152]{2,1,0:T(8,128)(2,1)} %all-to-all-done.2.got), custom_call_target="tpu_custom_call" | custom-call | tf_op jit(solution)/shard_map/reduce/pallas_call | solution.py:538
  111.5 4.7 %all-to-all-start.3 = ((bf16[64,16,1152]{2,1,0:T(8,128)(2,1)}), bf16[64,16,1152]{2,1,0:T(8,128)(2,1)S(1)}, u32[]{:S(2)}, u32[]{:S(2)}) async-start(bf16[64,16,1152]{2,1,0:T(8,128)(2,1)} %reduce.1), calls=%async_computation.3 | async-start | bytes 4718592 | tf_op jit(solution)/shard_map/all_to_all | solution.py:640
  116.3 2.7 %unpack_grads.1 = bf16[3,256,512]{2,1,0:T(8,128)(2,1)} custom-call(bf16[8,400,128]{2,1,0:T(8,128)(2,1)} %copy-done.2, f32[256,512]{1,0:T(8,128)} %get-tuple-element.33.grad, f32[8,512]{1,0:T(8,128)} %copy-done.8, f32[3,3,512]{2,1,0:T(4,128)} %short.9), custom_call_target="tpu_custom_call" | custom-call | flops 1000000 | bytes 2000000 | tf_op jit(solution)/shard_map/unpack_grads/pallas_call | solution.py:457
  119.0 27.9 %all-to-all-done.3.rows.mine = bf16[64,16,1152]{2,1,0:T(8,128)(2,1)S(1)} async-done(((bf16[64,16,1152]{2,1,0:T(8,128)(2,1)}), bf16[64,16,1152]{2,1,0:T(8,128)(2,1)S(1)}, u32[]{:S(2)}, u32[]{:S(2)}) %all-to-all-start.3) | async-done | bytes 2359328 | tf_op jit(solution)/shard_map/all_to_all | solution.py:640
  146.8 3.7 %collective-permute-start.8 = (bf16[64,16,1152]{2,1,0:T(8,128)(2,1)S(1)}, bf16[64,16,1152]{2,1,0:T(8,128)(2,1)}, u32[]{:S(2)}, u32[]{:S(2)}) collective-permute-start(bf16[64,16,1152]{2,1,0:T(8,128)(2,1)S(1)} %all-to-all-done.3.rows.mine), channel_id=1, source_target_pairs={{0,8},{8,0},{1,9},{9,1},{2,10},{10,2},{3,11},{11,3},{4,12},{12,4},... | collective-permute-start | bytes 7077896 | tf_op jit(solution)/shard_map/ppermute | solution.py:644
  150.5 3.1 %write_first.1.whole = f32[512,4096]{1,0:T(8,128)} custom-call(s32[1]{0:T(128)} %bitcast.13.place, bf16[64,16,1152]{2,1,0:T(8,128)(2,1)} %copy-done), custom_call_target="tpu_custom_call" | custom-call | flops 1000000 | bytes 6000000 | tf_op jit(solution)/shard_map/write_first/pallas_call | solution.py:611
  153.6 1.2 collective-permute-done.8.rows
  154.8 3.3 %write_last.1 = (f32[512,4096]{1,0:T(8,128)}, f32[256,512]{1,0:T(8,128)}) custom-call(s32[1]{0:T(128)S(6)} %sub.13.place, bf16[64,16,1152]{2,1,0:T(8,128)(2,1)} %collective-permute-done.8.rows, bf16[64,16,1152]{2,1,0:T(8,128)(2,1)} %copy-done, f32[512,4096]{1,0:T(8,128)} %write_first.1.whole), custom_call_target="tpu_custom_call", output_to_operand_aliasing={{0}: (3, {})} | custom-call | flops 1000000 | bytes 6000000 | tf_op jit(solution)/shard_map/write_last/pallas_call | solution.py:611
  (29 shorter events, 1.9 us)
Async XLA Ops:
  7.4 6.0 %copy-start.1 = (bf16[1,256,4096]{2,1,0:T(8,128)(2,1)S(1)}, bf16[1,256,4096]{2,1,0:T(8,128)(2,1)}, u32[]{:S(2)}) copy-start(bf16[1,256,4096]{2,1,0:T(8,128)(2,1)} %param.15) | copy-start | bytes 6291460
  7.4 22.3 %all-to-all-start = ((bf16[8,272,256]{2,1,0:T(8,128)(2,1)}), bf16[8,272,256]{2,1,0:T(8,128)(2,1)}, u32[]{:S(2)}, u32[]{:S(2)}) async-start(bf16[8,272,256]{2,1,0:T(8,128)(2,1)} %get-tuple-element.32), calls=%async_computation | async-start | bytes 2228224 | tf_op jit(solution)/shard_map/all_to_all | solution.py:640
  14.6 25.8 %collective-permute-start.2 = (bf16[256,1024]{1,0:T(8,128)(2,1)}, bf16[256,1024]{1,0:T(8,128)(2,1)S(1)}, u32[]{:S(2)}, u32[]{:S(2)}) collective-permute-start(bf16[256,1024]{1,0:T(8,128)(2,1)} %get-tuple-element.64), channel_id=1, source_target_pairs={{0,40},{8,32},{32,8},{40,0},{1,41},{9,33},{33,9},{41,1},{2,42},{10... | collective-permute-start | bytes 1572872 | tf_op jit(solution)/shard_map/ppermute | solution.py:656
  17.1 23.5 %collective-permute-start = (bf16[256,1024]{1,0:T(8,128)(2,1)}, bf16[256,1024]{1,0:T(8,128)(2,1)}, u32[]{:S(2)}, u32[]{:S(2)}) collective-permute-start(bf16[256,1024]{1,0:T(8,128)(2,1)} %get-tuple-element.65), channel_id=1, source_target_pairs={{0,32},{32,0},{1,33},{33,1},{2,34},{34,2},{3,35},{35,3},{4,36},{36... | collective-permute-start | bytes 1572872 | tf_op jit(solution)/shard_map/ppermute | solution.py:652
  17.1 23.5 %collective-permute-start.1 = (bf16[256,1024]{1,0:T(8,128)(2,1)}, bf16[256,1024]{1,0:T(8,128)(2,1)}, u32[]{:S(2)}, u32[]{:S(2)}) collective-permute-start(bf16[256,1024]{1,0:T(8,128)(2,1)} %get-tuple-element.66), channel_id=1, source_target_pairs={{0,8},{8,0},{1,9},{9,1},{2,10},{10,2},{3,11},{11,3},{4,12},{12,4},... | collective-permute-start | bytes 1572872 | tf_op jit(solution)/shard_map/ppermute | solution.py:644
  18.2 22.2 %collective-permute-start.3 = (bf16[8,512]{1,0:T(8,128)(2,1)S(1)}, bf16[8,512]{1,0:T(8,128)(2,1)S(1)}, u32[]{:S(2)}, u32[]{:S(2)}) collective-permute-start(bf16[8,512]{1,0:T(8,128)(2,1)S(1)} %slice_bitcast_fusion), channel_id=1, source_target_pairs={{0,1},{1,2},{2,3},{3,4},{4,5},{5,6},{6,7},{8,9},{9,10},{10,11},{11... | collective-permute-start | bytes 24584 | tf_op jit(solution)/shard_map/ppermute | solution.py:648
  22.6 17.8 %collective-permute-start.4 = (f32[8,512]{1,0:T(8,128)S(1)}, f32[8,512]{1,0:T(8,128)S(1)}, u32[]{:S(2)}, u32[]{:S(2)}) collective-permute-start(f32[8,512]{1,0:T(8,128)S(1)} %slice.10), channel_id=1, source_target_pairs={{1,0},{2,1},{3,2},{4,3},{5,4},{6,5},{7,6},{9,8},{10,9},{11,10},{12... | collective-permute-start | bytes 49160 | tf_op jit(solution)/shard_map/ppermute | solution.py:648
  40.4 14.8 %copy-start.9 = (bf16[8,512]{1,0:T(8,128)(2,1)}, bf16[8,512]{1,0:T(8,128)(2,1)S(1)}, u32[]{:S(2)}) copy-start(bf16[8,512]{1,0:T(8,128)(2,1)S(1)} %collective-permute-done.3.edge) | copy-start | bytes 24580
  40.4 14.8 %copy-start.8 = (f32[8,512]{1,0:T(8,128)}, f32[8,512]{1,0:T(8,128)S(1)}, u32[]{:S(2)}) copy-start(f32[8,512]{1,0:T(8,128)S(1)} %collective-permute-done.4.later) | copy-start | bytes 49156
  40.4 14.7 %copy-start.4 = (bf16[256,1024]{1,0:T(8,128)(2,1)}, bf16[256,1024]{1,0:T(8,128)(2,1)S(1)}, u32[]{:S(2)}) copy-start(bf16[256,1024]{1,0:T(8,128)(2,1)S(1)} %collective-permute-done.2.g11) | copy-start | bytes 1572868
  40.5 17.3 %all-to-all-start.1 = ((bf16[8,400,128]{2,1,0:T(8,128)(2,1)}), bf16[8,400,128]{2,1,0:T(8,128)(2,1)S(1)}, u32[]{:S(2)}, u32[]{:S(2)}) async-start(bf16[8,400,128]{2,1,0:T(8,128)(2,1)} %conv.1), calls=%async_computation.1 | async-start | bytes 1638400 | tf_op jit(solution)/shard_map/all_to_all | solution.py:640
  57.8 0.9 copy-start.2
  60.9 10.0 %collective-permute-start.5 = (bf16[256,768]{1,0:T(8,128)(2,1)}, bf16[256,768]{1,0:T(8,128)(2,1)S(1)}, u32[]{:S(2)}, u32[]{:S(2)}) collective-permute-start(bf16[256,768]{1,0:T(8,128)(2,1)} %get-tuple-element.43), channel_id=1, source_target_pairs={{0,32},{32,0},{1,33},{33,1},{2,34},{34,2},{3,35},{35,3},{4,36},{36... | collective-permute-start | bytes 1179656 | tf_op jit(solution)/shard_map/ppermute | solution.py:652
  62.8 10.4 %collective-permute-start.6 = (bf16[256,512]{1,0:T(8,128)(2,1)}, bf16[256,512]{1,0:T(8,128)(2,1)S(1)}, u32[]{:S(2)}, u32[]{:S(2)}) collective-permute-start(bf16[256,512]{1,0:T(8,128)(2,1)} %get-tuple-element.49.m00), channel_id=1, source_target_pairs={{0,8},{8,0},{1,9},{9,1},{2,10},{10,2},{3,11},{11,3},{4,12},{12,4},... | collective-permute-start | bytes 786440 | tf_op jit(solution)/shard_map/ppermute | solution.py:644
  70.9 3.5 %copy-start.3 = (bf16[256,768]{1,0:T(8,128)(2,1)}, bf16[256,768]{1,0:T(8,128)(2,1)S(1)}, u32[]{:S(2)}) copy-start(bf16[256,768]{1,0:T(8,128)(2,1)S(1)} %collective-permute-done.5.m01) | copy-start | bytes 1179652
  70.9 3.5 %collective-permute-start.7 = (bf16[256,512]{1,0:T(8,128)(2,1)S(1)}, bf16[256,512]{1,0:T(8,128)(2,1)S(1)}, u32[]{:S(2)}, u32[]{:S(2)}) collective-permute-start(bf16[256,512]{1,0:T(8,128)(2,1)S(1)} %slice.12), channel_id=1, source_target_pairs={{0,8},{8,0},{1,9},{9,1},{2,10},{10,2},{3,11},{11,3},{4,12},{12,4},... | collective-permute-start | bytes 786440 | tf_op jit(solution)/shard_map/ppermute | solution.py:644
  73.2 1.2 copy-start.6
  74.4 0.7 copy-start.7
  79.3 9.6 %copy-start.5 = (bf16[256,512]{1,0:T(8,128)(2,1)S(1)}, bf16[256,512]{1,0:T(8,128)(2,1)}, u32[]{:S(2)}) copy-start(bf16[256,512]{1,0:T(8,128)(2,1)} %get-tuple-element.49.m00) | copy-start | bytes 786436
  79.3 29.4 %all-to-all-start.2 = ((bf16[32,16,1152]{2,1,0:T(8,128)(2,1)}), bf16[32,16,1152]{2,1,0:T(8,128)(2,1)}, u32[]{:S(2)}, u32[]{:S(2)}) async-start(bf16[32,16,1152]{2,1,0:T(8,128)(2,1)} %partial.1), calls=%async_computation.2 | async-start | bytes 2359296 | tf_op jit(solution)/shard_map/all_to_all | solution.py:640
  111.5 35.3 %all-to-all-start.3 = ((bf16[64,16,1152]{2,1,0:T(8,128)(2,1)}), bf16[64,16,1152]{2,1,0:T(8,128)(2,1)S(1)}, u32[]{:S(2)}, u32[]{:S(2)}) async-start(bf16[64,16,1152]{2,1,0:T(8,128)(2,1)} %reduce.1), calls=%async_computation.3 | async-start | bytes 4718592 | tf_op jit(solution)/shard_map/all_to_all | solution.py:640
  146.8 3.7 %copy-start = (bf16[64,16,1152]{2,1,0:T(8,128)(2,1)}, bf16[64,16,1152]{2,1,0:T(8,128)(2,1)S(1)}, u32[]{:S(2)}) copy-start(bf16[64,16,1152]{2,1,0:T(8,128)(2,1)S(1)} %all-to-all-done.3.rows.mine) | copy-start | bytes 7077892
  146.8 8.0 %collective-permute-start.8 = (bf16[64,16,1152]{2,1,0:T(8,128)(2,1)S(1)}, bf16[64,16,1152]{2,1,0:T(8,128)(2,1)}, u32[]{:S(2)}, u32[]{:S(2)}) collective-permute-start(bf16[64,16,1152]{2,1,0:T(8,128)(2,1)S(1)} %all-to-all-done.3.rows.mine), channel_id=1, source_target_pairs={{0,8},{8,0},{1,9},{9,1},{2,10},{10,2},{3,11},{11,3},{4,12},{12,4},... | collective-permute-start | bytes 7077896 | tf_op jit(solution)/shard_map/ppermute | solution.py:644
